TPU v7x, 256 devices: a whole 4x4x8 slice. The times are simulated.
256 devices in a mesh: table: 16 (over x, y), dp: 8 (over z), col: 2 (over core).
Axes of the slice: x: 4, y: 4, z: 8, core: 2. Of those that a mesh axis runs over, the one named last changes fastest.
Arguments:
- table_weights: float32 [32768, 512], P('table', 'col'), may hold values from -6 to 6
- moment_first: float32 [32768, 512], P('table', 'col'), may hold values from -3 to 3
- moment_second: float32 [32768], P('table'), may hold values from 0.1 to 2
- hot_slices: int32 [16, 2], replicated, may hold values from 0 to 31, as said below
- upstream_grad: bfloat16 [131072, 512], P(('table', 'dp'), 'col'), may hold values from -20 to 20
- dedup_map: int32 [131072, 32], P(('table', 'dp')), may hold values from 0 to 4095, as said below
- unique_rows: int32 [128, 16, 256], P(('table', 'dp')), may hold values from 0 to 32767, as said below
- row_counts: int32 [128, 16], P(('table', 'dp')), may hold values from 192 to 256, as said below
Outputs:
- new_weights: float32 [32768, 512], P('table', 'col')
- new_first: float32 [32768, 512], P('table', 'col')
- new_second: float32 [32768], P('table')
Inputs may be any that keep to these rules, and one draw needn't show every extreme that they name: `hot_slices`: each row holds 2 different slice numbers below 32. `unique_rows`: for source device s and owner t, the first row_counts[s, t] entries are different rows r with physical(r) on table index t; the remaining entries are not used. `row_counts`: in every draw some owner receives 256 used slots from every source device. `dedup_map`: an entry in a row of source device s is a used slot t * 256 + k with k < row_counts[s, t].
All inputs are finite; a program needn't handle non-finite values.
Results may differ from a plain program's by a relative error of at most 0.0003.
Values sent between devices are 32-bit elements; how exact they have to be, the bound alone decides.
No kernel may reach another device: no remote copies, remote signals or barrier semaphores. Data moves between devices by JAX's collectives and lax.ppermute only.
A program may use at most 64 MiB of HBM per device.

v0:
```python
import jax
import jax.numpy as jnp
from jax import lax
from jax.sharding import PartitionSpec as P

SLICE = 64


beta_one = 0.9
beta_two = 0.99
learn_rate = 0.1
eps_value = 1e-08


def partner_2(block, axis, distance):
    count = lax.axis_size(axis)
    route = []
    for low in range(count):
        high = low | 1 << distance
        if high != low and high < count:
            route += [(low, high), (high, low)]
    return lax.ppermute(block, axis, route)


def local_targets(logical_rows, hot_slices, rows_dev):
    n_table = hot_slices.shape[0]
    row_owner = logical_rows // rows_dev
    local_row = logical_rows % rows_dev
    row_piece = local_row // SLICE
    row_offset = local_row % SLICE
    matches = hot_slices[row_owner] == row_piece[..., None]
    partner = (row_owner + n_table // 2) % n_table
    partner_piece = jnp.sum(jnp.where(matches, hot_slices[partner], 0), axis=-1)
    return jnp.where(jnp.any(matches, axis=-1), partner_piece * SLICE + row_offset, local_row)


def adam_rows(weights, first, second, gradient, squares, full_width):
    new_second = beta_two * second + (1.0 - beta_two) * (squares / full_width)
    new_first = beta_one * first + (1.0 - beta_one) * gradient
    scaled = jnp.sqrt(new_second / (1.0 - beta_two**8)) + eps_value
    new_weights = weights - learn_rate * (new_first / (1.0 - beta_one**8)) / scaled[:, None]
    return (new_weights, new_first, new_second)


def on_device(
    table_weights,
    moment_first,
    moment_second,
    hot_slices,
    upstream_grad,
    dedup_map,
    unique_rows,
    row_counts,
):
    n_table = lax.axis_size("table")
    position = lax.axis_index("table")
    rows_dev, col_width = table_weights.shape
    own_hot = hot_slices[position]
    n_hots = own_hot.shape[0]
    starts = [own_hot[k] * SLICE for k in range(n_hots)]
    out_weights = jnp.stack(
        [lax.dynamic_slice_in_dim(table_weights, starts[k], SLICE, 0) for k in range(n_hots)]
    )
    out_first = jnp.stack(
        [lax.dynamic_slice_in_dim(moment_first, starts[k], SLICE, 0) for k in range(n_hots)]
    )
    out_second = jnp.stack(
        [lax.dynamic_slice_in_dim(moment_second, starts[k], SLICE, 0) for k in range(n_hots)]
    )
    swap_bit = n_table.bit_length() - 2
    incoming = partner_2((out_weights, out_first, out_second), "table", swap_bit)
    placed_weights = table_weights
    placed_first = moment_first
    placed_second = moment_second
    for k in range(n_hots):
        placed_weights = lax.dynamic_update_slice_in_dim(
            placed_weights, incoming[0][k], starts[k], 0
        )
        placed_first = lax.dynamic_update_slice_in_dim(placed_first, incoming[1][k], starts[k], 0)
        placed_second = lax.dynamic_update_slice_in_dim(placed_second, incoming[2][k], starts[k], 0)
    slot_cap = unique_rows.shape[2]
    valid = jnp.arange(slot_cap)[None, :] < row_counts[0][:, None]
    targets = jnp.where(valid, local_targets(unique_rows[0], hot_slices, rows_dev), rows_dev)
    slot_iota = jnp.arange(slot_cap)

    def owner_block(carry, owner):
        wanted = slot_iota + owner * slot_cap
        tally = jnp.sum(
            (dedup_map[None, :, :] == wanted[:, None, None]).astype(jnp.float32), axis=2
        )
        block = jnp.dot(
            tally.astype(jnp.bfloat16), upstream_grad, preferred_element_type=jnp.float32
        )
        return (carry, block)

    _, slot_grad = lax.scan(owner_block, 0, jnp.arange(n_table))
    got_grad, got_target = (
        lax.all_to_all(slot_grad, "table", split_axis=0, concat_axis=0, tiled=True),
        lax.all_to_all(targets, "table", split_axis=0, concat_axis=0, tiled=True),
    )
    row_iota = jnp.arange(rows_dev)

    def add_source(total, inputs):
        grad_block, target_block = inputs
        select = (row_iota[:, None] == target_block[None, :]).astype(jnp.float32)
        return (
            total
            + jnp.dot(
                select,
                grad_block,
                precision=lax.Precision.HIGHEST,
                preferred_element_type=jnp.float32,
            ),
            None,
        )

    dense, _ = lax.scan(
        add_source, jnp.zeros((rows_dev, col_width), jnp.float32), (got_grad, got_target)
    )
    full_width = col_width * lax.axis_size("col")
    gradient = lax.psum(dense, "dp")
    squares = lax.psum(jnp.sum(gradient * gradient, axis=1), "col")
    new_weights, new_first, new_second = adam_rows(
        placed_weights, placed_first, placed_second, gradient, squares, full_width
    )
    return (new_weights, new_first, new_second)


def solution(mesh):
    placed = (
        P("table", "col"),
        P("table", "col"),
        P("table"),
        P(),
        P(("table", "dp"), "col"),
        P(("table", "dp"), None),
        P(("table", "dp"), None, None),
        P(("table", "dp"), None),
    )
    return jax.shard_map(
        on_device,
        mesh=mesh,
        in_specs=placed,
        out_specs=(P("table", "col"), P("table", "col"), P("table")),
        check_vma=False,
    )
```

profile of v0, /device:TPU:2, one launch (start us, length us, event | category | flops | bytes accessed | tf_op | source)
XLA Modules:
  0.0 477.9 jit_solution(15004162492710192044)
XLA Ops:
  7.2 3.2 copy.52
  10.4 1.3 copy.53
  11.9 10.8 %gather_fusion = s32[4096,2]{1,0:T(8,128)S(1)} fusion(s32[16,2]{1,0:T(8,128)S(1)} %copy.21, s32[4096]{0:T(1024)S(1)} %broadcast_clamp_fusion.1), kind=kCustom, calls=%fused_computation | custom fusion | bytes 81920 | tf_op jit(solution)/shard_map/gather | solution.py:31
  22.7 14.1 %gather_fusion.1 = s32[4096,2]{1,0:T(8,128)} fusion(s32[16,2]{1,0:T(8,128)S(1)} %copy.21, s32[4096]{0:T(1024)S(1)} %broadcast_clamp_fusion), kind=kCustom, calls=%fused_computation.1 | custom fusion | bytes 81920 | tf_op jit(solution)/shard_map/gather | solution.py:33
  36.8 1.3 fusion.29
  39.8 7.5 %all-to-all-start = ((s32[16,1,256]{2,1,0:T(1,128)}), s32[16,1,256]{2,1,0:T(1,128)S(1)}, u32[]{:S(2)}, u32[]{:S(2)}) async-start(s32[16,1,256]{2,1,0:T(1,128)} %copy.23), calls=%async_computation | async-start | bytes 32768 | tf_op jit(solution)/shard_map/all_to_all | solution.py:99
  47.3 217.9 %while.22 = (s32[]{:T(128)}, f32[16,256,256]{2,1,0:T(8,128)}, s32[1024,32]{0,1:T(8,128)S(1)}, s32[16]{0:T(128)S(1)}, bf16[1024,256]{1,0:T(8,128)(2,1)S(1)}, /*index=5*/s32[]{:T(128)}, s32[1]{0:T(128)}) while((s32[]{:T(128)}, f32[16,256,256]{2,1,0:T(8,128)}, s32[1024,32]{0,1:T(8,128)S(1)}, s32[16]{0:T(128)S(1)}, ...), condition=%wide.region_2.3_spmd.clone, body=%wide.region_0.2_spmd.clone.sunk | while | flops 159121664 | bytes 1968745 | solution.py:96
  48.8 11.3 %convert_reduce_fusion.2 = bf16[256,1024]{1,0:T(8,128)(2,1)S(1)} fusion(s32[1024,32]{0,1:T(8,128)S(1)} %get-tuple-element.201, s32[256]{0:T(256)S(1)} %iota_add_fusion.2), kind=kLoop, calls=%fused_computation.4.clone.1 | loop fusion | flops 24903680 | bytes 656384 | tf_op jit(solution)/shard_map/while/body/eval_jaxpr/reduce_sum | solution.py:88
  60.1 1.0 fusion.39
  62.4 11.3 %convert_reduce_fusion.2 = bf16[256,1024]{1,0:T(8,128)(2,1)S(1)} fusion(s32[1024,32]{0,1:T(8,128)S(1)} %get-tuple-element.201, s32[256]{0:T(256)S(1)} %iota_add_fusion.2), kind=kLoop, calls=%fused_computation.4.clone.1 | loop fusion | flops 24903680 | bytes 656384 | tf_op jit(solution)/shard_map/while/body/eval_jaxpr/reduce_sum | solution.py:88
  73.7 1.0 fusion.39
  76.0 11.3 %convert_reduce_fusion.2 = bf16[256,1024]{1,0:T(8,128)(2,1)S(1)} fusion(s32[1024,32]{0,1:T(8,128)S(1)} %get-tuple-element.201, s32[256]{0:T(256)S(1)} %iota_add_fusion.2), kind=kLoop, calls=%fused_computation.4.clone.1 | loop fusion | flops 24903680 | bytes 656384 | tf_op jit(solution)/shard_map/while/body/eval_jaxpr/reduce_sum | solution.py:88
  87.3 1.0 fusion.39
  89.6 11.3 %convert_reduce_fusion.2 = bf16[256,1024]{1,0:T(8,128)(2,1)S(1)} fusion(s32[1024,32]{0,1:T(8,128)S(1)} %get-tuple-element.201, s32[256]{0:T(256)S(1)} %iota_add_fusion.2), kind=kLoop, calls=%fused_computation.4.clone.1 | loop fusion | flops 24903680 | bytes 656384 | tf_op jit(solution)/shard_map/while/body/eval_jaxpr/reduce_sum | solution.py:88
  100.9 1.0 fusion.39
  103.2 11.3 %convert_reduce_fusion.2 = bf16[256,1024]{1,0:T(8,128)(2,1)S(1)} fusion(s32[1024,32]{0,1:T(8,128)S(1)} %get-tuple-element.201, s32[256]{0:T(256)S(1)} %iota_add_fusion.2), kind=kLoop, calls=%fused_computation.4.clone.1 | loop fusion | flops 24903680 | bytes 656384 | tf_op jit(solution)/shard_map/while/body/eval_jaxpr/reduce_sum | solution.py:88
  114.5 1.0 fusion.39
  116.8 11.3 %convert_reduce_fusion.2 = bf16[256,1024]{1,0:T(8,128)(2,1)S(1)} fusion(s32[1024,32]{0,1:T(8,128)S(1)} %get-tuple-element.201, s32[256]{0:T(256)S(1)} %iota_add_fusion.2), kind=kLoop, calls=%fused_computation.4.clone.1 | loop fusion | flops 24903680 | bytes 656384 | tf_op jit(solution)/shard_map/while/body/eval_jaxpr/reduce_sum | solution.py:88
  128.1 1.0 fusion.39
  130.4 11.3 %convert_reduce_fusion.2 = bf16[256,1024]{1,0:T(8,128)(2,1)S(1)} fusion(s32[1024,32]{0,1:T(8,128)S(1)} %get-tuple-element.201, s32[256]{0:T(256)S(1)} %iota_add_fusion.2), kind=kLoop, calls=%fused_computation.4.clone.1 | loop fusion | flops 24903680 | bytes 656384 | tf_op jit(solution)/shard_map/while/body/eval_jaxpr/reduce_sum | solution.py:88
  141.7 1.0 fusion.39
  144.0 11.3 %convert_reduce_fusion.2 = bf16[256,1024]{1,0:T(8,128)(2,1)S(1)} fusion(s32[1024,32]{0,1:T(8,128)S(1)} %get-tuple-element.201, s32[256]{0:T(256)S(1)} %iota_add_fusion.2), kind=kLoop, calls=%fused_computation.4.clone.1 | loop fusion | flops 24903680 | bytes 656384 | tf_op jit(solution)/shard_map/while/body/eval_jaxpr/reduce_sum | solution.py:88
  157.6 11.3 %convert_reduce_fusion.2 = bf16[256,1024]{1,0:T(8,128)(2,1)S(1)} fusion(s32[1024,32]{0,1:T(8,128)S(1)} %get-tuple-element.201, s32[256]{0:T(256)S(1)} %iota_add_fusion.2), kind=kLoop, calls=%fused_computation.4.clone.1 | loop fusion | flops 24903680 | bytes 656384 | tf_op jit(solution)/shard_map/while/body/eval_jaxpr/reduce_sum | solution.py:88
  168.9 1.0 fusion.39
  171.2 11.3 %convert_reduce_fusion.2 = bf16[256,1024]{1,0:T(8,128)(2,1)S(1)} fusion(s32[1024,32]{0,1:T(8,128)S(1)} %get-tuple-element.201, s32[256]{0:T(256)S(1)} %iota_add_fusion.2), kind=kLoop, calls=%fused_computation.4.clone.1 | loop fusion | flops 24903680 | bytes 656384 | tf_op jit(solution)/shard_map/while/body/eval_jaxpr/reduce_sum | solution.py:88
  182.5 1.0 fusion.39
  184.8 11.3 %convert_reduce_fusion.2 = bf16[256,1024]{1,0:T(8,128)(2,1)S(1)} fusion(s32[1024,32]{0,1:T(8,128)S(1)} %get-tuple-element.201, s32[256]{0:T(256)S(1)} %iota_add_fusion.2), kind=kLoop, calls=%fused_computation.4.clone.1 | loop fusion | flops 24903680 | bytes 656384 | tf_op jit(solution)/shard_map/while/body/eval_jaxpr/reduce_sum | solution.py:88
  196.1 1.0 fusion.39
  198.4 11.3 %convert_reduce_fusion.2 = bf16[256,1024]{1,0:T(8,128)(2,1)S(1)} fusion(s32[1024,32]{0,1:T(8,128)S(1)} %get-tuple-element.201, s32[256]{0:T(256)S(1)} %iota_add_fusion.2), kind=kLoop, calls=%fused_computation.4.clone.1 | loop fusion | flops 24903680 | bytes 656384 | tf_op jit(solution)/shard_map/while/body/eval_jaxpr/reduce_sum | solution.py:88
  209.7 1.0 fusion.39
  212.0 11.3 %convert_reduce_fusion.2 = bf16[256,1024]{1,0:T(8,128)(2,1)S(1)} fusion(s32[1024,32]{0,1:T(8,128)S(1)} %get-tuple-element.201, s32[256]{0:T(256)S(1)} %iota_add_fusion.2), kind=kLoop, calls=%fused_computation.4.clone.1 | loop fusion | flops 24903680 | bytes 656384 | tf_op jit(solution)/shard_map/while/body/eval_jaxpr/reduce_sum | solution.py:88
  225.6 11.3 %convert_reduce_fusion.2 = bf16[256,1024]{1,0:T(8,128)(2,1)S(1)} fusion(s32[1024,32]{0,1:T(8,128)S(1)} %get-tuple-element.201, s32[256]{0:T(256)S(1)} %iota_add_fusion.2), kind=kLoop, calls=%fused_computation.4.clone.1 | loop fusion | flops 24903680 | bytes 656384 | tf_op jit(solution)/shard_map/while/body/eval_jaxpr/reduce_sum | solution.py:88
  236.9 1.0 fusion.39
  239.2 11.3 %convert_reduce_fusion.2 = bf16[256,1024]{1,0:T(8,128)(2,1)S(1)} fusion(s32[1024,32]{0,1:T(8,128)S(1)} %get-tuple-element.201, s32[256]{0:T(256)S(1)} %iota_add_fusion.2), kind=kLoop, calls=%fused_computation.4.clone.1 | loop fusion | flops 24903680 | bytes 656384 | tf_op jit(solution)/shard_map/while/body/eval_jaxpr/reduce_sum | solution.py:88
  250.5 1.0 fusion.39
  252.8 11.3 %convert_reduce_fusion.2 = bf16[256,1024]{1,0:T(8,128)(2,1)S(1)} fusion(s32[1024,32]{0,1:T(8,128)S(1)} %get-tuple-element.201, s32[256]{0:T(256)S(1)} %iota_add_fusion.2), kind=kLoop, calls=%fused_computation.4.clone.1 | loop fusion | flops 24903680 | bytes 656384 | tf_op jit(solution)/shard_map/while/body/eval_jaxpr/reduce_sum | solution.py:88
  264.1 1.0 fusion.39
  265.2 7.2 %all-to-all-start.1 = ((f32[16,256,256]{2,1,0:T(8,128)}), f32[16,256,256]{2,1,0:T(8,128)}, u32[]{:S(2)}, u32[]{:S(2)}) async-start(f32[16,256,256]{2,1,0:T(8,128)} %get-tuple-element.62), calls=%async_computation.1 | async-start | bytes 8388608 | tf_op jit(solution)/shard_map/all_to_all | solution.py:98
  272.5 53.1 %all-to-all-done.1 = f32[16,256,256]{2,1,0:T(8,128)} async-done(((f32[16,256,256]{2,1,0:T(8,128)}), f32[16,256,256]{2,1,0:T(8,128)}, u32[]{:S(2)}, u32[]{:S(2)}) %all-to-all-start.1) | async-done | bytes 4194336 | tf_op jit(solution)/shard_map/all_to_all | solution.py:98
  325.6 45.4 %while.23 = (s32[]{:T(128)}, f32[2048,256]{1,0:T(8,128)S(1)}, s32[16,256]{1,0:T(8,128)S(1)}, f32[16,256,256]{2,1,0:T(8,128)}, s32[]{:T(128)}, /*index=5*/s32[]{:T(128)}) while((s32[]{:T(128)}, f32[2048,256]{1,0:T(8,128)S(1)}, s32[16,256]{1,0:T(8,128)S(1)}, f32[16,256,256]{2,1,0:T(8,128)}, s32[]{:T(128)}, /*index=5*/s32[]{:T(128)}) %tuple.62), condition=%wide.region_6.7_spmd.clone, body=%wide.region_5.6_spmd.clone.sunk | while | flops 1612185600 | bytes 4460115 | solution.py:117
  325.6 2.8 convolution_add_fusion.2
  328.4 2.8 convolution_add_fusion.2
  331.3 2.8 convolution_add_fusion.2
  334.1 2.8 convolution_add_fusion.2
  336.9 2.8 convolution_add_fusion.2
  339.8 2.8 convolution_add_fusion.2
  342.6 2.8 convolution_add_fusion.2
  345.5 2.8 convolution_add_fusion.2
  348.3 2.8 convolution_add_fusion.2
  351.1 2.8 convolution_add_fusion.2
  354.0 2.8 convolution_add_fusion.2
  356.8 2.8 convolution_add_fusion.2
  359.7 2.8 convolution_add_fusion.2
  362.5 2.8 convolution_add_fusion.2
  365.3 2.8 convolution_add_fusion.2
  368.2 2.8 convolution_add_fusion.2
  371.0 1.3 copy-done
  375.2 5.0 %collective-permute-start.1 = (f32[2,64,256]{2,1,0:T(8,128)S(1)}, f32[2,64,256]{2,1,0:T(8,128)S(1)}, u32[]{:S(2)}, u32[]{:S(2)}) collective-permute-start(f32[2,64,256]{2,1,0:T(8,128)S(1)} %pad_maximum_fusion.1), channel_id=1, source_target_pairs={{0,128},{128,0},{16,144},{144,16},{32,160},{160,32},{48,176},{176,... | collective-permute-start | bytes 393224 | tf_op jit(solution)/shard_map/ppermute | solution.py:22
  380.4 3.6 collective-permute-start
  384.0 1.4 collective-permute-done.2
  388.2 73.0 %all-reduce.2.cloned.1.call-done = f32[2048,256]{1,0:T(8,128)} async-done(((f32[2048,256]{1,0:T(8,128)}), f32[2048,256]{1,0:T(8,128)}) %all-reduce.2.cloned.1.call-update) | async-done | bytes 2097168 | tf_op jit(solution)/shard_map/psum | solution.py:121
  461.3 1.9 multiply_reduce_fusion
  463.2 2.5 psum.15
  466.3 4.8 divide_subtract_fusion
  (104 shorter events, 19.0 us)
Async XLA Ops:
  7.2 3.2 copy-start.5
  10.4 1.3 copy-start.7
  10.4 1.3 copy-start.6
  10.4 1.4 copy-start.8
  36.8 1.6 copy-start.3
  36.8 2.3 copy-start.9
  36.8 10.5 %copy-start.1 = (bf16[1024,256]{1,0:T(8,128)(2,1)S(1)}, bf16[1024,256]{1,0:T(8,128)(2,1)}, u32[]{:S(2)}) copy-start(bf16[1024,256]{1,0:T(8,128)(2,1)} %param.16) | copy-start | bytes 1572868
  36.8 10.5 %copy-start.4 = (s32[1024,32]{0,1:T(8,128)S(1)}, s32[1024,32]{0,1:T(8,128)}, u32[]{:S(2)}) copy-start(s32[1024,32]{0,1:T(8,128)} %param.17) | copy-start | bytes 393220
  39.8 225.4 %all-to-all-start = ((s32[16,1,256]{2,1,0:T(1,128)}), s32[16,1,256]{2,1,0:T(1,128)S(1)}, u32[]{:S(2)}, u32[]{:S(2)}) async-start(s32[16,1,256]{2,1,0:T(1,128)} %copy.23), calls=%async_computation | async-start | bytes 32768 | tf_op jit(solution)/shard_map/all_to_all | solution.py:99
  265.2 60.4 %all-to-all-start.1 = ((f32[16,256,256]{2,1,0:T(8,128)}), f32[16,256,256]{2,1,0:T(8,128)}, u32[]{:S(2)}, u32[]{:S(2)}) async-start(f32[16,256,256]{2,1,0:T(8,128)} %get-tuple-element.62), calls=%async_computation.1 | async-start | bytes 8388608 | tf_op jit(solution)/shard_map/all_to_all | solution.py:98
  272.4 188.8 %all-reduce.2.cloned.1.call-start = ((), (), s32[]{:S(2)}) async-start(), calls=%async_computation.2 | async-start | bytes 4194304 | tf_op jit(solution)/shard_map/psum | solution.py:121
  371.0 1.3 copy-start
  375.2 10.5 %collective-permute-start.1 = (f32[2,64,256]{2,1,0:T(8,128)S(1)}, f32[2,64,256]{2,1,0:T(8,128)S(1)}, u32[]{:S(2)}, u32[]{:S(2)}) collective-permute-start(f32[2,64,256]{2,1,0:T(8,128)S(1)} %pad_maximum_fusion.1), channel_id=1, source_target_pairs={{0,128},{128,0},{16,144},{144,16},{32,160},{160,32},{48,176},{176,... | collective-permute-start | bytes 393224 | tf_op jit(solution)/shard_map/ppermute | solution.py:22
  380.3 5.1 %collective-permute-start.2 = (f32[2,64]{1,0:T(2,128)S(1)}, f32[2,64]{1,0:T(2,128)S(1)}, u32[]{:S(2)}, u32[]{:S(2)}) collective-permute-start(f32[2,64]{1,0:T(2,128)S(1)} %pad_maximum_fusion.2), channel_id=1, source_target_pairs={{0,128},{128,0},{16,144},{144,16},{32,160},{160,32},{48,176},{176,... | collective-permute-start | bytes 1544 | tf_op jit(solution)/shard_map/ppermute | solution.py:22
  380.4 6.6 %collective-permute-start = (f32[2,64,256]{2,1,0:T(8,128)S(1)}, f32[2,64,256]{2,1,0:T(8,128)S(1)}, u32[]{:S(2)}, u32[]{:S(2)}) collective-permute-start(f32[2,64,256]{2,1,0:T(8,128)S(1)} %pad_maximum_fusion), channel_id=1, source_target_pairs={{0,128},{128,0},{16,144},{144,16},{32,160},{160,32},{48,176},{176,... | collective-permute-start | bytes 393224 | tf_op jit(solution)/shard_map/ppermute | solution.py:22
  388.2 78.1 %copy-start.2 = (f32[2048,256]{1,0:T(8,128)S(1)}, f32[2048,256]{1,0:T(8,128)}, u32[]{:S(2)}) copy-start(f32[2048,256]{1,0:T(8,128)} %fusion.12) | copy-start | bytes 6291460
Sparse Core Ops, SparseCore 0:
  372.5 88.7 all-reduce.1
where the time goes:
time: 480 us; the launch traced here: 478 us
  other arithmetic  191 us (40%)
  waiting for transfers between devices  128 us (27%)
  matrix products  60.9 us (13%)
  local copies, waits for them, and re-layouts  45.9 us (10%)
  starting transfers between devices  23.5 us (5%)
  between operations  15.5 us (3%)
  loops' own time  11.2 us (2%)
    reduce_sum x16, other arithmetic, owner_block(): jnp.sum((dedup_map[None, :, :] == wanted[:, None, None]).astype(jnp.float...  181 us
    psum x1, waiting for transfers between devices, on_device(): gradient = lax.psum(dense, 'dp')  73 us
    all_to_all x1, waiting for transfers between devices, on_device(): lax.all_to_all(slot_grad, 'table', split_axis=0, concat_axis=0, tiled=True)  53.1 us
    dot_general x16, matrix products, add_source(): jnp.dot(select, grad_block, precision=lax.Precision.HIGHEST, preferred_el...  44.7 us
    dot_general x16, matrix products, owner_block(): jnp.dot(tally.astype(jnp.bfloat16), upstream_grad, preferred_element_type...  16.2 us
    gather x1, local copies, waits for them, and re-layouts, local_targets(): partner_piece = jnp.sum(jnp.where(matches, hot_slices[partner], 0), axis=-1)  14.1 us
    gather x1, local copies, waits for them, and re-layouts, local_targets(): matches = hot_slices[row_owner] == row_piece[..., None]  10.8 us
    another operation x1, loops' own time, on_device(): _, slot_grad = lax.scan(owner_block, 0, jnp.arange(n_table))  10.7 us
  transfers between devices with their start and end apart: 6, of which 4 were waited for; matrix products, arithmetic and copies ran while one was open for 44% of the time, Pallas kernels for 0%

commit v1 on v0

--- a/solution.py
+++ b/solution.py
@@ -1,15 +1,22 @@
+import functools
 import jax
 import jax.numpy as jnp
 from jax import lax
+from jax.experimental import pallas as pl
+from jax.experimental.pallas import tpu as pltpu
 from jax.sharding import PartitionSpec as P
 
 SLICE = 64
-
+LOW = 256
+GROUP = 8
+TARGET_ROWS = 8
 
 beta_one = 0.9
 beta_two = 0.99
 learn_rate = 0.1
 eps_value = 1e-08
+
+NT = (((1,), (1,)), ((), ()))
 
 
 def partner_2(block, axis, distance):
@@ -22,16 +29,123 @@
     return lax.ppermute(block, axis, route)
 
 
-def local_targets(logical_rows, hot_slices, rows_dev):
-    n_table = hot_slices.shape[0]
-    row_owner = logical_rows // rows_dev
-    local_row = logical_rows % rows_dev
-    row_piece = local_row // SLICE
-    row_offset = local_row % SLICE
-    matches = hot_slices[row_owner] == row_piece[..., None]
-    partner = (row_owner + n_table // 2) % n_table
-    partner_piece = jnp.sum(jnp.where(matches, hot_slices[partner], 0), axis=-1)
-    return jnp.where(jnp.any(matches, axis=-1), partner_piece * SLICE + row_offset, local_row)
+def one_hot(positions, wanted):
+    return jnp.where(positions == wanted, 1.0, 0.0).astype(jnp.bfloat16)
+
+
+def slot_kernel(map_ref, grad_ref, target_ref, out_ref, tally):
+    groups, span = map_ref.shape
+    highs = tally.shape[0]
+    bag = span // GROUP
+    sample = lax.broadcasted_iota(jnp.int32, (1, span), 1) // bag
+    left_at = lax.broadcasted_iota(jnp.int32, (highs * GROUP, span), 0)
+    right_at = lax.broadcasted_iota(jnp.int32, (LOW, span), 0)
+
+    def count(step, carry):
+        first = pl.multiple_of(step * 8, 8)
+        slots = map_ref[pl.ds(first, 8), :]
+        for pair in range(4):
+            halves = []
+            for which in range(2):
+                at = 2 * pair + which
+                row = slots[at : at + 1, :]
+                left = one_hot(left_at, (row // LOW) * GROUP + sample)
+                right = one_hot(right_at, row % LOW)
+                part = lax.dot_general(left, right, NT, preferred_element_type=jnp.float32)
+                halves.append(part.reshape(highs, GROUP, LOW))
+            both = jnp.concatenate(halves, axis=1).astype(jnp.bfloat16)
+            begin = pl.multiple_of(first * GROUP + pair * 2 * GROUP, 2 * GROUP)
+            tally[:, pl.ds(begin, 2 * GROUP), :] = both
+        return carry
+
+    lax.fori_loop(0, groups // 8, count, 0)
+    columns = grad_ref.shape[0]
+
+    def total(owner, carry):
+        out_ref[owner, :columns, :] = jnp.dot(
+            grad_ref[...], tally[owner], preferred_element_type=jnp.float32
+        )
+        out_ref[owner, columns:, :] = jnp.broadcast_to(
+            target_ref[pl.ds(owner, 1), :], (TARGET_ROWS, LOW)
+        )
+        return carry
+
+    lax.fori_loop(0, highs, total, 0)
+
+
+def slot_sums(slots, grad_t, targets):
+    highs = targets.shape[0]
+    columns, samples = grad_t.shape
+    return pl.pallas_call(
+        slot_kernel,
+        out_shape=jax.ShapeDtypeStruct((highs, columns + TARGET_ROWS, LOW), jnp.float32),
+        in_specs=[pl.BlockSpec(memory_space=pltpu.VMEM)] * 3,
+        out_specs=pl.BlockSpec(memory_space=pltpu.VMEM),
+        scratch_shapes=[pltpu.VMEM((highs, samples, LOW), jnp.bfloat16)],
+        compiler_params=pltpu.CompilerParams(vmem_limit_bytes=40 << 20),
+        name="slot_sums",
+    )(slots, grad_t, targets)
+
+
+def place_kernel(got_ref, out_ref, select, pieces):
+    sources, height, cap = got_ref.shape
+    columns = height - TARGET_ROWS
+    rows = out_ref.shape[0]
+    block = select.shape[0]
+    for source in range(sources):
+        value = got_ref[source, :columns, :]
+        upper = value.astype(jnp.bfloat16)
+        lower = (value - upper.astype(jnp.float32)).astype(jnp.bfloat16)
+        at = source * cap
+        pieces[0, :, at : at + cap] = upper
+        pieces[1, :, at : at + cap] = lower
+    place = lax.broadcasted_iota(jnp.int32, (block, cap), 0)
+
+    def fill(step, carry):
+        start = step * block
+        for source in range(sources):
+            target = got_ref[source, columns : columns + 1, :].astype(jnp.int32)
+            at = source * cap
+            select[:, at : at + cap] = one_hot(place, target - start)
+        chosen = select[...]
+        total = lax.dot_general(chosen, pieces[0], NT, preferred_element_type=jnp.float32)
+        total += lax.dot_general(chosen, pieces[1], NT, preferred_element_type=jnp.float32)
+        out_ref[pl.ds(pl.multiple_of(start, block), block), :] = total
+        return carry
+
+    lax.fori_loop(0, rows // block, fill, 0)
+
+
+def place_sums(got, rows):
+    sources, height, cap = got.shape
+    columns = height - TARGET_ROWS
+    return pl.pallas_call(
+        place_kernel,
+        out_shape=jax.ShapeDtypeStruct((rows, columns), jnp.float32),
+        in_specs=[pl.BlockSpec(memory_space=pltpu.VMEM)],
+        out_specs=pl.BlockSpec(memory_space=pltpu.VMEM),
+        scratch_shapes=[
+            pltpu.VMEM((512, sources * cap), jnp.bfloat16),
+            pltpu.VMEM((2, columns, sources * cap), jnp.bfloat16),
+        ],
+        compiler_params=pltpu.CompilerParams(vmem_limit_bytes=40 << 20),
+        name="place_sums",
+    )(got)
+
+
+def local_targets(unique_rows, row_counts, hot_slices, rows_dev):
+    n_table, n_hots = hot_slices.shape
+    cap = unique_rows.shape[1]
+    partner = (jnp.arange(n_table) + n_table // 2) % n_table
+    partner_hot = jnp.concatenate([hot_slices[n_table // 2 :], hot_slices[: n_table // 2]], axis=0)
+    local_row = unique_rows % rows_dev
+    from_partner = unique_rows // rows_dev == partner[:, None]
+    target = local_row
+    for k in range(n_hots):
+        moved = from_partner & (local_row // SLICE == partner_hot[:, k : k + 1])
+        target = jnp.where(moved, hot_slices[:, k : k + 1] * SLICE + local_row % SLICE, target)
+    valid = jnp.arange(cap)[None, :] < row_counts[:, None]
+    return jnp.where(valid, target, rows_dev)
 
 
 def adam_rows(weights, first, second, gradient, squares, full_width):
@@ -78,45 +192,11 @@
         )
         placed_first = lax.dynamic_update_slice_in_dim(placed_first, incoming[1][k], starts[k], 0)
         placed_second = lax.dynamic_update_slice_in_dim(placed_second, incoming[2][k], starts[k], 0)
-    slot_cap = unique_rows.shape[2]
-    valid = jnp.arange(slot_cap)[None, :] < row_counts[0][:, None]
-    targets = jnp.where(valid, local_targets(unique_rows[0], hot_slices, rows_dev), rows_dev)
-    slot_iota = jnp.arange(slot_cap)
-
-    def owner_block(carry, owner):
-        wanted = slot_iota + owner * slot_cap
-        tally = jnp.sum(
-            (dedup_map[None, :, :] == wanted[:, None, None]).astype(jnp.float32), axis=2
-        )
-        block = jnp.dot(
-            tally.astype(jnp.bfloat16), upstream_grad, preferred_element_type=jnp.float32
-        )
-        return (carry, block)
-
-    _, slot_grad = lax.scan(owner_block, 0, jnp.arange(n_table))
-    got_grad, got_target = (
-        lax.all_to_all(slot_grad, "table", split_axis=0, concat_axis=0, tiled=True),
-        lax.all_to_all(targets, "table", split_axis=0, concat_axis=0, tiled=True),
-    )
-    row_iota = jnp.arange(rows_dev)
-
-    def add_source(total, inputs):
-        grad_block, target_block = inputs
-        select = (row_iota[:, None] == target_block[None, :]).astype(jnp.float32)
-        return (
-            total
-            + jnp.dot(
-                select,
-                grad_block,
-                precision=lax.Precision.HIGHEST,
-                preferred_element_type=jnp.float32,
-            ),
-            None,
-        )
-
-    dense, _ = lax.scan(
-        add_source, jnp.zeros((rows_dev, col_width), jnp.float32), (got_grad, got_target)
-    )
+    targets = local_targets(unique_rows[0], row_counts[0], hot_slices, rows_dev)
+    slots = dedup_map.reshape(-1, GROUP * dedup_map.shape[1])
+    slot_grad = slot_sums(slots, upstream_grad.T, targets.astype(jnp.float32))
+    got = lax.all_to_all(slot_grad, "table", split_axis=0, concat_axis=0, tiled=True)
+    dense = place_sums(got, rows_dev)
     full_width = col_width * lax.axis_size("col")
     gradient = lax.psum(dense, "dp")
     squares = lax.psum(jnp.sum(gradient * gradient, axis=1), "col")

time: 480 us -> 221 us (0.46)
  other arithmetic: 191 us -> 7.52 us
  matrix products: 60.9 us -> 0 us
  local copies, waits for them, and re-layouts: 45.9 us -> 10.5 us
  Pallas kernels: 0 us -> 26.7 us
  loops' own time: 11.2 us -> 0 us
  waiting for transfers between devices: 128 us -> 134 us
    reduce_sum x17 -> x0, other arithmetic: 182 us -> none  [the longest x16 181 us: owner_block(): jnp.sum((dedup_map[None, :, :] == wanted[:, None, None]).astype(jnp.float...]
    dot_general x32 -> x0, matrix products: 60.9 us -> none  [the longest x16 44.7 us: add_source(): jnp.dot(select, grad_block, precision=lax.Precision.HIGHEST, preferred_el...]
    pallas_call x0 -> x2, Pallas kernels: none -> 26.7 us  [the longest x1 13.7 us: place_sums(): pl.pallas_call(place_kernel, out_shape=jax.ShapeDtypeStruct((rows, column...]
    gather x2 -> x0, local copies, waits for them, and re-layouts: 24.9 us -> none  [the longest x1 14.1 us: local_targets(): partner_piece = jnp.sum(jnp.where(matches, hot_slices[partner], 0), axis=-1)]
    another operation x2 -> x0, loops' own time: 11.2 us -> none  [the longest x1 10.7 us: on_device(): _, slot_grad = lax.scan(owner_block, 0, jnp.arange(n_table))]
    dynamic_slice x32 -> x0, local copies, waits for them, and re-layouts: 9.84 us -> none  [the longest x16 9.69 us: on_device(): _, slot_grad = lax.scan(owner_block, 0, jnp.arange(n_table))]
    all_to_all x1 -> x0, starting transfers between devices: 7.48 us -> none  [on_device(): lax.all_to_all(targets, 'table', split_axis=0, concat_axis=0, tiled=True)]
    ppermute x3, starting transfers between devices: 8.74 us -> 15.1 us  [partner_2(): return lax.ppermute(block, axis, route)]
  transfers between devices with their start and end apart: 6 -> 5, of which waited for: 4 -> 4; matrix products, arithmetic and copies ran while one was open for 44% -> 1% of each run, Pallas kernels for 0% -> 0%
where the time goes in v1:
time: 221 us; the launch traced here: 219 us
  waiting for transfers between devices  134 us (61%)
  Pallas kernels  26.7 us (12%)
  starting transfers between devices  22.7 us (10%)
  between operations  15.5 us (7%)
  local copies, waits for them, and re-layouts  10.5 us (5%)
  other arithmetic  7.52 us (3%)
  blocking collectives  2.5 us (1%)
    psum x1, waiting for transfers between devices, on_device(): gradient = lax.psum(dense, 'dp')  75 us
    all_to_all x1, waiting for transfers between devices, on_device(): lax.all_to_all(slot_grad, 'table', split_axis=0, concat_axis=0, tiled=True)  55.8 us
    ppermute x3, starting transfers between devices, partner_2(): return lax.ppermute(block, axis, route)  15.1 us
    pallas_call x1, Pallas kernels, place_sums(): pl.pallas_call(place_kernel, out_shape=jax.ShapeDtypeStruct((rows, column...  13.7 us
    pallas_call x1, Pallas kernels, slot_sums(): pl.pallas_call(slot_kernel, out_shape=jax.ShapeDtypeStruct((highs, column...  12.9 us
    all_to_all x1, starting transfers between devices, on_device(): lax.all_to_all(slot_grad, 'table', split_axis=0, concat_axis=0, tiled=True)  7.48 us
    unnamed x19, local copies, waits for them, and re-layouts  7.22 us
    sub x1, other arithmetic, adam_rows(): weights - learn_rate * (new_first / (1.0 - beta_one ** 8)) / scaled[:, None]  4.77 us
  transfers between devices with their start and end apart: 5, of which 4 were waited for; matrix products, arithmetic and copies ran while one was open for 1% of the time, Pallas kernels for 0%

profile of v1, /device:TPU:2, one launch (start us, length us, event | category | flops | bytes accessed | tf_op | source)
XLA Modules:
  0.0 219.0 jit_solution(13521543276272662781)
XLA Ops:
  7.2 0.7 copy.27
  7.9 0.0 copy-start.1
  7.9 3.2 %copy.25 = f32[2048,256]{1,0:T(8,128)} copy(f32[2048,256]{1,0:T(8,128)} %param.8) | data formatting | bytes 4194304
  11.1 0.0 copy-done.1
  11.1 0.0 copy-start.5
  11.1 0.0 copy-start.2
  11.1 0.0 copy-start.3
  11.1 0.1 copy.26
  11.2 0.0 copy-start.4
  11.2 0.0 copy-start.6
  11.3 0.5 copy-done.5
  11.7 0.1 fusion.10
  11.8 0.1 pad_add_fusion
  11.9 0.2 copy-done.2
  12.1 0.2 copy.14
  12.3 0.0 copy-done.3
  12.3 0.2 copy.13
  12.5 0.2 reshape.34.map_ref
  12.7 0.0 copy-done.4
  12.7 0.0 copy-done.6
  12.8 0.1 select_convert_fusion.target_ref
  12.8 12.9 %slot_sums.1 = f32[16,264,256]{2,1,0:T(8,128)S(1)} custom-call(s32[128,256]{1,0:T(8,128)S(1)} %reshape.34.map_ref, bf16[256,1024]{1,0:T(8,128)(2,1)S(1)} %bitcast.62, f32[16,256]{1,0:T(8,128)S(1)} %select_convert_fusion.target_ref), custom_call_target="tpu_custom_call" | custom-call | tf_op jit(solution)/shard_map/slot_sums/pallas_call | solution.py:79
  25.8 0.0 copy-start
  25.8 2.1 copy-done
  27.8 7.5 %all-to-all-start = ((f32[16,264,256]{2,1,0:T(8,128)}), f32[16,264,256]{2,1,0:T(8,128)}, u32[]{:S(2)}, u32[]{:S(2)}) async-start(f32[16,264,256]{2,1,0:T(8,128)} %copy-done), calls=%async_computation | async-start | bytes 8650752 | tf_op jit(solution)/shard_map/all_to_all | solution.py:198
  35.3 0.0 all-reduce.2.cloned.1.call-start
  35.4 55.8 %all-to-all-done.got_ref = f32[16,264,256]{2,1,0:T(8,128)} async-done(((f32[16,264,256]{2,1,0:T(8,128)}), f32[16,264,256]{2,1,0:T(8,128)}, u32[]{:S(2)}, u32[]{:S(2)}) %all-to-all-start) | async-done | bytes 4325408 | tf_op jit(solution)/shard_map/all_to_all | solution.py:198
  91.2 13.7 %place_sums.1 = f32[2048,256]{1,0:T(8,128)} custom-call(f32[16,264,256]{2,1,0:T(8,128)} %all-to-all-done.got_ref), custom_call_target="tpu_custom_call" | custom-call | tf_op jit(solution)/shard_map/place_sums/pallas_call | solution.py:122
  104.9 0.0 all-reduce.2.cloned.1.call-update
  104.9 0.1 constant_dynamic-slice_fusion
  105.0 0.5 fusion.11
  106.8 0.1 dynamic-slice_bitcast_fusion.5
  106.9 11.4 %collective-permute-start.2 = (f32[2,64]{1,0:T(2,128)S(1)}, f32[2,64]{1,0:T(2,128)S(1)}, u32[]{:S(2)}, u32[]{:S(2)}) collective-permute-start(f32[2,64]{1,0:T(2,128)S(1)} %pad_maximum_fusion.2), channel_id=1, source_target_pairs={{0,128},{128,0},{16,144},{144,16},{32,160},{160,32},{48,176},{176,... | collective-permute-start | bytes 1544 | tf_op jit(solution)/shard_map/ppermute | solution.py:29
  118.4 0.9 dynamic-slice_bitcast_fusion.1
  119.3 0.1 collective-permute-start
  119.4 3.6 %collective-permute-start.1 = (f32[2,64,256]{2,1,0:T(8,128)S(1)}, f32[2,64,256]{2,1,0:T(8,128)S(1)}, u32[]{:S(2)}, u32[]{:S(2)}) collective-permute-start(f32[2,64,256]{2,1,0:T(8,128)S(1)} %pad_maximum_fusion.1), channel_id=1, source_target_pairs={{0,128},{128,0},{16,144},{144,16},{32,160},{160,32},{48,176},{176,... | collective-permute-start | bytes 393224 | tf_op jit(solution)/shard_map/ppermute | solution.py:29
  123.0 0.0 collective-permute-done.2
  123.0 0.1 bitcast_dynamic-update-slice_fusion.1
  123.1 0.1 bitcast_dynamic-update-slice_fusion
  123.2 2.7 %collective-permute-done = f32[2,64,256]{2,1,0:T(8,128)S(1)} collective-permute-done((f32[2,64,256]{2,1,0:T(8,128)S(1)}, f32[2,64,256]{2,1,0:T(8,128)S(1)}, u32[]{:S(2)}, u32[]{:S(2)}) %collective-permute-start) | collective-permute-done | bytes 131104 | tf_op jit(solution)/shard_map/ppermute | solution.py:29
  125.8 0.6 fusion.3
  126.5 0.6 fusion.2
  127.1 0.1 collective-permute-done.1
  127.3 75.0 %all-reduce.2.cloned.1.call-done = f32[2048,256]{1,0:T(8,128)} async-done(((f32[2048,256]{1,0:T(8,128)}), f32[2048,256]{1,0:T(8,128)}) %all-reduce.2.cloned.1.call-update) | async-done | bytes 2097168 | tf_op jit(solution)/shard_map/psum | solution.py:201
  202.3 1.9 multiply_reduce_fusion
  204.3 2.5 %psum.15 = f32[2048]{0:T(1024)S(1)} all-reduce(f32[2048]{0:T(1024)S(1)} %multiply_reduce_fusion), channel_id=1, replica_groups=mesh['table'=16,'dp'=8,'col'=2] {'col'}, use_global_device_ids=true, to_apply=%region_2.3 | all-reduce | flops 2048 | bytes 16384 | tf_op jit(solution)/shard_map/psum | solution.py:202
  206.8 0.6 sqrt_add_fusion
  207.4 4.8 %divide_subtract_fusion = (f32[2048,256]{1,0:T(8,128)}, f32[2048,256]{1,0:T(8,128)}) fusion(f32[2048,256]{1,0:T(8,128)} %fusion.2, f32[2048]{0:T(1024)S(1)} %get-tuple-element.5, f32[2048,256]{1,0:T(8,128)} %all-reduce.2.cloned.1.call-done, f32[2048,256]{1,0:T(8,128)S(1)} %fusion), kind=kLoop, calls=%fused_computation | loop fusion | flops 3145728 | bytes 10493952 | tf_op jit(solution)/shard_map/sub | solution.py:155
  (7 shorter events, 0.1 us)
Async XLA Ops:
  7.9 3.2 %copy-start.1 = (f32[2048,256]{1,0:T(8,128)S(1)}, f32[2048,256]{1,0:T(8,128)}, u32[]{:S(2)}) copy-start(f32[2048,256]{1,0:T(8,128)} %param.9) | copy-start | bytes 6291460
  11.1 0.7 copy-start.5
  11.1 1.1 copy-start.2
  11.1 1.3 copy-start.3
  11.2 1.5 copy-start.4
  11.2 1.5 copy-start.6
  25.8 2.1 copy-start
  27.8 63.3 %all-to-all-start = ((f32[16,264,256]{2,1,0:T(8,128)}), f32[16,264,256]{2,1,0:T(8,128)}, u32[]{:S(2)}, u32[]{:S(2)}) async-start(f32[16,264,256]{2,1,0:T(8,128)} %copy-done), calls=%async_computation | async-start | bytes 8650752 | tf_op jit(solution)/shard_map/all_to_all | solution.py:198
  35.3 167.0 %all-reduce.2.cloned.1.call-start = ((), (), s32[]{:S(2)}) async-start(), calls=%async_computation.1 | async-start | bytes 4194304 | tf_op jit(solution)/shard_map/psum | solution.py:201
  106.9 16.1 %collective-permute-start.2 = (f32[2,64]{1,0:T(2,128)S(1)}, f32[2,64]{1,0:T(2,128)S(1)}, u32[]{:S(2)}, u32[]{:S(2)}) collective-permute-start(f32[2,64]{1,0:T(2,128)S(1)} %pad_maximum_fusion.2), channel_id=1, source_target_pairs={{0,128},{128,0},{16,144},{144,16},{32,160},{160,32},{48,176},{176,... | collective-permute-start | bytes 1544 | tf_op jit(solution)/shard_map/ppermute | solution.py:29
  119.3 6.6 %collective-permute-start = (f32[2,64,256]{2,1,0:T(8,128)S(1)}, f32[2,64,256]{2,1,0:T(8,128)S(1)}, u32[]{:S(2)}, u32[]{:S(2)}) collective-permute-start(f32[2,64,256]{2,1,0:T(8,128)S(1)} %pad_maximum_fusion), channel_id=1, source_target_pairs={{0,128},{128,0},{16,144},{144,16},{32,160},{160,32},{48,176},{176,... | collective-permute-start | bytes 393224 | tf_op jit(solution)/shard_map/ppermute | solution.py:29
  119.4 7.8 %collective-permute-start.1 = (f32[2,64,256]{2,1,0:T(8,128)S(1)}, f32[2,64,256]{2,1,0:T(8,128)S(1)}, u32[]{:S(2)}, u32[]{:S(2)}) collective-permute-start(f32[2,64,256]{2,1,0:T(8,128)S(1)} %pad_maximum_fusion.1), channel_id=1, source_target_pairs={{0,128},{128,0},{16,144},{144,16},{32,160},{160,32},{48,176},{176,... | collective-permute-start | bytes 393224 | tf_op jit(solution)/shard_map/ppermute | solution.py:29
Sparse Core Ops, SparseCore 0:
  105.0 97.2 all-reduce.1

commit v2 on v1

v2 whole, which is shorter than its diff:
```python
import jax
import jax.numpy as jnp
from jax import lax
from jax.experimental import pallas as pl
from jax.experimental.pallas import tpu as pltpu
from jax.sharding import PartitionSpec as P

SLICE = 64
LOW = 256
GROUP = 8
EXTRA = 8
LANES = 128

beta_one = 0.9
beta_two = 0.99
learn_rate = 0.1
eps_value = 1e-08

NT = (((1,), (1,)), ((), ()))
VMEM = pl.BlockSpec(memory_space=pltpu.VMEM)
SMEM = pl.BlockSpec(memory_space=pltpu.SMEM)
HBM = pl.BlockSpec(memory_space=pl.ANY)


def one_hot(positions, wanted):
    return jnp.where(positions == wanted, 1.0, 0.0).astype(jnp.bfloat16)


def slot_kernel(map_ref, grad_ref, target_ref, out_ref, tally):
    groups, span = map_ref.shape
    highs = tally.shape[0]
    bag = span // GROUP
    owner = pl.program_id(0)

    @pl.when(owner == 0)
    def _():
        sample = lax.broadcasted_iota(jnp.int32, (1, span), 1) // bag
        left_at = lax.broadcasted_iota(jnp.int32, (highs * GROUP, span), 0)
        right_at = lax.broadcasted_iota(jnp.int32, (LOW, span), 0)

        def count(step, carry):
            first = pl.multiple_of(step * 8, 8)
            slots = map_ref[pl.ds(first, 8), :]
            for pair in range(4):
                halves = []
                for which in range(2):
                    at = 2 * pair + which
                    row = slots[at : at + 1, :]
                    left = one_hot(left_at, (row // LOW) * GROUP + sample)
                    right = one_hot(right_at, row % LOW)
                    part = lax.dot_general(left, right, NT, preferred_element_type=jnp.float32)
                    halves.append(part.reshape(highs, GROUP, LOW))
                both = jnp.concatenate(halves, axis=1).astype(jnp.bfloat16)
                begin = pl.multiple_of(first * GROUP + pair * 2 * GROUP, 2 * GROUP)
                tally[:, pl.ds(begin, 2 * GROUP), :] = both
            return carry

        lax.fori_loop(0, groups // 8, count, 0)

    columns = grad_ref.shape[0]
    out_ref[0, :columns, :] = jnp.dot(
        grad_ref[...], tally[owner], preferred_element_type=jnp.float32
    )
    out_ref[0, columns:, :] = jnp.broadcast_to(target_ref[pl.ds(owner, 1), :], (EXTRA, LOW))


def slot_sums(slots, grad_t, targets):
    highs = targets.shape[0]
    columns, samples = grad_t.shape
    height = columns + EXTRA
    return pl.pallas_call(
        slot_kernel,
        grid=(highs,),
        out_shape=jax.ShapeDtypeStruct((highs, height, LOW), jnp.float32),
        in_specs=[VMEM] * 3,
        out_specs=pl.BlockSpec((1, height, LOW), lambda owner: (owner, 0, 0)),
        scratch_shapes=[pltpu.VMEM((highs, samples, LOW), jnp.bfloat16)],
        compiler_params=pltpu.CompilerParams(vmem_limit_bytes=58 << 20),
        name="slot_sums",
    )(slots, grad_t, targets)


def add_block(pieces, aims, start, out_ref, select):
    block, width = select.shape
    step = 256
    place = lax.broadcasted_iota(jnp.int32, (block, step), 0)
    for at in range(0, width, step):
        select[:, at : at + step] = one_hot(place, aims[:1, at : at + step] - start)
    chosen = select[...]
    total = lax.dot_general(chosen, pieces[0], NT, preferred_element_type=jnp.float32)
    total += lax.dot_general(chosen, pieces[1], NT, preferred_element_type=jnp.float32)
    out_ref[...] = total


def place_first_kernel(start_ref, got_ref, pieces, aims, out_ref, select):
    sources, height, cap = got_ref.shape
    columns = height - EXTRA
    for source in range(sources):
        value = got_ref[source, :columns, :]
        upper = value.astype(jnp.bfloat16)
        lower = (value - upper.astype(jnp.float32)).astype(jnp.bfloat16)
        at = source * cap
        pieces[0, :, at : at + cap] = upper
        pieces[1, :, at : at + cap] = lower
        aims[:, at : at + cap] = got_ref[source, columns:, :].astype(jnp.int32)
    add_block(pieces, aims, start_ref[0], out_ref, select)


def place_next_kernel(start_ref, pieces, aims, *refs):
    outs, select = refs[:-1], refs[-1]
    for k, out_ref in enumerate(outs):
        add_block(pieces, aims, start_ref[k], out_ref, select)


def place_first(got, start, block):
    sources, height, cap = got.shape
    columns = height - EXTRA
    width = sources * cap
    return pl.pallas_call(
        place_first_kernel,
        out_shape=(
            jax.ShapeDtypeStruct((2, columns, width), jnp.bfloat16),
            jax.ShapeDtypeStruct((EXTRA, width), jnp.int32),
            jax.ShapeDtypeStruct((block, columns), jnp.float32),
        ),
        in_specs=[SMEM, VMEM],
        out_specs=[VMEM] * 3,
        scratch_shapes=[pltpu.VMEM((block, width), jnp.bfloat16)],
        compiler_params=pltpu.CompilerParams(vmem_limit_bytes=16 << 20),
        cost_estimate=pl.CostEstimate(
            flops=4 * block * width * columns, bytes_accessed=12 << 20, transcendentals=0
        ),
        name="place_first",
    )(start, got)


def place_next(pieces, aims, starts, block):
    _, columns, width = pieces.shape
    count = starts.shape[0]
    return pl.pallas_call(
        place_next_kernel,
        out_shape=tuple(jax.ShapeDtypeStruct((block, columns), jnp.float32) for _ in range(count)),
        in_specs=[SMEM, VMEM, VMEM],
        out_specs=[VMEM] * count,
        scratch_shapes=[pltpu.VMEM((block, width), jnp.bfloat16)],
        compiler_params=pltpu.CompilerParams(vmem_limit_bytes=16 << 20),
        cost_estimate=pl.CostEstimate(
            flops=4 * count * block * width * columns, bytes_accessed=8 << 20, transcendentals=0
        ),
        name="place_next",
    )(starts, pieces, aims)


def adam_kernel(groups, aliased, *refs):
    count = len(groups)
    block_ref, hot_ref = refs[:2]
    parts = refs[2 : 2 + sum(groups)]
    swapped, table, first, second = refs[2 + sum(groups) : 6 + sum(groups)]
    rest = refs[6 + sum(groups) + aliased :]
    out_table, out_first, out_second, held, grad, in_sem, out_sem = rest
    rows = grad.shape[1]
    n_hots = hot_ref.shape[0]
    per_block = rows // SLICE
    full_width = 2 * grad.shape[2]

    def at_block(i):
        return pl.ds(pl.multiple_of(block_ref[i] * rows, rows), rows)

    def arrivals(i):
        at = at_block(i)
        return (
            pltpu.make_async_copy(table.at[at, :], held.at[0, i], in_sem.at[0, i]),
            pltpu.make_async_copy(first.at[at, :], held.at[1, i], in_sem.at[1, i]),
        )

    def returns(i):
        at = at_block(i)
        return (
            pltpu.make_async_copy(held.at[0, i], out_table.at[at, :], out_sem.at[0, i]),
            pltpu.make_async_copy(held.at[1, i], out_first.at[at, :], out_sem.at[1, i]),
        )

    for i in range(count):
        for copy in arrivals(i):
            copy.start()
    begin = 0
    for i in range(count):
        for copy in arrivals(i):
            copy.wait()
        block = block_ref[i]
        for k in range(n_hots):
            hot = hot_ref[k]

            @pl.when(hot // per_block == block)
            def _():
                at = pl.ds(pl.multiple_of((hot % per_block) * SLICE, SLICE), SLICE)
                held[0, i, at, :] = swapped[k * SLICE : (k + 1) * SLICE, :]
                begin_first = (n_hots + k) * SLICE
                held[1, i, at, :] = swapped[begin_first : begin_first + SLICE, :]

        mine = parts[begin : begin + groups[i]]
        begin += groups[i]
        top = 0
        for part in mine:
            height = part.shape[0] - (EXTRA if part is mine[-1] else 0)
            grad[0, top : top + height, :] = part[:height, :]
            top += height
        tail = mine[-1].shape[0] - EXTRA
        lines = rows // LANES
        old = second[pl.ds(block * lines, lines), :]
        for line in range(lines):
            squares = mine[-1][tail : tail + 1, line * LANES : (line + 1) * LANES]
            fresh = beta_two * old[line : line + 1, :] + (1.0 - beta_two) * (squares / full_width)
            out_second[i * lines + line : i * lines + line + 1, :] = fresh
            scaled = jnp.sqrt(fresh / (1.0 - beta_two**8)) + eps_value
            rate = (learn_rate / (1.0 - beta_one**8)) / scaled
            rate = jnp.broadcast_to(rate, (LANES, LANES)).T
            at = slice(line * LANES, (line + 1) * LANES)
            for side in range(grad.shape[2] // LANES):
                cut = slice(side * LANES, (side + 1) * LANES)
                moment = beta_one * held[1, i, at, cut] + (1.0 - beta_one) * grad[0, at, cut]
                held[1, i, at, cut] = moment
                held[0, i, at, cut] = held[0, i, at, cut] - moment * rate
        for copy in returns(i):
            copy.start()
    for i in range(count):
        for copy in returns(i):
            copy.wait()


def adam_blocks(blocks, parts, own_hot, swapped, table, first, second, held=None):
    groups = tuple(len(p) for p in parts)
    flat = [ref for p in parts for ref in p]
    rows, columns = table.shape
    count = len(groups)
    block = SLICE * 4
    lines = block // LANES
    aliased = 0 if held is None else 2
    n_in = 6 + len(flat)
    outs = pl.pallas_call(
        lambda *refs: adam_kernel(groups, aliased, *refs),
        out_shape=(
            jax.ShapeDtypeStruct((rows, columns), jnp.float32),
            jax.ShapeDtypeStruct((rows, columns), jnp.float32),
            jax.ShapeDtypeStruct((count * lines, LANES), jnp.float32),
        ),
        in_specs=[SMEM, SMEM] + [VMEM] * (len(flat) + 1) + [HBM, HBM, VMEM] + [HBM] * aliased,
        out_specs=[HBM, HBM, VMEM],
        scratch_shapes=[
            pltpu.VMEM((2, count, block, columns), jnp.float32),
            pltpu.VMEM((1, block, columns), jnp.float32),
            pltpu.SemaphoreType.DMA((2, count)),
            pltpu.SemaphoreType.DMA((2, count)),
        ],
        input_output_aliases={n_in: 0, n_in + 1: 1} if aliased else {},
        compiler_params=pltpu.CompilerParams(vmem_limit_bytes=16 << 20),
        cost_estimate=pl.CostEstimate(
            flops=8 * count * block * columns,
            bytes_accessed=20 * count * block * columns,
            transcendentals=0,
        ),
        name="adam_blocks",
    )(blocks, own_hot, *flat, swapped, table, first, second, *(held or ()))
    return outs


def local_targets(unique_rows, row_counts, hot_slices, rows_dev):
    n_table, n_hots = hot_slices.shape
    cap = unique_rows.shape[1]
    partner = (jnp.arange(n_table) + n_table // 2) % n_table
    partner_hot = jnp.concatenate([hot_slices[n_table // 2 :], hot_slices[: n_table // 2]], axis=0)
    local_row = unique_rows % rows_dev
    from_partner = unique_rows // rows_dev == partner[:, None]
    target = local_row
    for k in range(n_hots):
        moved = from_partner & (local_row // SLICE == partner_hot[:, k : k + 1])
        target = jnp.where(moved, hot_slices[:, k : k + 1] * SLICE + local_row % SLICE, target)
    valid = jnp.arange(cap)[None, :] < row_counts[:, None]
    return jnp.where(valid, target, rows_dev)


def on_device(
    table_weights,
    moment_first,
    moment_second,
    hot_slices,
    upstream_grad,
    dedup_map,
    unique_rows,
    row_counts,
):
    n_table = lax.axis_size("table")
    n_dp = lax.axis_size("dp")
    position = lax.axis_index("table")
    me = lax.axis_index("dp")
    rows_dev, col_width = table_weights.shape
    block = rows_dev // n_dp
    half = block // 2

    targets = local_targets(unique_rows[0], row_counts[0], hot_slices, rows_dev)
    slots = dedup_map.reshape(-1, GROUP * dedup_map.shape[1])
    slot_grad = slot_sums(slots, upstream_grad.T, targets.astype(jnp.float32))
    got = lax.all_to_all(slot_grad, "table", split_axis=0, concat_axis=0, tiled=True)

    own_hot = hot_slices[position]
    n_hots = own_hot.shape[0]
    starts = [own_hot[k] * SLICE for k in range(n_hots)]
    leaving = [lax.dynamic_slice_in_dim(table_weights, s, SLICE, 0) for s in starts]
    leaving += [lax.dynamic_slice_in_dim(moment_first, s, SLICE, 0) for s in starts]
    leaving_second = [lax.dynamic_slice_in_dim(moment_second, s, SLICE, 0) for s in starts]
    lead = jnp.concatenate(leaving_second)[None, :]
    lead = jnp.broadcast_to(jnp.pad(lead, ((0, 0), (0, col_width - n_hots * SLICE))), (EXTRA, col_width))
    swap = [(t, (t + n_table // 2) % n_table) for t in range(n_table)]
    parcel, slot_grad_seen = lax.optimization_barrier(
        (jnp.concatenate(leaving + [lead], axis=0), slot_grad[0, :8, :128])
    )
    swapped = lax.ppermute(parcel, "table", swap)
    got, swapped = lax.optimization_barrier((got, swapped))
    new_lead = swapped[2 * n_hots * SLICE, : n_hots * SLICE].reshape(n_hots, SLICE)
    slices = moment_second.reshape(-1, SLICE)
    for k in range(n_hots):
        here = jnp.arange(slices.shape[0])[:, None] == own_hot[k]
        slices = jnp.where(here, new_lead[k][None, :], slices)
    placed_second = slices.reshape(-1, LANES)

    up = [(i, (i + 1) % n_dp) for i in range(n_dp)]
    down = [(i, (i - 1) % n_dp) for i in range(n_dp)]

    def send(value, route):
        return lax.ppermute(value, "dp", route)

    def block_at(offset):
        return (me + offset + n_dp) % n_dp

    def begin_at(*offsets):
        return jnp.stack([block_at(o) * block for o in offsets]).astype(jnp.int32)

    pieces, aims, far = place_first(got, begin_at(4), block)
    rise = send(far[:half], up)
    fall = send(far[half:], down)
    plus, minus = place_next(pieces, aims, begin_at(3, -3), block)
    rise = jnp.concatenate([plus[:half] + rise, plus[half:]], axis=0)
    fall = jnp.concatenate([minus[:half], minus[half:] + fall], axis=0)
    for distance in (2, 1):
        rise, fall = send(rise, up), send(fall, down)
        plus, minus = place_next(pieces, aims, begin_at(distance, -distance), block)
        rise, fall = plus + rise, minus + fall
    rise, fall = send(rise, up), send(fall, down)
    (mine,) = place_next(pieces, aims, begin_at(0), block)
    mine = mine + rise + fall
    squares = lax.psum(jnp.sum(mine * mine, axis=1), "col")
    own = jnp.concatenate([mine, jnp.broadcast_to(squares[None, :], (EXTRA, block))], axis=0)

    order, parts = [0], [[own]]
    rise = fall = own
    for distance in (1, 2, 3):
        rise, fall = send(rise, up), send(fall, down)
        order += [-distance, distance]
        parts += [[rise], [fall]]
    rise, fall = send(rise[:half], up), send(fall[half:], down)
    near = jnp.stack([block_at(o) for o in order]).astype(jnp.int32)
    common = (own_hot, swapped, table_weights, moment_first, placed_second)
    weights, first, near_second = adam_blocks(near, parts, *common)
    last = block_at(4).reshape(1).astype(jnp.int32)
    weights, first, last_second = adam_blocks(
        last, [[rise, fall]], *common, held=(weights, first)
    )
    lines = block // LANES
    together = jnp.concatenate([near_second, last_second], axis=0).reshape(n_dp, block)
    arrived = jnp.concatenate([near, last])
    second = jnp.zeros_like(together)
    wanted = jnp.arange(n_dp)
    for i in range(n_dp):
        second = jnp.where((wanted == arrived[i])[:, None], together[i][None, :], second)
    return (weights, first, second.reshape(-1))


def solution(mesh):
    placed = (
        P("table", "col"),
        P("table", "col"),
        P("table"),
        P(),
        P(("table", "dp"), "col"),
        P(("table", "dp"), None),
        P(("table", "dp"), None, None),
        P(("table", "dp"), None),
    )
    return jax.shard_map(
        on_device,
        mesh=mesh,
        in_specs=placed,
        out_specs=(P("table", "col"), P("table", "col"), P("table")),
        check_vma=False,
    )
```

time: 221 us -> 186 us (0.84)
  waiting for transfers between devices: 134 us -> 84.1 us
  starting transfers between devices: 22.7 us -> 39.8 us
  between operations: 15.5 us -> 2.29 us
  Pallas kernels: 26.7 us -> 36.3 us
  local copies, waits for them, and re-layouts: 10.5 us -> 14.2 us
  other arithmetic: 7.52 us -> 4.28 us
    ppermute x3 -> x17, waiting for transfers between devices: 2.8 us -> 84.1 us  [the longest x1 66 us: on_device(): swapped = lax.ppermute(parcel, 'table', swap)]
    psum x1 -> x0, waiting for transfers between devices: 75 us -> none  [on_device(): gradient = lax.psum(dense, 'dp')]
    all_to_all x1, waiting for transfers between devices: 55.8 us -> 0.01 us  [on_device(): lax.all_to_all(slot_grad, 'table', split_axis=0, concat_axis=0, tiled=True)]
    ppermute x3 -> x17, starting transfers between devices: 15.1 us -> 32.2 us  [the longest x16 30.2 us: send(): return lax.ppermute(value, 'dp', route)]
    pallas_call x2 -> x8, Pallas kernels: 26.7 us -> 36.3 us  [the longest x1 17.6 us: slot_sums(): pl.pallas_call(slot_kernel, grid=(highs,), out_shape=jax.ShapeDtypeStruct...]
    sub x1 -> x0, other arithmetic: 4.77 us -> none  [adam_rows(): weights - learn_rate * (new_first / (1.0 - beta_one ** 8)) / scaled[:, None]]
    unnamed x19 -> x27, local copies, waits for them, and re-layouts: 7.22 us -> 10.9 us
  transfers between devices with their start and end apart: 5 -> 18, of which waited for: 4 -> 7; matrix products, arithmetic and copies ran while one was open for 1% -> 3% of each run, Pallas kernels for 0% -> 7%
where the time goes in v2:
time: 186 us; the launch traced here: 183 us
  waiting for transfers between devices  84.1 us (45%)
  starting transfers between devices  39.8 us (21%)
  Pallas kernels  36.3 us (20%)
  local copies, waits for them, and re-layouts  14.2 us (8%)
  other arithmetic  4.28 us (2%)
  blocking collectives  2.47 us (1%)
  between operations  2.29 us (1%)
    ppermute x1, waiting for transfers between devices, on_device(): swapped = lax.ppermute(parcel, 'table', swap)  66 us
    ppermute x16, starting transfers between devices, send(): return lax.ppermute(value, 'dp', route)  30.2 us
    ppermute x16, waiting for transfers between devices, send(): return lax.ppermute(value, 'dp', route)  18.1 us
    pallas_call x1, Pallas kernels, slot_sums(): pl.pallas_call(slot_kernel, grid=(highs,), out_shape=jax.ShapeDtypeStruct...  17.6 us
    unnamed x27, local copies, waits for them, and re-layouts  10.9 us
    pallas_call x4, Pallas kernels, place_next(): pl.pallas_call(place_next_kernel, out_shape=tuple((jax.ShapeDtypeStruct((...  10 us
    all_to_all x1, starting transfers between devices, on_device(): lax.all_to_all(slot_grad, 'table', split_axis=0, concat_axis=0, tiled=True)  7.62 us
    pallas_call x2, Pallas kernels, adam_blocks(): pl.pallas_call(lambda *refs: adam_kernel(groups, aliased, *refs), out_sha...  5.13 us
  transfers between devices with their start and end apart: 18, of which 7 were waited for; matrix products, arithmetic and copies ran while one was open for 3% of the time, Pallas kernels for 7%

profile of v2, /device:TPU:2, one launch (start us, length us, event | category | flops | bytes accessed | tf_op | source)
XLA Modules:
  0.0 183.5 jit_solution(10830540761166747871)
XLA Ops:
  0.7 0.8 fusion.14
  1.5 0.1 pad_add_fusion
  1.6 0.8 multiply_bitcast_fusion.1
  2.3 1.1 copy.15
  3.4 0.8 reshape.130.map_ref
  4.3 2.0 %copy.16 = bf16[1024,256]{0,1:T(8,128)(2,1)} copy(bf16[1024,256]{1,0:T(8,128)(2,1)} %param.12) | data formatting | bytes 1048576 | tf_op args[4]
  6.3 0.7 select_convert_fusion.target_ref
  7.0 17.6 %slot_sums.1 = f32[16,264,256]{2,1,0:T(8,128)} custom-call(s32[128,256]{1,0:T(8,128)} %reshape.130.map_ref, bf16[256,1024]{1,0:T(8,128)(2,1)} %bitcast.76, f32[16,256]{1,0:T(8,128)} %select_convert_fusion.target_ref), custom_call_target="tpu_custom_call" | custom-call | tf_op jit(solution)/shard_map/slot_sums/pallas_call | solution.py:71
  24.6 7.6 %all-to-all-start = ((f32[16,264,256]{2,1,0:T(8,128)}), f32[16,264,256]{2,1,0:T(8,128)}, u32[]{:S(2)}, u32[]{:S(2)}) async-start(f32[16,264,256]{2,1,0:T(8,128)} %slot_sums.1), calls=%async_computation | async-start | bytes 8650752 | tf_op jit(solution)/shard_map/all_to_all | solution.py:303
  32.2 0.2 fusion.9
  32.4 0.6 fusion.13
  34.3 0.1 fusion.12
  34.4 0.1 maximum_bitcast_fusion
  34.5 0.9 dynamic-slice_dynamic-update-slice_fusion.1
  35.4 0.8 dynamic-slice_dynamic-update-slice_fusion
  36.2 2.1 %collective-permute-start = (f32[264,256]{1,0:T(8,128)S(1)}, f32[264,256]{1,0:T(8,128)S(1)}, u32[]{:S(2)}, u32[]{:S(2)}) collective-permute-start(f32[264,256]{1,0:T(8,128)S(1)} %constant_dynamic-update-slice_fusion), channel_id=1, source_target_pairs={{0,128},{16,144},{32,160},{48,176},{64,192},{80,208},{96,224},{112... | collective-permute-start | bytes 811016 | tf_op jit(solution)/shard_map/ppermute | solution.py:317
  38.3 0.1 pad_add_fusion.3.start_ref
  38.4 66.0 %collective-permute-done.refs_9_.refs_4_ = f32[264,256]{1,0:T(8,128)S(1)} collective-permute-done((f32[264,256]{1,0:T(8,128)S(1)}, f32[264,256]{1,0:T(8,128)S(1)}, u32[]{:S(2)}, u32[]{:S(2)}) %collective-permute-start) | collective-permute-done | bytes 270368 | tf_op jit(solution)/shard_map/ppermute | solution.py:317
  104.4 3.5 %place_first.1 = (bf16[2,256,4096]{2,1,0:T(8,128)(2,1)S(1)}, s32[8,4096]{1,0:T(8,128)S(1)}, f32[256,256]{1,0:T(8,128)S(1)}) custom-call(s32[1]{0:T(128)} %bitcast.2.start_ref, f32[16,264,256]{2,1,0:T(8,128)} %all-to-all-done.got_ref), custom_call_target="tpu_custom_call" | custom-call | flops 1073741824 | bytes 12582912 | tf_op jit(solution)/shard_map/place_first/pallas_call | solution.py:119
  108.0 1.8 collective-permute-start.1
  109.7 4.0 %collective-permute-start.5 = (f32[128,256]{1,0:T(8,128)S(1)}, f32[128,256]{1,0:T(8,128)S(1)}, u32[]{:S(2)}, u32[]{:S(2)}) collective-permute-start(f32[128,256]{1,0:T(8,128)S(1)} %get-tuple-element.46), channel_id=1, source_target_pairs={{0,14},{2,0},{4,2},{6,4},{8,6},{10,8},{12,10},{14,12},{1,15},{3,1}... | collective-permute-start | bytes 393224 | tf_op jit(solution)/shard_map/ppermute | solution.py:330
  113.8 2.9 %place_next.7 = (f32[256,256]{1,0:T(8,128)S(1)}, f32[256,256]{1,0:T(8,128)S(1)}) custom-call(s32[2]{0:T(128)S(1)} %pad_add_fusion.3.start_ref, bf16[2,256,4096]{2,1,0:T(8,128)(2,1)S(1)} %get-tuple-element.21.pieces, s32[8,4096]{1,0:T(8,128)S(1)} %get-tuple-element.22.aims), custom_call_target="tpu_custom_call" | custom-call | flops 2147483648 | bytes 8388608 | tf_op jit(solution)/shard_map/place_next/pallas_call | solution.py:140
  116.8 0.1 collective-permute-start.2
  116.9 3.3 %collective-permute-start.6 = (f32[256,256]{1,0:T(8,128)S(1)}, f32[256,256]{1,0:T(8,128)S(1)}, u32[]{:S(2)}, u32[]{:S(2)}) collective-permute-start(f32[256,256]{1,0:T(8,128)S(1)} %pad_maximum_fusion.2), channel_id=1, source_target_pairs={{0,14},{2,0},{4,2},{6,4},{8,6},{10,8},{12,10},{14,12},{1,15},{3,1}... | collective-permute-start | bytes 786440 | tf_op jit(solution)/shard_map/ppermute | solution.py:330
  120.2 0.1 pad_add_fusion.1
  120.3 2.9 %place_next.6 = (f32[256,256]{1,0:T(8,128)S(1)}, f32[256,256]{1,0:T(8,128)S(1)}) custom-call(s32[2]{0:T(128)S(1)} %get-tuple-element.67.start_ref, bf16[2,256,4096]{2,1,0:T(8,128)(2,1)S(1)} %get-tuple-element.21.pieces, s32[8,4096]{1,0:T(8,128)S(1)} %get-tuple-element.22.aims), custom_call_target="tpu_custom_call" | custom-call | flops 2147483648 | bytes 8388608 | tf_op jit(solution)/shard_map/place_next/pallas_call | solution.py:140
  123.2 1.4 collective-permute-done.2
  124.7 0.1 collective-permute-start.3
  124.8 3.5 %collective-permute-start.7 = (f32[256,256]{1,0:T(8,128)S(1)}, f32[256,256]{1,0:T(8,128)S(1)}, u32[]{:S(2)}, u32[]{:S(2)}) collective-permute-start(f32[256,256]{1,0:T(8,128)S(1)} %add.221), channel_id=1, source_target_pairs={{0,14},{2,0},{4,2},{6,4},{8,6},{10,8},{12,10},{14,12},{1,15},{3,1}... | collective-permute-start | bytes 786440 | tf_op jit(solution)/shard_map/ppermute | solution.py:330
  128.3 2.9 %place_next.5 = (f32[256,256]{1,0:T(8,128)S(1)}, f32[256,256]{1,0:T(8,128)S(1)}) custom-call(s32[2]{0:T(128)S(1)} %get-tuple-element.66.start_ref, bf16[2,256,4096]{2,1,0:T(8,128)(2,1)S(1)} %get-tuple-element.21.pieces, s32[8,4096]{1,0:T(8,128)S(1)} %get-tuple-element.22.aims), custom_call_target="tpu_custom_call" | custom-call | flops 2147483648 | bytes 8388608 | tf_op jit(solution)/shard_map/place_next/pallas_call | solution.py:140
  131.2 1.1 collective-permute-done.3
  132.4 0.1 collective-permute-start.4
  132.5 0.7 add.222
  133.2 3.4 %collective-permute-start.8 = (f32[256,256]{1,0:T(8,128)}, f32[256,256]{1,0:T(8,128)S(1)}, u32[]{:S(2)}, u32[]{:S(2)}) collective-permute-start(f32[256,256]{1,0:T(8,128)} %add.222), channel_id=1, source_target_pairs={{0,14},{2,0},{4,2},{6,4},{8,6},{10,8},{12,10},{14,12},{1,15},{3,1}... | collective-permute-start | bytes 786440 | tf_op jit(solution)/shard_map/ppermute | solution.py:330
  136.6 2.2 %copy-done.3 = bf16[2,256,4096]{2,1,0:T(8,128)(2,1)S(1)} copy-done((bf16[2,256,4096]{2,1,0:T(8,128)(2,1)S(1)}, bf16[2,256,4096]{2,1,0:T(8,128)(2,1)}, u32[]{:S(2)}) %copy-start.3) | copy-done | bytes 4194328
  138.8 1.3 place_next.4
  140.1 0.7 collective-permute-done.8
  140.8 0.1 multiply_reduce_fusion
  141.0 2.5 %psum.7 = f32[256]{0:T(256)S(1)} all-reduce(f32[256]{0:T(256)S(1)} %get-tuple-element.37), channel_id=1, replica_groups=mesh['table'=16,'dp'=8,'col'=2] {'col'}, use_global_device_ids=true, to_apply=%region_1.2 | all-reduce | flops 256 | bytes 2048 | tf_op jit(solution)/shard_map/psum | solution.py:351
  143.5 0.1 collective-permute-start.9
  143.6 3.7 %collective-permute-start.13 = (f32[264,256]{1,0:T(8,128)S(1)}, f32[264,256]{1,0:T(8,128)S(1)}, u32[]{:S(2)}, u32[]{:S(2)}) collective-permute-start(f32[264,256]{1,0:T(8,128)S(1)} %pad_maximum_fusion.refs_2_), channel_id=1, source_target_pairs={{0,14},{2,0},{4,2},{6,4},{8,6},{10,8},{12,10},{14,12},{1,15},{3,1}... | collective-permute-start | bytes 811016 | tf_op jit(solution)/shard_map/ppermute | solution.py:330
  147.2 0.6 fusion.7
  147.9 0.7 fusion.6
  148.6 5.4 %collective-permute-done.9.refs_3_ = f32[264,256]{1,0:T(8,128)S(1)} collective-permute-done((f32[264,256]{1,0:T(8,128)S(1)}, f32[264,256]{1,0:T(8,128)S(1)}, u32[]{:S(2)}, u32[]{:S(2)}) %collective-permute-start.9) | collective-permute-done | bytes 270368 | tf_op jit(solution)/shard_map/ppermute | solution.py:330
  154.0 3.2 %collective-permute-start.14 = (f32[264,256]{1,0:T(8,128)S(1)}, f32[264,256]{1,0:T(8,128)}, u32[]{:S(2)}, u32[]{:S(2)}) collective-permute-start(f32[264,256]{1,0:T(8,128)S(1)} %collective-permute-done.13.refs_4_), channel_id=1, source_target_pairs={{0,14},{2,0},{4,2},{6,4},{8,6},{10,8},{12,10},{14,12},{1,15},{3,1}... | collective-permute-start | bytes 811016 | tf_op jit(solution)/shard_map/ppermute | solution.py:330
  157.2 0.7 copy-done.4
  157.9 0.1 broadcast_in_dim.197
  158.0 0.1 broadcast_in_dim.198
  158.1 0.1 broadcast_in_dim.203
  158.2 0.1 broadcast_in_dim.204
  158.3 0.1 stack.75.refs_0_
  158.4 5.0 %collective-permute-done.10.refs_5_ = f32[264,256]{1,0:T(8,128)} collective-permute-done((f32[264,256]{1,0:T(8,128)S(1)}, f32[264,256]{1,0:T(8,128)}, u32[]{:S(2)}, u32[]{:S(2)}) %collective-permute-start.10) | collective-permute-done | bytes 270368 | tf_op jit(solution)/shard_map/ppermute | solution.py:330
  163.3 3.2 %collective-permute-start.15 = (f32[264,256]{1,0:T(8,128)}, f32[264,256]{1,0:T(8,128)S(1)}, u32[]{:S(2)}, u32[]{:S(2)}) collective-permute-start(f32[264,256]{1,0:T(8,128)} %collective-permute-done.14.refs_6_), channel_id=1, source_target_pairs={{0,14},{2,0},{4,2},{6,4},{8,6},{10,8},{12,10},{14,12},{1,15},{3,1}... | collective-permute-start | bytes 811016 | tf_op jit(solution)/shard_map/ppermute | solution.py:330
  166.6 0.1 broadcast_in_dim.201
  166.7 0.1 broadcast_in_dim.207
  166.8 4.4 %collective-permute-done.15.refs_8_ = f32[264,256]{1,0:T(8,128)S(1)} collective-permute-done((f32[264,256]{1,0:T(8,128)}, f32[264,256]{1,0:T(8,128)S(1)}, u32[]{:S(2)}, u32[]{:S(2)}) %collective-permute-start.15) | collective-permute-done | bytes 270368 | tf_op jit(solution)/shard_map/ppermute | solution.py:330
  171.3 3.7 %collective-permute-start.16 = (f32[136,256]{1,0:T(8,128)S(1)}, f32[136,256]{1,0:T(8,128)S(1)}, u32[]{:S(2)}, u32[]{:S(2)}) collective-permute-start(f32[136,256]{1,0:T(8,128)S(1)} %slice.127), channel_id=1, source_target_pairs={{0,14},{2,0},{4,2},{6,4},{8,6},{10,8},{12,10},{14,12},{1,15},{3,1}... | collective-permute-start | bytes 417800 | tf_op jit(solution)/shard_map/ppermute | solution.py:330
  175.0 0.1 collective-permute-start.12
  175.1 1.6 copy-done.1
  176.6 1.0 copy-done.5
  177.6 3.6 %adam_blocks.2 = (f32[2048,256]{1,0:T(8,128)}, f32[2048,256]{1,0:T(8,128)}, f32[14,128]{1,0:T(8,128)S(1)}) custom-call(s32[7]{0:T(128)S(1)} %stack.75.refs_0_, s32[2]{0:T(128)S(1)} %get-tuple-element.39.refs_1_, f32[264,256]{1,0:T(8,128)S(1)} %pad_maximum_fusion.refs_2_, f32[264,256]{1,0:T(8,128)S(1)} %collective-permute-done.9.refs_3_, ...), custom_call_target="tpu_custom_call" | custom-call | flops 3670016 | bytes 9175040 | tf_op jit(solution)/shard_map/adam_blocks/pallas_call | solution.py:240
  181.2 1.6 adam_blocks.3
  182.8 0.1 select_bitcast_fusion
  182.9 0.6 copy.17
  (55 shorter events, 0.5 us)
Async XLA Ops:
  0.6 5.7 %copy-start.9 = (s32[1,16]{1,0:T(1,128)S(1)}, s32[1,16]{1,0:T(1,128)}, u32[]{:S(2)}) copy-start(s32[1,16]{1,0:T(1,128)} %param.15) | copy-start | bytes 196
  0.6 5.7 %copy-start.6 = (s32[1,16,256]{2,1,0:T(8,128)S(1)}, s32[1,16,256]{2,1,0:T(8,128)}, u32[]{:S(2)}) copy-start(s32[1,16,256]{2,1,0:T(8,128)} %param.14) | copy-start | bytes 49156
  24.6 7.6 %copy-start.7 = (s32[16,2]{0,1:T(2,128)S(1)}, s32[16,2]{0,1:T(2,128)}, u32[]{:S(2)}) copy-start(s32[16,2]{0,1:T(2,128)} %param.11) | copy-start | bytes 388
  24.6 9.7 %copy-start.8 = (f32[2048]{0:T(1024)S(1)}, f32[2048]{0:T(1024)}, u32[]{:S(2)}) copy-start(f32[2048]{0:T(1024)} %param.10) | copy-start | bytes 24580
  24.6 9.9 %copy-start = (f32[2048,256]{1,0:T(8,128)S(1)}, f32[2048,256]{1,0:T(8,128)}, u32[]{:S(2)}) copy-start(f32[2048,256]{1,0:T(8,128)} %refs_5_.1) | copy-start | bytes 6291460
  24.6 79.8 %all-to-all-start = ((f32[16,264,256]{2,1,0:T(8,128)}), f32[16,264,256]{2,1,0:T(8,128)}, u32[]{:S(2)}, u32[]{:S(2)}) async-start(f32[16,264,256]{2,1,0:T(8,128)} %slot_sums.1), calls=%async_computation | async-start | bytes 8650752 | tf_op jit(solution)/shard_map/all_to_all | solution.py:303
  36.2 68.2 %collective-permute-start = (f32[264,256]{1,0:T(8,128)S(1)}, f32[264,256]{1,0:T(8,128)S(1)}, u32[]{:S(2)}, u32[]{:S(2)}) collective-permute-start(f32[264,256]{1,0:T(8,128)S(1)} %constant_dynamic-update-slice_fusion), channel_id=1, source_target_pairs={{0,128},{16,144},{32,160},{48,176},{64,192},{80,208},{96,224},{112... | collective-permute-start | bytes 811016 | tf_op jit(solution)/shard_map/ppermute | solution.py:317
  108.0 20.4 %copy-start.2 = (bf16[2,256,4096]{2,1,0:T(8,128)(2,1)}, bf16[2,256,4096]{2,1,0:T(8,128)(2,1)S(1)}, u32[]{:S(2)}) copy-start(bf16[2,256,4096]{2,1,0:T(8,128)(2,1)S(1)} %get-tuple-element.21.pieces) | copy-start | bytes 12582916
  108.0 8.7 %collective-permute-start.1 = (f32[128,256]{1,0:T(8,128)S(1)}, f32[128,256]{1,0:T(8,128)S(1)}, u32[]{:S(2)}, u32[]{:S(2)}) collective-permute-start(f32[128,256]{1,0:T(8,128)S(1)} %get-tuple-element.45), channel_id=1, source_target_pairs={{0,2},{2,4},{4,6},{6,8},{8,10},{10,12},{12,14},{14,0},{1,3},{3,5},... | collective-permute-start | bytes 393224 | tf_op jit(solution)/shard_map/ppermute | solution.py:330
  109.7 7.1 %collective-permute-start.5 = (f32[128,256]{1,0:T(8,128)S(1)}, f32[128,256]{1,0:T(8,128)S(1)}, u32[]{:S(2)}, u32[]{:S(2)}) collective-permute-start(f32[128,256]{1,0:T(8,128)S(1)} %get-tuple-element.46), channel_id=1, source_target_pairs={{0,14},{2,0},{4,2},{6,4},{8,6},{10,8},{12,10},{14,12},{1,15},{3,1}... | collective-permute-start | bytes 393224 | tf_op jit(solution)/shard_map/ppermute | solution.py:330
  116.8 7.9 %collective-permute-start.2 = (f32[256,256]{1,0:T(8,128)S(1)}, f32[256,256]{1,0:T(8,128)S(1)}, u32[]{:S(2)}, u32[]{:S(2)}) collective-permute-start(f32[256,256]{1,0:T(8,128)S(1)} %pad_maximum_fusion.1), channel_id=1, source_target_pairs={{0,2},{2,4},{4,6},{6,8},{8,10},{10,12},{12,14},{14,0},{1,3},{3,5},... | collective-permute-start | bytes 786440 | tf_op jit(solution)/shard_map/ppermute | solution.py:330
  116.9 7.9 %collective-permute-start.6 = (f32[256,256]{1,0:T(8,128)S(1)}, f32[256,256]{1,0:T(8,128)S(1)}, u32[]{:S(2)}, u32[]{:S(2)}) collective-permute-start(f32[256,256]{1,0:T(8,128)S(1)} %pad_maximum_fusion.2), channel_id=1, source_target_pairs={{0,14},{2,0},{4,2},{6,4},{8,6},{10,8},{12,10},{14,12},{1,15},{3,1}... | collective-permute-start | bytes 786440 | tf_op jit(solution)/shard_map/ppermute | solution.py:330
  124.7 7.7 %collective-permute-start.3 = (f32[256,256]{1,0:T(8,128)S(1)}, f32[256,256]{1,0:T(8,128)S(1)}, u32[]{:S(2)}, u32[]{:S(2)}) collective-permute-start(f32[256,256]{1,0:T(8,128)S(1)} %add.217), channel_id=1, source_target_pairs={{0,2},{2,4},{4,6},{6,8},{8,10},{10,12},{12,14},{14,0},{1,3},{3,5},... | collective-permute-start | bytes 786440 | tf_op jit(solution)/shard_map/ppermute | solution.py:330
  124.8 7.6 %collective-permute-start.7 = (f32[256,256]{1,0:T(8,128)S(1)}, f32[256,256]{1,0:T(8,128)S(1)}, u32[]{:S(2)}, u32[]{:S(2)}) collective-permute-start(f32[256,256]{1,0:T(8,128)S(1)} %add.221), channel_id=1, source_target_pairs={{0,14},{2,0},{4,2},{6,4},{8,6},{10,8},{12,10},{14,12},{1,15},{3,1}... | collective-permute-start | bytes 786440 | tf_op jit(solution)/shard_map/ppermute | solution.py:330
  132.4 7.7 %collective-permute-start.4 = (f32[256,256]{1,0:T(8,128)S(1)}, f32[256,256]{1,0:T(8,128)S(1)}, u32[]{:S(2)}, u32[]{:S(2)}) collective-permute-start(f32[256,256]{1,0:T(8,128)S(1)} %add.218), channel_id=1, source_target_pairs={{0,2},{2,4},{4,6},{6,8},{8,10},{10,12},{12,14},{14,0},{1,3},{3,5},... | collective-permute-start | bytes 786440 | tf_op jit(solution)/shard_map/ppermute | solution.py:330
  133.2 7.6 %collective-permute-start.8 = (f32[256,256]{1,0:T(8,128)}, f32[256,256]{1,0:T(8,128)S(1)}, u32[]{:S(2)}, u32[]{:S(2)}) collective-permute-start(f32[256,256]{1,0:T(8,128)} %add.222), channel_id=1, source_target_pairs={{0,14},{2,0},{4,2},{6,4},{8,6},{10,8},{12,10},{14,12},{1,15},{3,1}... | collective-permute-start | bytes 786440 | tf_op jit(solution)/shard_map/ppermute | solution.py:330
  136.6 2.2 %copy-start.3 = (bf16[2,256,4096]{2,1,0:T(8,128)(2,1)S(1)}, bf16[2,256,4096]{2,1,0:T(8,128)(2,1)}, u32[]{:S(2)}) copy-start(bf16[2,256,4096]{2,1,0:T(8,128)(2,1)} %copy-done.2) | copy-start | bytes 12582916
  143.5 10.5 %collective-permute-start.9 = (f32[264,256]{1,0:T(8,128)S(1)}, f32[264,256]{1,0:T(8,128)S(1)}, u32[]{:S(2)}, u32[]{:S(2)}) collective-permute-start(f32[264,256]{1,0:T(8,128)S(1)} %pad_maximum_fusion.refs_2_), channel_id=1, source_target_pairs={{0,2},{2,4},{4,6},{6,8},{8,10},{10,12},{12,14},{14,0},{1,3},{3,5},... | collective-permute-start | bytes 811016 | tf_op jit(solution)/shard_map/ppermute | solution.py:330
  143.6 10.4 %collective-permute-start.13 = (f32[264,256]{1,0:T(8,128)S(1)}, f32[264,256]{1,0:T(8,128)S(1)}, u32[]{:S(2)}, u32[]{:S(2)}) collective-permute-start(f32[264,256]{1,0:T(8,128)S(1)} %pad_maximum_fusion.refs_2_), channel_id=1, source_target_pairs={{0,14},{2,0},{4,2},{6,4},{8,6},{10,8},{12,10},{14,12},{1,15},{3,1}... | collective-permute-start | bytes 811016 | tf_op jit(solution)/shard_map/ppermute | solution.py:330
  154.0 9.4 %collective-permute-start.10 = (f32[264,256]{1,0:T(8,128)S(1)}, f32[264,256]{1,0:T(8,128)}, u32[]{:S(2)}, u32[]{:S(2)}) collective-permute-start(f32[264,256]{1,0:T(8,128)S(1)} %collective-permute-done.9.refs_3_), channel_id=1, source_target_pairs={{0,2},{2,4},{4,6},{6,8},{8,10},{10,12},{12,14},{14,0},{1,3},{3,5},... | collective-permute-start | bytes 811016 | tf_op jit(solution)/shard_map/ppermute | solution.py:330
  154.0 9.4 %collective-permute-start.14 = (f32[264,256]{1,0:T(8,128)S(1)}, f32[264,256]{1,0:T(8,128)}, u32[]{:S(2)}, u32[]{:S(2)}) collective-permute-start(f32[264,256]{1,0:T(8,128)S(1)} %collective-permute-done.13.refs_4_), channel_id=1, source_target_pairs={{0,14},{2,0},{4,2},{6,4},{8,6},{10,8},{12,10},{14,12},{1,15},{3,1}... | collective-permute-start | bytes 811016 | tf_op jit(solution)/shard_map/ppermute | solution.py:330
  157.2 0.7 copy-start.4
  163.3 11.6 %collective-permute-start.11 = (f32[264,256]{1,0:T(8,128)}, f32[264,256]{1,0:T(8,128)S(1)}, u32[]{:S(2)}, u32[]{:S(2)}) collective-permute-start(f32[264,256]{1,0:T(8,128)} %collective-permute-done.10.refs_5_), channel_id=1, source_target_pairs={{0,2},{2,4},{4,6},{6,8},{8,10},{10,12},{12,14},{14,0},{1,3},{3,5},... | collective-permute-start | bytes 811016 | tf_op jit(solution)/shard_map/ppermute | solution.py:330
  163.3 7.9 %collective-permute-start.15 = (f32[264,256]{1,0:T(8,128)}, f32[264,256]{1,0:T(8,128)S(1)}, u32[]{:S(2)}, u32[]{:S(2)}) collective-permute-start(f32[264,256]{1,0:T(8,128)} %collective-permute-done.14.refs_6_), channel_id=1, source_target_pairs={{0,14},{2,0},{4,2},{6,4},{8,6},{10,8},{12,10},{14,12},{1,15},{3,1}... | collective-permute-start | bytes 811016 | tf_op jit(solution)/shard_map/ppermute | solution.py:330
  171.3 9.9 %collective-permute-start.16 = (f32[136,256]{1,0:T(8,128)S(1)}, f32[136,256]{1,0:T(8,128)S(1)}, u32[]{:S(2)}, u32[]{:S(2)}) collective-permute-start(f32[136,256]{1,0:T(8,128)S(1)} %slice.127), channel_id=1, source_target_pairs={{0,14},{2,0},{4,2},{6,4},{8,6},{10,8},{12,10},{14,12},{1,15},{3,1}... | collective-permute-start | bytes 417800 | tf_op jit(solution)/shard_map/ppermute | solution.py:330
  175.0 6.3 %collective-permute-start.12 = (f32[128,256]{1,0:T(8,128)S(1)}, f32[128,256]{1,0:T(8,128)S(1)}, u32[]{:S(2)}, u32[]{:S(2)}) collective-permute-start(f32[128,256]{1,0:T(8,128)S(1)} %slice.126), channel_id=1, source_target_pairs={{0,2},{2,4},{4,6},{6,8},{8,10},{10,12},{12,14},{14,0},{1,3},{3,5},... | collective-permute-start | bytes 393224 | tf_op jit(solution)/shard_map/ppermute | solution.py:330
  175.0 1.6 copy-start.1
  176.6 1.0 copy-start.5

commit v3 on v2

v3 whole, which is shorter than its diff:
```python
import jax
import jax.numpy as jnp
from jax import lax
from jax.experimental import pallas as pl
from jax.experimental.pallas import tpu as pltpu
from jax.sharding import Mesh
from jax.sharding import PartitionSpec as P

SLICE = 64
CAP = 256
LOW = 128
GROUP = 8
EXTRA = 8
LANES = 128

beta_one = 0.9
beta_two = 0.99
learn_rate = 0.1
eps_value = 1e-08

NT = (((1,), (1,)), ((), ()))
VMEM = pl.BlockSpec(memory_space=pltpu.VMEM)
SMEM = pl.BlockSpec(memory_space=pltpu.SMEM)
HBM = pl.BlockSpec(memory_space=pltpu.HBM)
ANY = pl.BlockSpec(memory_space=pl.ANY)


def digits(values):
    return values.astype(jnp.float32).astype(jnp.bfloat16)


def counting(shape):
    return digits(lax.broadcasted_iota(jnp.int32, shape, 0))


def one_hot(positions, wanted):
    return jnp.where(positions == wanted, jnp.bfloat16(1), jnp.bfloat16(0))


def slot_kernel(map_ref, grad_ref, target_ref, out_ref, tally, held, sems):
    groups, span = map_ref.shape
    owners, _, cap = tally.shape
    per_owner = cap // LOW
    highs = owners * per_owner
    sample = lax.broadcasted_iota(jnp.int32, (1, span), 1) // (span // GROUP)
    left_at = counting((highs * GROUP, span))
    right_at = counting((LOW, span))
    batch = 16

    def count(step, carry):
        first = pl.multiple_of(step * batch, batch)
        slots = map_ref[pl.ds(first, batch), :]
        lefts = digits((slots // LOW) * GROUP + sample)
        rights = digits(slots % LOW)
        for pair in range(batch // 2):
            halves = []
            for at in (2 * pair, 2 * pair + 1):
                left = one_hot(left_at, lefts[at : at + 1, :])
                right = one_hot(right_at, rights[at : at + 1, :])
                part = lax.dot_general(left, right, NT, preferred_element_type=jnp.float32)
                halves.append(part.reshape(highs, GROUP, LOW))
            both = jnp.concatenate(halves, axis=1).astype(jnp.bfloat16)
            both = both.reshape(owners, per_owner, 2 * GROUP, LOW)
            begin = pl.multiple_of(first * GROUP + pair * 2 * GROUP, 2 * GROUP)
            for k in range(per_owner):
                tally[:, pl.ds(begin, 2 * GROUP), k * LOW : (k + 1) * LOW] = both[:, k]
        return carry

    lax.fori_loop(0, groups // batch, count, 0)
    depth, shares, height, _ = held.shape
    columns = height - EXTRA

    def leave(owner):
        slot = owner % depth
        at = pl.ds(owner * shares, shares)
        return pltpu.make_async_copy(held.at[slot], out_ref.at[at], sems.at[slot])

    for owner in range(owners):
        if owner >= depth:
            leave(owner - depth).wait()
        slot = owner % depth
        total = jnp.dot(grad_ref[...], tally[owner], preferred_element_type=jnp.float32)
        aim = jnp.broadcast_to(target_ref[owner : owner + 1, :], (EXTRA, cap))
        for share in range(shares):
            held[slot, share, :columns, :] = total[share * columns : (share + 1) * columns, :]
            held[slot, share, columns:, :] = aim
        leave(owner).start()
    for owner in range(owners - depth, owners):
        leave(owner).wait()


def slot_sums(slots, grad_t, targets, shares):
    owners, cap = targets.shape
    columns, samples = grad_t.shape
    height = columns // shares + EXTRA
    depth = 4
    return pl.pallas_call(
        slot_kernel,
        out_shape=jax.ShapeDtypeStruct((owners * shares, height, cap), jnp.float32),
        in_specs=[VMEM] * 3,
        out_specs=HBM,
        scratch_shapes=[
            pltpu.VMEM((owners, samples, cap), jnp.bfloat16),
            pltpu.VMEM((depth, shares, height, cap), jnp.float32),
            pltpu.SemaphoreType.DMA((depth,)),
        ],
        compiler_params=pltpu.CompilerParams(vmem_limit_bytes=50 << 20),
        name="slot_sums",
    )(slots, grad_t, targets)


def add_block(pieces, aims, start, out_ref, select):
    part, width = select.shape
    columns = out_ref.shape[1]
    place = counting((part, CAP))
    for top in range(0, out_ref.shape[0], part):
        for at in range(0, width, CAP):
            row = aims[:1, at : at + CAP] - (start + top)
            row = digits(jnp.where((row >= 0) & (row < part), row, -1))
            select[:, at : at + CAP] = one_hot(place, row)
        both = lax.dot_general(select[...], pieces[...], NT, preferred_element_type=jnp.float32)
        out_ref[top : top + part, :] = both[:, :columns] + both[:, columns:]


def place_first_kernel(start_ref, got_ref, pieces, aims, out_ref, select, held, sems):
    sources, height, cap = got_ref.shape
    columns = height - EXTRA
    batch = sources // sems.shape[0]

    def fetch(k):
        at = pl.ds(k * batch, batch)
        return pltpu.make_async_copy(got_ref.at[at], held.at[at], sems.at[k])

    for k in range(sems.shape[0]):
        fetch(k).start()
    for source in range(sources):
        if source % batch == 0:
            fetch(source // batch).wait()
        value = held[source, :columns, :]
        upper = value.astype(jnp.bfloat16)
        lower = (value - upper.astype(jnp.float32)).astype(jnp.bfloat16)
        at = source * cap
        pieces[:columns, at : at + cap] = upper
        pieces[columns:, at : at + cap] = lower
        aims[:, at : at + cap] = held[source, columns:, :].astype(jnp.int32)
    add_block(pieces, aims, start_ref[0], out_ref, select)


def place_next_kernel(start_ref, pieces, aims, *refs):
    outs, select = refs[:-1], refs[-1]
    for k, out_ref in enumerate(outs):
        add_block(pieces, aims, start_ref[k], out_ref, select)


def place_cost(blocks, block, width, columns):
    flops = 4 * blocks * block * width * columns
    return pl.CostEstimate(flops=flops, bytes_accessed=8 << 20, transcendentals=0)


def place_first(got, start, block):
    sources, height, cap = got.shape
    columns = height - EXTRA
    width = sources * cap
    return pl.pallas_call(
        place_first_kernel,
        out_shape=(
            jax.ShapeDtypeStruct((2 * columns, width), jnp.bfloat16),
            jax.ShapeDtypeStruct((EXTRA, width), jnp.int32),
            jax.ShapeDtypeStruct((block, columns), jnp.float32),
        ),
        in_specs=[SMEM, HBM],
        out_specs=[VMEM] * 3,
        scratch_shapes=[
            pltpu.VMEM((CAP, width), jnp.bfloat16),
            pltpu.VMEM(got.shape, jnp.float32),
            pltpu.SemaphoreType.DMA((8,)),
        ],
        compiler_params=pltpu.CompilerParams(vmem_limit_bytes=24 << 20),
        cost_estimate=place_cost(1, block, width, columns),
        name="place_first",
    )(start, got)


def place_next(pieces, aims, starts, block):
    columns, width = pieces.shape[0] // 2, pieces.shape[1]
    count = starts.shape[0]
    return pl.pallas_call(
        place_next_kernel,
        out_shape=tuple(jax.ShapeDtypeStruct((block, columns), jnp.float32) for _ in range(count)),
        in_specs=[SMEM, VMEM, VMEM],
        out_specs=[VMEM] * count,
        scratch_shapes=[pltpu.VMEM((CAP, width), jnp.bfloat16)],
        compiler_params=pltpu.CompilerParams(vmem_limit_bytes=18 << 20),
        cost_estimate=place_cost(count, block, width, columns),
        name="place_next",
    )(starts, pieces, aims)


def adam_kernel(groups, full_width, aliased, *refs):
    count = len(groups)
    row_ref, column_ref = refs[:2]
    parts = refs[2 : 2 + sum(groups)]
    table, first, second, before = refs[2 + sum(groups) : 6 + sum(groups)]
    rest = refs[6 + sum(groups) + aliased :]
    out_table, out_first, out_second, held, in_sem, out_sem = rest
    rows, columns = held.shape[2:]
    lines = rows // LANES

    def place_of(i):
        at = pl.ds(pl.multiple_of(row_ref[i] * rows, rows), rows)
        cut = pl.ds(pl.multiple_of(column_ref[i] * columns, columns), columns)
        return at, cut

    def arrivals(i):
        at, cut = place_of(i)
        return (
            pltpu.make_async_copy(table.at[at, cut], held.at[0, i], in_sem.at[0, i]),
            pltpu.make_async_copy(first.at[at, cut], held.at[1, i], in_sem.at[1, i]),
        )

    def returns(i):
        at, cut = place_of(i)
        return (
            pltpu.make_async_copy(held.at[0, i], out_table.at[at, cut], out_sem.at[0, i]),
            pltpu.make_async_copy(held.at[1, i], out_first.at[at, cut], out_sem.at[1, i]),
        )

    for i in range(count):
        for copy in arrivals(i):
            copy.start()
    out_second[...] = before[...]
    begin = 0
    for i in range(count):
        mine = parts[begin : begin + groups[i]]
        begin += groups[i]
        block = row_ref[i]
        for copy in arrivals(i):
            copy.wait()
        old = second[pl.ds(block * lines, lines), :]
        tail = mine[-1].shape[0] - EXTRA
        squares = mine[-1][tail : tail + lines, :]
        fresh = beta_two * old + (1.0 - beta_two) * (squares / full_width)
        out_second[pl.ds(block * lines, lines), :] = fresh
        scaled = jnp.sqrt(fresh / (1.0 - beta_two**8)) + eps_value
        rates = (learn_rate / (1.0 - beta_one**8)) / scaled
        at = 0
        for part in mine:
            for top in range(0, part.shape[0] - LANES + 1, LANES):
                line = at // LANES
                rate = jnp.broadcast_to(rates[line : line + 1, :], (LANES, LANES)).T
                span = slice(at, at + LANES)
                gradient = part[top : top + LANES, :]
                moment = beta_one * held[1, i, span, :] + (1.0 - beta_one) * gradient
                held[1, i, span, :] = moment
                held[0, i, span, :] = held[0, i, span, :] - moment * rate
                at += LANES
        for copy in returns(i):
            copy.start()
    for i in range(count):
        for copy in returns(i):
            copy.wait()


def adam_blocks(rows_at, columns_at, parts, shape, full_width, common, before, held=None):
    groups = tuple(len(p) for p in parts)
    flat = [ref for p in parts for ref in p]
    table, first, second = common
    rows, columns = table.shape
    count = len(groups)
    aliased = 0 if held is None else 2
    n_in = 6 + len(flat)
    size = shape[0] * shape[1]
    return pl.pallas_call(
        lambda *refs: adam_kernel(groups, full_width, aliased, *refs),
        out_shape=(
            jax.ShapeDtypeStruct((rows, columns), jnp.float32),
            jax.ShapeDtypeStruct((rows, columns), jnp.float32),
            jax.ShapeDtypeStruct(second.shape, jnp.float32),
        ),
        in_specs=[SMEM] * 2 + [VMEM] * len(flat) + [ANY, ANY, VMEM, VMEM] + [HBM] * aliased,
        out_specs=[HBM, HBM, VMEM],
        scratch_shapes=[
            pltpu.VMEM((2, count) + shape, jnp.float32),
            pltpu.SemaphoreType.DMA((2, count)),
            pltpu.SemaphoreType.DMA((2, count)),
        ],
        input_output_aliases={n_in: 0, n_in + 1: 1} if aliased else {},
        compiler_params=pltpu.CompilerParams(vmem_limit_bytes=12 << 20),
        cost_estimate=pl.CostEstimate(
            flops=8 * count * size, bytes_accessed=20 * count * size, transcendentals=0
        ),
        name="adam_blocks",
    )(rows_at, columns_at, *flat, table, first, second, before, *(held or ()))


def local_targets(unique_rows, row_counts, hot_slices, rows_dev):
    n_table, n_hots = hot_slices.shape
    cap = unique_rows.shape[1]
    partner = (jnp.arange(n_table) + n_table // 2) % n_table
    partner_hot = jnp.concatenate([hot_slices[n_table // 2 :], hot_slices[: n_table // 2]], axis=0)
    local_row = unique_rows % rows_dev
    from_partner = unique_rows // rows_dev == partner[:, None]
    target = local_row
    for k in range(n_hots):
        moved = from_partner & (local_row // SLICE == partner_hot[:, k : k + 1])
        target = jnp.where(moved, hot_slices[:, k : k + 1] * SLICE + local_row % SLICE, target)
    valid = jnp.arange(cap)[None, :] < row_counts[:, None]
    return jnp.where(valid, target, rows_dev)


def on_device(
    table_weights,
    moment_first,
    moment_second,
    hot_slices,
    upstream_grad,
    dedup_map,
    unique_rows,
    row_counts,
):
    n_table = lax.axis_size("table")
    n_far, n_pair = lax.axis_size("far"), lax.axis_size("pair")
    n_dp = n_far * n_pair
    position = lax.axis_index("table")
    far_at, pair_at = lax.axis_index("far"), lax.axis_index("pair")
    rows_dev, col_width = table_weights.shape
    full_width = col_width * lax.axis_size("col")
    block, share = rows_dev // n_far, col_width // n_pair
    half = block // 2

    targets = local_targets(unique_rows[0], row_counts[0], hot_slices, rows_dev)
    slots = dedup_map.reshape(-1, GROUP * dedup_map.shape[1])
    slot_grad = slot_sums(slots, upstream_grad.T, targets.astype(jnp.float32), n_pair)
    got = lax.all_to_all(slot_grad, ("table", "pair"), split_axis=0, concat_axis=0, tiled=True)

    own_hot = hot_slices[position]
    n_hots = own_hot.shape[0]
    starts = [own_hot[k] * SLICE for k in range(n_hots)]
    leaving = [lax.dynamic_slice_in_dim(table_weights, s, SLICE, 0) for s in starts]
    leaving += [lax.dynamic_slice_in_dim(moment_first, s, SLICE, 0) for s in starts]
    leaving_second = [lax.dynamic_slice_in_dim(moment_second, s, SLICE, 0) for s in starts]
    lead = jnp.concatenate(leaving_second)[None, :]
    lead = jnp.broadcast_to(jnp.pad(lead, ((0, 0), (0, col_width - n_hots * SLICE))), (EXTRA, col_width))
    swap = [(t, (t + n_table // 2) % n_table) for t in range(n_table)]
    swapped = lax.ppermute(jnp.concatenate(leaving + [lead], axis=0), "table", swap)
    size = n_hots * SLICE

    def place(old, new):
        slices = old.reshape((-1, SLICE) + old.shape[1:])
        new = new.reshape((n_hots, SLICE) + old.shape[1:])
        at = jnp.arange(slices.shape[0]).reshape((-1,) + (1,) * old.ndim)
        for k in range(n_hots):
            slices = jnp.where(at == own_hot[k], new[k], slices)
        return slices.reshape(old.shape)

    placed_weights = place(table_weights, swapped[:size])
    placed_first = place(moment_first, swapped[size : 2 * size])
    placed_second = place(moment_second, swapped[2 * size, :size]).reshape(-1, LANES)
    got, placed_weights, placed_first, placed_second = lax.optimization_barrier(
        (got, placed_weights, placed_first, placed_second)
    )

    def begin_at(*offsets):
        return jnp.stack([(far_at + o + n_far) % n_far * block for o in offsets]).astype(jnp.int32)

    def send(value, axes, count, step):
        return lax.ppermute(value, axes, [(i, (i + step) % count) for i in range(count)])

    pieces, aims, other = place_first(got, begin_at(2), block)
    rise = send(other[:half], "far", n_far, 1)
    fall = send(other[half:], "far", n_far, -1)
    plus, minus = place_next(pieces, aims, begin_at(1, -1), block)
    rise = jnp.concatenate([plus[:half] + rise, plus[half:]], axis=0)
    fall = jnp.concatenate([minus[:half], minus[half:] + fall], axis=0)
    rise, fall = send(rise, "far", n_far, 1), send(fall, "far", n_far, -1)
    (mine,) = place_next(pieces, aims, begin_at(0), block)
    mine = mine + rise + fall
    squares = lax.psum(jnp.sum(mine * mine, axis=1), ("pair", "col")).reshape(-1, share)
    squares = jnp.pad(squares, ((0, EXTRA - squares.shape[0]), (0, 0)))
    own = jnp.concatenate([mine, squares], axis=0)

    ring = ("far", "pair")
    me = far_at * n_pair + pair_at
    common = (placed_weights, placed_first, placed_second)

    def update(arrived, second, held=None):
        at = jnp.stack([(me + o + n_dp) % n_dp for o, _ in arrived]).astype(jnp.int32)
        parts = [p for _, p in arrived]
        return adam_blocks(
            at // n_pair, at % n_pair, parts, (block, share), full_width, common, second, held
        )

    rise, fall = send(own, ring, n_dp, 1), send(own, ring, n_dp, -1)
    arrived = [(0, [own]), (-1, [rise]), (1, [fall])]
    rise, fall = send(rise, ring, n_dp, 1), send(fall, ring, n_dp, -1)
    weights, first, second = update(arrived, placed_second)
    rise, fall, second = lax.optimization_barrier((rise, fall, second))
    arrived = [(-2, [rise]), (2, [fall])]
    rise, fall = send(rise, ring, n_dp, 1), send(fall, ring, n_dp, -1)
    arrived += [(-3, [rise]), (3, [fall])]
    rise, fall = send(rise[:half], ring, n_dp, 1), send(fall[half:], ring, n_dp, -1)
    weights, first, second = update(arrived, second, (weights, first))
    weights, first, second = update([(4, [rise, fall])], second, (weights, first))
    return (weights, first, second.reshape(-1))


def solution(mesh):
    n_table, n_dp, n_col = (mesh.shape[a] for a in ("table", "dp", "col"))
    inner = Mesh(mesh.devices.reshape(n_table, n_dp // 2, 2, n_col), ("table", "far", "pair", "col"))
    samples = ("table", "far", "pair")
    placed = (
        P("table", "col"),
        P("table", "col"),
        P("table"),
        P(),
        P(samples, "col"),
        P(samples, None),
        P(samples, None, None),
        P(samples, None),
    )
    return jax.shard_map(
        on_device,
        mesh=inner,
        in_specs=placed,
        out_specs=(P("table", "col"), P("table", "col"), P("table")),
        check_vma=False,
    )
```

time: 186 us -> 171 us (0.919)
  the two profiles are of different devices: /device:TPU:2 before, /device:TPU:20 now
where the time goes in v3:
time: 171 us; the launch traced here: 170 us
  waiting for transfers between devices  78.3 us (46%)
  starting transfers between devices  31.2 us (18%)
  Pallas kernels  30.9 us (18%)
  local copies, waits for them, and re-layouts  13.8 us (8%)
  other arithmetic  7.67 us (4%)
  blocking collectives  5.76 us (3%)
  between operations  2.46 us (1%)
    ppermute x1, waiting for transfers between devices, on_device(): lax.ppermute(jnp.concatenate(leaving + [lead], axis=0), 'table', swap)  60.5 us
    ppermute x12, starting transfers between devices, send(): lax.ppermute(value, axes, [(i, (i + step) % count) for i in range(count)])  21.8 us
    ppermute x12, waiting for transfers between devices, send(): lax.ppermute(value, axes, [(i, (i + step) % count) for i in range(count)])  17.8 us
    pallas_call x1, Pallas kernels, slot_sums(): pl.pallas_call(slot_kernel, out_shape=jax.ShapeDtypeStruct((owners * shar...  12.8 us
    unnamed x22, local copies, waits for them, and re-layouts  11.1 us
    all_to_all x1, starting transfers between devices, on_device(): lax.all_to_all(slot_grad, ('table', 'pair'), split_axis=0, concat_axis=0,...  8.8 us
    pallas_call x2, Pallas kernels, place_next(): pl.pallas_call(place_next_kernel, out_shape=tuple((jax.ShapeDtypeStruct((...  7.41 us
    pallas_call x3, Pallas kernels, adam_blocks(): pl.pallas_call(lambda *refs: adam_kernel(groups, full_width, aliased, *re...  6.05 us
  transfers between devices with their start and end apart: 14, of which 10 were waited for; matrix products, arithmetic and copies ran while one was open for 7% of the time, Pallas kernels for 7%

profile of v3, /device:TPU:20, one launch (start us, length us, event | category | flops | bytes accessed | tf_op | source)
XLA Modules:
  0.0 170.1 jit_solution(10436553873124352539)
XLA Ops:
  0.7 0.8 fusion.16
  1.5 0.1 pad_add_fusion
  1.6 0.8 multiply_bitcast_fusion.1
  2.3 1.1 copy.17
  3.4 0.2 reshape.100.map_ref
  3.6 1.2 copy.18
  4.9 0.1 select_convert_fusion.target_ref
  5.0 12.8 %slot_sums.1 = f32[32,136,256]{2,1,0:T(8,128)} custom-call(s32[128,256]{1,0:T(8,128)S(1)} %reshape.100.map_ref, bf16[256,1024]{1,0:T(8,128)(2,1)S(1)} %bitcast.67, f32[16,256]{1,0:T(8,128)S(1)} %select_convert_fusion.target_ref), custom_call_target="tpu_custom_call" | custom-call | tf_op jit(solution)/shard_map/slot_sums/pallas_call | solution.py:97
  17.8 8.8 %all-to-all-start = ((f32[32,136,256]{2,1,0:T(8,128)}), f32[32,136,256]{2,1,0:T(8,128)}, u32[]{:S(2)}, u32[]{:S(2)}) async-start(f32[32,136,256]{2,1,0:T(8,128)} %slot_sums.1), calls=%async_computation | async-start | bytes 8912896 | tf_op jit(solution)/shard_map/all_to_all | solution.py:334
  26.7 0.5 fusion.15
  28.6 0.1 fusion.14
  28.6 0.1 maximum_bitcast_fusion
  28.7 0.8 dynamic-slice_dynamic-update-slice_fusion.3
  29.6 0.8 dynamic-slice_dynamic-update-slice_fusion.2
  30.4 0.8 dynamic-slice_dynamic-update-slice_fusion.1
  31.3 0.8 dynamic-slice_dynamic-update-slice_fusion
  32.1 0.5 collective-permute-start
  32.7 0.6 iota_compare_fusion.2
  33.3 0.7 fusion.9
  34.0 0.7 iota_compare_fusion.3
  34.7 0.1 broadcast_in_dim.103
  34.9 0.1 broadcast_in_dim.95
  35.0 0.1 broadcast_in_dim.111
  35.1 0.1 broadcast_in_dim.112
  35.2 0.7 fusion.8
  35.8 0.1 broadcast_in_dim.116
  35.9 0.1 broadcast_in_dim.117
  36.1 60.5 %collective-permute-done = f32[264,256]{1,0:T(8,128)S(1)} collective-permute-done((f32[264,256]{1,0:T(8,128)S(1)}, f32[264,256]{1,0:T(8,128)S(1)}, u32[]{:S(2)}, u32[]{:S(2)}) %collective-permute-start) | collective-permute-done | bytes 270368 | tf_op jit(solution)/shard_map/ppermute | solution.py:345
  96.7 0.1 broadcast_in_dim.114
  96.7 0.1 broadcast_in_dim.119
  96.8 3.5 %fusion = (f32[2048,256]{1,0:T(8,128)S(1)}, f32[2048,256]{1,0:T(8,128)}) fusion(f32[2048,256]{1,0:T(8,128)} %param.9, f32[64,256]{1,0:T(8,128)S(1)} %get-tuple-element.54, f32[64,256]{1,0:T(8,128)S(1)} %get-tuple-element.53, pred[2048]{0:T(1024)(128)(4,1)S(1)} %broadcast_in_dim.103, pred[2048]{0:T(1024)(128)(4,1)S(1)} %broadcast_in_dim.95, ...), kind=kLoop, calls=%fused_computation.1 | loop fusion | flops 2097152 | bytes 8654848 | tf_op jit(solution)/shard_map/jit(_where)/select_n | solution.py:353
  100.4 4.7 %place_first.1 = (bf16[256,8192]{1,0:T(8,128)(2,1)S(1)}, s32[8,8192]{1,0:T(8,128)S(1)}, f32[512,128]{1,0:T(8,128)S(1)}) custom-call(s32[1]{0:T(128)} %bitcast.2.start_ref, f32[32,136,256]{2,1,0:T(8,128)} %all-to-all-done.got_ref), custom_call_target="tpu_custom_call" | custom-call | flops 2147483648 | bytes 8388608 | tf_op jit(solution)/shard_map/place_first/pallas_call | solution.py:164
  105.1 3.2 %collective-permute-start.1 = (f32[256,128]{1,0:T(8,128)S(1)}, f32[256,128]{1,0:T(8,128)S(1)}, u32[]{:S(2)}, u32[]{:S(2)}) collective-permute-start(f32[256,128]{1,0:T(8,128)S(1)} %get-tuple-element.59), channel_id=1, source_target_pairs={{0,4},{4,8},{8,12},{12,0},{1,5},{5,9},{9,13},{13,1},{2,6},{6,10},{... | collective-permute-start | bytes 393224 | tf_op jit(solution)/shard_map/ppermute | solution.py:367
  108.3 2.4 %collective-permute-start.3 = (f32[256,128]{1,0:T(8,128)S(1)}, f32[256,128]{1,0:T(8,128)S(1)}, u32[]{:S(2)}, u32[]{:S(2)}) collective-permute-start(f32[256,128]{1,0:T(8,128)S(1)} %get-tuple-element.60), channel_id=1, source_target_pairs={{0,12},{4,0},{8,4},{12,8},{1,13},{5,1},{9,5},{13,9},{2,14},{6,2},{... | collective-permute-start | bytes 393224 | tf_op jit(solution)/shard_map/ppermute | solution.py:367
  110.7 5.1 %place_next.3 = (f32[512,128]{1,0:T(8,128)S(1)}, f32[512,128]{1,0:T(8,128)S(1)}) custom-call(s32[2]{0:T(128)S(1)} %pad_add_fusion.1.start_ref, bf16[256,8192]{1,0:T(8,128)(2,1)S(1)} %get-tuple-element.25.pieces, s32[8,8192]{1,0:T(8,128)S(1)} %get-tuple-element.26.aims), custom_call_target="tpu_custom_call" | custom-call | flops 4294967296 | bytes 8388608 | tf_op jit(solution)/shard_map/place_next/pallas_call | solution.py:187
  115.7 1.3 collective-permute-done.1
  117.0 1.4 collective-permute-start.2
  118.5 0.7 collective-permute-done.3
  119.2 2.2 %collective-permute-start.4 = (f32[512,128]{1,0:T(8,128)S(1)}, f32[512,128]{1,0:T(8,128)S(1)}, u32[]{:S(2)}, u32[]{:S(2)}) collective-permute-start(f32[512,128]{1,0:T(8,128)S(1)} %pad_maximum_fusion.1), channel_id=1, source_target_pairs={{0,12},{4,0},{8,4},{12,8},{1,13},{5,1},{9,5},{13,9},{2,14},{6,2},{... | collective-permute-start | bytes 786440 | tf_op jit(solution)/shard_map/ppermute | solution.py:367
  121.4 2.2 %copy-done.3 = bf16[256,8192]{1,0:T(8,128)(2,1)S(1)} copy-done((bf16[256,8192]{1,0:T(8,128)(2,1)S(1)}, bf16[256,8192]{1,0:T(8,128)(2,1)}, u32[]{:S(2)}) %copy-start.3) | copy-done | bytes 4194328
  123.6 2.4 %place_next.2 = f32[512,128]{1,0:T(8,128)S(1)} custom-call(s32[1]{0:T(128)} %bitcast.1.start_ref, bf16[256,8192]{1,0:T(8,128)(2,1)S(1)} %copy-done.3, s32[8,8192]{1,0:T(8,128)S(1)} %get-tuple-element.26.aims), custom_call_target="tpu_custom_call" | custom-call | flops 2147483648 | bytes 8388608 | tf_op jit(solution)/shard_map/place_next/pallas_call | solution.py:187
  126.0 1.7 collective-permute-done.4
  127.7 0.1 multiply_reduce_fusion
  127.8 5.8 %psum.7 = f32[4,128]{1,0:T(4,128)S(1)} all-reduce(f32[4,128]{1,0:T(4,128)S(1)} %bitcast.68), channel_id=1, replica_groups=mesh['table'=16,'far'=4,'pair'=2,'col'=2] {'pair','col'}, use_global_device_ids=true, to_apply=%region_1.2 | all-reduce | flops 512 | bytes 4096 | tf_op jit(solution)/shard_map/psum | solution.py:378
  133.6 0.1 collective-permute-start.5
  133.7 3.2 %collective-permute-start.7 = (f32[520,128]{1,0:T(8,128)S(1)}, f32[520,128]{1,0:T(8,128)S(1)}, u32[]{:S(2)}, u32[]{:S(2)}) collective-permute-start(f32[520,128]{1,0:T(8,128)S(1)} %select_maximum_fusion.refs_2_), channel_id=1, source_target_pairs={{0,14},{2,0},{4,2},{6,4},{8,6},{10,8},{12,10},{14,12},{1,15},{3,1}... | collective-permute-start | bytes 798728 | tf_op jit(solution)/shard_map/ppermute | solution.py:367
  136.9 6.0 %collective-permute-done.5.refs_3_ = f32[520,128]{1,0:T(8,128)S(1)} collective-permute-done((f32[520,128]{1,0:T(8,128)S(1)}, f32[520,128]{1,0:T(8,128)S(1)}, u32[]{:S(2)}, u32[]{:S(2)}) %collective-permute-start.5) | collective-permute-done | bytes 266272 | tf_op jit(solution)/shard_map/ppermute | solution.py:367
  143.0 1.0 collective-permute-start.6
  144.0 0.5 collective-permute-done.7.refs_4_
  144.4 1.8 %collective-permute-start.8 = (f32[520,128]{1,0:T(8,128)S(1)}, f32[520,128]{1,0:T(8,128)S(1)}, u32[]{:S(2)}, u32[]{:S(2)}) collective-permute-start(f32[520,128]{1,0:T(8,128)S(1)} %collective-permute-done.7.refs_4_), channel_id=1, source_target_pairs={{0,14},{2,0},{4,2},{6,4},{8,6},{10,8},{12,10},{14,12},{1,15},{3,1}... | collective-permute-start | bytes 798728 | tf_op jit(solution)/shard_map/ppermute | solution.py:367
  146.2 0.1 and_select_fusion.2
  146.3 1.6 copy-done
  147.9 2.1 %adam_blocks.3 = (f32[2048,256]{1,0:T(8,128)}, f32[2048,256]{1,0:T(8,128)}, f32[16,128]{1,0:T(8,128)S(1)}) custom-call(s32[3]{0:T(128)S(1)} %and_select_fusion.3.refs_0_, s32[3]{0:T(128)S(1)} %get-tuple-element.47.refs_1_, f32[520,128]{1,0:T(8,128)S(1)} %select_maximum_fusion.refs_2_, f32[520,128]{1,0:T(8,128)S(1)} %collective-permute-done.5.refs_3_, ...), custom_call_target="tpu_custom_call" | custom-call | flops 1572864 | bytes 3932160 | tf_op jit(solution)/shard_map/adam_blocks/pallas_call | solution.py:273
  150.0 1.4 collective-permute-done.6.refs_2_
  151.3 0.3 collective-permute-done.8.refs_3_
  151.6 2.7 %collective-permute-start.11 = (f32[520,128]{1,0:T(8,128)S(1)}, f32[520,128]{1,0:T(8,128)S(1)}, u32[]{:S(2)}, u32[]{:S(2)}) collective-permute-start(f32[520,128]{1,0:T(8,128)S(1)} %collective-permute-done.8.refs_3_), channel_id=1, source_target_pairs={{0,14},{2,0},{4,2},{6,4},{8,6},{10,8},{12,10},{14,12},{1,15},{3,1}... | collective-permute-start | bytes 798728 | tf_op jit(solution)/shard_map/ppermute | solution.py:367
  154.3 0.1 and_select_fusion
  154.4 3.8 %collective-permute-done.11.refs_5_ = f32[520,128]{1,0:T(8,128)S(1)} collective-permute-done((f32[520,128]{1,0:T(8,128)S(1)}, f32[520,128]{1,0:T(8,128)S(1)}, u32[]{:S(2)}, u32[]{:S(2)}) %collective-permute-start.11) | collective-permute-done | bytes 266272 | tf_op jit(solution)/shard_map/ppermute | solution.py:367
  158.3 3.8 %collective-permute-start.12 = (f32[264,128]{1,0:T(8,128)S(1)}, f32[264,128]{1,0:T(8,128)S(1)}, u32[]{:S(2)}, u32[]{:S(2)}) collective-permute-start(f32[264,128]{1,0:T(8,128)S(1)} %slice.118), channel_id=1, source_target_pairs={{0,14},{2,0},{4,2},{6,4},{8,6},{10,8},{12,10},{14,12},{1,15},{3,1}... | collective-permute-start | bytes 405512 | tf_op jit(solution)/shard_map/ppermute | solution.py:367
  162.0 0.1 collective-permute-start.10
  162.2 1.6 copy-done.1
  163.7 2.3 %adam_blocks.4 = (f32[2048,256]{1,0:T(8,128)}, f32[2048,256]{1,0:T(8,128)}, f32[16,128]{1,0:T(8,128)S(1)}) custom-call(s32[4]{0:T(128)S(1)} %and_select_fusion.1.refs_0_, s32[4]{0:T(128)S(1)} %get-tuple-element.45.refs_1_, f32[520,128]{1,0:T(8,128)S(1)} %collective-permute-done.6.refs_2_, ...), custom_call_target="tpu_custom_call", output_to_operand_aliasing={{0}: (10, {}), {1}: (11, {})} | custom-call | flops 2097152 | bytes 5242880 | tf_op jit(solution)/shard_map/adam_blocks/pallas_call | solution.py:273
  166.1 2.2 %collective-permute-done.10.refs_2_ = f32[256,128]{1,0:T(8,128)S(1)} collective-permute-done((f32[256,128]{1,0:T(8,128)S(1)}, f32[256,128]{1,0:T(8,128)S(1)}, u32[]{:S(2)}, u32[]{:S(2)}) %collective-permute-start.10) | collective-permute-done | bytes 131104 | tf_op jit(solution)/shard_map/ppermute | solution.py:367
  168.3 1.6 adam_blocks.5
  (40 shorter events, 0.6 us)
Async XLA Ops:
  0.6 4.2 %copy-start.7 = (s32[1,16]{1,0:T(1,128)S(1)}, s32[1,16]{1,0:T(1,128)}, u32[]{:S(2)}) copy-start(s32[1,16]{1,0:T(1,128)} %param.15) | copy-start | bytes 196
  0.6 4.2 %copy-start.4 = (s32[1,16,256]{2,1,0:T(8,128)S(1)}, s32[1,16,256]{2,1,0:T(8,128)}, u32[]{:S(2)}) copy-start(s32[1,16,256]{2,1,0:T(8,128)} %param.14) | copy-start | bytes 49156
  17.8 8.8 %copy-start.5 = (s32[16,2]{0,1:T(2,128)S(1)}, s32[16,2]{0,1:T(2,128)}, u32[]{:S(2)}) copy-start(s32[16,2]{0,1:T(2,128)} %param.11) | copy-start | bytes 388
  17.8 10.7 %copy-start.6 = (f32[2048]{0:T(1024)S(1)}, f32[2048]{0:T(1024)}, u32[]{:S(2)}) copy-start(f32[2048]{0:T(1024)} %param.10) | copy-start | bytes 24580
  17.8 82.6 %all-to-all-start = ((f32[32,136,256]{2,1,0:T(8,128)}), f32[32,136,256]{2,1,0:T(8,128)}, u32[]{:S(2)}, u32[]{:S(2)}) async-start(f32[32,136,256]{2,1,0:T(8,128)} %slot_sums.1), calls=%async_computation | async-start | bytes 8912896 | tf_op jit(solution)/shard_map/all_to_all | solution.py:334
  32.1 64.5 %collective-permute-start = (f32[264,256]{1,0:T(8,128)S(1)}, f32[264,256]{1,0:T(8,128)S(1)}, u32[]{:S(2)}, u32[]{:S(2)}) collective-permute-start(f32[264,256]{1,0:T(8,128)S(1)} %constant_dynamic-update-slice_fusion), channel_id=1, source_target_pairs={{0,128},{16,144},{32,160},{48,176},{64,192},{80,208},{96,224},{112... | collective-permute-start | bytes 811016 | tf_op jit(solution)/shard_map/ppermute | solution.py:345
  105.1 10.7 %copy-start.2 = (bf16[256,8192]{1,0:T(8,128)(2,1)}, bf16[256,8192]{1,0:T(8,128)(2,1)S(1)}, u32[]{:S(2)}) copy-start(bf16[256,8192]{1,0:T(8,128)(2,1)S(1)} %get-tuple-element.25.pieces) | copy-start | bytes 12582916
  105.1 11.9 %collective-permute-start.1 = (f32[256,128]{1,0:T(8,128)S(1)}, f32[256,128]{1,0:T(8,128)S(1)}, u32[]{:S(2)}, u32[]{:S(2)}) collective-permute-start(f32[256,128]{1,0:T(8,128)S(1)} %get-tuple-element.59), channel_id=1, source_target_pairs={{0,4},{4,8},{8,12},{12,0},{1,5},{5,9},{9,13},{13,1},{2,6},{6,10},{... | collective-permute-start | bytes 393224 | tf_op jit(solution)/shard_map/ppermute | solution.py:367
  108.3 10.9 %collective-permute-start.3 = (f32[256,128]{1,0:T(8,128)S(1)}, f32[256,128]{1,0:T(8,128)S(1)}, u32[]{:S(2)}, u32[]{:S(2)}) collective-permute-start(f32[256,128]{1,0:T(8,128)S(1)} %get-tuple-element.60), channel_id=1, source_target_pairs={{0,12},{4,0},{8,4},{12,8},{1,13},{5,1},{9,5},{13,9},{2,14},{6,2},{... | collective-permute-start | bytes 393224 | tf_op jit(solution)/shard_map/ppermute | solution.py:367
  117.0 8.9 %collective-permute-start.2 = (f32[512,128]{1,0:T(8,128)S(1)}, f32[512,128]{1,0:T(8,128)S(1)}, u32[]{:S(2)}, u32[]{:S(2)}) collective-permute-start(f32[512,128]{1,0:T(8,128)S(1)} %pad_maximum_fusion), channel_id=1, source_target_pairs={{0,4},{4,8},{8,12},{12,0},{1,5},{5,9},{9,13},{13,1},{2,6},{6,10},{... | collective-permute-start | bytes 786440 | tf_op jit(solution)/shard_map/ppermute | solution.py:367
  119.2 8.4 %collective-permute-start.4 = (f32[512,128]{1,0:T(8,128)S(1)}, f32[512,128]{1,0:T(8,128)S(1)}, u32[]{:S(2)}, u32[]{:S(2)}) collective-permute-start(f32[512,128]{1,0:T(8,128)S(1)} %pad_maximum_fusion.1), channel_id=1, source_target_pairs={{0,12},{4,0},{8,4},{12,8},{1,13},{5,1},{9,5},{13,9},{2,14},{6,2},{... | collective-permute-start | bytes 786440 | tf_op jit(solution)/shard_map/ppermute | solution.py:367
  121.4 2.2 %copy-start.3 = (bf16[256,8192]{1,0:T(8,128)(2,1)S(1)}, bf16[256,8192]{1,0:T(8,128)(2,1)}, u32[]{:S(2)}) copy-start(bf16[256,8192]{1,0:T(8,128)(2,1)} %copy-done.2) | copy-start | bytes 12582916
  133.6 9.4 %collective-permute-start.5 = (f32[520,128]{1,0:T(8,128)S(1)}, f32[520,128]{1,0:T(8,128)S(1)}, u32[]{:S(2)}, u32[]{:S(2)}) collective-permute-start(f32[520,128]{1,0:T(8,128)S(1)} %select_maximum_fusion.refs_2_), channel_id=1, source_target_pairs={{0,2},{2,4},{4,6},{6,8},{8,10},{10,12},{12,14},{14,0},{1,3},{3,5},... | collective-permute-start | bytes 798728 | tf_op jit(solution)/shard_map/ppermute | solution.py:367
  133.7 10.7 %collective-permute-start.7 = (f32[520,128]{1,0:T(8,128)S(1)}, f32[520,128]{1,0:T(8,128)S(1)}, u32[]{:S(2)}, u32[]{:S(2)}) collective-permute-start(f32[520,128]{1,0:T(8,128)S(1)} %select_maximum_fusion.refs_2_), channel_id=1, source_target_pairs={{0,14},{2,0},{4,2},{6,4},{8,6},{10,8},{12,10},{14,12},{1,15},{3,1}... | collective-permute-start | bytes 798728 | tf_op jit(solution)/shard_map/ppermute | solution.py:367
  143.0 8.4 %collective-permute-start.6 = (f32[520,128]{1,0:T(8,128)S(1)}, f32[520,128]{1,0:T(8,128)S(1)}, u32[]{:S(2)}, u32[]{:S(2)}) collective-permute-start(f32[520,128]{1,0:T(8,128)S(1)} %collective-permute-done.5.refs_3_), channel_id=1, source_target_pairs={{0,2},{2,4},{4,6},{6,8},{8,10},{10,12},{12,14},{14,0},{1,3},{3,5},... | collective-permute-start | bytes 798728 | tf_op jit(solution)/shard_map/ppermute | solution.py:367
  144.4 7.2 %collective-permute-start.8 = (f32[520,128]{1,0:T(8,128)S(1)}, f32[520,128]{1,0:T(8,128)S(1)}, u32[]{:S(2)}, u32[]{:S(2)}) collective-permute-start(f32[520,128]{1,0:T(8,128)S(1)} %collective-permute-done.7.refs_4_), channel_id=1, source_target_pairs={{0,14},{2,0},{4,2},{6,4},{8,6},{10,8},{12,10},{14,12},{1,15},{3,1}... | collective-permute-start | bytes 798728 | tf_op jit(solution)/shard_map/ppermute | solution.py:367
  146.3 1.6 copy-start
  151.6 6.6 %collective-permute-start.11 = (f32[520,128]{1,0:T(8,128)S(1)}, f32[520,128]{1,0:T(8,128)S(1)}, u32[]{:S(2)}, u32[]{:S(2)}) collective-permute-start(f32[520,128]{1,0:T(8,128)S(1)} %collective-permute-done.8.refs_3_), channel_id=1, source_target_pairs={{0,14},{2,0},{4,2},{6,4},{8,6},{10,8},{12,10},{14,12},{1,15},{3,1}... | collective-permute-start | bytes 798728 | tf_op jit(solution)/shard_map/ppermute | solution.py:367
  154.3 7.7 %collective-permute-start.9 = (f32[520,128]{1,0:T(8,128)S(1)}, f32[520,128]{1,0:T(8,128)S(1)}, u32[]{:S(2)}, u32[]{:S(2)}) collective-permute-start(f32[520,128]{1,0:T(8,128)S(1)} %collective-permute-done.6.refs_2_), channel_id=1, source_target_pairs={{0,2},{2,4},{4,6},{6,8},{8,10},{10,12},{12,14},{14,0},{1,3},{3,5},... | collective-permute-start | bytes 798728 | tf_op jit(solution)/shard_map/ppermute | solution.py:367
  158.3 10.0 %collective-permute-start.12 = (f32[264,128]{1,0:T(8,128)S(1)}, f32[264,128]{1,0:T(8,128)S(1)}, u32[]{:S(2)}, u32[]{:S(2)}) collective-permute-start(f32[264,128]{1,0:T(8,128)S(1)} %slice.118), channel_id=1, source_target_pairs={{0,14},{2,0},{4,2},{6,4},{8,6},{10,8},{12,10},{14,12},{1,15},{3,1}... | collective-permute-start | bytes 405512 | tf_op jit(solution)/shard_map/ppermute | solution.py:367
  162.0 6.3 %collective-permute-start.10 = (f32[256,128]{1,0:T(8,128)S(1)}, f32[256,128]{1,0:T(8,128)S(1)}, u32[]{:S(2)}, u32[]{:S(2)}) collective-permute-start(f32[256,128]{1,0:T(8,128)S(1)} %slice.117), channel_id=1, source_target_pairs={{0,2},{2,4},{4,6},{6,8},{8,10},{10,12},{12,14},{14,0},{1,3},{3,5},... | collective-permute-start | bytes 393224 | tf_op jit(solution)/shard_map/ppermute | solution.py:367
  162.1 1.6 copy-start.1

commit v4 on v3

--- a/solution.py
+++ b/solution.py
@@ -37,7 +37,20 @@
     return jnp.where(positions == wanted, jnp.bfloat16(1), jnp.bfloat16(0))
 
 
-def slot_kernel(map_ref, grad_ref, target_ref, out_ref, tally, held, sems):
+def target_row(owner, hot_ref, count_ref, rows, rows_dev):
+    owners, n_hots = hot_ref.shape
+    partner = (owner + owners // 2) % owners
+    local_row = rows % rows_dev
+    from_partner = rows // rows_dev == partner
+    target = local_row
+    for k in range(n_hots):
+        moved = from_partner & (local_row // SLICE == hot_ref[partner, k])
+        target = jnp.where(moved, hot_ref[owner, k] * SLICE + local_row % SLICE, target)
+    used = lax.broadcasted_iota(jnp.int32, rows.shape, 1) < count_ref[0, owner]
+    return jnp.where(used, target, rows_dev)
+
+
+def slot_kernel(rows_dev, map_ref, grad_ref, hot_ref, count_ref, rows_ref, out_ref, tally, held, sems):
     groups, span = map_ref.shape
     owners, _, cap = tally.shape
     per_owner = cap // LOW
@@ -80,7 +93,8 @@
             leave(owner - depth).wait()
         slot = owner % depth
         total = jnp.dot(grad_ref[...], tally[owner], preferred_element_type=jnp.float32)
-        aim = jnp.broadcast_to(target_ref[owner : owner + 1, :], (EXTRA, cap))
+        aim = target_row(owner, hot_ref, count_ref, rows_ref[0, owner : owner + 1, :], rows_dev)
+        aim = jnp.broadcast_to(aim.astype(jnp.float32), (EXTRA, cap))
         for share in range(shares):
             held[slot, share, :columns, :] = total[share * columns : (share + 1) * columns, :]
             held[slot, share, columns:, :] = aim
@@ -89,15 +103,15 @@
         leave(owner).wait()
 
 
-def slot_sums(slots, grad_t, targets, shares):
-    owners, cap = targets.shape
+def slot_sums(slots, grad_t, hot_slices, row_counts, unique_rows, shares, rows_dev):
+    _, owners, cap = unique_rows.shape
     columns, samples = grad_t.shape
     height = columns // shares + EXTRA
     depth = 4
     return pl.pallas_call(
-        slot_kernel,
+        lambda *refs: slot_kernel(rows_dev, *refs),
         out_shape=jax.ShapeDtypeStruct((owners * shares, height, cap), jnp.float32),
-        in_specs=[VMEM] * 3,
+        in_specs=[VMEM, VMEM, SMEM, SMEM, VMEM],
         out_specs=HBM,
         scratch_shapes=[
             pltpu.VMEM((owners, samples, cap), jnp.bfloat16),
@@ -106,7 +120,7 @@
         ],
         compiler_params=pltpu.CompilerParams(vmem_limit_bytes=50 << 20),
         name="slot_sums",
-    )(slots, grad_t, targets)
+    )(slots, grad_t, hot_slices, row_counts, unique_rows)
 
 
 def add_block(pieces, aims, start, out_ref, select):
@@ -175,7 +189,7 @@
             pltpu.VMEM(got.shape, jnp.float32),
             pltpu.SemaphoreType.DMA((8,)),
         ],
-        compiler_params=pltpu.CompilerParams(vmem_limit_bytes=24 << 20),
+        compiler_params=pltpu.CompilerParams(vmem_limit_bytes=46 << 20),
         cost_estimate=place_cost(1, block, width, columns),
         name="place_first",
     )(start, got)
@@ -198,10 +212,12 @@
 
 def adam_kernel(groups, full_width, aliased, *refs):
     count = len(groups)
-    row_ref, column_ref = refs[:2]
-    parts = refs[2 : 2 + sum(groups)]
-    table, first, second, before = refs[2 + sum(groups) : 6 + sum(groups)]
-    rest = refs[6 + sum(groups) + aliased :]
+    row_ref, column_ref, hot_ref = refs[:3]
+    parts = refs[3 : 3 + sum(groups)]
+    swapped, table, first, second, before = refs[3 + sum(groups) : 8 + sum(groups)]
+    rest = refs[8 + sum(groups) + aliased :]
+    placed_second = rest[-1]
+    rest = rest[:-1]
     out_table, out_first, out_second, held, in_sem, out_sem = rest
     rows, columns = held.shape[2:]
     lines = rows // LANES
@@ -229,6 +245,16 @@
         for copy in arrivals(i):
             copy.start()
     out_second[...] = before[...]
+    placed = second[...]
+    lead = swapped[4 * SLICE : 4 * SLICE + 1, :LANES]
+    line_at = lax.broadcasted_iota(jnp.int32, placed.shape, 0)
+    side_at = lax.broadcasted_iota(jnp.int32, placed.shape, 1) // SLICE
+    for k in range(2):
+        hot = hot_ref[k]
+        here = (line_at == hot // 2) & (side_at == hot % 2)
+        placed = jnp.where(here, turned(lead, hot % 2 != k), placed)
+    placed_second[...] = placed
+    per_block = rows // SLICE
     begin = 0
     for i in range(count):
         mine = parts[begin : begin + groups[i]]
@@ -236,7 +262,17 @@
         block = row_ref[i]
         for copy in arrivals(i):
             copy.wait()
-        old = second[pl.ds(block * lines, lines), :]
+        for k in range(2):
+            hot = hot_ref[k]
+
+            @pl.when(hot // per_block == block)
+            def _():
+                at = pl.ds(pl.multiple_of((hot % per_block) * SLICE, SLICE), SLICE)
+                for which in range(2):
+                    begin_at = (2 * which + k) * SLICE
+                    held[which, i, at, :] = swapped[begin_at : begin_at + SLICE, place_of(i)[1]]
+
+        old = placed_second[pl.ds(block * lines, lines), :]
         tail = mine[-1].shape[0] - EXTRA
         squares = mine[-1][tail : tail + lines, :]
         fresh = beta_two * old + (1.0 - beta_two) * (squares / full_width)
@@ -264,11 +300,11 @@
 def adam_blocks(rows_at, columns_at, parts, shape, full_width, common, before, held=None):
     groups = tuple(len(p) for p in parts)
     flat = [ref for p in parts for ref in p]
-    table, first, second = common
+    own_hot, swapped, table, first, second = common
     rows, columns = table.shape
     count = len(groups)
     aliased = 0 if held is None else 2
-    n_in = 6 + len(flat)
+    n_in = 8 + len(flat)
     size = shape[0] * shape[1]
     return pl.pallas_call(
         lambda *refs: adam_kernel(groups, full_width, aliased, *refs),
@@ -277,35 +313,58 @@
             jax.ShapeDtypeStruct((rows, columns), jnp.float32),
             jax.ShapeDtypeStruct(second.shape, jnp.float32),
         ),
-        in_specs=[SMEM] * 2 + [VMEM] * len(flat) + [ANY, ANY, VMEM, VMEM] + [HBM] * aliased,
+        in_specs=[SMEM] * 3 + [VMEM] * (len(flat) + 1) + [ANY, ANY, VMEM, VMEM] + [HBM] * aliased,
         out_specs=[HBM, HBM, VMEM],
         scratch_shapes=[
             pltpu.VMEM((2, count) + shape, jnp.float32),
             pltpu.SemaphoreType.DMA((2, count)),
             pltpu.SemaphoreType.DMA((2, count)),
+            pltpu.VMEM(second.shape, jnp.float32),
         ],
         input_output_aliases={n_in: 0, n_in + 1: 1} if aliased else {},
-        compiler_params=pltpu.CompilerParams(vmem_limit_bytes=12 << 20),
+        compiler_params=pltpu.CompilerParams(vmem_limit_bytes=52 << 20),
         cost_estimate=pl.CostEstimate(
             flops=8 * count * size, bytes_accessed=20 * count * size, transcendentals=0
         ),
         name="adam_blocks",
-    )(rows_at, columns_at, *flat, table, first, second, before, *(held or ()))
-
-
-def local_targets(unique_rows, row_counts, hot_slices, rows_dev):
-    n_table, n_hots = hot_slices.shape
-    cap = unique_rows.shape[1]
-    partner = (jnp.arange(n_table) + n_table // 2) % n_table
-    partner_hot = jnp.concatenate([hot_slices[n_table // 2 :], hot_slices[: n_table // 2]], axis=0)
-    local_row = unique_rows % rows_dev
-    from_partner = unique_rows // rows_dev == partner[:, None]
-    target = local_row
-    for k in range(n_hots):
-        moved = from_partner & (local_row // SLICE == partner_hot[:, k : k + 1])
-        target = jnp.where(moved, hot_slices[:, k : k + 1] * SLICE + local_row % SLICE, target)
-    valid = jnp.arange(cap)[None, :] < row_counts[:, None]
-    return jnp.where(valid, target, rows_dev)
+    )(rows_at, columns_at, own_hot, *flat, swapped, table, first, second, before, *(held or ()))
+
+
+def turned(row, wanted):
+    return jnp.where(wanted, pltpu.roll(row, SLICE, 1), row)
+
+
+def parcel_kernel(hot_ref, table, first, second, out_ref, sems):
+    copies = []
+    for which, source in enumerate((table, first)):
+        for k in range(2):
+            at = pl.ds(pl.multiple_of(hot_ref[k] * SLICE, SLICE), SLICE)
+            to = pl.ds((2 * which + k) * SLICE, SLICE)
+            copies.append(pltpu.make_async_copy(source.at[at, :], out_ref.at[to, :], sems.at[which, k]))
+    for copy in copies:
+        copy.start()
+    left, right = (second[pl.ds(hot_ref[k] // 2, 1), :] for k in range(2))
+    lane = lax.broadcasted_iota(jnp.int32, left.shape, 1)
+    row = jnp.where(
+        lane < SLICE, turned(left, hot_ref[0] % 2 == 1), turned(right, hot_ref[1] % 2 == 0)
+    )
+    out_ref[4 * SLICE :, :] = jnp.broadcast_to(
+        jnp.concatenate([row, row], axis=1), (EXTRA, out_ref.shape[1])
+    )
+    for copy in copies:
+        copy.wait()
+
+
+def parcel_of(own_hot, table, first, second):
+    return pl.pallas_call(
+        parcel_kernel,
+        out_shape=jax.ShapeDtypeStruct((4 * SLICE + EXTRA, table.shape[1]), jnp.float32),
+        in_specs=[SMEM, ANY, ANY, VMEM],
+        out_specs=VMEM,
+        scratch_shapes=[pltpu.SemaphoreType.DMA((2, 2))],
+        compiler_params=pltpu.CompilerParams(vmem_limit_bytes=52 << 20),
+        name="parcel",
+    )(own_hot, table, first, second)
 
 
 def on_device(
@@ -328,36 +387,21 @@
     block, share = rows_dev // n_far, col_width // n_pair
     half = block // 2
 
-    targets = local_targets(unique_rows[0], row_counts[0], hot_slices, rows_dev)
+    own_hot = hot_slices[position]
+    second_lines = moment_second.reshape(-1, LANES)
+    parcel = parcel_of(own_hot, table_weights, moment_first, second_lines)
+    swap = [(t, (t + n_table // 2) % n_table) for t in range(n_table)]
+    swapped = lax.ppermute(parcel, "table", swap)
     slots = dedup_map.reshape(-1, GROUP * dedup_map.shape[1])
-    slot_grad = slot_sums(slots, upstream_grad.T, targets.astype(jnp.float32), n_pair)
+    slot_grad = slot_sums(
+        slots, upstream_grad.T, hot_slices, row_counts, unique_rows, n_pair, rows_dev
+    )
+    slot_grad, swapped, own_hot, second_lines, far_at, pair_at = lax.optimization_barrier(
+        (slot_grad, swapped, own_hot, second_lines, far_at, pair_at)
+    )
     got = lax.all_to_all(slot_grad, ("table", "pair"), split_axis=0, concat_axis=0, tiled=True)
-
-    own_hot = hot_slices[position]
-    n_hots = own_hot.shape[0]
-    starts = [own_hot[k] * SLICE for k in range(n_hots)]
-    leaving = [lax.dynamic_slice_in_dim(table_weights, s, SLICE, 0) for s in starts]
-    leaving += [lax.dynamic_slice_in_dim(moment_first, s, SLICE, 0) for s in starts]
-    leaving_second = [lax.dynamic_slice_in_dim(moment_second, s, SLICE, 0) for s in starts]
-    lead = jnp.concatenate(leaving_second)[None, :]
-    lead = jnp.broadcast_to(jnp.pad(lead, ((0, 0), (0, col_width - n_hots * SLICE))), (EXTRA, col_width))
-    swap = [(t, (t + n_table // 2) % n_table) for t in range(n_table)]
-    swapped = lax.ppermute(jnp.concatenate(leaving + [lead], axis=0), "table", swap)
-    size = n_hots * SLICE
-
-    def place(old, new):
-        slices = old.reshape((-1, SLICE) + old.shape[1:])
-        new = new.reshape((n_hots, SLICE) + old.shape[1:])
-        at = jnp.arange(slices.shape[0]).reshape((-1,) + (1,) * old.ndim)
-        for k in range(n_hots):
-            slices = jnp.where(at == own_hot[k], new[k], slices)
-        return slices.reshape(old.shape)
-
-    placed_weights = place(table_weights, swapped[:size])
-    placed_first = place(moment_first, swapped[size : 2 * size])
-    placed_second = place(moment_second, swapped[2 * size, :size]).reshape(-1, LANES)
-    got, placed_weights, placed_first, placed_second = lax.optimization_barrier(
-        (got, placed_weights, placed_first, placed_second)
+    got, swapped, own_hot, second_lines, far_at, pair_at = lax.optimization_barrier(
+        (got, swapped, own_hot, second_lines, far_at, pair_at)
     )
 
     def begin_at(*offsets):
@@ -381,7 +425,7 @@
 
     ring = ("far", "pair")
     me = far_at * n_pair + pair_at
-    common = (placed_weights, placed_first, placed_second)
+    common = (own_hot, swapped, table_weights, moment_first, second_lines)
 
     def update(arrived, second, held=None):
         at = jnp.stack([(me + o + n_dp) % n_dp for o, _ in arrived]).astype(jnp.int32)
@@ -393,7 +437,7 @@
     rise, fall = send(own, ring, n_dp, 1), send(own, ring, n_dp, -1)
     arrived = [(0, [own]), (-1, [rise]), (1, [fall])]
     rise, fall = send(rise, ring, n_dp, 1), send(fall, ring, n_dp, -1)
-    weights, first, second = update(arrived, placed_second)
+    weights, first, second = update(arrived, second_lines)
     rise, fall, second = lax.optimization_barrier((rise, fall, second))
     arrived = [(-2, [rise]), (2, [fall])]
     rise, fall = send(rise, ring, n_dp, 1), send(fall, ring, n_dp, -1)

time: 171 us -> 157 us (0.918)
  the two profiles are of different devices: /device:TPU:20 before, /device:TPU:2 now
where the time goes in v4:
time: 157 us; the launch traced here: 155 us
  blocking collectives  66 us (42%)
  Pallas kernels  36.6 us (23%)
  starting transfers between devices  25.8 us (16%)
  waiting for transfers between devices  20.9 us (13%)
  local copies, waits for them, and re-layouts  4.49 us (3%)
    all_to_all x1, blocking collectives, on_device(): lax.all_to_all(slot_grad, ('table', 'pair'), split_axis=0, concat_axis=0,...  60.3 us
    ppermute x12, starting transfers between devices, send(): lax.ppermute(value, axes, [(i, (i + step) % count) for i in range(count)])  23.6 us
    ppermute x12, waiting for transfers between devices, send(): lax.ppermute(value, axes, [(i, (i + step) % count) for i in range(count)])  20.9 us
    pallas_call x1, Pallas kernels, slot_sums(): pl.pallas_call(lambda *refs: slot_kernel(rows_dev, *refs), out_shape=jax....  13.5 us
    pallas_call x3, Pallas kernels, adam_blocks(): pl.pallas_call(lambda *refs: adam_kernel(groups, full_width, aliased, *re...  9.44 us
    pallas_call x2, Pallas kernels, place_next(): pl.pallas_call(place_next_kernel, out_shape=tuple((jax.ShapeDtypeStruct((...  7.41 us
    psum x1, blocking collectives, on_device(): lax.psum(jnp.sum(mine * mine, axis=1), ('pair', 'col')).reshape(-1, share)  5.67 us
    pallas_call x1, Pallas kernels, place_first(): pl.pallas_call(place_first_kernel, out_shape=(jax.ShapeDtypeStruct((2 * c...  4.66 us
  transfers between devices with their start and end apart: 13, of which 8 were waited for; matrix products, arithmetic and copies ran while one was open for 1% of the time, Pallas kernels for 18%

profile of v4, /device:TPU:2, one launch (start us, length us, event | category | flops | bytes accessed | tf_op | source)
XLA Modules:
  0.0 155.3 jit_solution(10779050610588275818)
XLA Ops:
  0.6 0.9 dynamic-slice_reduce_fusion.hot_ref.refs_2_
  1.5 0.0 copy-start
  1.5 0.7 copy-done
  2.2 0.0 copy-start.8
  2.2 0.0 copy-start.7
  2.2 0.0 copy-start.6
  2.2 1.5 parcel.1
  3.7 0.0 copy-start.2
  3.7 0.0 copy-start.3
  3.8 2.2 %collective-permute-start = (f32[264,256]{1,0:T(8,128)S(1)}, f32[264,256]{1,0:T(8,128)S(1)}, u32[]{:S(2)}, u32[]{:S(2)}) collective-permute-start(f32[264,256]{1,0:T(8,128)S(1)} %parcel.1), channel_id=1, source_target_pairs={{0,128},{16,144},{32,160},{48,176},{64,192},{80,208},{96,224},{112... | collective-permute-start | bytes 811016 | tf_op jit(solution)/shard_map/ppermute | solution.py:394
  6.0 0.0 copy-done.8
  6.0 0.1 copy.20.refs_2_
  6.1 0.0 copy-done.7
  6.1 0.2 copy.18
  6.3 0.2 reshape.22.refs_0_
  6.5 0.0 copy-done.6
  6.5 0.2 copy.19
  6.7 0.0 copy-done.2
  6.7 0.0 copy-done.3
  6.7 13.5 %slot_sums.1 = f32[32,136,256]{2,1,0:T(8,128)} custom-call(s32[128,256]{1,0:T(8,128)S(1)} %reshape.22.refs_0_, bf16[256,1024]{1,0:T(8,128)(2,1)S(1)} %bitcast.16, s32[16,2]{1,0:T(8,128)S(1)} %copy.20.refs_2_, s32[1,16]{1,0:T(1,128)S(1)} %copy-done.3, s32[1,16,256]{2,1,0:T(8,128)S(1)} %copy-done.2), custom_call_target="tpu_custom_call" | custom-call | tf_op jit(solution)/shard_map/slot_sums/pallas_call | solution.py:111
  20.2 0.0 collective-permute-done.refs_6_.refs_7_.refs_5_
  20.2 60.3 %all_to_all.5.got_ref = f32[32,136,256]{2,1,0:T(8,128)} all-to-all(f32[32,136,256]{2,1,0:T(8,128)} %slot_sums.1), channel_id=1, replica_groups=mesh['table'=16,'far'=4,'pair'=2,'col'=2] {'table','pair'}, dimensions={0} | all-to-all | bytes 8912896 | tf_op jit(solution)/shard_map/all_to_all | solution.py:402
  80.6 4.7 %place_first.1 = (bf16[256,8192]{1,0:T(8,128)(2,1)S(1)}, s32[8,8192]{1,0:T(8,128)S(1)}, f32[512,128]{1,0:T(8,128)S(1)}) custom-call(s32[1]{0:T(128)} %bitcast.4.start_ref, f32[32,136,256]{2,1,0:T(8,128)} %all_to_all.5.got_ref), custom_call_target="tpu_custom_call" | custom-call | flops 2147483648 | bytes 8388608 | tf_op jit(solution)/shard_map/place_first/pallas_call | solution.py:178
  85.2 0.0 copy-start.4
  85.3 3.3 %collective-permute-start.1 = (f32[256,128]{1,0:T(8,128)S(1)}, f32[256,128]{1,0:T(8,128)S(1)}, u32[]{:S(2)}, u32[]{:S(2)}) collective-permute-start(f32[256,128]{1,0:T(8,128)S(1)} %get-tuple-element.69), channel_id=1, source_target_pairs={{0,4},{4,8},{8,12},{12,0},{1,5},{5,9},{9,13},{13,1},{2,6},{6,10},{... | collective-permute-start | bytes 393224 | tf_op jit(solution)/shard_map/ppermute | solution.py:411
  88.6 2.4 %collective-permute-start.3 = (f32[256,128]{1,0:T(8,128)S(1)}, f32[256,128]{1,0:T(8,128)S(1)}, u32[]{:S(2)}, u32[]{:S(2)}) collective-permute-start(f32[256,128]{1,0:T(8,128)S(1)} %get-tuple-element.70), channel_id=1, source_target_pairs={{0,12},{4,0},{8,4},{12,8},{1,13},{5,1},{9,5},{13,9},{2,14},{6,2},{... | collective-permute-start | bytes 393224 | tf_op jit(solution)/shard_map/ppermute | solution.py:411
  91.0 0.1 pad_add_fusion.start_ref
  91.1 5.1 %place_next.3 = (f32[512,128]{1,0:T(8,128)S(1)}, f32[512,128]{1,0:T(8,128)S(1)}) custom-call(s32[2]{0:T(128)S(1)} %pad_add_fusion.start_ref, bf16[256,8192]{1,0:T(8,128)(2,1)S(1)} %get-tuple-element.42.pieces, s32[8,8192]{1,0:T(8,128)S(1)} %get-tuple-element.43.aims), custom_call_target="tpu_custom_call" | custom-call | flops 4294967296 | bytes 8388608 | tf_op jit(solution)/shard_map/place_next/pallas_call | solution.py:201
  96.2 0.0 copy-done.4
  96.2 0.0 collective-permute-done.1
  96.2 0.4 collective-permute-done.3
  96.6 0.1 slice_add_fusion.1
  96.6 3.0 %collective-permute-start.2 = (f32[512,128]{1,0:T(8,128)S(1)}, f32[512,128]{1,0:T(8,128)S(1)}, u32[]{:S(2)}, u32[]{:S(2)}) collective-permute-start(f32[512,128]{1,0:T(8,128)S(1)} %pad_maximum_fusion), channel_id=1, source_target_pairs={{0,4},{4,8},{8,12},{12,0},{1,5},{5,9},{9,13},{13,1},{2,6},{6,10},{... | collective-permute-start | bytes 786440 | tf_op jit(solution)/shard_map/ppermute | solution.py:411
  99.7 1.3 collective-permute-start.4
  101.0 0.0 copy-start.5
  101.0 2.2 %copy-done.5 = bf16[256,8192]{1,0:T(8,128)(2,1)S(1)} copy-done((bf16[256,8192]{1,0:T(8,128)(2,1)S(1)}, bf16[256,8192]{1,0:T(8,128)(2,1)}, u32[]{:S(2)}) %copy-start.5) | copy-done | bytes 4194328
  103.1 0.0 copy-start.1
  103.2 2.4 %place_next.2 = f32[512,128]{1,0:T(8,128)S(1)} custom-call(s32[1]{0:T(128)} %bitcast.3.start_ref, bf16[256,8192]{1,0:T(8,128)(2,1)S(1)} %copy-done.5, s32[8,8192]{1,0:T(8,128)S(1)} %get-tuple-element.43.aims), custom_call_target="tpu_custom_call" | custom-call | flops 2147483648 | bytes 8388608 | tf_op jit(solution)/shard_map/place_next/pallas_call | solution.py:201
  105.5 2.8 %collective-permute-done.2 = f32[512,128]{1,0:T(8,128)S(1)} collective-permute-done((f32[512,128]{1,0:T(8,128)S(1)}, f32[512,128]{1,0:T(8,128)S(1)}, u32[]{:S(2)}, u32[]{:S(2)}) %collective-permute-start.2) | collective-permute-done | bytes 262176 | tf_op jit(solution)/shard_map/ppermute | solution.py:411
  108.3 1.9 %collective-permute-done.4 = f32[512,128]{1,0:T(8,128)S(1)} collective-permute-done((f32[512,128]{1,0:T(8,128)S(1)}, f32[512,128]{1,0:T(8,128)S(1)}, u32[]{:S(2)}, u32[]{:S(2)}) %collective-permute-start.4) | collective-permute-done | bytes 262176 | tf_op jit(solution)/shard_map/ppermute | solution.py:411
  110.3 0.2 multiply_reduce_fusion
  110.5 5.7 %psum.7 = f32[4,128]{1,0:T(4,128)S(1)} all-reduce(f32[4,128]{1,0:T(4,128)S(1)} %bitcast.22), channel_id=1, replica_groups=mesh['table'=16,'far'=4,'pair'=2,'col'=2] {'pair','col'}, use_global_device_ids=true, to_apply=%region_1.2 | all-reduce | flops 512 | bytes 4096 | tf_op jit(solution)/shard_map/psum | solution.py:422
  116.2 2.1 %collective-permute-start.5 = (f32[520,128]{1,0:T(8,128)S(1)}, f32[520,128]{1,0:T(8,128)S(1)}, u32[]{:S(2)}, u32[]{:S(2)}) collective-permute-start(f32[520,128]{1,0:T(8,128)S(1)} %select_maximum_fusion.refs_3_), channel_id=1, source_target_pairs={{0,2},{2,4},{4,6},{6,8},{8,10},{10,12},{12,14},{14,0},{1,3},{3,5},... | collective-permute-start | bytes 798728 | tf_op jit(solution)/shard_map/ppermute | solution.py:411
  118.2 1.9 %collective-permute-start.7 = (f32[520,128]{1,0:T(8,128)S(1)}, f32[520,128]{1,0:T(8,128)S(1)}, u32[]{:S(2)}, u32[]{:S(2)}) collective-permute-start(f32[520,128]{1,0:T(8,128)S(1)} %select_maximum_fusion.refs_3_), channel_id=1, source_target_pairs={{0,14},{2,0},{4,2},{6,4},{8,6},{10,8},{12,10},{14,12},{1,15},{3,1}... | collective-permute-start | bytes 798728 | tf_op jit(solution)/shard_map/ppermute | solution.py:411
  120.1 6.2 %collective-permute-done.5.refs_4_ = f32[520,128]{1,0:T(8,128)S(1)} collective-permute-done((f32[520,128]{1,0:T(8,128)S(1)}, f32[520,128]{1,0:T(8,128)S(1)}, u32[]{:S(2)}, u32[]{:S(2)}) %collective-permute-start.5) | collective-permute-done | bytes 266272 | tf_op jit(solution)/shard_map/ppermute | solution.py:411
  126.3 0.9 collective-permute-start.6
  127.3 0.5 collective-permute-done.7.refs_5_
  127.7 1.8 %collective-permute-start.8 = (f32[520,128]{1,0:T(8,128)S(1)}, f32[520,128]{1,0:T(8,128)S(1)}, u32[]{:S(2)}, u32[]{:S(2)}) collective-permute-start(f32[520,128]{1,0:T(8,128)S(1)} %collective-permute-done.7.refs_5_), channel_id=1, source_target_pairs={{0,14},{2,0},{4,2},{6,4},{8,6},{10,8},{12,10},{14,12},{1,15},{3,1}... | collective-permute-start | bytes 798728 | tf_op jit(solution)/shard_map/ppermute | solution.py:411
  129.6 0.1 and_select_fusion.2
  129.7 0.0 copy-done.1
  129.7 3.0 %adam_blocks.3 = (f32[2048,256]{1,0:T(8,128)}, f32[2048,256]{1,0:T(8,128)}, f32[16,128]{1,0:T(8,128)S(1)}) custom-call(s32[3]{0:T(128)S(1)} %and_select_fusion.3.refs_0_, s32[3]{0:T(128)S(1)} %get-tuple-element.63.refs_1_, s32[2]{0:T(128)S(1)} %dynamic-slice_reduce_fusion.hot_ref.refs_2_, f32[520,128]{1,0:T(8,128)S(1)} %select_maximum_fusion.refs_3_, ...), custom_call_target="tpu_custom_call" | custom-call | flops 1572864 | bytes 3932160 | tf_op jit(solution)/shard_map/adam_blocks/pallas_call | solution.py:309
  132.7 2.3 %collective-permute-done.6.refs_3_ = f32[520,128]{1,0:T(8,128)S(1)} collective-permute-done((f32[520,128]{1,0:T(8,128)S(1)}, f32[520,128]{1,0:T(8,128)S(1)}, u32[]{:S(2)}, u32[]{:S(2)}) %collective-permute-start.6) | collective-permute-done | bytes 266272 | tf_op jit(solution)/shard_map/ppermute | solution.py:411
  135.0 0.0 collective-permute-done.8.refs_4_
  135.0 3.0 %collective-permute-start.11 = (f32[520,128]{1,0:T(8,128)S(1)}, f32[520,128]{1,0:T(8,128)S(1)}, u32[]{:S(2)}, u32[]{:S(2)}) collective-permute-start(f32[520,128]{1,0:T(8,128)S(1)} %collective-permute-done.8.refs_4_), channel_id=1, source_target_pairs={{0,14},{2,0},{4,2},{6,4},{8,6},{10,8},{12,10},{14,12},{1,15},{3,1}... | collective-permute-start | bytes 798728 | tf_op jit(solution)/shard_map/ppermute | solution.py:411
  138.0 0.0 collective-permute-start.9
  138.0 0.1 and_select_fusion
  138.1 3.8 %collective-permute-done.11.refs_6_ = f32[520,128]{1,0:T(8,128)S(1)} collective-permute-done((f32[520,128]{1,0:T(8,128)S(1)}, f32[520,128]{1,0:T(8,128)S(1)}, u32[]{:S(2)}, u32[]{:S(2)}) %collective-permute-start.11) | collective-permute-done | bytes 266272 | tf_op jit(solution)/shard_map/ppermute | solution.py:411
  141.9 3.8 %collective-permute-start.12 = (f32[264,128]{1,0:T(8,128)S(1)}, f32[264,128]{1,0:T(8,128)S(1)}, u32[]{:S(2)}, u32[]{:S(2)}) collective-permute-start(f32[264,128]{1,0:T(8,128)S(1)} %slice.33), channel_id=1, source_target_pairs={{0,14},{2,0},{4,2},{6,4},{8,6},{10,8},{12,10},{14,12},{1,15},{3,1}... | collective-permute-start | bytes 405512 | tf_op jit(solution)/shard_map/ppermute | solution.py:411
  145.7 0.0 collective-permute-done.9.refs_5_
  145.7 0.1 collective-permute-start.10
  145.8 3.3 %adam_blocks.4 = (f32[2048,256]{1,0:T(8,128)}, f32[2048,256]{1,0:T(8,128)}, f32[16,128]{1,0:T(8,128)S(1)}) custom-call(s32[4]{0:T(128)S(1)} %and_select_fusion.1.refs_0_, s32[4]{0:T(128)S(1)} %get-tuple-element.61.refs_1_, s32[2]{0:T(128)S(1)} %dynamic-slice_reduce_fusion.hot_ref.refs_2_, ...), custom_call_target="tpu_custom_call", output_to_operand_aliasing={{0}: (12, {}), {1}: (13, {})} | custom-call | flops 2097152 | bytes 5242880 | tf_op jit(solution)/shard_map/adam_blocks/pallas_call | solution.py:309
  149.1 2.9 %collective-permute-done.10.refs_3_ = f32[256,128]{1,0:T(8,128)S(1)} collective-permute-done((f32[256,128]{1,0:T(8,128)S(1)}, f32[256,128]{1,0:T(8,128)S(1)}, u32[]{:S(2)}, u32[]{:S(2)}) %collective-permute-start.10) | collective-permute-done | bytes 131104 | tf_op jit(solution)/shard_map/ppermute | solution.py:411
  152.0 0.0 collective-permute-done.12.refs_4_
  152.0 3.2 %adam_blocks.5 = (f32[2048,256]{1,0:T(8,128)}, f32[2048,256]{1,0:T(8,128)}, f32[16,128]{1,0:T(8,128)}) custom-call(s32[1]{0:T(128)S(6)} %select_n.89.refs_0_, s32[1]{0:T(128)S(6)} %select_n.90.refs_1_, s32[2]{0:T(128)S(1)} %dynamic-slice_reduce_fusion.hot_ref.refs_2_, ...), custom_call_target="tpu_custom_call", output_to_operand_aliasing={{0}: (10, {}), {1}: (11, {})} | custom-call | flops 524288 | bytes 1310720 | tf_op jit(solution)/shard_map/adam_blocks/pallas_call | solution.py:309
  (8 shorter events, 0.1 us)
Async XLA Ops:
  1.5 0.7 copy-start
  2.2 3.8 %copy-start.8 = (s32[16,2]{0,1:T(2,128)S(1)}, s32[16,2]{0,1:T(2,128)}, u32[]{:S(2)}) copy-start(s32[16,2]{0,1:T(2,128)} %param.11) | copy-start | bytes 388
  2.2 3.9 %copy-start.7 = (s32[1024,32]{0,1:T(8,128)S(1)}, s32[1024,32]{0,1:T(8,128)}, u32[]{:S(2)}) copy-start(s32[1024,32]{0,1:T(8,128)} %param.13) | copy-start | bytes 393220
  2.2 4.3 %copy-start.6 = (bf16[1024,256]{1,0:T(8,128)(2,1)S(1)}, bf16[1024,256]{1,0:T(8,128)(2,1)}, u32[]{:S(2)}) copy-start(bf16[1024,256]{1,0:T(8,128)(2,1)} %param.12) | copy-start | bytes 1572868
  3.7 2.9 %copy-start.2 = (s32[1,16,256]{2,1,0:T(8,128)S(1)}, s32[1,16,256]{2,1,0:T(8,128)}, u32[]{:S(2)}) copy-start(s32[1,16,256]{2,1,0:T(8,128)} %refs_4_.1) | copy-start | bytes 49156
  3.7 2.9 %copy-start.3 = (s32[1,16]{1,0:T(1,128)S(1)}, s32[1,16]{1,0:T(1,128)}, u32[]{:S(2)}) copy-start(s32[1,16]{1,0:T(1,128)} %refs_3_.1) | copy-start | bytes 196
  3.8 16.5 %collective-permute-start = (f32[264,256]{1,0:T(8,128)S(1)}, f32[264,256]{1,0:T(8,128)S(1)}, u32[]{:S(2)}, u32[]{:S(2)}) collective-permute-start(f32[264,256]{1,0:T(8,128)S(1)} %parcel.1), channel_id=1, source_target_pairs={{0,128},{16,144},{32,160},{48,176},{64,192},{80,208},{96,224},{112... | collective-permute-start | bytes 811016 | tf_op jit(solution)/shard_map/ppermute | solution.py:394
  85.2 10.9 %copy-start.4 = (bf16[256,8192]{1,0:T(8,128)(2,1)}, bf16[256,8192]{1,0:T(8,128)(2,1)S(1)}, u32[]{:S(2)}) copy-start(bf16[256,8192]{1,0:T(8,128)(2,1)S(1)} %get-tuple-element.42.pieces) | copy-start | bytes 12582916
  85.3 10.9 %collective-permute-start.1 = (f32[256,128]{1,0:T(8,128)S(1)}, f32[256,128]{1,0:T(8,128)S(1)}, u32[]{:S(2)}, u32[]{:S(2)}) collective-permute-start(f32[256,128]{1,0:T(8,128)S(1)} %get-tuple-element.69), channel_id=1, source_target_pairs={{0,4},{4,8},{8,12},{12,0},{1,5},{5,9},{9,13},{13,1},{2,6},{6,10},{... | collective-permute-start | bytes 393224 | tf_op jit(solution)/shard_map/ppermute | solution.py:411
  88.6 7.9 %collective-permute-start.3 = (f32[256,128]{1,0:T(8,128)S(1)}, f32[256,128]{1,0:T(8,128)S(1)}, u32[]{:S(2)}, u32[]{:S(2)}) collective-permute-start(f32[256,128]{1,0:T(8,128)S(1)} %get-tuple-element.70), channel_id=1, source_target_pairs={{0,12},{4,0},{8,4},{12,8},{1,13},{5,1},{9,5},{13,9},{2,14},{6,2},{... | collective-permute-start | bytes 393224 | tf_op jit(solution)/shard_map/ppermute | solution.py:411
  96.6 11.7 %collective-permute-start.2 = (f32[512,128]{1,0:T(8,128)S(1)}, f32[512,128]{1,0:T(8,128)S(1)}, u32[]{:S(2)}, u32[]{:S(2)}) collective-permute-start(f32[512,128]{1,0:T(8,128)S(1)} %pad_maximum_fusion), channel_id=1, source_target_pairs={{0,4},{4,8},{8,12},{12,0},{1,5},{5,9},{9,13},{13,1},{2,6},{6,10},{... | collective-permute-start | bytes 786440 | tf_op jit(solution)/shard_map/ppermute | solution.py:411
  99.7 10.6 %collective-permute-start.4 = (f32[512,128]{1,0:T(8,128)S(1)}, f32[512,128]{1,0:T(8,128)S(1)}, u32[]{:S(2)}, u32[]{:S(2)}) collective-permute-start(f32[512,128]{1,0:T(8,128)S(1)} %pad_maximum_fusion.1), channel_id=1, source_target_pairs={{0,12},{4,0},{8,4},{12,8},{1,13},{5,1},{9,5},{13,9},{2,14},{6,2},{... | collective-permute-start | bytes 786440 | tf_op jit(solution)/shard_map/ppermute | solution.py:411
  101.0 2.2 %copy-start.5 = (bf16[256,8192]{1,0:T(8,128)(2,1)S(1)}, bf16[256,8192]{1,0:T(8,128)(2,1)}, u32[]{:S(2)}) copy-start(bf16[256,8192]{1,0:T(8,128)(2,1)} %copy-done.4) | copy-start | bytes 12582916
  103.1 26.5 %copy-start.1 = (f32[2048]{0:T(1024)S(1)}, f32[2048]{0:T(1024)}, u32[]{:S(2)}) copy-start(f32[2048]{0:T(1024)} %param.10) | copy-start | bytes 24580
  116.2 10.2 %collective-permute-start.5 = (f32[520,128]{1,0:T(8,128)S(1)}, f32[520,128]{1,0:T(8,128)S(1)}, u32[]{:S(2)}, u32[]{:S(2)}) collective-permute-start(f32[520,128]{1,0:T(8,128)S(1)} %select_maximum_fusion.refs_3_), channel_id=1, source_target_pairs={{0,2},{2,4},{4,6},{6,8},{8,10},{10,12},{12,14},{14,0},{1,3},{3,5},... | collective-permute-start | bytes 798728 | tf_op jit(solution)/shard_map/ppermute | solution.py:411
  118.2 9.5 %collective-permute-start.7 = (f32[520,128]{1,0:T(8,128)S(1)}, f32[520,128]{1,0:T(8,128)S(1)}, u32[]{:S(2)}, u32[]{:S(2)}) collective-permute-start(f32[520,128]{1,0:T(8,128)S(1)} %select_maximum_fusion.refs_3_), channel_id=1, source_target_pairs={{0,14},{2,0},{4,2},{6,4},{8,6},{10,8},{12,10},{14,12},{1,15},{3,1}... | collective-permute-start | bytes 798728 | tf_op jit(solution)/shard_map/ppermute | solution.py:411
  126.3 8.7 %collective-permute-start.6 = (f32[520,128]{1,0:T(8,128)S(1)}, f32[520,128]{1,0:T(8,128)S(1)}, u32[]{:S(2)}, u32[]{:S(2)}) collective-permute-start(f32[520,128]{1,0:T(8,128)S(1)} %collective-permute-done.5.refs_4_), channel_id=1, source_target_pairs={{0,2},{2,4},{4,6},{6,8},{8,10},{10,12},{12,14},{14,0},{1,3},{3,5},... | collective-permute-start | bytes 798728 | tf_op jit(solution)/shard_map/ppermute | solution.py:411
  127.7 7.3 %collective-permute-start.8 = (f32[520,128]{1,0:T(8,128)S(1)}, f32[520,128]{1,0:T(8,128)S(1)}, u32[]{:S(2)}, u32[]{:S(2)}) collective-permute-start(f32[520,128]{1,0:T(8,128)S(1)} %collective-permute-done.7.refs_5_), channel_id=1, source_target_pairs={{0,14},{2,0},{4,2},{6,4},{8,6},{10,8},{12,10},{14,12},{1,15},{3,1}... | collective-permute-start | bytes 798728 | tf_op jit(solution)/shard_map/ppermute | solution.py:411
  135.0 6.9 %collective-permute-start.11 = (f32[520,128]{1,0:T(8,128)S(1)}, f32[520,128]{1,0:T(8,128)S(1)}, u32[]{:S(2)}, u32[]{:S(2)}) collective-permute-start(f32[520,128]{1,0:T(8,128)S(1)} %collective-permute-done.8.refs_4_), channel_id=1, source_target_pairs={{0,14},{2,0},{4,2},{6,4},{8,6},{10,8},{12,10},{14,12},{1,15},{3,1}... | collective-permute-start | bytes 798728 | tf_op jit(solution)/shard_map/ppermute | solution.py:411
  138.0 7.7 %collective-permute-start.9 = (f32[520,128]{1,0:T(8,128)S(1)}, f32[520,128]{1,0:T(8,128)S(1)}, u32[]{:S(2)}, u32[]{:S(2)}) collective-permute-start(f32[520,128]{1,0:T(8,128)S(1)} %collective-permute-done.6.refs_3_), channel_id=1, source_target_pairs={{0,2},{2,4},{4,6},{6,8},{8,10},{10,12},{12,14},{14,0},{1,3},{3,5},... | collective-permute-start | bytes 798728 | tf_op jit(solution)/shard_map/ppermute | solution.py:411
  141.9 10.0 %collective-permute-start.12 = (f32[264,128]{1,0:T(8,128)S(1)}, f32[264,128]{1,0:T(8,128)S(1)}, u32[]{:S(2)}, u32[]{:S(2)}) collective-permute-start(f32[264,128]{1,0:T(8,128)S(1)} %slice.33), channel_id=1, source_target_pairs={{0,14},{2,0},{4,2},{6,4},{8,6},{10,8},{12,10},{14,12},{1,15},{3,1}... | collective-permute-start | bytes 405512 | tf_op jit(solution)/shard_map/ppermute | solution.py:411
  145.7 6.3 %collective-permute-start.10 = (f32[256,128]{1,0:T(8,128)S(1)}, f32[256,128]{1,0:T(8,128)S(1)}, u32[]{:S(2)}, u32[]{:S(2)}) collective-permute-start(f32[256,128]{1,0:T(8,128)S(1)} %slice.32), channel_id=1, source_target_pairs={{0,2},{2,4},{4,6},{6,8},{8,10},{10,12},{12,14},{14,0},{1,3},{3,5},... | collective-permute-start | bytes 393224 | tf_op jit(solution)/shard_map/ppermute | solution.py:411

commit v5 on v4

--- a/solution.py
+++ b/solution.py
@@ -80,8 +80,8 @@
         return carry
 
     lax.fori_loop(0, groups // batch, count, 0)
-    depth, shares, height, _ = held.shape
-    columns = height - EXTRA
+    depth, shares, height, lanes = held.shape
+    columns = (height - EXTRA) * lanes // cap
 
     def leave(owner):
         slot = owner % depth
@@ -95,9 +95,13 @@
         total = jnp.dot(grad_ref[...], tally[owner], preferred_element_type=jnp.float32)
         aim = target_row(owner, hot_ref, count_ref, rows_ref[0, owner : owner + 1, :], rows_dev)
         aim = jnp.broadcast_to(aim.astype(jnp.float32), (EXTRA, cap))
-        for share in range(shares):
-            held[slot, share, :columns, :] = total[share * columns : (share + 1) * columns, :]
-            held[slot, share, columns:, :] = aim
+        for side in range(cap // lanes):
+            cut = slice(side * lanes, (side + 1) * lanes)
+            aim_at = height - EXTRA + side * EXTRA * lanes // cap
+            for share in range(shares):
+                part = total[share * columns : (share + 1) * columns, cut]
+                held[slot, share, side * columns : (side + 1) * columns, :] = part
+                held[slot, share, aim_at : aim_at + EXTRA * lanes // cap, :] = aim[: EXTRA * lanes // cap, cut]
         leave(owner).start()
     for owner in range(owners - depth, owners):
         leave(owner).wait()
@@ -106,16 +110,16 @@
 def slot_sums(slots, grad_t, hot_slices, row_counts, unique_rows, shares, rows_dev):
     _, owners, cap = unique_rows.shape
     columns, samples = grad_t.shape
-    height = columns // shares + EXTRA
+    height = columns // shares * cap // LANES + EXTRA
     depth = 4
     return pl.pallas_call(
         lambda *refs: slot_kernel(rows_dev, *refs),
-        out_shape=jax.ShapeDtypeStruct((owners * shares, height, cap), jnp.float32),
+        out_shape=jax.ShapeDtypeStruct((owners * shares, height, LANES), jnp.float32),
         in_specs=[VMEM, VMEM, SMEM, SMEM, VMEM],
         out_specs=HBM,
         scratch_shapes=[
             pltpu.VMEM((owners, samples, cap), jnp.bfloat16),
-            pltpu.VMEM((depth, shares, height, cap), jnp.float32),
+            pltpu.VMEM((depth, shares, height, LANES), jnp.float32),
             pltpu.SemaphoreType.DMA((depth,)),
         ],
         compiler_params=pltpu.CompilerParams(vmem_limit_bytes=50 << 20),
@@ -137,8 +141,8 @@
 
 
 def place_first_kernel(start_ref, got_ref, pieces, aims, out_ref, select, held, sems):
-    sources, height, cap = got_ref.shape
-    columns = height - EXTRA
+    sources, height, lanes = got_ref.shape
+    columns = (height - EXTRA) * lanes // CAP
     batch = sources // sems.shape[0]
 
     def fetch(k):
@@ -150,13 +154,16 @@
     for source in range(sources):
         if source % batch == 0:
             fetch(source // batch).wait()
-        value = held[source, :columns, :]
-        upper = value.astype(jnp.bfloat16)
-        lower = (value - upper.astype(jnp.float32)).astype(jnp.bfloat16)
-        at = source * cap
-        pieces[:columns, at : at + cap] = upper
-        pieces[columns:, at : at + cap] = lower
-        aims[:, at : at + cap] = held[source, columns:, :].astype(jnp.int32)
+        for side in range(CAP // lanes):
+            value = held[source, side * columns : (side + 1) * columns, :]
+            upper = value.astype(jnp.bfloat16)
+            lower = (value - upper.astype(jnp.float32)).astype(jnp.bfloat16)
+            at = source * CAP + side * lanes
+            pieces[:columns, at : at + lanes] = upper
+            pieces[columns:, at : at + lanes] = lower
+            aim_at = height - EXTRA + side * EXTRA * lanes // CAP
+            aim = held[source, aim_at : aim_at + 1, :].astype(jnp.int32)
+            aims[:, at : at + lanes] = jnp.broadcast_to(aim, (EXTRA, lanes))
     add_block(pieces, aims, start_ref[0], out_ref, select)
 
 
@@ -172,9 +179,9 @@
 
 
 def place_first(got, start, block):
-    sources, height, cap = got.shape
-    columns = height - EXTRA
-    width = sources * cap
+    sources, height, lanes = got.shape
+    columns = (height - EXTRA) * lanes // CAP
+    width = sources * CAP
     return pl.pallas_call(
         place_first_kernel,
         out_shape=(
@@ -210,85 +217,110 @@
     )(starts, pieces, aims)
 
 
-def adam_kernel(groups, full_width, aliased, *refs):
+def block_copies(table, first, held, sems, rows_at, columns_at, i, back):
+    rows, columns = held.shape[2:]
+    at = pl.ds(pl.multiple_of(rows_at * rows, rows), rows)
+    cut = pl.ds(pl.multiple_of(columns_at * columns, columns), columns)
+    pairs = [(source.at[at, cut], held.at[which, i]) for which, source in enumerate((table, first))]
+    if back:
+        pairs = [(here, there) for there, here in pairs]
+    return [pltpu.make_async_copy(a, b, sems.at[which, i]) for which, (a, b) in enumerate(pairs)]
+
+
+def put_swapped(where_ref, hots, swapped, held, rows_at, columns_at, i):
+    rows, columns = held.shape[2:]
+    per_block = rows // SLICE
+    for k in range(2):
+        hot = hots[where_ref[0], k]
+
+        @pl.when(hot // per_block == rows_at)
+        def _():
+            at = pl.ds(pl.multiple_of((hot % per_block) * SLICE, SLICE), SLICE)
+            cut = pl.ds(pl.multiple_of(columns_at * columns, columns), columns)
+            for which in range(2):
+                begin = (2 * which + k) * SLICE
+                held[which, i, at, :] = swapped[begin : begin + SLICE, cut]
+
+
+def fetch_kernel(row_ref, column_ref, where_ref, hots, swapped, table, first, held, sems):
+    for copy in block_copies(table, first, held, sems, row_ref[0], column_ref[0], 0, False):
+        copy.start()
+    for copy in block_copies(table, first, held, sems, row_ref[0], column_ref[0], 0, False):
+        copy.wait()
+    put_swapped(where_ref, hots, swapped, held, row_ref[0], column_ref[0], 0)
+
+
+def fetch_block(rows_at, columns_at, shape, common):
+    where, hots, swapped, _, table, first, _ = common
+    return pl.pallas_call(
+        fetch_kernel,
+        out_shape=jax.ShapeDtypeStruct((2, 1) + shape, jnp.float32),
+        in_specs=[SMEM] * 4 + [VMEM, ANY, ANY],
+        out_specs=VMEM,
+        scratch_shapes=[pltpu.SemaphoreType.DMA((2, 1))],
+        compiler_params=pltpu.CompilerParams(vmem_limit_bytes=52 << 20),
+        name="fetch_block",
+    )(rows_at, columns_at, where, hots, swapped, table, first)
+
+
+def adam_kernel(groups, full_width, fetched, *refs):
     count = len(groups)
-    row_ref, column_ref, hot_ref = refs[:3]
-    parts = refs[3 : 3 + sum(groups)]
-    swapped, table, first, second, before = refs[3 + sum(groups) : 8 + sum(groups)]
-    rest = refs[8 + sum(groups) + aliased :]
-    placed_second = rest[-1]
-    rest = rest[:-1]
-    out_table, out_first, out_second, held, in_sem, out_sem = rest
+    row_ref, column_ref, where_ref, hots = refs[:4]
+    parts = refs[4 : 4 + sum(groups)]
+    swapped, squares, table, first, second, before = refs[4 + sum(groups) : 10 + sum(groups)]
+    out_table, out_first, out_second, held, in_sem, out_sem, placed_second = refs[-7:]
     rows, columns = held.shape[2:]
     lines = rows // LANES
-
-    def place_of(i):
-        at = pl.ds(pl.multiple_of(row_ref[i] * rows, rows), rows)
-        cut = pl.ds(pl.multiple_of(column_ref[i] * columns, columns), columns)
-        return at, cut
+    source = refs[10 + sum(groups)] if fetched else held
 
     def arrivals(i):
-        at, cut = place_of(i)
-        return (
-            pltpu.make_async_copy(table.at[at, cut], held.at[0, i], in_sem.at[0, i]),
-            pltpu.make_async_copy(first.at[at, cut], held.at[1, i], in_sem.at[1, i]),
-        )
+        return block_copies(table, first, held, in_sem, row_ref[i], column_ref[i], i, False)
 
     def returns(i):
-        at, cut = place_of(i)
-        return (
-            pltpu.make_async_copy(held.at[0, i], out_table.at[at, cut], out_sem.at[0, i]),
-            pltpu.make_async_copy(held.at[1, i], out_first.at[at, cut], out_sem.at[1, i]),
-        )
-
-    for i in range(count):
-        for copy in arrivals(i):
-            copy.start()
+        return block_copies(out_table, out_first, held, out_sem, row_ref[i], column_ref[i], i, True)
+
+    if not fetched:
+        for i in range(count):
+            for copy in arrivals(i):
+                copy.start()
     out_second[...] = before[...]
     placed = second[...]
     lead = swapped[4 * SLICE : 4 * SLICE + 1, :LANES]
     line_at = lax.broadcasted_iota(jnp.int32, placed.shape, 0)
     side_at = lax.broadcasted_iota(jnp.int32, placed.shape, 1) // SLICE
     for k in range(2):
-        hot = hot_ref[k]
+        hot = hots[where_ref[0], k]
         here = (line_at == hot // 2) & (side_at == hot % 2)
         placed = jnp.where(here, turned(lead, hot % 2 != k), placed)
     placed_second[...] = placed
-    per_block = rows // SLICE
+    blocks = second.shape[0] // lines
+    sharers = squares.shape[0] // blocks
     begin = 0
     for i in range(count):
         mine = parts[begin : begin + groups[i]]
         begin += groups[i]
         block = row_ref[i]
-        for copy in arrivals(i):
-            copy.wait()
-        for k in range(2):
-            hot = hot_ref[k]
-
-            @pl.when(hot // per_block == block)
-            def _():
-                at = pl.ds(pl.multiple_of((hot % per_block) * SLICE, SLICE), SLICE)
-                for which in range(2):
-                    begin_at = (2 * which + k) * SLICE
-                    held[which, i, at, :] = swapped[begin_at : begin_at + SLICE, place_of(i)[1]]
-
+        total = jnp.sum(squares[pl.ds(block * sharers, sharers)], axis=0)[:lines]
         old = placed_second[pl.ds(block * lines, lines), :]
-        tail = mine[-1].shape[0] - EXTRA
-        squares = mine[-1][tail : tail + lines, :]
-        fresh = beta_two * old + (1.0 - beta_two) * (squares / full_width)
+        fresh = beta_two * old + (1.0 - beta_two) * (total / full_width)
         out_second[pl.ds(block * lines, lines), :] = fresh
         scaled = jnp.sqrt(fresh / (1.0 - beta_two**8)) + eps_value
         rates = (learn_rate / (1.0 - beta_one**8)) / scaled
+        if not fetched:
+            for copy in arrivals(i):
+                copy.wait()
+            put_swapped(where_ref, hots, swapped, held, block, column_ref[i], i)
         at = 0
         for part in mine:
-            for top in range(0, part.shape[0] - LANES + 1, LANES):
+            for top in range(0, part.shape[0], LANES):
                 line = at // LANES
                 rate = jnp.broadcast_to(rates[line : line + 1, :], (LANES, LANES)).T
                 span = slice(at, at + LANES)
                 gradient = part[top : top + LANES, :]
-                moment = beta_one * held[1, i, span, :] + (1.0 - beta_one) * gradient
+                moment = beta_one * source[1, i, span, :] + (1.0 - beta_one) * gradient
+                weight = source[0, i, span, :] - moment * rate
                 held[1, i, span, :] = moment
-                held[0, i, span, :] = held[0, i, span, :] - moment * rate
+                held[0, i, span, :] = weight
                 at += LANES
         for copy in returns(i):
             copy.start()
@@ -297,23 +329,27 @@
             copy.wait()
 
 
-def adam_blocks(rows_at, columns_at, parts, shape, full_width, common, before, held=None):
+def adam_blocks(rows_at, columns_at, parts, shape, full_width, common, before, held=None, fetched=None):
     groups = tuple(len(p) for p in parts)
     flat = [ref for p in parts for ref in p]
-    own_hot, swapped, table, first, second = common
-    rows, columns = table.shape
+    where, hots, swapped, squares, table, first, second = common
     count = len(groups)
-    aliased = 0 if held is None else 2
-    n_in = 8 + len(flat)
+    more = [] if fetched is None else [fetched]
+    n_in = 10 + len(flat) + len(more)
     size = shape[0] * shape[1]
+    kept = [] if held is None else list(held)
     return pl.pallas_call(
-        lambda *refs: adam_kernel(groups, full_width, aliased, *refs),
+        lambda *refs: adam_kernel(groups, full_width, fetched is not None, *refs),
         out_shape=(
-            jax.ShapeDtypeStruct((rows, columns), jnp.float32),
-            jax.ShapeDtypeStruct((rows, columns), jnp.float32),
+            jax.ShapeDtypeStruct(table.shape, jnp.float32),
+            jax.ShapeDtypeStruct(table.shape, jnp.float32),
             jax.ShapeDtypeStruct(second.shape, jnp.float32),
         ),
-        in_specs=[SMEM] * 3 + [VMEM] * (len(flat) + 1) + [ANY, ANY, VMEM, VMEM] + [HBM] * aliased,
+        in_specs=[SMEM] * 4
+        + [VMEM] * (len(flat) + 2)
+        + [ANY, ANY, VMEM, VMEM]
+        + [VMEM] * len(more)
+        + [HBM] * len(kept),
         out_specs=[HBM, HBM, VMEM],
         scratch_shapes=[
             pltpu.VMEM((2, count) + shape, jnp.float32),
@@ -321,20 +357,24 @@
             pltpu.SemaphoreType.DMA((2, count)),
             pltpu.VMEM(second.shape, jnp.float32),
         ],
-        input_output_aliases={n_in: 0, n_in + 1: 1} if aliased else {},
+        input_output_aliases={n_in: 0, n_in + 1: 1} if kept else {},
         compiler_params=pltpu.CompilerParams(vmem_limit_bytes=52 << 20),
         cost_estimate=pl.CostEstimate(
             flops=8 * count * size, bytes_accessed=20 * count * size, transcendentals=0
         ),
         name="adam_blocks",
-    )(rows_at, columns_at, own_hot, *flat, swapped, table, first, second, before, *(held or ()))
+    )(
+        rows_at, columns_at, where, hots, *flat, swapped, squares, table, first, second, before,
+        *more, *kept,
+    )
 
 
 def turned(row, wanted):
     return jnp.where(wanted, pltpu.roll(row, SLICE, 1), row)
 
 
-def parcel_kernel(hot_ref, table, first, second, out_ref, sems):
+def parcel_kernel(where_ref, hots, table, first, second, out_ref, sems):
+    hot_ref = [hots[where_ref[0], k] for k in range(2)]
     copies = []
     for which, source in enumerate((table, first)):
         for k in range(2):
@@ -355,16 +395,16 @@
         copy.wait()
 
 
-def parcel_of(own_hot, table, first, second):
+def parcel_of(where, hots, table, first, second):
     return pl.pallas_call(
         parcel_kernel,
         out_shape=jax.ShapeDtypeStruct((4 * SLICE + EXTRA, table.shape[1]), jnp.float32),
-        in_specs=[SMEM, ANY, ANY, VMEM],
+        in_specs=[SMEM, SMEM, ANY, ANY, VMEM],
         out_specs=VMEM,
         scratch_shapes=[pltpu.SemaphoreType.DMA((2, 2))],
         compiler_params=pltpu.CompilerParams(vmem_limit_bytes=52 << 20),
         name="parcel",
-    )(own_hot, table, first, second)
+    )(where, hots, table, first, second)
 
 
 def on_device(
@@ -387,21 +427,17 @@
     block, share = rows_dev // n_far, col_width // n_pair
     half = block // 2
 
-    own_hot = hot_slices[position]
     second_lines = moment_second.reshape(-1, LANES)
-    parcel = parcel_of(own_hot, table_weights, moment_first, second_lines)
-    swap = [(t, (t + n_table // 2) % n_table) for t in range(n_table)]
-    swapped = lax.ppermute(parcel, "table", swap)
     slots = dedup_map.reshape(-1, GROUP * dedup_map.shape[1])
     slot_grad = slot_sums(
         slots, upstream_grad.T, hot_slices, row_counts, unique_rows, n_pair, rows_dev
     )
-    slot_grad, swapped, own_hot, second_lines, far_at, pair_at = lax.optimization_barrier(
-        (slot_grad, swapped, own_hot, second_lines, far_at, pair_at)
+    slot_grad, position, far_at, pair_at = lax.optimization_barrier(
+        (slot_grad, position, far_at, pair_at)
     )
     got = lax.all_to_all(slot_grad, ("table", "pair"), split_axis=0, concat_axis=0, tiled=True)
-    got, swapped, own_hot, second_lines, far_at, pair_at = lax.optimization_barrier(
-        (got, swapped, own_hot, second_lines, far_at, pair_at)
+    got, position, far_at, pair_at, second_lines = lax.optimization_barrier(
+        (got, position, far_at, pair_at, second_lines)
     )
 
     def begin_at(*offsets):
@@ -416,35 +452,51 @@
     plus, minus = place_next(pieces, aims, begin_at(1, -1), block)
     rise = jnp.concatenate([plus[:half] + rise, plus[half:]], axis=0)
     fall = jnp.concatenate([minus[:half], minus[half:] + fall], axis=0)
+    where = position.reshape(1)
+    rise, fall, where, second_lines = lax.optimization_barrier((rise, fall, where, second_lines))
     rise, fall = send(rise, "far", n_far, 1), send(fall, "far", n_far, -1)
+    parcel = parcel_of(where, hot_slices, table_weights, moment_first, second_lines)
+    swapped = send(parcel, "table", n_table, n_table // 2)
     (mine,) = place_next(pieces, aims, begin_at(0), block)
     mine = mine + rise + fall
-    squares = lax.psum(jnp.sum(mine * mine, axis=1), ("pair", "col")).reshape(-1, share)
-    squares = jnp.pad(squares, ((0, EXTRA - squares.shape[0]), (0, 0)))
-    own = jnp.concatenate([mine, squares], axis=0)
+    mine, swapped = lax.optimization_barrier((mine, swapped))
 
     ring = ("far", "pair")
     me = far_at * n_pair + pair_at
-    common = (own_hot, swapped, table_weights, moment_first, second_lines)
-
-    def update(arrived, second, held=None):
-        at = jnp.stack([(me + o + n_dp) % n_dp for o, _ in arrived]).astype(jnp.int32)
-        parts = [p for _, p in arrived]
-        return adam_blocks(
-            at // n_pair, at % n_pair, parts, (block, share), full_width, common, second, held
-        )
-
-    rise, fall = send(own, ring, n_dp, 1), send(own, ring, n_dp, -1)
-    arrived = [(0, [own]), (-1, [rise]), (1, [fall])]
+    n_all = n_dp * lax.axis_size("col")
+    own_squares = jnp.sum(mine * mine, axis=1).reshape(-1, LANES)
+    own_squares = jnp.pad(own_squares, ((0, EXTRA - own_squares.shape[0]), (0, 0)))
+    squares = lax.all_to_all(
+        jnp.broadcast_to(own_squares[None], (n_all,) + own_squares.shape),
+        ("far", "pair", "col"),
+        split_axis=0,
+        concat_axis=0,
+        tiled=True,
+    )
+    common = (where, hot_slices, swapped, squares, table_weights, moment_first, second_lines)
+    shape = (block, share)
+
+    def at_ring(offsets):
+        at = jnp.stack([(me + o + n_dp) % n_dp for o in offsets]).astype(jnp.int32)
+        return at // n_pair, at % n_pair
+
+    def update(offsets, parts, second, held=None, fetched=None):
+        return adam_blocks(*at_ring(offsets), parts, shape, full_width, common, second, held, fetched)
+
+    rise, fall = send(mine, ring, n_dp, 1), send(mine, ring, n_dp, -1)
+    parts = [[mine], [rise], [fall]]
     rise, fall = send(rise, ring, n_dp, 1), send(fall, ring, n_dp, -1)
-    weights, first, second = update(arrived, second_lines)
+    weights, first, second = update((0, -1, 1), parts, second_lines)
     rise, fall, second = lax.optimization_barrier((rise, fall, second))
-    arrived = [(-2, [rise]), (2, [fall])]
+    parts = [[rise], [fall]]
     rise, fall = send(rise, ring, n_dp, 1), send(fall, ring, n_dp, -1)
-    arrived += [(-3, [rise]), (3, [fall])]
+    fetched = fetch_block(*at_ring((4,)), shape, common)
+    weights, first, second = update((-2, 2), parts, second, (weights, first))
+    rise, fall, second, fetched = lax.optimization_barrier((rise, fall, second, fetched))
+    parts = [[rise], [fall]]
     rise, fall = send(rise[:half], ring, n_dp, 1), send(fall[half:], ring, n_dp, -1)
-    weights, first, second = update(arrived, second, (weights, first))
-    weights, first, second = update([(4, [rise, fall])], second, (weights, first))
+    weights, first, second = update((-3, 3), parts, second, (weights, first))
+    weights, first, second = update((4,), [[rise, fall]], second, (weights, first), fetched)
     return (weights, first, second.reshape(-1))
 
 

time: 157 us -> 150 us (0.955)
  waiting for transfers between devices: 20.9 us -> 13.7 us
  blocking collectives: 66 us -> 61 us
  Pallas kernels: 36.6 us -> 40.6 us
  starting transfers between devices: 25.8 us -> 28.6 us
    ppermute x12 -> x13, waiting for transfers between devices: 20.9 us -> 9.22 us  [send(): lax.ppermute(value, axes, [(i, (i + step) % count) for i in range(count)])]
    psum x1 -> x0, blocking collectives: 5.67 us -> none  [on_device(): lax.psum(jnp.sum(mine * mine, axis=1), ('pair', 'col')).reshape(-1, share)]
    all_to_all x0 -> x1, starting transfers between devices: none -> 4.61 us  [on_device(): lax.all_to_all(jnp.broadcast_to(own_squares[None], (n_all,) + own_squares...]
    all_to_all x0 -> x1, waiting for transfers between devices: none -> 4.52 us  [on_device(): lax.all_to_all(jnp.broadcast_to(own_squares[None], (n_all,) + own_squares...]
    pallas_call x3 -> x5, Pallas kernels: 9.44 us -> 13 us  [the longest x4 11.3 us: adam_blocks(): pl.pallas_call(lambda *refs: adam_kernel(groups, full_width, fetched is n...]
    ppermute x1 -> x0, starting transfers between devices: 2.21 us -> none  [on_device(): swapped = lax.ppermute(parcel, 'table', swap)]
    ppermute x12 -> x13, starting transfers between devices: 23.6 us -> 24 us  [send(): lax.ppermute(value, axes, [(i, (i + step) % count) for i in range(count)])]
    unnamed x21 -> x13, local copies, waits for them, and re-layouts: 3.4 us -> 3.13 us
  transfers between devices with their start and end apart: 13 -> 14, of which waited for: 8 -> 5; matrix products, arithmetic and copies ran while one was open for 1% -> 1% of each run, Pallas kernels for 18% -> 13%
where the time goes in v5:
time: 150 us
  blocking collectives  61 us (41%)
  Pallas kernels  40.6 us (27%)
  starting transfers between devices  28.6 us (19%)
  waiting for transfers between devices  13.7 us (9%)
  local copies, waits for them, and re-layouts  3.99 us (3%)
    all_to_all x1, blocking collectives, on_device(): lax.all_to_all(slot_grad, ('table', 'pair'), split_axis=0, concat_axis=0,...  61 us
    ppermute x13, starting transfers between devices, send(): lax.ppermute(value, axes, [(i, (i + step) % count) for i in range(count)])  24 us
    pallas_call x1, Pallas kernels, slot_sums(): pl.pallas_call(lambda *refs: slot_kernel(rows_dev, *refs), out_shape=jax....  13.6 us
    pallas_call x4, Pallas kernels, adam_blocks(): pl.pallas_call(lambda *refs: adam_kernel(groups, full_width, fetched is n...  11.3 us
    ppermute x13, waiting for transfers between devices, send(): lax.ppermute(value, axes, [(i, (i + step) % count) for i in range(count)])  9.22 us
    pallas_call x2, Pallas kernels, place_next(): pl.pallas_call(place_next_kernel, out_shape=tuple((jax.ShapeDtypeStruct((...  7.41 us
    pallas_call x1, Pallas kernels, place_first(): pl.pallas_call(place_first_kernel, out_shape=(jax.ShapeDtypeStruct((2 * c...  4.63 us
    all_to_all x1, starting transfers between devices, on_device(): lax.all_to_all(jnp.broadcast_to(own_squares[None], (n_all,) + own_squares...  4.61 us
  transfers between devices with their start and end apart: 14, of which 5 were waited for; matrix products, arithmetic and copies ran while one was open for 1% of the time, Pallas kernels for 13%

profile of v5, /device:TPU:2, one launch (start us, length us, event | category | flops | bytes accessed | tf_op | source)
XLA Modules:
  0.0 149.8 jit_solution(4881253877065600628)
XLA Ops:
  0.6 0.0 copy-start.2
  0.6 0.0 copy-start.1
  0.7 0.8 copy.28.refs_2_.hots.refs_3_
  1.4 1.2 copy.27
  2.7 1.1 copy.26
  3.8 0.2 reshape.26.refs_0_
  4.0 0.0 copy-done.2
  4.0 0.0 copy-done.1
  4.0 13.6 %slot_sums.1 = f32[32,264,128]{2,1,0:T(8,128)} custom-call(s32[128,256]{1,0:T(8,128)S(1)} %reshape.26.refs_0_, bf16[256,1024]{1,0:T(8,128)(2,1)S(1)} %bitcast.17, s32[16,2]{1,0:T(8,128)S(1)} %copy.28.refs_2_.hots.refs_3_, s32[1,16]{1,0:T(1,128)S(1)} %copy-done.2, s32[1,16,256]{2,1,0:T(8,128)S(1)} %copy-done.1), custom_call_target="tpu_custom_call" | custom-call | tf_op jit(solution)/shard_map/slot_sums/pallas_call | solution.py:115
  17.5 61.0 %all_to_all.10.got_ref = f32[32,264,128]{2,1,0:T(8,128)} all-to-all(f32[32,264,128]{2,1,0:T(8,128)} %slot_sums.1), channel_id=1, replica_groups=mesh['table'=16,'far'=4,'pair'=2,'col'=2] {'table','pair'}, dimensions={0} | all-to-all | bytes 8650752 | tf_op jit(solution)/shard_map/all_to_all | solution.py:438
  78.6 4.6 %place_first.1 = (bf16[256,8192]{1,0:T(8,128)(2,1)S(1)}, s32[8,8192]{1,0:T(8,128)S(1)}, f32[512,128]{1,0:T(8,128)S(1)}) custom-call(s32[1]{0:T(128)} %bitcast.5.start_ref, f32[32,264,128]{2,1,0:T(8,128)} %all_to_all.10.got_ref), custom_call_target="tpu_custom_call" | custom-call | flops 2147483648 | bytes 8388608 | tf_op jit(solution)/shard_map/place_first/pallas_call | solution.py:185
  83.2 0.0 copy-start.3
  83.3 5.5 %collective-permute-start.1 = (f32[256,128]{1,0:T(8,128)S(1)}, f32[256,128]{1,0:T(8,128)S(1)}, u32[]{:S(2)}, u32[]{:S(2)}) collective-permute-start(f32[256,128]{1,0:T(8,128)S(1)} %get-tuple-element.89), channel_id=1, source_target_pairs={{0,12},{4,0},{8,4},{12,8},{1,13},{5,1},{9,5},{13,9},{2,14},{6,2},{... | collective-permute-start | bytes 393224 | tf_op jit(solution)/shard_map/ppermute | solution.py:447
  88.7 0.0 collective-permute-start
  88.7 0.1 pad_add_fusion.start_ref
  88.8 5.1 %place_next.2 = (f32[512,128]{1,0:T(8,128)S(1)}, f32[512,128]{1,0:T(8,128)S(1)}) custom-call(s32[2]{0:T(128)S(1)} %pad_add_fusion.start_ref, bf16[256,8192]{1,0:T(8,128)(2,1)S(1)} %get-tuple-element.49.pieces, s32[8,8192]{1,0:T(8,128)S(1)} %get-tuple-element.50.aims), custom_call_target="tpu_custom_call" | custom-call | flops 4294967296 | bytes 8388608 | tf_op jit(solution)/shard_map/place_next/pallas_call | solution.py:208
  93.9 0.0 copy-done.3
  93.9 0.0 copy-start
  93.9 0.0 collective-permute-done.1
  93.9 2.7 %collective-permute-done = f32[256,128]{1,0:T(8,128)S(1)} collective-permute-done((f32[256,128]{1,0:T(8,128)S(1)}, f32[256,128]{1,0:T(8,128)S(1)}, u32[]{:S(2)}, u32[]{:S(2)}) %collective-permute-start) | collective-permute-done | bytes 131104 | tf_op jit(solution)/shard_map/ppermute | solution.py:447
  96.6 0.1 slice_add_fusion.1
  96.8 0.3 collective-permute-start.2
  97.0 4.1 %collective-permute-start.3 = (f32[512,128]{1,0:T(8,128)S(1)}, f32[512,128]{1,0:T(8,128)S(1)}, u32[]{:S(2)}, u32[]{:S(2)}) collective-permute-start(f32[512,128]{1,0:T(8,128)S(1)} %pad_maximum_fusion.1), channel_id=1, source_target_pairs={{0,12},{4,0},{8,4},{12,8},{1,13},{5,1},{9,5},{13,9},{2,14},{6,2},{... | collective-permute-start | bytes 786440 | tf_op jit(solution)/shard_map/ppermute | solution.py:447
  101.1 0.0 copy-done
  101.2 0.0 copy-start.4
  101.2 2.0 %parcel.1 = f32[264,256]{1,0:T(8,128)S(1)} custom-call(s32[1]{0:T(128)} %bitcast.6.where_ref.refs_2_, s32[16,2]{1,0:T(8,128)S(1)} %copy.28.refs_2_.hots.refs_3_, f32[2048,256]{1,0:T(8,128)} %refs_8_.5, f32[2048,256]{1,0:T(8,128)} %refs_9_.7, f32[16,128]{1,0:T(8,128)S(1)} %bitcast.18), custom_call_target="tpu_custom_call" | custom-call | tf_op jit(solution)/shard_map/parcel/pallas_call | solution.py:399
  103.1 1.5 %collective-permute-start.4 = (f32[264,256]{1,0:T(8,128)S(1)}, f32[264,256]{1,0:T(8,128)S(1)}, u32[]{:S(2)}, u32[]{:S(2)}) collective-permute-start(f32[264,256]{1,0:T(8,128)S(1)} %parcel.1), channel_id=1, source_target_pairs={{0,128},{16,144},{32,160},{48,176},{64,192},{80,208},{96,224},{112... | collective-permute-start | bytes 811016 | tf_op jit(solution)/shard_map/ppermute | solution.py:447
  104.6 0.0 copy-done.4
  104.7 2.4 %place_next.3 = f32[512,128]{1,0:T(8,128)S(1)} custom-call(s32[1]{0:T(128)} %bitcast.7.start_ref, bf16[256,8192]{1,0:T(8,128)(2,1)S(1)} %copy-done.4, s32[8,8192]{1,0:T(8,128)S(1)} %get-tuple-element.50.aims), custom_call_target="tpu_custom_call" | custom-call | flops 2147483648 | bytes 8388608 | tf_op jit(solution)/shard_map/place_next/pallas_call | solution.py:208
  107.0 4.2 %collective-permute-done.2 = f32[512,128]{1,0:T(8,128)S(1)} collective-permute-done((f32[512,128]{1,0:T(8,128)S(1)}, f32[512,128]{1,0:T(8,128)S(1)}, u32[]{:S(2)}, u32[]{:S(2)}) %collective-permute-start.2) | collective-permute-done | bytes 262176 | tf_op jit(solution)/shard_map/ppermute | solution.py:447
  111.2 0.0 collective-permute-done.3
  111.3 0.0 collective-permute-done.4.refs_7_.refs_6_.swapped
  111.3 2.8 %collective-permute-start.7 = (f32[512,128]{1,0:T(8,128)S(1)}, f32[512,128]{1,0:T(8,128)S(1)}, u32[]{:S(2)}, u32[]{:S(2)}) collective-permute-start(f32[512,128]{1,0:T(8,128)S(1)} %add_add_fusion.refs_4_), channel_id=1, source_target_pairs={{0,14},{2,0},{4,2},{6,4},{8,6},{10,8},{12,10},{14,12},{1,15},{3,1}... | collective-permute-start | bytes 786440 | tf_op jit(solution)/shard_map/ppermute | solution.py:447
  114.1 0.0 collective-permute-start.5
  114.1 0.1 and_select_fusion.4
  114.2 0.1 multiply_reduce_fusion
  114.4 0.6 broadcast_in_dim.2
  115.0 4.6 %all-to-all-start.1 = ((f32[16,8,128]{2,1,0:T(8,128)}), f32[16,8,128]{2,1,0:T(8,128)S(1)}, u32[]{:S(2)}, u32[]{:S(2)}) async-start(f32[16,8,128]{2,1,0:T(8,128)} %broadcast_in_dim.2), calls=%async_computation.1 | async-start | bytes 131072 | tf_op jit(solution)/shard_map/all_to_all | solution.py:469
  119.6 0.0 collective-permute-done.7.refs_6_
  119.6 3.2 %collective-permute-start.8 = (f32[512,128]{1,0:T(8,128)S(1)}, f32[512,128]{1,0:T(8,128)S(1)}, u32[]{:S(2)}, u32[]{:S(2)}) collective-permute-start(f32[512,128]{1,0:T(8,128)S(1)} %collective-permute-done.7.refs_6_), channel_id=1, source_target_pairs={{0,14},{2,0},{4,2},{6,4},{8,6},{10,8},{12,10},{14,12},{1,15},{3,1}... | collective-permute-start | bytes 786440 | tf_op jit(solution)/shard_map/ppermute | solution.py:447
  122.9 0.0 collective-permute-done.5.refs_5_
  122.9 0.0 collective-permute-start.6
  122.9 0.1 and_select_fusion.2
  123.0 4.5 %all-to-all-done.1.refs_8_.refs_7_ = f32[16,8,128]{2,1,0:T(8,128)S(1)} async-done(((f32[16,8,128]{2,1,0:T(8,128)}), f32[16,8,128]{2,1,0:T(8,128)S(1)}, u32[]{:S(2)}, u32[]{:S(2)}) %all-to-all-start.1) | async-done | bytes 65568 | tf_op jit(solution)/shard_map/all_to_all | solution.py:469
  127.5 3.1 %adam_blocks.4 = (f32[2048,256]{1,0:T(8,128)}, f32[2048,256]{1,0:T(8,128)}, f32[16,128]{1,0:T(8,128)S(1)}) custom-call(s32[3]{0:T(128)S(1)} %and_select_fusion.5.refs_0_, s32[3]{0:T(128)S(1)} %get-tuple-element.85.refs_1_, s32[1]{0:T(128)} %bitcast.6.where_ref.refs_2_, s32[16,2]{1,0:T(8,128)S(1)} %copy.28.refs_2_.hots.refs_3_, ...), custom_call_target="tpu_custom_call" | custom-call | flops 1572864 | bytes 3932160 | tf_op jit(solution)/shard_map/adam_blocks/pallas_call | solution.py:341
  130.7 0.0 collective-permute-done.8.refs_5_
  130.7 1.7 %collective-permute-done.6.refs_4_ = f32[512,128]{1,0:T(8,128)S(1)} collective-permute-done((f32[512,128]{1,0:T(8,128)S(1)}, f32[512,128]{1,0:T(8,128)S(1)}, u32[]{:S(2)}, u32[]{:S(2)}) %collective-permute-start.6) | collective-permute-done | bytes 262176 | tf_op jit(solution)/shard_map/ppermute | solution.py:447
  132.4 0.0 collective-permute-start.9
  132.4 3.2 %collective-permute-start.10 = (f32[512,128]{1,0:T(8,128)S(1)}, f32[512,128]{1,0:T(8,128)S(1)}, u32[]{:S(2)}, u32[]{:S(2)}) collective-permute-start(f32[512,128]{1,0:T(8,128)S(1)} %collective-permute-done.8.refs_5_), channel_id=1, source_target_pairs={{0,14},{2,0},{4,2},{6,4},{8,6},{10,8},{12,10},{14,12},{1,15},{3,1}... | collective-permute-start | bytes 786440 | tf_op jit(solution)/shard_map/ppermute | solution.py:447
  135.6 0.1 and_select_fusion
  135.7 0.1 and_select_fusion.3.refs_0_
  135.8 1.7 %fetch_block.1.refs_12_ = f32[2,1,512,128]{3,2,1,0:T(8,128)S(1)} custom-call(s32[1]{0:T(128)S(6)} %select_n.97.row_ref.refs_0_, s32[1]{0:T(128)S(6)} %select_n.98.column_ref.refs_1_, s32[1]{0:T(128)} %bitcast.6.where_ref.refs_2_, s32[16,2]{1,0:T(8,128)S(1)} %copy.28.refs_2_.hots.refs_3_, f32[264,256]{1,0:T(8,128)S(1)} %collective-permute-done.4.refs_7_.refs_6_.swapped, ...), custom_call_target="tpu_custom_call" | custom-call | tf_op jit(solution)/shard_map/fetch_block/pallas_call | solution.py:255
  137.5 2.9 %adam_blocks.5 = (f32[2048,256]{1,0:T(8,128)}, f32[2048,256]{1,0:T(8,128)}, f32[16,128]{1,0:T(8,128)S(1)}) custom-call(s32[2]{0:T(128)S(1)} %and_select_fusion.3.refs_0_, s32[2]{0:T(128)S(1)} %get-tuple-element.83.refs_1_, s32[1]{0:T(128)} %bitcast.6.where_ref.refs_2_, ...), custom_call_target="tpu_custom_call", output_to_operand_aliasing={{0}: (12, {}), {1}: (13, {})} | custom-call | flops 1048576 | bytes 2621440 | tf_op jit(solution)/shard_map/adam_blocks/pallas_call | solution.py:341
  140.4 0.5 collective-permute-done.9.refs_4_
  141.0 0.0 collective-permute-done.10.refs_5_
  141.0 0.6 collective-permute-start.11
  141.6 2.7 %collective-permute-start.12 = (f32[256,128]{1,0:T(8,128)S(1)}, f32[256,128]{1,0:T(8,128)S(1)}, u32[]{:S(2)}, u32[]{:S(2)}) collective-permute-start(f32[256,128]{1,0:T(8,128)S(1)} %slice.31), channel_id=1, source_target_pairs={{0,14},{2,0},{4,2},{6,4},{8,6},{10,8},{12,10},{14,12},{1,15},{3,1}... | collective-permute-start | bytes 393224 | tf_op jit(solution)/shard_map/ppermute | solution.py:447
  144.3 0.1 and_select_fusion.1.refs_0_
  144.4 2.9 %adam_blocks.6 = (f32[2048,256]{1,0:T(8,128)}, f32[2048,256]{1,0:T(8,128)}, f32[16,128]{1,0:T(8,128)S(1)}) custom-call(s32[2]{0:T(128)S(1)} %and_select_fusion.1.refs_0_, s32[2]{0:T(128)S(1)} %get-tuple-element.81.refs_1_, s32[1]{0:T(128)} %bitcast.6.where_ref.refs_2_, ...), custom_call_target="tpu_custom_call", output_to_operand_aliasing={{0}: (12, {}), {1}: (13, {})} | custom-call | flops 1048576 | bytes 2621440 | tf_op jit(solution)/shard_map/adam_blocks/pallas_call | solution.py:341
  147.3 0.0 collective-permute-done.11.refs_4_
  147.3 0.0 collective-permute-done.12.refs_5_
  147.3 2.3 %adam_blocks.7 = (f32[2048,256]{1,0:T(8,128)}, f32[2048,256]{1,0:T(8,128)}, f32[16,128]{1,0:T(8,128)}) custom-call(s32[1]{0:T(128)S(6)} %select_n.97.row_ref.refs_0_, s32[1]{0:T(128)S(6)} %select_n.98.column_ref.refs_1_, s32[1]{0:T(128)} %bitcast.6.where_ref.refs_2_, ...), custom_call_target="tpu_custom_call", output_to_operand_aliasing={{0}: (13, {}), {1}: (14, {})} | custom-call | flops 524288 | bytes 1310720 | tf_op jit(solution)/shard_map/adam_blocks/pallas_call | solution.py:341
  (8 shorter events, 0.1 us)
Async XLA Ops:
  0.6 3.3 %copy-start.2 = (s32[1,16]{1,0:T(1,128)S(1)}, s32[1,16]{1,0:T(1,128)}, u32[]{:S(2)}) copy-start(s32[1,16]{1,0:T(1,128)} %refs_3_.5) | copy-start | bytes 196
  0.6 3.3 %copy-start.1 = (s32[1,16,256]{2,1,0:T(8,128)S(1)}, s32[1,16,256]{2,1,0:T(8,128)}, u32[]{:S(2)}) copy-start(s32[1,16,256]{2,1,0:T(8,128)} %refs_4_.1) | copy-start | bytes 49156
  83.2 10.7 %copy-start.3 = (bf16[256,8192]{1,0:T(8,128)(2,1)}, bf16[256,8192]{1,0:T(8,128)(2,1)S(1)}, u32[]{:S(2)}) copy-start(bf16[256,8192]{1,0:T(8,128)(2,1)S(1)} %get-tuple-element.49.pieces) | copy-start | bytes 12582916
  83.3 10.6 %collective-permute-start.1 = (f32[256,128]{1,0:T(8,128)S(1)}, f32[256,128]{1,0:T(8,128)S(1)}, u32[]{:S(2)}, u32[]{:S(2)}) collective-permute-start(f32[256,128]{1,0:T(8,128)S(1)} %get-tuple-element.89), channel_id=1, source_target_pairs={{0,12},{4,0},{8,4},{12,8},{1,13},{5,1},{9,5},{13,9},{2,14},{6,2},{... | collective-permute-start | bytes 393224 | tf_op jit(solution)/shard_map/ppermute | solution.py:447
  88.7 7.9 %collective-permute-start = (f32[256,128]{1,0:T(8,128)S(1)}, f32[256,128]{1,0:T(8,128)S(1)}, u32[]{:S(2)}, u32[]{:S(2)}) collective-permute-start(f32[256,128]{1,0:T(8,128)S(1)} %get-tuple-element.90), channel_id=1, source_target_pairs={{0,4},{4,8},{8,12},{12,0},{1,5},{5,9},{9,13},{13,1},{2,6},{6,10},{... | collective-permute-start | bytes 393224 | tf_op jit(solution)/shard_map/ppermute | solution.py:447
  93.9 7.3 %copy-start = (f32[2048]{0:T(1024)S(1)}, f32[2048]{0:T(1024)}, u32[]{:S(2)}) copy-start(f32[2048]{0:T(1024)} %param.10) | copy-start | bytes 24580
  96.8 14.5 %collective-permute-start.2 = (f32[512,128]{1,0:T(8,128)S(1)}, f32[512,128]{1,0:T(8,128)S(1)}, u32[]{:S(2)}, u32[]{:S(2)}) collective-permute-start(f32[512,128]{1,0:T(8,128)S(1)} %pad_maximum_fusion), channel_id=1, source_target_pairs={{0,4},{4,8},{8,12},{12,0},{1,5},{5,9},{9,13},{13,1},{2,6},{6,10},{... | collective-permute-start | bytes 786440 | tf_op jit(solution)/shard_map/ppermute | solution.py:447
  97.0 14.2 %collective-permute-start.3 = (f32[512,128]{1,0:T(8,128)S(1)}, f32[512,128]{1,0:T(8,128)S(1)}, u32[]{:S(2)}, u32[]{:S(2)}) collective-permute-start(f32[512,128]{1,0:T(8,128)S(1)} %pad_maximum_fusion.1), channel_id=1, source_target_pairs={{0,12},{4,0},{8,4},{12,8},{1,13},{5,1},{9,5},{13,9},{2,14},{6,2},{... | collective-permute-start | bytes 786440 | tf_op jit(solution)/shard_map/ppermute | solution.py:447
  101.2 3.5 %copy-start.4 = (bf16[256,8192]{1,0:T(8,128)(2,1)S(1)}, bf16[256,8192]{1,0:T(8,128)(2,1)}, u32[]{:S(2)}) copy-start(bf16[256,8192]{1,0:T(8,128)(2,1)} %copy-done.3) | copy-start | bytes 12582916
  103.1 8.1 %collective-permute-start.4 = (f32[264,256]{1,0:T(8,128)S(1)}, f32[264,256]{1,0:T(8,128)S(1)}, u32[]{:S(2)}, u32[]{:S(2)}) collective-permute-start(f32[264,256]{1,0:T(8,128)S(1)} %parcel.1), channel_id=1, source_target_pairs={{0,128},{16,144},{32,160},{48,176},{64,192},{80,208},{96,224},{112... | collective-permute-start | bytes 811016 | tf_op jit(solution)/shard_map/ppermute | solution.py:447
  111.3 8.3 %collective-permute-start.7 = (f32[512,128]{1,0:T(8,128)S(1)}, f32[512,128]{1,0:T(8,128)S(1)}, u32[]{:S(2)}, u32[]{:S(2)}) collective-permute-start(f32[512,128]{1,0:T(8,128)S(1)} %add_add_fusion.refs_4_), channel_id=1, source_target_pairs={{0,14},{2,0},{4,2},{6,4},{8,6},{10,8},{12,10},{14,12},{1,15},{3,1}... | collective-permute-start | bytes 786440 | tf_op jit(solution)/shard_map/ppermute | solution.py:447
  114.1 8.7 %collective-permute-start.5 = (f32[512,128]{1,0:T(8,128)S(1)}, f32[512,128]{1,0:T(8,128)S(1)}, u32[]{:S(2)}, u32[]{:S(2)}) collective-permute-start(f32[512,128]{1,0:T(8,128)S(1)} %add_add_fusion.refs_4_), channel_id=1, source_target_pairs={{0,2},{2,4},{4,6},{6,8},{8,10},{10,12},{12,14},{14,0},{1,3},{3,5},... | collective-permute-start | bytes 786440 | tf_op jit(solution)/shard_map/ppermute | solution.py:447
  115.0 12.5 %all-to-all-start.1 = ((f32[16,8,128]{2,1,0:T(8,128)}), f32[16,8,128]{2,1,0:T(8,128)S(1)}, u32[]{:S(2)}, u32[]{:S(2)}) async-start(f32[16,8,128]{2,1,0:T(8,128)} %broadcast_in_dim.2), calls=%async_computation.1 | async-start | bytes 131072 | tf_op jit(solution)/shard_map/all_to_all | solution.py:469
  119.6 11.0 %collective-permute-start.8 = (f32[512,128]{1,0:T(8,128)S(1)}, f32[512,128]{1,0:T(8,128)S(1)}, u32[]{:S(2)}, u32[]{:S(2)}) collective-permute-start(f32[512,128]{1,0:T(8,128)S(1)} %collective-permute-done.7.refs_6_), channel_id=1, source_target_pairs={{0,14},{2,0},{4,2},{6,4},{8,6},{10,8},{12,10},{14,12},{1,15},{3,1}... | collective-permute-start | bytes 786440 | tf_op jit(solution)/shard_map/ppermute | solution.py:447
  122.9 9.5 %collective-permute-start.6 = (f32[512,128]{1,0:T(8,128)S(1)}, f32[512,128]{1,0:T(8,128)S(1)}, u32[]{:S(2)}, u32[]{:S(2)}) collective-permute-start(f32[512,128]{1,0:T(8,128)S(1)} %collective-permute-done.5.refs_5_), channel_id=1, source_target_pairs={{0,2},{2,4},{4,6},{6,8},{8,10},{10,12},{12,14},{14,0},{1,3},{3,5},... | collective-permute-start | bytes 786440 | tf_op jit(solution)/shard_map/ppermute | solution.py:447
  132.4 8.6 %collective-permute-start.9 = (f32[512,128]{1,0:T(8,128)S(1)}, f32[512,128]{1,0:T(8,128)S(1)}, u32[]{:S(2)}, u32[]{:S(2)}) collective-permute-start(f32[512,128]{1,0:T(8,128)S(1)} %collective-permute-done.6.refs_4_), channel_id=1, source_target_pairs={{0,2},{2,4},{4,6},{6,8},{8,10},{10,12},{12,14},{14,0},{1,3},{3,5},... | collective-permute-start | bytes 786440 | tf_op jit(solution)/shard_map/ppermute | solution.py:447
  132.4 8.6 %collective-permute-start.10 = (f32[512,128]{1,0:T(8,128)S(1)}, f32[512,128]{1,0:T(8,128)S(1)}, u32[]{:S(2)}, u32[]{:S(2)}) collective-permute-start(f32[512,128]{1,0:T(8,128)S(1)} %collective-permute-done.8.refs_5_), channel_id=1, source_target_pairs={{0,14},{2,0},{4,2},{6,4},{8,6},{10,8},{12,10},{14,12},{1,15},{3,1}... | collective-permute-start | bytes 786440 | tf_op jit(solution)/shard_map/ppermute | solution.py:447
  141.0 6.3 %collective-permute-start.11 = (f32[256,128]{1,0:T(8,128)S(1)}, f32[256,128]{1,0:T(8,128)S(1)}, u32[]{:S(2)}, u32[]{:S(2)}) collective-permute-start(f32[256,128]{1,0:T(8,128)S(1)} %slice.30), channel_id=1, source_target_pairs={{0,2},{2,4},{4,6},{6,8},{8,10},{10,12},{12,14},{14,0},{1,3},{3,5},... | collective-permute-start | bytes 393224 | tf_op jit(solution)/shard_map/ppermute | solution.py:447
  141.6 5.7 %collective-permute-start.12 = (f32[256,128]{1,0:T(8,128)S(1)}, f32[256,128]{1,0:T(8,128)S(1)}, u32[]{:S(2)}, u32[]{:S(2)}) collective-permute-start(f32[256,128]{1,0:T(8,128)S(1)} %slice.31), channel_id=1, source_target_pairs={{0,14},{2,0},{4,2},{6,4},{8,6},{10,8},{12,10},{14,12},{1,15},{3,1}... | collective-permute-start | bytes 393224 | tf_op jit(solution)/shard_map/ppermute | solution.py:447

commit v6 on v5

--- a/solution.py
+++ b/solution.py
@@ -38,14 +38,14 @@
 
 
 def target_row(owner, hot_ref, count_ref, rows, rows_dev):
-    owners, n_hots = hot_ref.shape
+    n_hots, owners = hot_ref.shape
     partner = (owner + owners // 2) % owners
     local_row = rows % rows_dev
     from_partner = rows // rows_dev == partner
     target = local_row
     for k in range(n_hots):
-        moved = from_partner & (local_row // SLICE == hot_ref[partner, k])
-        target = jnp.where(moved, hot_ref[owner, k] * SLICE + local_row % SLICE, target)
+        moved = from_partner & (local_row // SLICE == hot_ref[k, partner])
+        target = jnp.where(moved, hot_ref[k, owner] * SLICE + local_row % SLICE, target)
     used = lax.broadcasted_iota(jnp.int32, rows.shape, 1) < count_ref[0, owner]
     return jnp.where(used, target, rows_dev)
 
@@ -58,7 +58,7 @@
     sample = lax.broadcasted_iota(jnp.int32, (1, span), 1) // (span // GROUP)
     left_at = counting((highs * GROUP, span))
     right_at = counting((LOW, span))
-    batch = 16
+    batch = 32
 
     def count(step, carry):
         first = pl.multiple_of(step * batch, batch)
@@ -151,20 +151,39 @@
 
     for k in range(sems.shape[0]):
         fetch(k).start()
-    for source in range(sources):
-        if source % batch == 0:
-            fetch(source // batch).wait()
-        for side in range(CAP // lanes):
-            value = held[source, side * columns : (side + 1) * columns, :]
-            upper = value.astype(jnp.bfloat16)
-            lower = (value - upper.astype(jnp.float32)).astype(jnp.bfloat16)
-            at = source * CAP + side * lanes
-            pieces[:columns, at : at + lanes] = upper
-            pieces[columns:, at : at + lanes] = lower
-            aim_at = height - EXTRA + side * EXTRA * lanes // CAP
-            aim = held[source, aim_at : aim_at + 1, :].astype(jnp.int32)
-            aims[:, at : at + lanes] = jnp.broadcast_to(aim, (EXTRA, lanes))
-    add_block(pieces, aims, start_ref[0], out_ref, select)
+    rows = out_ref.shape[0]
+    place = counting((CAP, CAP))
+    span = batch * CAP
+    sums = [jnp.zeros((CAP, 2 * columns), jnp.float32) for _ in range(rows // CAP)]
+    for k in range(sems.shape[0]):
+        fetch(k).wait()
+        for source in range(k * batch, (k + 1) * batch):
+            for side in range(CAP // lanes):
+                value = held[source, side * columns : (side + 1) * columns, :]
+                upper = value.astype(jnp.bfloat16)
+                lower = (value - upper.astype(jnp.float32)).astype(jnp.bfloat16)
+                at = source * CAP + side * lanes
+                pieces[:columns, at : at + lanes] = upper
+                pieces[columns:, at : at + lanes] = lower
+                aim_at = height - EXTRA + side * EXTRA * lanes // CAP
+                aim = held[source, aim_at : aim_at + 1, :].astype(jnp.int32)
+                aims[:, at : at + lanes] = jnp.broadcast_to(aim, (EXTRA, lanes))
+        for part in range(rows // CAP):
+            for at in range(k * span, (k + 1) * span, CAP):
+                row = aims[:1, at : at + CAP] - (start_ref[0] + part * CAP)
+                row = digits(jnp.where((row >= 0) & (row < CAP), row, -1))
+                select[part * CAP : (part + 1) * CAP, at - k * span : at - k * span + CAP] = one_hot(
+                    place, row
+                )
+            sums[part] += lax.dot_general(
+                select[part * CAP : (part + 1) * CAP, :span],
+                pieces[:, k * span : (k + 1) * span],
+                NT,
+                preferred_element_type=jnp.float32,
+            )
+    for part in range(rows // CAP):
+        both = sums[part]
+        out_ref[part * CAP : (part + 1) * CAP, :] = both[:, :columns] + both[:, columns:]
 
 
 def place_next_kernel(start_ref, pieces, aims, *refs):
@@ -192,7 +211,7 @@
         in_specs=[SMEM, HBM],
         out_specs=[VMEM] * 3,
         scratch_shapes=[
-            pltpu.VMEM((CAP, width), jnp.bfloat16),
+            pltpu.VMEM((block, width // 8), jnp.bfloat16),
             pltpu.VMEM(got.shape, jnp.float32),
             pltpu.SemaphoreType.DMA((8,)),
         ],
@@ -231,7 +250,7 @@
     rows, columns = held.shape[2:]
     per_block = rows // SLICE
     for k in range(2):
-        hot = hots[where_ref[0], k]
+        hot = hots[k, where_ref[0]]
 
         @pl.when(hot // per_block == rows_at)
         def _():
@@ -243,41 +262,56 @@
 
 
 def fetch_kernel(row_ref, column_ref, where_ref, hots, swapped, table, first, held, sems):
-    for copy in block_copies(table, first, held, sems, row_ref[0], column_ref[0], 0, False):
-        copy.start()
-    for copy in block_copies(table, first, held, sems, row_ref[0], column_ref[0], 0, False):
-        copy.wait()
-    put_swapped(where_ref, hots, swapped, held, row_ref[0], column_ref[0], 0)
-
-
-def fetch_block(rows_at, columns_at, shape, common):
-    where, hots, swapped, _, table, first, _ = common
+    count = held.shape[1]
+    copies = [
+        block_copies(table, first, held, sems, row_ref[0], column_ref[i], i, False)
+        for i in range(count)
+    ]
+    for i in range(count):
+        for copy in copies[i]:
+            copy.start()
+    for i in range(count):
+        for copy in copies[i]:
+            copy.wait()
+        put_swapped(where_ref, hots, swapped, held, row_ref[0], column_ref[i], i)
+
+
+def fetch_blocks(rows_at, columns_at, shape, common):
+    where, hots, swapped, table, first, _ = common
+    count = columns_at.shape[0]
     return pl.pallas_call(
         fetch_kernel,
-        out_shape=jax.ShapeDtypeStruct((2, 1) + shape, jnp.float32),
+        out_shape=jax.ShapeDtypeStruct((2, count) + shape, jnp.float32),
         in_specs=[SMEM] * 4 + [VMEM, ANY, ANY],
         out_specs=VMEM,
-        scratch_shapes=[pltpu.SemaphoreType.DMA((2, 1))],
+        scratch_shapes=[pltpu.SemaphoreType.DMA((2, count))],
         compiler_params=pltpu.CompilerParams(vmem_limit_bytes=52 << 20),
-        name="fetch_block",
+        name="fetch_blocks",
     )(rows_at, columns_at, where, hots, swapped, table, first)
 
 
-def adam_kernel(groups, full_width, fetched, *refs):
-    count = len(groups)
-    row_ref, column_ref, where_ref, hots = refs[:4]
-    parts = refs[4 : 4 + sum(groups)]
-    swapped, squares, table, first, second, before = refs[4 + sum(groups) : 10 + sum(groups)]
+def adam_kernel(layout, n_parts, full_width, fetched, *refs):
+    count = len(layout)
+    row_ref, column_ref, flip_ref, where_ref, hots = refs[:5]
+    parts = refs[5 : 5 + n_parts]
+    swapped, table, first, second, before = refs[5 + n_parts : 10 + n_parts]
     out_table, out_first, out_second, held, in_sem, out_sem, placed_second = refs[-7:]
     rows, columns = held.shape[2:]
     lines = rows // LANES
-    source = refs[10 + sum(groups)] if fetched else held
+    source = refs[10 + n_parts] if fetched else held
+    block = row_ref[0]
 
     def arrivals(i):
-        return block_copies(table, first, held, in_sem, row_ref[i], column_ref[i], i, False)
+        return block_copies(table, first, held, in_sem, block, column_ref[i], i, False)
 
     def returns(i):
-        return block_copies(out_table, out_first, held, out_sem, row_ref[i], column_ref[i], i, True)
+        return block_copies(out_table, out_first, held, out_sem, block, column_ref[i], i, True)
+
+    def read(piece, begin, end):
+        here, there = (parts[k] for k in piece)
+        if here is there:
+            return here[begin:end, :]
+        return jnp.where(flip_ref[0] == 0, here[begin:end, :], there[begin:end, :])
 
     if not fetched:
         for i in range(count):
@@ -289,36 +323,32 @@
     line_at = lax.broadcasted_iota(jnp.int32, placed.shape, 0)
     side_at = lax.broadcasted_iota(jnp.int32, placed.shape, 1) // SLICE
     for k in range(2):
-        hot = hots[where_ref[0], k]
+        hot = hots[k, where_ref[0]]
         here = (line_at == hot // 2) & (side_at == hot % 2)
         placed = jnp.where(here, turned(lead, hot % 2 != k), placed)
     placed_second[...] = placed
-    blocks = second.shape[0] // lines
-    sharers = squares.shape[0] // blocks
-    begin = 0
+    total = jnp.zeros((lines, LANES), jnp.float32)
+    for pieces in layout:
+        tail = parts[pieces[-1][0]].shape[0] - EXTRA
+        total += read(pieces[-1], tail, tail + lines)
+    old = placed_second[pl.ds(block * lines, lines), :]
+    fresh = beta_two * old + (1.0 - beta_two) * (total / full_width)
+    out_second[pl.ds(block * lines, lines), :] = fresh
+    scaled = jnp.sqrt(fresh / (1.0 - beta_two**8)) + eps_value
+    rates = (learn_rate / (1.0 - beta_one**8)) / scaled
+    rates = [jnp.broadcast_to(rates[k : k + 1, :], (LANES, LANES)).T for k in range(lines)]
     for i in range(count):
-        mine = parts[begin : begin + groups[i]]
-        begin += groups[i]
-        block = row_ref[i]
-        total = jnp.sum(squares[pl.ds(block * sharers, sharers)], axis=0)[:lines]
-        old = placed_second[pl.ds(block * lines, lines), :]
-        fresh = beta_two * old + (1.0 - beta_two) * (total / full_width)
-        out_second[pl.ds(block * lines, lines), :] = fresh
-        scaled = jnp.sqrt(fresh / (1.0 - beta_two**8)) + eps_value
-        rates = (learn_rate / (1.0 - beta_one**8)) / scaled
         if not fetched:
             for copy in arrivals(i):
                 copy.wait()
             put_swapped(where_ref, hots, swapped, held, block, column_ref[i], i)
         at = 0
-        for part in mine:
-            for top in range(0, part.shape[0], LANES):
-                line = at // LANES
-                rate = jnp.broadcast_to(rates[line : line + 1, :], (LANES, LANES)).T
+        for piece in layout[i]:
+            for top in range(0, parts[piece[0]].shape[0] - LANES + 1, LANES):
                 span = slice(at, at + LANES)
-                gradient = part[top : top + LANES, :]
+                gradient = read(piece, top, top + LANES)
                 moment = beta_one * source[1, i, span, :] + (1.0 - beta_one) * gradient
-                weight = source[0, i, span, :] - moment * rate
+                weight = source[0, i, span, :] - moment * rates[at // LANES]
                 held[1, i, span, :] = moment
                 held[0, i, span, :] = weight
                 at += LANES
@@ -329,24 +359,23 @@
             copy.wait()
 
 
-def adam_blocks(rows_at, columns_at, parts, shape, full_width, common, before, held=None, fetched=None):
-    groups = tuple(len(p) for p in parts)
-    flat = [ref for p in parts for ref in p]
-    where, hots, swapped, squares, table, first, second = common
-    count = len(groups)
+def adam_block(rows_at, columns_at, flip, layout, parts, full_width, common, before, held=None, fetched=None):
+    where, hots, swapped, table, first, second = common
+    count = len(layout)
+    shape = (parts[0].shape[0] - EXTRA, parts[0].shape[1])
     more = [] if fetched is None else [fetched]
-    n_in = 10 + len(flat) + len(more)
+    kept = [] if held is None else list(held)
+    n_in = 10 + len(parts) + len(more)
     size = shape[0] * shape[1]
-    kept = [] if held is None else list(held)
     return pl.pallas_call(
-        lambda *refs: adam_kernel(groups, full_width, fetched is not None, *refs),
+        lambda *refs: adam_kernel(layout, len(parts), full_width, fetched is not None, *refs),
         out_shape=(
             jax.ShapeDtypeStruct(table.shape, jnp.float32),
             jax.ShapeDtypeStruct(table.shape, jnp.float32),
             jax.ShapeDtypeStruct(second.shape, jnp.float32),
         ),
-        in_specs=[SMEM] * 4
-        + [VMEM] * (len(flat) + 2)
+        in_specs=[SMEM] * 5
+        + [VMEM] * (len(parts) + 1)
         + [ANY, ANY, VMEM, VMEM]
         + [VMEM] * len(more)
         + [HBM] * len(kept),
@@ -358,13 +387,13 @@
             pltpu.VMEM(second.shape, jnp.float32),
         ],
         input_output_aliases={n_in: 0, n_in + 1: 1} if kept else {},
-        compiler_params=pltpu.CompilerParams(vmem_limit_bytes=52 << 20),
+        compiler_params=pltpu.CompilerParams(vmem_limit_bytes=51 << 20),
         cost_estimate=pl.CostEstimate(
             flops=8 * count * size, bytes_accessed=20 * count * size, transcendentals=0
         ),
-        name="adam_blocks",
+        name="adam_block",
     )(
-        rows_at, columns_at, where, hots, *flat, swapped, squares, table, first, second, before,
+        rows_at, columns_at, flip, where, hots, *parts, swapped, table, first, second, before,
         *more, *kept,
     )
 
@@ -374,7 +403,7 @@
 
 
 def parcel_kernel(where_ref, hots, table, first, second, out_ref, sems):
-    hot_ref = [hots[where_ref[0], k] for k in range(2)]
+    hot_ref = [hots[k, where_ref[0]] for k in range(2)]
     copies = []
     for which, source in enumerate((table, first)):
         for k in range(2):
@@ -427,10 +456,11 @@
     block, share = rows_dev // n_far, col_width // n_pair
     half = block // 2
 
+    hots = hot_slices.T
     second_lines = moment_second.reshape(-1, LANES)
     slots = dedup_map.reshape(-1, GROUP * dedup_map.shape[1])
     slot_grad = slot_sums(
-        slots, upstream_grad.T, hot_slices, row_counts, unique_rows, n_pair, rows_dev
+        slots, upstream_grad.T, hots, row_counts, unique_rows, n_pair, rows_dev
     )
     slot_grad, position, far_at, pair_at = lax.optimization_barrier(
         (slot_grad, position, far_at, pair_at)
@@ -455,48 +485,50 @@
     where = position.reshape(1)
     rise, fall, where, second_lines = lax.optimization_barrier((rise, fall, where, second_lines))
     rise, fall = send(rise, "far", n_far, 1), send(fall, "far", n_far, -1)
-    parcel = parcel_of(where, hot_slices, table_weights, moment_first, second_lines)
+    parcel = parcel_of(where, hots, table_weights, moment_first, second_lines)
     swapped = send(parcel, "table", n_table, n_table // 2)
     (mine,) = place_next(pieces, aims, begin_at(0), block)
     mine = mine + rise + fall
     mine, swapped = lax.optimization_barrier((mine, swapped))
 
     ring = ("far", "pair")
-    me = far_at * n_pair + pair_at
-    n_all = n_dp * lax.axis_size("col")
-    own_squares = jnp.sum(mine * mine, axis=1).reshape(-1, LANES)
-    own_squares = jnp.pad(own_squares, ((0, EXTRA - own_squares.shape[0]), (0, 0)))
-    squares = lax.all_to_all(
-        jnp.broadcast_to(own_squares[None], (n_all,) + own_squares.shape),
-        ("far", "pair", "col"),
-        split_axis=0,
-        concat_axis=0,
-        tiled=True,
-    )
-    common = (where, hot_slices, swapped, squares, table_weights, moment_first, second_lines)
-    shape = (block, share)
-
-    def at_ring(offsets):
-        at = jnp.stack([(me + o + n_dp) % n_dp for o in offsets]).astype(jnp.int32)
-        return at // n_pair, at % n_pair
-
-    def update(offsets, parts, second, held=None, fetched=None):
-        return adam_blocks(*at_ring(offsets), parts, shape, full_width, common, second, held, fetched)
-
-    rise, fall = send(mine, ring, n_dp, 1), send(mine, ring, n_dp, -1)
-    parts = [[mine], [rise], [fall]]
-    rise, fall = send(rise, ring, n_dp, 1), send(fall, ring, n_dp, -1)
-    weights, first, second = update((0, -1, 1), parts, second_lines)
-    rise, fall, second = lax.optimization_barrier((rise, fall, second))
-    parts = [[rise], [fall]]
-    rise, fall = send(rise, ring, n_dp, 1), send(fall, ring, n_dp, -1)
-    fetched = fetch_block(*at_ring((4,)), shape, common)
-    weights, first, second = update((-2, 2), parts, second, (weights, first))
-    rise, fall, second, fetched = lax.optimization_barrier((rise, fall, second, fetched))
-    parts = [[rise], [fall]]
-    rise, fall = send(rise[:half], ring, n_dp, 1), send(fall[half:], ring, n_dp, -1)
-    weights, first, second = update((-3, 3), parts, second, (weights, first))
-    weights, first, second = update((4,), [[rise, fall]], second, (weights, first), fetched)
+    squares = lax.psum(jnp.sum(mine * mine, axis=1).reshape(-1, LANES), "col")
+    squares = jnp.pad(squares, ((0, EXTRA - squares.shape[0]), (0, 0)))
+    own = jnp.concatenate([mine, squares], axis=0)
+    common = (where, hots, swapped, table_weights, moment_first, second_lines)
+    flip = pair_at.reshape(1)
+    away = 2 * pair_at - 1
+    straight = jnp.stack([pair_at, 1 - pair_at])
+    crossed = jnp.stack([1 - pair_at, pair_at])
+
+    def row_at(offset):
+        return ((far_at + offset + n_far) % n_far).reshape(1)
+
+    def update(offset, columns_at, layout, parts, second, held=None, fetched=None):
+        at = row_at(offset)
+        return adam_block(at, columns_at, flip, layout, parts, full_width, common, second, held, fetched)
+
+    rise_1, fall_1 = send(own, ring, n_dp, 1), send(own, ring, n_dp, -1)
+    rise_2, fall_2 = send(rise_1, ring, n_dp, 1), send(fall_1, ring, n_dp, -1)
+    layout = (((0, 0),), ((2, 1),))
+    weights, first, second = update(0, straight, layout, [own, rise_1, fall_1], second_lines)
+    rise_2, fall_2, second = lax.optimization_barrier((rise_2, fall_2, second))
+    rise_3, fall_3 = send(rise_2, ring, n_dp, 1), send(fall_2, ring, n_dp, -1)
+    parts = [rise_1, fall_1, rise_2, fall_2]
+    fetched = fetch_blocks(row_at(2), crossed, (block, share), common)
+    weights, first, second = update(
+        away, crossed, (((0, 1),), ((2, 3),)), parts, second, (weights, first)
+    )
+    rise_3, fall_3, second, fetched = lax.optimization_barrier((rise_3, fall_3, second, fetched))
+    rise_4, fall_4 = send(rise_3[:half], ring, n_dp, 1), send(fall_3[half:], ring, n_dp, -1)
+    parts = [rise_2, fall_2, rise_3, fall_3]
+    weights, first, second = update(
+        -away, straight, (((1, 0),), ((3, 2),)), parts, second, (weights, first)
+    )
+    parts = [rise_3, fall_3, rise_4, fall_4]
+    weights, first, second = update(
+        2, crossed, (((0, 1),), ((2, 2), (3, 3))), parts, second, (weights, first), fetched
+    )
     return (weights, first, second.reshape(-1))
 
 

time: 150 us -> 153 us (1.020)
  waiting for transfers between devices: 13.7 us -> 22.1 us
  starting transfers between devices: 28.6 us -> 24.2 us
  blocking collectives: 61 us -> 63.5 us
  Pallas kernels: 40.6 us -> 39 us
    ppermute x13, waiting for transfers between devices: 9.22 us -> 22.1 us  [send(): lax.ppermute(value, axes, [(i, (i + step) % count) for i in range(count)])]
    all_to_all x1 -> x0, starting transfers between devices: 4.61 us -> none  [on_device(): lax.all_to_all(jnp.broadcast_to(own_squares[None], (n_all,) + own_squares...]
    all_to_all x1 -> x0, waiting for transfers between devices: 4.52 us -> none  [on_device(): lax.all_to_all(jnp.broadcast_to(own_squares[None], (n_all,) + own_squares...]
    psum x0 -> x1, blocking collectives: none -> 2.47 us  [on_device(): squares = lax.psum(jnp.sum(mine * mine, axis=1).reshape(-1, LANES), 'col')]
    unnamed x13 -> x14, local copies, waits for them, and re-layouts: 3.13 us -> 2.38 us
  transfers between devices with their start and end apart: 14 -> 13, of which waited for: 5 -> 6; matrix products, arithmetic and copies ran while one was open for 1% -> 0% of each run, Pallas kernels for 13% -> 13%
where the time goes in v6:
time: 153 us
  blocking collectives  63.5 us (42%)
  Pallas kernels  39 us (25%)
  starting transfers between devices  24.2 us (16%)
  waiting for transfers between devices  22.1 us (14%)
  local copies, waits for them, and re-layouts  2.6 us (2%)
    all_to_all x1, blocking collectives, on_device(): lax.all_to_all(slot_grad, ('table', 'pair'), split_axis=0, concat_axis=0,...  61 us
    ppermute x13, starting transfers between devices, send(): lax.ppermute(value, axes, [(i, (i + step) % count) for i in range(count)])  24.2 us
    ppermute x13, waiting for transfers between devices, send(): lax.ppermute(value, axes, [(i, (i + step) % count) for i in range(count)])  22.1 us
    pallas_call x1, Pallas kernels, slot_sums(): pl.pallas_call(lambda *refs: slot_kernel(rows_dev, *refs), out_shape=jax....  12.6 us
    pallas_call x4, Pallas kernels, adam_block(): pl.pallas_call(lambda *refs: adam_kernel(layout, len(parts), full_width,...  10.8 us
    pallas_call x2, Pallas kernels, place_next(): pl.pallas_call(place_next_kernel, out_shape=tuple((jax.ShapeDtypeStruct((...  7.41 us
    pallas_call x1, Pallas kernels, place_first(): pl.pallas_call(place_first_kernel, out_shape=(jax.ShapeDtypeStruct((2 * c...  4.51 us
  transfers between devices with their start and end apart: 13, of which 6 were waited for; matrix products, arithmetic and copies ran while one was open for 0% of the time, Pallas kernels for 13%

profile of v6, /device:TPU:2, one launch (start us, length us, event | category | flops | bytes accessed | tf_op | source)
XLA Modules:
  0.0 152.9 jit_solution(5499961350329639456)
XLA Ops:
  0.6 0.0 copy-start.3
  0.6 0.0 copy-start.2
  0.7 0.0 copy-start.1
  0.7 1.3 copy.20
  1.9 1.1 copy.19
  3.0 0.2 reshape.35.refs_0_
  3.2 0.0 copy-done.3
  3.2 0.0 copy-done.2
  3.2 0.0 copy-done.1
  3.3 12.6 %slot_sums.1 = f32[32,264,128]{2,1,0:T(8,128)} custom-call(s32[128,256]{1,0:T(8,128)S(1)} %reshape.35.refs_0_, bf16[256,1024]{1,0:T(8,128)(2,1)S(1)} %bitcast.16, s32[2,16]{1,0:T(2,128)S(1)} %bitcast.23, s32[1,16]{1,0:T(1,128)S(1)} %copy-done.3, s32[1,16,256]{2,1,0:T(8,128)S(1)} %copy-done.2), custom_call_target="tpu_custom_call" | custom-call | tf_op jit(solution)/shard_map/slot_sums/pallas_call | solution.py:115
  15.9 61.0 %all_to_all.5.got_ref = f32[32,264,128]{2,1,0:T(8,128)} all-to-all(f32[32,264,128]{2,1,0:T(8,128)} %slot_sums.1), channel_id=1, replica_groups=mesh['table'=16,'far'=4,'pair'=2,'col'=2] {'table','pair'}, dimensions={0} | all-to-all | bytes 8650752 | tf_op jit(solution)/shard_map/all_to_all | solution.py:468
  76.9 4.5 %place_first.1 = (bf16[256,8192]{1,0:T(8,128)(2,1)S(1)}, s32[8,8192]{1,0:T(8,128)S(1)}, f32[512,128]{1,0:T(8,128)S(1)}) custom-call(s32[1]{0:T(128)} %bitcast.8.start_ref, f32[32,264,128]{2,1,0:T(8,128)} %all_to_all.5.got_ref), custom_call_target="tpu_custom_call" | custom-call | flops 2147483648 | bytes 8388608 | tf_op jit(solution)/shard_map/place_first/pallas_call | solution.py:204
  81.4 0.0 copy-start.4
  81.5 5.5 %collective-permute-start.1 = (f32[256,128]{1,0:T(8,128)S(1)}, f32[256,128]{1,0:T(8,128)S(1)}, u32[]{:S(2)}, u32[]{:S(2)}) collective-permute-start(f32[256,128]{1,0:T(8,128)S(1)} %get-tuple-element.83), channel_id=1, source_target_pairs={{0,12},{4,0},{8,4},{12,8},{1,13},{5,1},{9,5},{13,9},{2,14},{6,2},{... | collective-permute-start | bytes 393224 | tf_op jit(solution)/shard_map/ppermute | solution.py:477
  87.0 0.0 collective-permute-start
  87.0 0.1 pad_add_fusion.1.start_ref
  87.0 5.1 %place_next.2 = (f32[512,128]{1,0:T(8,128)S(1)}, f32[512,128]{1,0:T(8,128)S(1)}) custom-call(s32[2]{0:T(128)S(1)} %pad_add_fusion.1.start_ref, bf16[256,8192]{1,0:T(8,128)(2,1)S(1)} %get-tuple-element.49.pieces, s32[8,8192]{1,0:T(8,128)S(1)} %get-tuple-element.50.aims), custom_call_target="tpu_custom_call" | custom-call | flops 4294967296 | bytes 8388608 | tf_op jit(solution)/shard_map/place_next/pallas_call | solution.py:227
  92.1 0.0 copy-done.4
  92.1 0.0 copy-start
  92.1 0.0 collective-permute-done.1
  92.1 2.8 %collective-permute-done = f32[256,128]{1,0:T(8,128)S(1)} collective-permute-done((f32[256,128]{1,0:T(8,128)S(1)}, f32[256,128]{1,0:T(8,128)S(1)}, u32[]{:S(2)}, u32[]{:S(2)}) %collective-permute-start) | collective-permute-done | bytes 131104 | tf_op jit(solution)/shard_map/ppermute | solution.py:477
  95.0 0.1 collective-permute-start.2
  95.1 4.1 %collective-permute-start.3 = (f32[512,128]{1,0:T(8,128)S(1)}, f32[512,128]{1,0:T(8,128)S(1)}, u32[]{:S(2)}, u32[]{:S(2)}) collective-permute-start(f32[512,128]{1,0:T(8,128)S(1)} %pad_maximum_fusion.1), channel_id=1, source_target_pairs={{0,12},{4,0},{8,4},{12,8},{1,13},{5,1},{9,5},{13,9},{2,14},{6,2},{... | collective-permute-start | bytes 786440 | tf_op jit(solution)/shard_map/ppermute | solution.py:477
  99.2 0.0 copy-done
  99.2 0.0 copy-start.5
  99.2 1.8 %parcel.1 = f32[264,256]{1,0:T(8,128)S(1)} custom-call(s32[1]{0:T(128)} %bitcast.9.where_ref.refs_3_, s32[2,16]{1,0:T(2,128)S(1)} %bitcast.24, f32[2048,256]{1,0:T(8,128)} %refs_10_.7, f32[2048,256]{1,0:T(8,128)} %refs_11_.5, f32[16,128]{1,0:T(8,128)S(1)} %bitcast.17), custom_call_target="tpu_custom_call" | custom-call | tf_op jit(solution)/shard_map/parcel/pallas_call | solution.py:428
  101.0 1.5 collective-permute-start.4
  102.5 0.0 copy-done.5
  102.5 2.4 %place_next.3 = f32[512,128]{1,0:T(8,128)S(1)} custom-call(s32[1]{0:T(128)} %bitcast.10.start_ref, bf16[256,8192]{1,0:T(8,128)(2,1)S(1)} %copy-done.5, s32[8,8192]{1,0:T(8,128)S(1)} %get-tuple-element.50.aims), custom_call_target="tpu_custom_call" | custom-call | flops 2147483648 | bytes 8388608 | tf_op jit(solution)/shard_map/place_next/pallas_call | solution.py:227
  104.9 4.3 %collective-permute-done.2 = f32[512,128]{1,0:T(8,128)S(1)} collective-permute-done((f32[512,128]{1,0:T(8,128)S(1)}, f32[512,128]{1,0:T(8,128)S(1)}, u32[]{:S(2)}, u32[]{:S(2)}) %collective-permute-start.2) | collective-permute-done | bytes 262176 | tf_op jit(solution)/shard_map/ppermute | solution.py:477
  109.1 0.0 collective-permute-done.3
  109.2 0.0 collective-permute-done.4.refs_8_.refs_9_.swapped
  109.2 0.1 multiply_reduce_fusion
  109.4 2.5 %psum.7 = f32[4,128]{1,0:T(4,128)S(1)} all-reduce(f32[4,128]{1,0:T(4,128)S(1)} %bitcast.30), channel_id=1, replica_groups=mesh['table'=16,'far'=4,'pair'=2,'col'=2] {'col'}, use_global_device_ids=true, to_apply=%region_1.2 | all-reduce | flops 512 | bytes 4096 | tf_op jit(solution)/shard_map/psum | solution.py:495
  111.8 3.0 %collective-permute-start.7 = (f32[520,128]{1,0:T(8,128)S(1)}, f32[520,128]{1,0:T(8,128)S(1)}, u32[]{:S(2)}, u32[]{:S(2)}) collective-permute-start(f32[520,128]{1,0:T(8,128)S(1)} %select_maximum_fusion.refs_5_), channel_id=1, source_target_pairs={{0,14},{2,0},{4,2},{6,4},{8,6},{10,8},{12,10},{14,12},{1,15},{3,1}... | collective-permute-start | bytes 798728 | tf_op jit(solution)/shard_map/ppermute | solution.py:477
  114.8 0.0 collective-permute-start.5
  114.8 6.0 %collective-permute-done.7.refs_7_.refs_6_ = f32[520,128]{1,0:T(8,128)S(1)} collective-permute-done((f32[520,128]{1,0:T(8,128)S(1)}, f32[520,128]{1,0:T(8,128)S(1)}, u32[]{:S(2)}, u32[]{:S(2)}) %collective-permute-start.7) | collective-permute-done | bytes 266272 | tf_op jit(solution)/shard_map/ppermute | solution.py:477
  120.8 3.7 %collective-permute-start.8 = (f32[520,128]{1,0:T(8,128)S(1)}, f32[520,128]{1,0:T(8,128)S(1)}, u32[]{:S(2)}, u32[]{:S(2)}) collective-permute-start(f32[520,128]{1,0:T(8,128)S(1)} %collective-permute-done.7.refs_7_.refs_6_), channel_id=1, source_target_pairs={{0,14},{2,0},{4,2},{6,4},{8,6},{10,8},{12,10},{14,12},{1,15},{3,1}... | collective-permute-start | bytes 798728 | tf_op jit(solution)/shard_map/ppermute | solution.py:477
  124.5 0.0 collective-permute-done.5.refs_6_.refs_5_
  124.5 0.0 collective-permute-start.6
  124.5 0.1 pad_add_fusion.2.refs_1_
  124.6 2.8 %adam_block.4 = (f32[2048,256]{1,0:T(8,128)}, f32[2048,256]{1,0:T(8,128)}, f32[16,128]{1,0:T(8,128)S(1)}) custom-call(s32[1]{0:T(128)} %bitcast.12.refs_0_, s32[2]{0:T(128)S(1)} %pad_add_fusion.2.refs_1_, s32[1]{0:T(128)} %bitcast.5.refs_2_, s32[1]{0:T(128)} %bitcast.9.where_ref.refs_3_, s32[2,16]{1,0:T(2,128)S(1)} %bitcast.25, ...), custom_call_target="tpu_custom_call" | custom-call | flops 1048576 | bytes 2621440 | tf_op jit(solution)/shard_map/adam_block/pallas_call | solution.py:370
  127.4 2.3 %collective-permute-done.8.refs_8_.refs_6_ = f32[520,128]{1,0:T(8,128)S(1)} collective-permute-done((f32[520,128]{1,0:T(8,128)S(1)}, f32[520,128]{1,0:T(8,128)S(1)}, u32[]{:S(2)}, u32[]{:S(2)}) %collective-permute-start.8) | collective-permute-done | bytes 266272 | tf_op jit(solution)/shard_map/ppermute | solution.py:477
  129.6 3.4 %collective-permute-done.6.refs_7_.refs_5_ = f32[520,128]{1,0:T(8,128)S(1)} collective-permute-done((f32[520,128]{1,0:T(8,128)S(1)}, f32[520,128]{1,0:T(8,128)S(1)}, u32[]{:S(2)}, u32[]{:S(2)}) %collective-permute-start.6) | collective-permute-done | bytes 266272 | tf_op jit(solution)/shard_map/ppermute | solution.py:477
  133.1 0.0 collective-permute-start.9
  133.1 3.2 %collective-permute-start.10 = (f32[520,128]{1,0:T(8,128)S(1)}, f32[520,128]{1,0:T(8,128)S(1)}, u32[]{:S(2)}, u32[]{:S(2)}) collective-permute-start(f32[520,128]{1,0:T(8,128)S(1)} %collective-permute-done.8.refs_8_.refs_6_), channel_id=1, source_target_pairs={{0,14},{2,0},{4,2},{6,4},{8,6},{10,8},{12,10},{14,12},{1,15},{3,1}... | collective-permute-start | bytes 798728 | tf_op jit(solution)/shard_map/ppermute | solution.py:477
  136.3 0.1 pad_add_fusion.refs_1_.column_ref
  136.4 1.8 %fetch_blocks.1.refs_14_ = f32[2,2,512,128]{3,2,1,0:T(8,128)S(1)} custom-call(s32[1]{0:T(128)} %bitcast.3.row_ref.refs_0_, s32[2]{0:T(128)S(1)} %pad_add_fusion.refs_1_.column_ref, s32[1]{0:T(128)} %bitcast.9.where_ref.refs_3_, s32[2,16]{1,0:T(2,128)S(1)} %bitcast.26, f32[264,256]{1,0:T(8,128)S(1)} %collective-permute-done.4.refs_8_.refs_9_.swapped, ...), custom_call_target="tpu_custom_call" | custom-call | tf_op jit(solution)/shard_map/fetch_blocks/pallas_call | solution.py:282
  138.2 2.8 %adam_block.5 = (f32[2048,256]{1,0:T(8,128)}, f32[2048,256]{1,0:T(8,128)}, f32[16,128]{1,0:T(8,128)S(1)}) custom-call(s32[1]{0:T(128)} %bitcast.13.refs_0_, s32[2]{0:T(128)S(1)} %pad_add_fusion.refs_1_.column_ref, s32[1]{0:T(128)} %bitcast.5.refs_2_, s32[1]{0:T(128)} %bitcast.9.where_ref.refs_3_, ...), custom_call_target="tpu_custom_call", output_to_operand_aliasing={{0}: (14, {}), {1}: (15, {})} | custom-call | flops 1048576 | bytes 2621440 | tf_op jit(solution)/shard_map/adam_block/pallas_call | solution.py:370
  141.0 0.0 collective-permute-done.9.refs_7_.refs_5_
  141.0 0.0 collective-permute-done.10.refs_8_.refs_6_
  141.0 3.0 %collective-permute-start.12 = (f32[264,128]{1,0:T(8,128)S(1)}, f32[264,128]{1,0:T(8,128)S(1)}, u32[]{:S(2)}, u32[]{:S(2)}) collective-permute-start(f32[264,128]{1,0:T(8,128)S(1)} %slice.31), channel_id=1, source_target_pairs={{0,14},{2,0},{4,2},{6,4},{8,6},{10,8},{12,10},{14,12},{1,15},{3,1}... | collective-permute-start | bytes 405512 | tf_op jit(solution)/shard_map/ppermute | solution.py:477
  144.0 0.1 collective-permute-start.11
  144.1 2.8 %adam_block.6 = (f32[2048,256]{1,0:T(8,128)}, f32[2048,256]{1,0:T(8,128)}, f32[16,128]{1,0:T(8,128)S(1)}) custom-call(s32[1]{0:T(128)} %bitcast.14.refs_0_, s32[2]{0:T(128)S(1)} %pad_add_fusion.2.refs_1_, s32[1]{0:T(128)} %bitcast.5.refs_2_, s32[1]{0:T(128)} %bitcast.9.where_ref.refs_3_, ...), custom_call_target="tpu_custom_call", output_to_operand_aliasing={{0}: (14, {}), {1}: (15, {})} | custom-call | flops 1048576 | bytes 2621440 | tf_op jit(solution)/shard_map/adam_block/pallas_call | solution.py:370
  146.9 3.3 %collective-permute-done.11.refs_7_ = f32[256,128]{1,0:T(8,128)S(1)} collective-permute-done((f32[256,128]{1,0:T(8,128)S(1)}, f32[256,128]{1,0:T(8,128)S(1)}, u32[]{:S(2)}, u32[]{:S(2)}) %collective-permute-start.11) | collective-permute-done | bytes 131104 | tf_op jit(solution)/shard_map/ppermute | solution.py:477
  150.3 0.0 collective-permute-done.12.refs_8_
  150.3 2.5 %adam_block.7 = (f32[2048,256]{1,0:T(8,128)}, f32[2048,256]{1,0:T(8,128)}, f32[16,128]{1,0:T(8,128)}) custom-call(s32[1]{0:T(128)} %bitcast.3.row_ref.refs_0_, s32[2]{0:T(128)S(1)} %pad_add_fusion.refs_1_.column_ref, s32[1]{0:T(128)} %bitcast.5.refs_2_, s32[1]{0:T(128)} %bitcast.9.where_ref.refs_3_, ...), custom_call_target="tpu_custom_call", output_to_operand_aliasing={{0}: (15, {}), {1}: (16, {})} | custom-call | flops 1048576 | bytes 2621440 | tf_op jit(solution)/shard_map/adam_block/pallas_call | solution.py:370
  (8 shorter events, 0.2 us)
Async XLA Ops:
  0.6 2.6 %copy-start.3 = (s32[1,16]{1,0:T(1,128)S(1)}, s32[1,16]{1,0:T(1,128)}, u32[]{:S(2)}) copy-start(s32[1,16]{1,0:T(1,128)} %refs_3_.1) | copy-start | bytes 196
  0.6 2.6 %copy-start.2 = (s32[1,16,256]{2,1,0:T(8,128)S(1)}, s32[1,16,256]{2,1,0:T(8,128)}, u32[]{:S(2)}) copy-start(s32[1,16,256]{2,1,0:T(8,128)} %refs_4_.1) | copy-start | bytes 49156
  0.7 2.6 %copy-start.1 = (s32[16,2]{0,1:T(2,128)S(1)}, s32[16,2]{0,1:T(2,128)}, u32[]{:S(2)}) copy-start(s32[16,2]{0,1:T(2,128)} %param.11) | copy-start | bytes 388
  81.4 10.7 %copy-start.4 = (bf16[256,8192]{1,0:T(8,128)(2,1)}, bf16[256,8192]{1,0:T(8,128)(2,1)S(1)}, u32[]{:S(2)}) copy-start(bf16[256,8192]{1,0:T(8,128)(2,1)S(1)} %get-tuple-element.49.pieces) | copy-start | bytes 12582916
  81.5 10.7 %collective-permute-start.1 = (f32[256,128]{1,0:T(8,128)S(1)}, f32[256,128]{1,0:T(8,128)S(1)}, u32[]{:S(2)}, u32[]{:S(2)}) collective-permute-start(f32[256,128]{1,0:T(8,128)S(1)} %get-tuple-element.83), channel_id=1, source_target_pairs={{0,12},{4,0},{8,4},{12,8},{1,13},{5,1},{9,5},{13,9},{2,14},{6,2},{... | collective-permute-start | bytes 393224 | tf_op jit(solution)/shard_map/ppermute | solution.py:477
  87.0 7.9 %collective-permute-start = (f32[256,128]{1,0:T(8,128)S(1)}, f32[256,128]{1,0:T(8,128)S(1)}, u32[]{:S(2)}, u32[]{:S(2)}) collective-permute-start(f32[256,128]{1,0:T(8,128)S(1)} %get-tuple-element.84), channel_id=1, source_target_pairs={{0,4},{4,8},{8,12},{12,0},{1,5},{5,9},{9,13},{13,1},{2,6},{6,10},{... | collective-permute-start | bytes 393224 | tf_op jit(solution)/shard_map/ppermute | solution.py:477
  92.1 7.1 %copy-start = (f32[2048]{0:T(1024)S(1)}, f32[2048]{0:T(1024)}, u32[]{:S(2)}) copy-start(f32[2048]{0:T(1024)} %param.10) | copy-start | bytes 24580
  95.0 14.1 %collective-permute-start.2 = (f32[512,128]{1,0:T(8,128)S(1)}, f32[512,128]{1,0:T(8,128)S(1)}, u32[]{:S(2)}, u32[]{:S(2)}) collective-permute-start(f32[512,128]{1,0:T(8,128)S(1)} %pad_maximum_fusion), channel_id=1, source_target_pairs={{0,4},{4,8},{8,12},{12,0},{1,5},{5,9},{9,13},{13,1},{2,6},{6,10},{... | collective-permute-start | bytes 786440 | tf_op jit(solution)/shard_map/ppermute | solution.py:477
  95.1 14.1 %collective-permute-start.3 = (f32[512,128]{1,0:T(8,128)S(1)}, f32[512,128]{1,0:T(8,128)S(1)}, u32[]{:S(2)}, u32[]{:S(2)}) collective-permute-start(f32[512,128]{1,0:T(8,128)S(1)} %pad_maximum_fusion.1), channel_id=1, source_target_pairs={{0,12},{4,0},{8,4},{12,8},{1,13},{5,1},{9,5},{13,9},{2,14},{6,2},{... | collective-permute-start | bytes 786440 | tf_op jit(solution)/shard_map/ppermute | solution.py:477
  99.2 3.3 %copy-start.5 = (bf16[256,8192]{1,0:T(8,128)(2,1)S(1)}, bf16[256,8192]{1,0:T(8,128)(2,1)}, u32[]{:S(2)}) copy-start(bf16[256,8192]{1,0:T(8,128)(2,1)} %copy-done.4) | copy-start | bytes 12582916
  101.0 8.2 %collective-permute-start.4 = (f32[264,256]{1,0:T(8,128)S(1)}, f32[264,256]{1,0:T(8,128)S(1)}, u32[]{:S(2)}, u32[]{:S(2)}) collective-permute-start(f32[264,256]{1,0:T(8,128)S(1)} %parcel.1), channel_id=1, source_target_pairs={{0,128},{16,144},{32,160},{48,176},{64,192},{80,208},{96,224},{112... | collective-permute-start | bytes 811016 | tf_op jit(solution)/shard_map/ppermute | solution.py:477
  111.8 9.0 %collective-permute-start.7 = (f32[520,128]{1,0:T(8,128)S(1)}, f32[520,128]{1,0:T(8,128)S(1)}, u32[]{:S(2)}, u32[]{:S(2)}) collective-permute-start(f32[520,128]{1,0:T(8,128)S(1)} %select_maximum_fusion.refs_5_), channel_id=1, source_target_pairs={{0,14},{2,0},{4,2},{6,4},{8,6},{10,8},{12,10},{14,12},{1,15},{3,1}... | collective-permute-start | bytes 798728 | tf_op jit(solution)/shard_map/ppermute | solution.py:477
  114.8 9.7 %collective-permute-start.5 = (f32[520,128]{1,0:T(8,128)S(1)}, f32[520,128]{1,0:T(8,128)S(1)}, u32[]{:S(2)}, u32[]{:S(2)}) collective-permute-start(f32[520,128]{1,0:T(8,128)S(1)} %select_maximum_fusion.refs_5_), channel_id=1, source_target_pairs={{0,2},{2,4},{4,6},{6,8},{8,10},{10,12},{12,14},{14,0},{1,3},{3,5},... | collective-permute-start | bytes 798728 | tf_op jit(solution)/shard_map/ppermute | solution.py:477
  120.8 8.8 %collective-permute-start.8 = (f32[520,128]{1,0:T(8,128)S(1)}, f32[520,128]{1,0:T(8,128)S(1)}, u32[]{:S(2)}, u32[]{:S(2)}) collective-permute-start(f32[520,128]{1,0:T(8,128)S(1)} %collective-permute-done.7.refs_7_.refs_6_), channel_id=1, source_target_pairs={{0,14},{2,0},{4,2},{6,4},{8,6},{10,8},{12,10},{14,12},{1,15},{3,1}... | collective-permute-start | bytes 798728 | tf_op jit(solution)/shard_map/ppermute | solution.py:477
  124.5 8.6 %collective-permute-start.6 = (f32[520,128]{1,0:T(8,128)S(1)}, f32[520,128]{1,0:T(8,128)S(1)}, u32[]{:S(2)}, u32[]{:S(2)}) collective-permute-start(f32[520,128]{1,0:T(8,128)S(1)} %collective-permute-done.5.refs_6_.refs_5_), channel_id=1, source_target_pairs={{0,2},{2,4},{4,6},{6,8},{8,10},{10,12},{12,14},{14,0},{1,3},{3,5},... | collective-permute-start | bytes 798728 | tf_op jit(solution)/shard_map/ppermute | solution.py:477
  133.1 7.9 %collective-permute-start.9 = (f32[520,128]{1,0:T(8,128)S(1)}, f32[520,128]{1,0:T(8,128)S(1)}, u32[]{:S(2)}, u32[]{:S(2)}) collective-permute-start(f32[520,128]{1,0:T(8,128)S(1)} %collective-permute-done.6.refs_7_.refs_5_), channel_id=1, source_target_pairs={{0,2},{2,4},{4,6},{6,8},{8,10},{10,12},{12,14},{14,0},{1,3},{3,5},... | collective-permute-start | bytes 798728 | tf_op jit(solution)/shard_map/ppermute | solution.py:477
  133.1 7.9 %collective-permute-start.10 = (f32[520,128]{1,0:T(8,128)S(1)}, f32[520,128]{1,0:T(8,128)S(1)}, u32[]{:S(2)}, u32[]{:S(2)}) collective-permute-start(f32[520,128]{1,0:T(8,128)S(1)} %collective-permute-done.8.refs_8_.refs_6_), channel_id=1, source_target_pairs={{0,14},{2,0},{4,2},{6,4},{8,6},{10,8},{12,10},{14,12},{1,15},{3,1}... | collective-permute-start | bytes 798728 | tf_op jit(solution)/shard_map/ppermute | solution.py:477
  141.0 9.3 %collective-permute-start.12 = (f32[264,128]{1,0:T(8,128)S(1)}, f32[264,128]{1,0:T(8,128)S(1)}, u32[]{:S(2)}, u32[]{:S(2)}) collective-permute-start(f32[264,128]{1,0:T(8,128)S(1)} %slice.31), channel_id=1, source_target_pairs={{0,14},{2,0},{4,2},{6,4},{8,6},{10,8},{12,10},{14,12},{1,15},{3,1}... | collective-permute-start | bytes 405512 | tf_op jit(solution)/shard_map/ppermute | solution.py:477
  144.0 6.3 %collective-permute-start.11 = (f32[256,128]{1,0:T(8,128)S(1)}, f32[256,128]{1,0:T(8,128)S(1)}, u32[]{:S(2)}, u32[]{:S(2)}) collective-permute-start(f32[256,128]{1,0:T(8,128)S(1)} %slice.30), channel_id=1, source_target_pairs={{0,2},{2,4},{4,6},{6,8},{8,10},{10,12},{12,14},{14,0},{1,3},{3,5},... | collective-permute-start | bytes 393224 | tf_op jit(solution)/shard_map/ppermute | solution.py:477

commit v7 on v5

--- a/solution.py
+++ b/solution.py
@@ -38,19 +38,23 @@
 
 
 def target_row(owner, hot_ref, count_ref, rows, rows_dev):
-    owners, n_hots = hot_ref.shape
+    n_hots, owners = hot_ref.shape
     partner = (owner + owners // 2) % owners
     local_row = rows % rows_dev
     from_partner = rows // rows_dev == partner
     target = local_row
     for k in range(n_hots):
-        moved = from_partner & (local_row // SLICE == hot_ref[partner, k])
-        target = jnp.where(moved, hot_ref[owner, k] * SLICE + local_row % SLICE, target)
+        moved = from_partner & (local_row // SLICE == hot_ref[k, partner])
+        target = jnp.where(moved, hot_ref[k, owner] * SLICE + local_row % SLICE, target)
     used = lax.broadcasted_iota(jnp.int32, rows.shape, 1) < count_ref[0, owner]
     return jnp.where(used, target, rows_dev)
 
 
-def slot_kernel(rows_dev, map_ref, grad_ref, hot_ref, count_ref, rows_ref, out_ref, tally, held, sems):
+def slot_kernel(
+    rows_dev, map_ref, grad, hot_ref, count_ref, rows_ref, out_ref, tally, held, natural, grad_ref, sems, sem
+):
+    load = pltpu.make_async_copy(grad, natural, sem)
+    load.start()
     groups, span = map_ref.shape
     owners, _, cap = tally.shape
     per_owner = cap // LOW
@@ -58,7 +62,7 @@
     sample = lax.broadcasted_iota(jnp.int32, (1, span), 1) // (span // GROUP)
     left_at = counting((highs * GROUP, span))
     right_at = counting((LOW, span))
-    batch = 16
+    batch = 32
 
     def count(step, carry):
         first = pl.multiple_of(step * batch, batch)
@@ -80,6 +84,8 @@
         return carry
 
     lax.fori_loop(0, groups // batch, count, 0)
+    load.wait()
+    grad_ref[...] = natural[...].T
     depth, shares, height, lanes = held.shape
     columns = (height - EXTRA) * lanes // cap
 
@@ -107,24 +113,27 @@
         leave(owner).wait()
 
 
-def slot_sums(slots, grad_t, hot_slices, row_counts, unique_rows, shares, rows_dev):
+def slot_sums(slots, grad, hot_slices, row_counts, unique_rows, shares, rows_dev):
     _, owners, cap = unique_rows.shape
-    columns, samples = grad_t.shape
+    samples, columns = grad.shape
     height = columns // shares * cap // LANES + EXTRA
     depth = 4
     return pl.pallas_call(
         lambda *refs: slot_kernel(rows_dev, *refs),
         out_shape=jax.ShapeDtypeStruct((owners * shares, height, LANES), jnp.float32),
-        in_specs=[VMEM, VMEM, SMEM, SMEM, VMEM],
+        in_specs=[VMEM, ANY, SMEM, SMEM, VMEM],
         out_specs=HBM,
         scratch_shapes=[
             pltpu.VMEM((owners, samples, cap), jnp.bfloat16),
             pltpu.VMEM((depth, shares, height, LANES), jnp.float32),
+            pltpu.VMEM(grad.shape, grad.dtype),
+            pltpu.VMEM((columns, samples), grad.dtype),
             pltpu.SemaphoreType.DMA((depth,)),
+            pltpu.SemaphoreType.DMA,
         ],
         compiler_params=pltpu.CompilerParams(vmem_limit_bytes=50 << 20),
         name="slot_sums",
-    )(slots, grad_t, hot_slices, row_counts, unique_rows)
+    )(slots, grad, hot_slices, row_counts, unique_rows)
 
 
 def add_block(pieces, aims, start, out_ref, select):
@@ -151,20 +160,39 @@
 
     for k in range(sems.shape[0]):
         fetch(k).start()
-    for source in range(sources):
-        if source % batch == 0:
-            fetch(source // batch).wait()
-        for side in range(CAP // lanes):
-            value = held[source, side * columns : (side + 1) * columns, :]
-            upper = value.astype(jnp.bfloat16)
-            lower = (value - upper.astype(jnp.float32)).astype(jnp.bfloat16)
-            at = source * CAP + side * lanes
-            pieces[:columns, at : at + lanes] = upper
-            pieces[columns:, at : at + lanes] = lower
-            aim_at = height - EXTRA + side * EXTRA * lanes // CAP
-            aim = held[source, aim_at : aim_at + 1, :].astype(jnp.int32)
-            aims[:, at : at + lanes] = jnp.broadcast_to(aim, (EXTRA, lanes))
-    add_block(pieces, aims, start_ref[0], out_ref, select)
+    rows = out_ref.shape[0]
+    place = counting((CAP, CAP))
+    span = batch * CAP
+    sums = [jnp.zeros((CAP, 2 * columns), jnp.float32) for _ in range(rows // CAP)]
+    for k in range(sems.shape[0]):
+        fetch(k).wait()
+        for source in range(k * batch, (k + 1) * batch):
+            for side in range(CAP // lanes):
+                value = held[source, side * columns : (side + 1) * columns, :]
+                upper = value.astype(jnp.bfloat16)
+                lower = (value - upper.astype(jnp.float32)).astype(jnp.bfloat16)
+                at = source * CAP + side * lanes
+                pieces[:columns, at : at + lanes] = upper
+                pieces[columns:, at : at + lanes] = lower
+                aim_at = height - EXTRA + side * EXTRA * lanes // CAP
+                aim = held[source, aim_at : aim_at + 1, :].astype(jnp.int32)
+                aims[:, at : at + lanes] = jnp.broadcast_to(aim, (EXTRA, lanes))
+        for part in range(rows // CAP):
+            for at in range(k * span, (k + 1) * span, CAP):
+                row = aims[:1, at : at + CAP] - (start_ref[0] + part * CAP)
+                row = digits(jnp.where((row >= 0) & (row < CAP), row, -1))
+                select[part * CAP : (part + 1) * CAP, at - k * span : at - k * span + CAP] = one_hot(
+                    place, row
+                )
+            sums[part] += lax.dot_general(
+                select[part * CAP : (part + 1) * CAP, :span],
+                pieces[:, k * span : (k + 1) * span],
+                NT,
+                preferred_element_type=jnp.float32,
+            )
+    for part in range(rows // CAP):
+        both = sums[part]
+        out_ref[part * CAP : (part + 1) * CAP, :] = both[:, :columns] + both[:, columns:]
 
 
 def place_next_kernel(start_ref, pieces, aims, *refs):
@@ -192,7 +220,7 @@
         in_specs=[SMEM, HBM],
         out_specs=[VMEM] * 3,
         scratch_shapes=[
-            pltpu.VMEM((CAP, width), jnp.bfloat16),
+            pltpu.VMEM((block, width // 8), jnp.bfloat16),
             pltpu.VMEM(got.shape, jnp.float32),
             pltpu.SemaphoreType.DMA((8,)),
         ],
@@ -231,7 +259,7 @@
     rows, columns = held.shape[2:]
     per_block = rows // SLICE
     for k in range(2):
-        hot = hots[where_ref[0], k]
+        hot = hots[k, where_ref[0]]
 
         @pl.when(hot // per_block == rows_at)
         def _():
@@ -289,7 +317,7 @@
     line_at = lax.broadcasted_iota(jnp.int32, placed.shape, 0)
     side_at = lax.broadcasted_iota(jnp.int32, placed.shape, 1) // SLICE
     for k in range(2):
-        hot = hots[where_ref[0], k]
+        hot = hots[k, where_ref[0]]
         here = (line_at == hot // 2) & (side_at == hot % 2)
         placed = jnp.where(here, turned(lead, hot % 2 != k), placed)
     placed_second[...] = placed
@@ -374,7 +402,7 @@
 
 
 def parcel_kernel(where_ref, hots, table, first, second, out_ref, sems):
-    hot_ref = [hots[where_ref[0], k] for k in range(2)]
+    hot_ref = [hots[k, where_ref[0]] for k in range(2)]
     copies = []
     for which, source in enumerate((table, first)):
         for k in range(2):
@@ -427,10 +455,11 @@
     block, share = rows_dev // n_far, col_width // n_pair
     half = block // 2
 
+    hots = hot_slices.T
     second_lines = moment_second.reshape(-1, LANES)
     slots = dedup_map.reshape(-1, GROUP * dedup_map.shape[1])
     slot_grad = slot_sums(
-        slots, upstream_grad.T, hot_slices, row_counts, unique_rows, n_pair, rows_dev
+        slots, upstream_grad, hots, row_counts, unique_rows, n_pair, rows_dev
     )
     slot_grad, position, far_at, pair_at = lax.optimization_barrier(
         (slot_grad, position, far_at, pair_at)
@@ -455,7 +484,7 @@
     where = position.reshape(1)
     rise, fall, where, second_lines = lax.optimization_barrier((rise, fall, where, second_lines))
     rise, fall = send(rise, "far", n_far, 1), send(fall, "far", n_far, -1)
-    parcel = parcel_of(where, hot_slices, table_weights, moment_first, second_lines)
+    parcel = parcel_of(where, hots, table_weights, moment_first, second_lines)
     swapped = send(parcel, "table", n_table, n_table // 2)
     (mine,) = place_next(pieces, aims, begin_at(0), block)
     mine = mine + rise + fall
@@ -473,7 +502,7 @@
         concat_axis=0,
         tiled=True,
     )
-    common = (where, hot_slices, swapped, squares, table_weights, moment_first, second_lines)
+    common = (where, hots, swapped, squares, table_weights, moment_first, second_lines)
     shape = (block, share)
 
     def at_ring(offsets):

time: 150 us -> 151 us (level)
  Pallas kernels: 40.6 us -> 38.8 us
    unnamed x13 -> x17, local copies, waits for them, and re-layouts: 3.13 us -> 4.21 us
  transfers between devices with their start and end apart: 14 -> 14, of which waited for: 5 -> 6; matrix products, arithmetic and copies ran while one was open for 1% -> 1% of each run, Pallas kernels for 13% -> 13%
where the time goes in v7:
time: 151 us; the launch traced here: 149 us
  blocking collectives  61 us (40%)
  Pallas kernels  38.8 us (26%)
  starting transfers between devices  28.4 us (19%)
  waiting for transfers between devices  14.3 us (9%)
  local copies, waits for them, and re-layouts  5.07 us (3%)
    all_to_all x1, blocking collectives, on_device(): lax.all_to_all(slot_grad, ('table', 'pair'), split_axis=0, concat_axis=0,...  61 us
    ppermute x13, starting transfers between devices, send(): lax.ppermute(value, axes, [(i, (i + step) % count) for i in range(count)])  23.8 us
    pallas_call x1, Pallas kernels, slot_sums(): pl.pallas_call(lambda *refs: slot_kernel(rows_dev, *refs), out_shape=jax....  12.7 us
    pallas_call x4, Pallas kernels, adam_blocks(): pl.pallas_call(lambda *refs: adam_kernel(groups, full_width, fetched is n...  10.8 us
    ppermute x13, waiting for transfers between devices, send(): lax.ppermute(value, axes, [(i, (i + step) % count) for i in range(count)])  9.75 us
    pallas_call x2, Pallas kernels, place_next(): pl.pallas_call(place_next_kernel, out_shape=tuple((jax.ShapeDtypeStruct((...  7.42 us
    all_to_all x1, starting transfers between devices, on_device(): lax.all_to_all(jnp.broadcast_to(own_squares[None], (n_all,) + own_squares...  4.63 us
    pallas_call x1, Pallas kernels, place_first(): pl.pallas_call(place_first_kernel, out_shape=(jax.ShapeDtypeStruct((2 * c...  4.53 us
  transfers between devices with their start and end apart: 14, of which 6 were waited for; matrix products, arithmetic and copies ran while one was open for 1% of the time, Pallas kernels for 13%

profile of v7, /device:TPU:2, one launch (start us, length us, event | category | flops | bytes accessed | tf_op | source)
XLA Modules:
  0.0 149.5 jit_solution(3435893587423466735)
XLA Ops:
  0.6 1.1 copy.18
  1.7 0.2 reshape.26.refs_0_
  1.9 0.0 copy-start
  1.9 1.0 copy-done
  3.0 0.0 copy-start.2
  3.0 0.7 copy-done.2
  3.7 0.0 copy-start.4
  3.7 0.7 copy-done.4
  4.4 0.7 copy-done.5
  5.0 12.7 %slot_sums.1 = f32[32,264,128]{2,1,0:T(8,128)} custom-call(s32[128,256]{1,0:T(8,128)S(1)} %reshape.26.refs_0_, bf16[1024,256]{1,0:T(8,128)(2,1)S(1)} %copy-done, s32[2,16]{1,0:T(2,128)S(1)} %bitcast.23, s32[1,16]{1,0:T(1,128)S(1)} %copy-done.5, s32[1,16,256]{2,1,0:T(8,128)S(1)} %copy-done.4), custom_call_target="tpu_custom_call" | custom-call | tf_op jit(solution)/shard_map/slot_sums/pallas_call | solution.py:121
  17.7 61.0 %all_to_all.10.got_ref = f32[32,264,128]{2,1,0:T(8,128)} all-to-all(f32[32,264,128]{2,1,0:T(8,128)} %slot_sums.1), channel_id=1, replica_groups=mesh['table'=16,'far'=4,'pair'=2,'col'=2] {'table','pair'}, dimensions={0} | all-to-all | bytes 8650752 | tf_op jit(solution)/shard_map/all_to_all | solution.py:467
  78.8 4.5 %place_first.1 = (bf16[256,8192]{1,0:T(8,128)(2,1)S(1)}, s32[8,8192]{1,0:T(8,128)S(1)}, f32[512,128]{1,0:T(8,128)S(1)}) custom-call(s32[1]{0:T(128)} %bitcast.5.start_ref, f32[32,264,128]{2,1,0:T(8,128)} %all_to_all.10.got_ref), custom_call_target="tpu_custom_call" | custom-call | flops 2147483648 | bytes 8388608 | tf_op jit(solution)/shard_map/place_first/pallas_call | solution.py:213
  83.3 0.0 copy-start.6
  83.3 5.5 %collective-permute-start.1 = (f32[256,128]{1,0:T(8,128)S(1)}, f32[256,128]{1,0:T(8,128)S(1)}, u32[]{:S(2)}, u32[]{:S(2)}) collective-permute-start(f32[256,128]{1,0:T(8,128)S(1)} %get-tuple-element.89), channel_id=1, source_target_pairs={{0,12},{4,0},{8,4},{12,8},{1,13},{5,1},{9,5},{13,9},{2,14},{6,2},{... | collective-permute-start | bytes 393224 | tf_op jit(solution)/shard_map/ppermute | solution.py:476
  88.9 0.0 collective-permute-start
  88.9 0.1 pad_add_fusion.start_ref
  88.9 5.1 %place_next.2 = (f32[512,128]{1,0:T(8,128)S(1)}, f32[512,128]{1,0:T(8,128)S(1)}) custom-call(s32[2]{0:T(128)S(1)} %pad_add_fusion.start_ref, bf16[256,8192]{1,0:T(8,128)(2,1)S(1)} %get-tuple-element.49.pieces, s32[8,8192]{1,0:T(8,128)S(1)} %get-tuple-element.50.aims), custom_call_target="tpu_custom_call" | custom-call | flops 4294967296 | bytes 8388608 | tf_op jit(solution)/shard_map/place_next/pallas_call | solution.py:236
  94.0 0.0 copy-done.6
  94.0 0.0 copy-start.1
  94.0 0.0 copy-start.3
  94.0 0.0 collective-permute-done.1
  94.0 2.7 %collective-permute-done = f32[256,128]{1,0:T(8,128)S(1)} collective-permute-done((f32[256,128]{1,0:T(8,128)S(1)}, f32[256,128]{1,0:T(8,128)S(1)}, u32[]{:S(2)}, u32[]{:S(2)}) %collective-permute-start) | collective-permute-done | bytes 131104 | tf_op jit(solution)/shard_map/ppermute | solution.py:476
  96.8 0.1 slice_add_fusion.1
  96.9 0.4 collective-permute-start.2
  97.2 4.0 %collective-permute-start.3 = (f32[512,128]{1,0:T(8,128)S(1)}, f32[512,128]{1,0:T(8,128)S(1)}, u32[]{:S(2)}, u32[]{:S(2)}) collective-permute-start(f32[512,128]{1,0:T(8,128)S(1)} %pad_maximum_fusion.1), channel_id=1, source_target_pairs={{0,12},{4,0},{8,4},{12,8},{1,13},{5,1},{9,5},{13,9},{2,14},{6,2},{... | collective-permute-start | bytes 786440 | tf_op jit(solution)/shard_map/ppermute | solution.py:476
  101.3 0.0 copy-done.1
  101.3 0.0 copy-done.3
  101.3 1.8 %parcel.1 = f32[264,256]{1,0:T(8,128)S(1)} custom-call(s32[1]{0:T(128)} %bitcast.6.where_ref.refs_2_, s32[2,16]{1,0:T(2,128)S(1)} %bitcast.24, f32[2048,256]{1,0:T(8,128)} %refs_8_.5, f32[2048,256]{1,0:T(8,128)} %refs_9_.7, f32[16,128]{1,0:T(8,128)S(1)} %bitcast.17), custom_call_target="tpu_custom_call" | custom-call | tf_op jit(solution)/shard_map/parcel/pallas_call | solution.py:427
  103.1 1.5 collective-permute-start.4
  104.6 0.0 copy-done.7
  104.6 2.4 %place_next.3 = f32[512,128]{1,0:T(8,128)S(1)} custom-call(s32[1]{0:T(128)} %bitcast.7.start_ref, bf16[256,8192]{1,0:T(8,128)(2,1)S(1)} %copy-done.7, s32[8,8192]{1,0:T(8,128)S(1)} %get-tuple-element.50.aims), custom_call_target="tpu_custom_call" | custom-call | flops 2147483648 | bytes 8388608 | tf_op jit(solution)/shard_map/place_next/pallas_call | solution.py:236
  106.9 4.4 %collective-permute-done.2 = f32[512,128]{1,0:T(8,128)S(1)} collective-permute-done((f32[512,128]{1,0:T(8,128)S(1)}, f32[512,128]{1,0:T(8,128)S(1)}, u32[]{:S(2)}, u32[]{:S(2)}) %collective-permute-start.2) | collective-permute-done | bytes 262176 | tf_op jit(solution)/shard_map/ppermute | solution.py:476
  111.3 0.0 collective-permute-done.3
  111.3 0.0 collective-permute-done.4.refs_7_.refs_6_.swapped
  111.3 2.6 %collective-permute-start.7 = (f32[512,128]{1,0:T(8,128)S(1)}, f32[512,128]{1,0:T(8,128)S(1)}, u32[]{:S(2)}, u32[]{:S(2)}) collective-permute-start(f32[512,128]{1,0:T(8,128)S(1)} %add_add_fusion.refs_4_), channel_id=1, source_target_pairs={{0,14},{2,0},{4,2},{6,4},{8,6},{10,8},{12,10},{14,12},{1,15},{3,1}... | collective-permute-start | bytes 786440 | tf_op jit(solution)/shard_map/ppermute | solution.py:476
  113.9 0.0 collective-permute-start.5
  113.9 0.1 and_select_fusion.4
  114.0 0.1 multiply_reduce_fusion
  114.2 0.6 broadcast_in_dim.2
  114.8 4.6 %all-to-all-start.1 = ((f32[16,8,128]{2,1,0:T(8,128)}), f32[16,8,128]{2,1,0:T(8,128)S(1)}, u32[]{:S(2)}, u32[]{:S(2)}) async-start(f32[16,8,128]{2,1,0:T(8,128)} %broadcast_in_dim.2), calls=%async_computation.1 | async-start | bytes 131072 | tf_op jit(solution)/shard_map/all_to_all | solution.py:498
  119.5 0.0 collective-permute-done.7.refs_6_
  119.5 3.2 %collective-permute-start.8 = (f32[512,128]{1,0:T(8,128)S(1)}, f32[512,128]{1,0:T(8,128)S(1)}, u32[]{:S(2)}, u32[]{:S(2)}) collective-permute-start(f32[512,128]{1,0:T(8,128)S(1)} %collective-permute-done.7.refs_6_), channel_id=1, source_target_pairs={{0,14},{2,0},{4,2},{6,4},{8,6},{10,8},{12,10},{14,12},{1,15},{3,1}... | collective-permute-start | bytes 786440 | tf_op jit(solution)/shard_map/ppermute | solution.py:476
  122.7 0.0 collective-permute-done.5.refs_5_
  122.7 0.0 collective-permute-start.6
  122.7 0.1 and_select_fusion.2
  122.8 4.5 %all-to-all-done.1.refs_8_.refs_7_ = f32[16,8,128]{2,1,0:T(8,128)S(1)} async-done(((f32[16,8,128]{2,1,0:T(8,128)}), f32[16,8,128]{2,1,0:T(8,128)S(1)}, u32[]{:S(2)}, u32[]{:S(2)}) %all-to-all-start.1) | async-done | bytes 65568 | tf_op jit(solution)/shard_map/all_to_all | solution.py:498
  127.3 3.0 %adam_blocks.4 = (f32[2048,256]{1,0:T(8,128)}, f32[2048,256]{1,0:T(8,128)}, f32[16,128]{1,0:T(8,128)S(1)}) custom-call(s32[3]{0:T(128)S(1)} %and_select_fusion.5.refs_0_, s32[3]{0:T(128)S(1)} %get-tuple-element.85.refs_1_, s32[1]{0:T(128)} %bitcast.6.where_ref.refs_2_, s32[2,16]{1,0:T(2,128)S(1)} %bitcast.25, f32[512,128]{1,0:T(8,128)S(1)} %add_add_fusion.refs_4_, ...), custom_call_target="tpu_custom_call" | custom-call | flops 1572864 | bytes 3932160 | tf_op jit(solution)/shard_map/adam_blocks/pallas_call | solution.py:369
  130.4 0.0 collective-permute-done.8.refs_5_
  130.4 1.8 %collective-permute-done.6.refs_4_ = f32[512,128]{1,0:T(8,128)S(1)} collective-permute-done((f32[512,128]{1,0:T(8,128)S(1)}, f32[512,128]{1,0:T(8,128)S(1)}, u32[]{:S(2)}, u32[]{:S(2)}) %collective-permute-start.6) | collective-permute-done | bytes 262176 | tf_op jit(solution)/shard_map/ppermute | solution.py:476
  132.2 0.0 collective-permute-start.9
  132.2 3.2 %collective-permute-start.10 = (f32[512,128]{1,0:T(8,128)S(1)}, f32[512,128]{1,0:T(8,128)S(1)}, u32[]{:S(2)}, u32[]{:S(2)}) collective-permute-start(f32[512,128]{1,0:T(8,128)S(1)} %collective-permute-done.8.refs_5_), channel_id=1, source_target_pairs={{0,14},{2,0},{4,2},{6,4},{8,6},{10,8},{12,10},{14,12},{1,15},{3,1}... | collective-permute-start | bytes 786440 | tf_op jit(solution)/shard_map/ppermute | solution.py:476
  135.4 0.1 and_select_fusion
  135.5 0.1 and_select_fusion.3.refs_0_
  135.6 1.6 %fetch_block.1.refs_12_ = f32[2,1,512,128]{3,2,1,0:T(8,128)S(1)} custom-call(s32[1]{0:T(128)S(6)} %select_n.97.row_ref.refs_0_, s32[1]{0:T(128)S(6)} %select_n.98.column_ref.refs_1_, s32[1]{0:T(128)} %bitcast.6.where_ref.refs_2_, s32[2,16]{1,0:T(2,128)S(1)} %bitcast.26, f32[264,256]{1,0:T(8,128)S(1)} %collective-permute-done.4.refs_7_.refs_6_.swapped, ...), custom_call_target="tpu_custom_call" | custom-call | tf_op jit(solution)/shard_map/fetch_block/pallas_call | solution.py:283
  137.2 2.8 %adam_blocks.5 = (f32[2048,256]{1,0:T(8,128)}, f32[2048,256]{1,0:T(8,128)}, f32[16,128]{1,0:T(8,128)S(1)}) custom-call(s32[2]{0:T(128)S(1)} %and_select_fusion.3.refs_0_, s32[2]{0:T(128)S(1)} %get-tuple-element.83.refs_1_, s32[1]{0:T(128)} %bitcast.6.where_ref.refs_2_, s32[2,16]{1,0:T(2,128)S(1)} %bitcast.27, ...), custom_call_target="tpu_custom_call", output_to_operand_aliasing={{0}: (12, {}), {1}: (13, {})} | custom-call | flops 1048576 | bytes 2621440 | tf_op jit(solution)/shard_map/adam_blocks/pallas_call | solution.py:369
  140.0 0.8 collective-permute-done.9.refs_4_
  140.8 0.0 collective-permute-done.10.refs_5_
  140.8 0.6 collective-permute-start.11
  141.4 2.7 %collective-permute-start.12 = (f32[256,128]{1,0:T(8,128)S(1)}, f32[256,128]{1,0:T(8,128)S(1)}, u32[]{:S(2)}, u32[]{:S(2)}) collective-permute-start(f32[256,128]{1,0:T(8,128)S(1)} %slice.31), channel_id=1, source_target_pairs={{0,14},{2,0},{4,2},{6,4},{8,6},{10,8},{12,10},{14,12},{1,15},{3,1}... | collective-permute-start | bytes 393224 | tf_op jit(solution)/shard_map/ppermute | solution.py:476
  144.1 0.1 and_select_fusion.1.refs_0_
  144.2 2.8 %adam_blocks.6 = (f32[2048,256]{1,0:T(8,128)}, f32[2048,256]{1,0:T(8,128)}, f32[16,128]{1,0:T(8,128)S(1)}) custom-call(s32[2]{0:T(128)S(1)} %and_select_fusion.1.refs_0_, s32[2]{0:T(128)S(1)} %get-tuple-element.81.refs_1_, s32[1]{0:T(128)} %bitcast.6.where_ref.refs_2_, s32[2,16]{1,0:T(2,128)S(1)} %bitcast.28, ...), custom_call_target="tpu_custom_call", output_to_operand_aliasing={{0}: (12, {}), {1}: (13, {})} | custom-call | flops 1048576 | bytes 2621440 | tf_op jit(solution)/shard_map/adam_blocks/pallas_call | solution.py:369
  147.0 0.1 collective-permute-done.11.refs_4_
  147.1 0.0 collective-permute-done.12.refs_5_
  147.1 2.2 %adam_blocks.7 = (f32[2048,256]{1,0:T(8,128)}, f32[2048,256]{1,0:T(8,128)}, f32[16,128]{1,0:T(8,128)}) custom-call(s32[1]{0:T(128)S(6)} %select_n.97.row_ref.refs_0_, s32[1]{0:T(128)S(6)} %select_n.98.column_ref.refs_1_, s32[1]{0:T(128)} %bitcast.6.where_ref.refs_2_, s32[2,16]{1,0:T(2,128)S(1)} %bitcast.29, ...), custom_call_target="tpu_custom_call", output_to_operand_aliasing={{0}: (13, {}), {1}: (14, {})} | custom-call | flops 524288 | bytes 1310720 | tf_op jit(solution)/shard_map/adam_blocks/pallas_call | solution.py:369
  (10 shorter events, 0.1 us)
Async XLA Ops:
  1.9 1.0 copy-start
  3.0 0.7 copy-start.2
  3.7 0.7 copy-start.4
  4.4 0.7 copy-start.5
  83.3 10.7 %copy-start.6 = (bf16[256,8192]{1,0:T(8,128)(2,1)}, bf16[256,8192]{1,0:T(8,128)(2,1)S(1)}, u32[]{:S(2)}) copy-start(bf16[256,8192]{1,0:T(8,128)(2,1)S(1)} %get-tuple-element.49.pieces) | copy-start | bytes 12582916
  83.3 10.7 %collective-permute-start.1 = (f32[256,128]{1,0:T(8,128)S(1)}, f32[256,128]{1,0:T(8,128)S(1)}, u32[]{:S(2)}, u32[]{:S(2)}) collective-permute-start(f32[256,128]{1,0:T(8,128)S(1)} %get-tuple-element.89), channel_id=1, source_target_pairs={{0,12},{4,0},{8,4},{12,8},{1,13},{5,1},{9,5},{13,9},{2,14},{6,2},{... | collective-permute-start | bytes 393224 | tf_op jit(solution)/shard_map/ppermute | solution.py:476
  88.9 7.9 %collective-permute-start = (f32[256,128]{1,0:T(8,128)S(1)}, f32[256,128]{1,0:T(8,128)S(1)}, u32[]{:S(2)}, u32[]{:S(2)}) collective-permute-start(f32[256,128]{1,0:T(8,128)S(1)} %get-tuple-element.90), channel_id=1, source_target_pairs={{0,4},{4,8},{8,12},{12,0},{1,5},{5,9},{9,13},{13,1},{2,6},{6,10},{... | collective-permute-start | bytes 393224 | tf_op jit(solution)/shard_map/ppermute | solution.py:476
  94.0 7.3 %copy-start.1 = (f32[2048]{0:T(1024)S(1)}, f32[2048]{0:T(1024)}, u32[]{:S(2)}) copy-start(f32[2048]{0:T(1024)} %param.10) | copy-start | bytes 24580
  94.0 7.2 %copy-start.3 = (s32[16,2]{0,1:T(2,128)S(1)}, s32[16,2]{0,1:T(2,128)}, u32[]{:S(2)}) copy-start(s32[16,2]{0,1:T(2,128)} %param.11) | copy-start | bytes 388
  96.9 14.4 %collective-permute-start.2 = (f32[512,128]{1,0:T(8,128)S(1)}, f32[512,128]{1,0:T(8,128)S(1)}, u32[]{:S(2)}, u32[]{:S(2)}) collective-permute-start(f32[512,128]{1,0:T(8,128)S(1)} %pad_maximum_fusion), channel_id=1, source_target_pairs={{0,4},{4,8},{8,12},{12,0},{1,5},{5,9},{9,13},{13,1},{2,6},{6,10},{... | collective-permute-start | bytes 786440 | tf_op jit(solution)/shard_map/ppermute | solution.py:476
  97.2 14.1 %collective-permute-start.3 = (f32[512,128]{1,0:T(8,128)S(1)}, f32[512,128]{1,0:T(8,128)S(1)}, u32[]{:S(2)}, u32[]{:S(2)}) collective-permute-start(f32[512,128]{1,0:T(8,128)S(1)} %pad_maximum_fusion.1), channel_id=1, source_target_pairs={{0,12},{4,0},{8,4},{12,8},{1,13},{5,1},{9,5},{13,9},{2,14},{6,2},{... | collective-permute-start | bytes 786440 | tf_op jit(solution)/shard_map/ppermute | solution.py:476
  101.3 3.3 %copy-start.7 = (bf16[256,8192]{1,0:T(8,128)(2,1)S(1)}, bf16[256,8192]{1,0:T(8,128)(2,1)}, u32[]{:S(2)}) copy-start(bf16[256,8192]{1,0:T(8,128)(2,1)} %copy-done.6) | copy-start | bytes 12582916
  103.1 8.3 %collective-permute-start.4 = (f32[264,256]{1,0:T(8,128)S(1)}, f32[264,256]{1,0:T(8,128)S(1)}, u32[]{:S(2)}, u32[]{:S(2)}) collective-permute-start(f32[264,256]{1,0:T(8,128)S(1)} %parcel.1), channel_id=1, source_target_pairs={{0,128},{16,144},{32,160},{48,176},{64,192},{80,208},{96,224},{112... | collective-permute-start | bytes 811016 | tf_op jit(solution)/shard_map/ppermute | solution.py:476
  111.3 8.1 %collective-permute-start.7 = (f32[512,128]{1,0:T(8,128)S(1)}, f32[512,128]{1,0:T(8,128)S(1)}, u32[]{:S(2)}, u32[]{:S(2)}) collective-permute-start(f32[512,128]{1,0:T(8,128)S(1)} %add_add_fusion.refs_4_), channel_id=1, source_target_pairs={{0,14},{2,0},{4,2},{6,4},{8,6},{10,8},{12,10},{14,12},{1,15},{3,1}... | collective-permute-start | bytes 786440 | tf_op jit(solution)/shard_map/ppermute | solution.py:476
  113.9 8.8 %collective-permute-start.5 = (f32[512,128]{1,0:T(8,128)S(1)}, f32[512,128]{1,0:T(8,128)S(1)}, u32[]{:S(2)}, u32[]{:S(2)}) collective-permute-start(f32[512,128]{1,0:T(8,128)S(1)} %add_add_fusion.refs_4_), channel_id=1, source_target_pairs={{0,2},{2,4},{4,6},{6,8},{8,10},{10,12},{12,14},{14,0},{1,3},{3,5},... | collective-permute-start | bytes 786440 | tf_op jit(solution)/shard_map/ppermute | solution.py:476
  114.8 12.5 %all-to-all-start.1 = ((f32[16,8,128]{2,1,0:T(8,128)}), f32[16,8,128]{2,1,0:T(8,128)S(1)}, u32[]{:S(2)}, u32[]{:S(2)}) async-start(f32[16,8,128]{2,1,0:T(8,128)} %broadcast_in_dim.2), calls=%async_computation.1 | async-start | bytes 131072 | tf_op jit(solution)/shard_map/all_to_all | solution.py:498
  119.5 10.9 %collective-permute-start.8 = (f32[512,128]{1,0:T(8,128)S(1)}, f32[512,128]{1,0:T(8,128)S(1)}, u32[]{:S(2)}, u32[]{:S(2)}) collective-permute-start(f32[512,128]{1,0:T(8,128)S(1)} %collective-permute-done.7.refs_6_), channel_id=1, source_target_pairs={{0,14},{2,0},{4,2},{6,4},{8,6},{10,8},{12,10},{14,12},{1,15},{3,1}... | collective-permute-start | bytes 786440 | tf_op jit(solution)/shard_map/ppermute | solution.py:476
  122.7 9.5 %collective-permute-start.6 = (f32[512,128]{1,0:T(8,128)S(1)}, f32[512,128]{1,0:T(8,128)S(1)}, u32[]{:S(2)}, u32[]{:S(2)}) collective-permute-start(f32[512,128]{1,0:T(8,128)S(1)} %collective-permute-done.5.refs_5_), channel_id=1, source_target_pairs={{0,2},{2,4},{4,6},{6,8},{8,10},{10,12},{12,14},{14,0},{1,3},{3,5},... | collective-permute-start | bytes 786440 | tf_op jit(solution)/shard_map/ppermute | solution.py:476
  132.2 8.6 %collective-permute-start.9 = (f32[512,128]{1,0:T(8,128)S(1)}, f32[512,128]{1,0:T(8,128)S(1)}, u32[]{:S(2)}, u32[]{:S(2)}) collective-permute-start(f32[512,128]{1,0:T(8,128)S(1)} %collective-permute-done.6.refs_4_), channel_id=1, source_target_pairs={{0,2},{2,4},{4,6},{6,8},{8,10},{10,12},{12,14},{14,0},{1,3},{3,5},... | collective-permute-start | bytes 786440 | tf_op jit(solution)/shard_map/ppermute | solution.py:476
  132.2 8.6 %collective-permute-start.10 = (f32[512,128]{1,0:T(8,128)S(1)}, f32[512,128]{1,0:T(8,128)S(1)}, u32[]{:S(2)}, u32[]{:S(2)}) collective-permute-start(f32[512,128]{1,0:T(8,128)S(1)} %collective-permute-done.8.refs_5_), channel_id=1, source_target_pairs={{0,14},{2,0},{4,2},{6,4},{8,6},{10,8},{12,10},{14,12},{1,15},{3,1}... | collective-permute-start | bytes 786440 | tf_op jit(solution)/shard_map/ppermute | solution.py:476
  140.8 6.3 %collective-permute-start.11 = (f32[256,128]{1,0:T(8,128)S(1)}, f32[256,128]{1,0:T(8,128)S(1)}, u32[]{:S(2)}, u32[]{:S(2)}) collective-permute-start(f32[256,128]{1,0:T(8,128)S(1)} %slice.30), channel_id=1, source_target_pairs={{0,2},{2,4},{4,6},{6,8},{8,10},{10,12},{12,14},{14,0},{1,3},{3,5},... | collective-permute-start | bytes 393224 | tf_op jit(solution)/shard_map/ppermute | solution.py:476
  141.4 5.7 %collective-permute-start.12 = (f32[256,128]{1,0:T(8,128)S(1)}, f32[256,128]{1,0:T(8,128)S(1)}, u32[]{:S(2)}, u32[]{:S(2)}) collective-permute-start(f32[256,128]{1,0:T(8,128)S(1)} %slice.31), channel_id=1, source_target_pairs={{0,14},{2,0},{4,2},{6,4},{8,6},{10,8},{12,10},{14,12},{1,15},{3,1}... | collective-permute-start | bytes 393224 | tf_op jit(solution)/shard_map/ppermute | solution.py:476

commit v8 on v7

--- a/solution.py
+++ b/solution.py
@@ -50,11 +50,7 @@
     return jnp.where(used, target, rows_dev)
 
 
-def slot_kernel(
-    rows_dev, map_ref, grad, hot_ref, count_ref, rows_ref, out_ref, tally, held, natural, grad_ref, sems, sem
-):
-    load = pltpu.make_async_copy(grad, natural, sem)
-    load.start()
+def slot_kernel(rows_dev, map_ref, grad_ref, hot_ref, count_ref, rows_ref, out_ref, tally, held, sems):
     groups, span = map_ref.shape
     owners, _, cap = tally.shape
     per_owner = cap // LOW
@@ -84,8 +80,6 @@
         return carry
 
     lax.fori_loop(0, groups // batch, count, 0)
-    load.wait()
-    grad_ref[...] = natural[...].T
     depth, shares, height, lanes = held.shape
     columns = (height - EXTRA) * lanes // cap
 
@@ -113,27 +107,24 @@
         leave(owner).wait()
 
 
-def slot_sums(slots, grad, hot_slices, row_counts, unique_rows, shares, rows_dev):
+def slot_sums(slots, grad_t, hot_slices, row_counts, unique_rows, shares, rows_dev):
     _, owners, cap = unique_rows.shape
-    samples, columns = grad.shape
+    columns, samples = grad_t.shape
     height = columns // shares * cap // LANES + EXTRA
     depth = 4
     return pl.pallas_call(
         lambda *refs: slot_kernel(rows_dev, *refs),
         out_shape=jax.ShapeDtypeStruct((owners * shares, height, LANES), jnp.float32),
-        in_specs=[VMEM, ANY, SMEM, SMEM, VMEM],
+        in_specs=[VMEM, VMEM, SMEM, SMEM, VMEM],
         out_specs=HBM,
         scratch_shapes=[
             pltpu.VMEM((owners, samples, cap), jnp.bfloat16),
             pltpu.VMEM((depth, shares, height, LANES), jnp.float32),
-            pltpu.VMEM(grad.shape, grad.dtype),
-            pltpu.VMEM((columns, samples), grad.dtype),
             pltpu.SemaphoreType.DMA((depth,)),
-            pltpu.SemaphoreType.DMA,
         ],
         compiler_params=pltpu.CompilerParams(vmem_limit_bytes=50 << 20),
         name="slot_sums",
-    )(slots, grad, hot_slices, row_counts, unique_rows)
+    )(slots, grad_t, hot_slices, row_counts, unique_rows)
 
 
 def add_block(pieces, aims, start, out_ref, select):
@@ -459,7 +450,7 @@
     second_lines = moment_second.reshape(-1, LANES)
     slots = dedup_map.reshape(-1, GROUP * dedup_map.shape[1])
     slot_grad = slot_sums(
-        slots, upstream_grad, hots, row_counts, unique_rows, n_pair, rows_dev
+        slots, upstream_grad.T, hots, row_counts, unique_rows, n_pair, rows_dev
     )
     slot_grad, position, far_at, pair_at = lax.optimization_barrier(
         (slot_grad, position, far_at, pair_at)
@@ -512,20 +503,24 @@
     def update(offsets, parts, second, held=None, fetched=None):
         return adam_blocks(*at_ring(offsets), parts, shape, full_width, common, second, held, fetched)
 
-    rise, fall = send(mine, ring, n_dp, 1), send(mine, ring, n_dp, -1)
-    parts = [[mine], [rise], [fall]]
-    rise, fall = send(rise, ring, n_dp, 1), send(fall, ring, n_dp, -1)
+    def hop(pieces, step):
+        return [send(piece, ring, n_dp, step) for piece in pieces]
+
+    own = [mine[:half], mine[half:]]
+    rise, fall = hop(own, 1), hop(own, -1)
+    parts = [own, rise, fall]
+    rise, fall = hop(rise, 1), hop(fall, -1)
     weights, first, second = update((0, -1, 1), parts, second_lines)
-    rise, fall, second = lax.optimization_barrier((rise, fall, second))
-    parts = [[rise], [fall]]
-    rise, fall = send(rise, ring, n_dp, 1), send(fall, ring, n_dp, -1)
+    rise[1], fall[1], second = lax.optimization_barrier((rise[1], fall[1], second))
+    parts = [rise, fall]
+    rise, fall = hop(rise, 1), hop(fall, -1)
     fetched = fetch_block(*at_ring((4,)), shape, common)
     weights, first, second = update((-2, 2), parts, second, (weights, first))
-    rise, fall, second, fetched = lax.optimization_barrier((rise, fall, second, fetched))
-    parts = [[rise], [fall]]
-    rise, fall = send(rise[:half], ring, n_dp, 1), send(fall[half:], ring, n_dp, -1)
+    rise[1], fall[1], second, fetched = lax.optimization_barrier((rise[1], fall[1], second, fetched))
+    parts = [rise, fall]
+    last = [send(rise[0], ring, n_dp, 1), send(fall[1], ring, n_dp, -1)]
     weights, first, second = update((-3, 3), parts, second, (weights, first))
-    weights, first, second = update((4,), [[rise, fall]], second, (weights, first), fetched)
+    weights, first, second = update((4,), [last], second, (weights, first), fetched)
     return (weights, first, second.reshape(-1))
 
 

time: 151 us -> 152 us (level)
  starting transfers between devices: 28.4 us -> 37.4 us
  waiting for transfers between devices: 14.3 us -> 8.29 us
  local copies, waits for them, and re-layouts: 5.07 us -> 3.25 us
    ppermute x13 -> x19, starting transfers between devices: 23.8 us -> 32.1 us  [send(): lax.ppermute(value, axes, [(i, (i + step) % count) for i in range(count)])]
    all_to_all x1, waiting for transfers between devices: 4.52 us -> 1.24 us  [on_device(): lax.all_to_all(jnp.broadcast_to(own_squares[None], (n_all,) + own_squares...]
    ppermute x13 -> x19, waiting for transfers between devices: 9.75 us -> 7.05 us  [send(): lax.ppermute(value, axes, [(i, (i + step) % count) for i in range(count)])]
    unnamed x17 -> x14, local copies, waits for them, and re-layouts: 4.21 us -> 2.39 us
  transfers between devices with their start and end apart: 14 -> 20, of which waited for: 6 -> 4; matrix products, arithmetic and copies ran while one was open for 1% -> 1% of each run, Pallas kernels for 13% -> 13%
where the time goes in v8:
time: 152 us; the launch traced here: 151 us
  blocking collectives  61 us (40%)
  Pallas kernels  38.8 us (26%)
  starting transfers between devices  37.4 us (25%)
  waiting for transfers between devices  8.29 us (5%)
  local copies, waits for them, and re-layouts  3.25 us (2%)
    all_to_all x1, blocking collectives, on_device(): lax.all_to_all(slot_grad, ('table', 'pair'), split_axis=0, concat_axis=0,...  61 us
    ppermute x19, starting transfers between devices, send(): lax.ppermute(value, axes, [(i, (i + step) % count) for i in range(count)])  32.1 us
    pallas_call x1, Pallas kernels, slot_sums(): pl.pallas_call(lambda *refs: slot_kernel(rows_dev, *refs), out_shape=jax....  12.7 us
    pallas_call x4, Pallas kernels, adam_blocks(): pl.pallas_call(lambda *refs: adam_kernel(groups, full_width, fetched is n...  10.8 us
    pallas_call x2, Pallas kernels, place_next(): pl.pallas_call(place_next_kernel, out_shape=tuple((jax.ShapeDtypeStruct((...  7.41 us
    ppermute x19, waiting for transfers between devices, send(): lax.ppermute(value, axes, [(i, (i + step) % count) for i in range(count)])  7.05 us
    all_to_all x1, starting transfers between devices, on_device(): lax.all_to_all(jnp.broadcast_to(own_squares[None], (n_all,) + own_squares...  5.25 us
    pallas_call x1, Pallas kernels, place_first(): pl.pallas_call(place_first_kernel, out_shape=(jax.ShapeDtypeStruct((2 * c...  4.49 us
  transfers between devices with their start and end apart: 20, of which 4 were waited for; matrix products, arithmetic and copies ran while one was open for 1% of the time, Pallas kernels for 13%

profile of v8, /device:TPU:2, one launch (start us, length us, event | category | flops | bytes accessed | tf_op | source)
XLA Modules:
  0.0 150.7 jit_solution(18175776637585611673)
XLA Ops:
  0.7 1.1 copy.19
  1.8 0.2 reshape.26.refs_0_
  2.0 1.2 copy.20
  3.3 12.7 %slot_sums.1 = f32[32,264,128]{2,1,0:T(8,128)} custom-call(s32[128,256]{1,0:T(8,128)S(1)} %reshape.26.refs_0_, bf16[256,1024]{1,0:T(8,128)(2,1)S(1)} %bitcast.18, s32[2,16]{1,0:T(2,128)S(1)} %bitcast.25, s32[1,16]{1,0:T(1,128)S(1)} %copy-done.3, s32[1,16,256]{2,1,0:T(8,128)S(1)} %copy-done.2), custom_call_target="tpu_custom_call" | custom-call | tf_op jit(solution)/shard_map/slot_sums/pallas_call | solution.py:115
  15.9 61.0 %all_to_all.10.got_ref = f32[32,264,128]{2,1,0:T(8,128)} all-to-all(f32[32,264,128]{2,1,0:T(8,128)} %slot_sums.1), channel_id=1, replica_groups=mesh['table'=16,'far'=4,'pair'=2,'col'=2] {'table','pair'}, dimensions={0} | all-to-all | bytes 8650752 | tf_op jit(solution)/shard_map/all_to_all | solution.py:458
  77.0 4.5 %place_first.1 = (bf16[256,8192]{1,0:T(8,128)(2,1)S(1)}, s32[8,8192]{1,0:T(8,128)S(1)}, f32[512,128]{1,0:T(8,128)S(1)}) custom-call(s32[1]{0:T(128)} %bitcast.6.start_ref, f32[32,264,128]{2,1,0:T(8,128)} %all_to_all.10.got_ref), custom_call_target="tpu_custom_call" | custom-call | flops 2147483648 | bytes 8388608 | tf_op jit(solution)/shard_map/place_first/pallas_call | solution.py:204
  81.5 3.3 %collective-permute-start = (f32[256,128]{1,0:T(8,128)S(1)}, f32[256,128]{1,0:T(8,128)S(1)}, u32[]{:S(2)}, u32[]{:S(2)}) collective-permute-start(f32[256,128]{1,0:T(8,128)S(1)} %get-tuple-element.92), channel_id=1, source_target_pairs={{0,4},{4,8},{8,12},{12,0},{1,5},{5,9},{9,13},{13,1},{2,6},{6,10},{... | collective-permute-start | bytes 393224 | tf_op jit(solution)/shard_map/ppermute | solution.py:467
  84.9 2.4 %collective-permute-start.1 = (f32[256,128]{1,0:T(8,128)S(1)}, f32[256,128]{1,0:T(8,128)S(1)}, u32[]{:S(2)}, u32[]{:S(2)}) collective-permute-start(f32[256,128]{1,0:T(8,128)S(1)} %get-tuple-element.91), channel_id=1, source_target_pairs={{0,12},{4,0},{8,4},{12,8},{1,13},{5,1},{9,5},{13,9},{2,14},{6,2},{... | collective-permute-start | bytes 393224 | tf_op jit(solution)/shard_map/ppermute | solution.py:467
  87.3 0.1 pad_add_fusion.start_ref
  87.3 5.0 %place_next.2 = (f32[512,128]{1,0:T(8,128)S(1)}, f32[512,128]{1,0:T(8,128)S(1)}) custom-call(s32[2]{0:T(128)S(1)} %pad_add_fusion.start_ref, bf16[256,8192]{1,0:T(8,128)(2,1)S(1)} %get-tuple-element.49.pieces, s32[8,8192]{1,0:T(8,128)S(1)} %get-tuple-element.50.aims), custom_call_target="tpu_custom_call" | custom-call | flops 4294967296 | bytes 8388608 | tf_op jit(solution)/shard_map/place_next/pallas_call | solution.py:227
  92.4 0.0 copy-start
  92.4 0.0 collective-permute-done
  92.4 0.0 collective-permute-done.1
  92.4 0.1 slice_add_fusion.1
  92.6 4.2 %collective-permute-start.2 = (f32[512,128]{1,0:T(8,128)S(1)}, f32[512,128]{1,0:T(8,128)S(1)}, u32[]{:S(2)}, u32[]{:S(2)}) collective-permute-start(f32[512,128]{1,0:T(8,128)S(1)} %pad_maximum_fusion), channel_id=1, source_target_pairs={{0,4},{4,8},{8,12},{12,0},{1,5},{5,9},{9,13},{13,1},{2,6},{6,10},{... | collective-permute-start | bytes 786440 | tf_op jit(solution)/shard_map/ppermute | solution.py:467
  96.8 0.0 collective-permute-start.3
  96.8 1.8 %parcel.1 = f32[264,256]{1,0:T(8,128)S(1)} custom-call(s32[1]{0:T(128)} %bitcast.7.where_ref.refs_2_, s32[2,16]{1,0:T(2,128)S(1)} %bitcast.26, f32[2048,256]{1,0:T(8,128)} %refs_8_.1, f32[2048,256]{1,0:T(8,128)} %refs_9_.1, f32[16,128]{1,0:T(8,128)S(1)} %bitcast.19), custom_call_target="tpu_custom_call" | custom-call | tf_op jit(solution)/shard_map/parcel/pallas_call | solution.py:418
  98.6 1.5 collective-permute-start.4
  100.1 2.4 %place_next.3 = f32[512,128]{1,0:T(8,128)S(1)} custom-call(s32[1]{0:T(128)} %bitcast.8.start_ref, bf16[256,8192]{1,0:T(8,128)(2,1)S(1)} %copy-done.5, s32[8,8192]{1,0:T(8,128)S(1)} %get-tuple-element.50.aims), custom_call_target="tpu_custom_call" | custom-call | flops 2147483648 | bytes 8388608 | tf_op jit(solution)/shard_map/place_next/pallas_call | solution.py:227
  102.5 3.4 %collective-permute-done.2 = f32[512,128]{1,0:T(8,128)S(1)} collective-permute-done((f32[512,128]{1,0:T(8,128)S(1)}, f32[512,128]{1,0:T(8,128)S(1)}, u32[]{:S(2)}, u32[]{:S(2)}) %collective-permute-start.2) | collective-permute-done | bytes 262176 | tf_op jit(solution)/shard_map/ppermute | solution.py:467
  105.8 2.3 %collective-permute-done.3 = f32[512,128]{1,0:T(8,128)S(1)} collective-permute-done((f32[512,128]{1,0:T(8,128)S(1)}, f32[512,128]{1,0:T(8,128)S(1)}, u32[]{:S(2)}, u32[]{:S(2)}) %collective-permute-start.3) | collective-permute-done | bytes 262176 | tf_op jit(solution)/shard_map/ppermute | solution.py:467
  108.2 0.0 collective-permute-done.4.refs_10_.refs_8_.swapped.refs_6_
  108.2 0.3 collective-permute-start.11
  108.5 1.8 %collective-permute-start.9 = (f32[256,128]{1,0:T(8,128)S(1)}, f32[256,128]{1,0:T(8,128)S(1)}, u32[]{:S(2)}, u32[]{:S(2)}) collective-permute-start(f32[256,128]{1,0:T(8,128)S(1)} %get-tuple-element.87.refs_5_), channel_id=1, source_target_pairs={{0,2},{2,4},{4,6},{6,8},{8,10},{10,12},{12,14},{14,0},{1,3},{3,5},... | collective-permute-start | bytes 393224 | tf_op jit(solution)/shard_map/ppermute | solution.py:467
  110.3 0.6 collective-permute-start.5
  111.0 0.1 and_select_fusion.4
  111.0 2.6 %collective-permute-start.13 = (f32[256,128]{1,0:T(8,128)S(1)}, f32[256,128]{1,0:T(8,128)S(1)}, u32[]{:S(2)}, u32[]{:S(2)}) collective-permute-start(f32[256,128]{1,0:T(8,128)S(1)} %get-tuple-element.88.refs_4_), channel_id=1, source_target_pairs={{0,14},{2,0},{4,2},{6,4},{8,6},{10,8},{12,10},{14,12},{1,15},{3,1}... | collective-permute-start | bytes 393224 | tf_op jit(solution)/shard_map/ppermute | solution.py:467
  113.7 0.1 multiply_reduce_fusion
  113.8 0.6 broadcast_in_dim.2
  114.4 5.2 %all-to-all-start.1 = ((f32[16,8,128]{2,1,0:T(8,128)}), f32[16,8,128]{2,1,0:T(8,128)S(1)}, u32[]{:S(2)}, u32[]{:S(2)}) async-start(f32[16,8,128]{2,1,0:T(8,128)} %broadcast_in_dim.2), calls=%async_computation.1 | async-start | bytes 131072 | tf_op jit(solution)/shard_map/all_to_all | solution.py:489
  119.7 0.0 collective-permute-done.9.refs_7_
  119.7 2.0 %collective-permute-start.10 = (f32[256,128]{1,0:T(8,128)S(1)}, f32[256,128]{1,0:T(8,128)S(1)}, u32[]{:S(2)}, u32[]{:S(2)}) collective-permute-start(f32[256,128]{1,0:T(8,128)S(1)} %collective-permute-done.9.refs_7_), channel_id=1, source_target_pairs={{0,2},{2,4},{4,6},{6,8},{8,10},{10,12},{12,14},{14,0},{1,3},{3,5},... | collective-permute-start | bytes 393224 | tf_op jit(solution)/shard_map/ppermute | solution.py:467
  121.7 0.0 collective-permute-done.11.refs_9_
  121.7 1.3 collective-permute-start.12
  123.0 0.0 collective-permute-done.5.refs_6_
  123.0 0.7 collective-permute-start.6
  123.8 0.1 and_select_fusion.2
  123.8 0.0 collective-permute-done.13.refs_8_
  123.8 2.6 %collective-permute-start.16 = (f32[256,128]{1,0:T(8,128)S(1)}, f32[256,128]{1,0:T(8,128)S(1)}, u32[]{:S(2)}, u32[]{:S(2)}) collective-permute-start(f32[256,128]{1,0:T(8,128)S(1)} %collective-permute-done.13.refs_8_), channel_id=1, source_target_pairs={{0,14},{2,0},{4,2},{6,4},{8,6},{10,8},{12,10},{14,12},{1,15},{3,1}... | collective-permute-start | bytes 393224 | tf_op jit(solution)/shard_map/ppermute | solution.py:467
  126.4 1.2 all-to-all-done.1.refs_11_.refs_9_.refs_7_
  127.7 3.0 %adam_blocks.4 = (f32[2048,256]{1,0:T(8,128)}, f32[2048,256]{1,0:T(8,128)}, f32[16,128]{1,0:T(8,128)S(1)}) custom-call(s32[3]{0:T(128)S(1)} %and_select_fusion.5.refs_0_, s32[3]{0:T(128)S(1)} %get-tuple-element.85.refs_1_, s32[1]{0:T(128)} %bitcast.7.where_ref.refs_2_, s32[2,16]{1,0:T(2,128)S(1)} %bitcast.27, f32[256,128]{1,0:T(8,128)S(1)} %get-tuple-element.88.refs_4_, ...), custom_call_target="tpu_custom_call" | custom-call | flops 1572864 | bytes 3932160 | tf_op jit(solution)/shard_map/adam_blocks/pallas_call | solution.py:360
  130.7 0.0 collective-permute-done.10.refs_5_
  130.7 0.0 collective-permute-done.12.refs_7_
  130.7 0.6 collective-permute-start.14
  131.3 2.7 %collective-permute-start.15 = (f32[256,128]{1,0:T(8,128)S(1)}, f32[256,128]{1,0:T(8,128)S(1)}, u32[]{:S(2)}, u32[]{:S(2)}) collective-permute-start(f32[256,128]{1,0:T(8,128)S(1)} %collective-permute-done.12.refs_7_), channel_id=1, source_target_pairs={{0,14},{2,0},{4,2},{6,4},{8,6},{10,8},{12,10},{14,12},{1,15},{3,1}... | collective-permute-start | bytes 393224 | tf_op jit(solution)/shard_map/ppermute | solution.py:467
  134.0 0.0 collective-permute-done.6.refs_4_
  134.0 0.0 collective-permute-start.7
  134.0 0.1 and_select_fusion.3.refs_0_
  134.1 0.1 and_select_fusion
  134.2 1.6 %fetch_block.1.refs_12_ = f32[2,1,512,128]{3,2,1,0:T(8,128)S(1)} custom-call(s32[1]{0:T(128)S(6)} %select_n.97.row_ref.refs_0_, s32[1]{0:T(128)S(6)} %select_n.98.column_ref.refs_1_, s32[1]{0:T(128)} %bitcast.7.where_ref.refs_2_, s32[2,16]{1,0:T(2,128)S(1)} %bitcast.28, f32[264,256]{1,0:T(8,128)S(1)} %collective-permute-done.4.refs_10_.refs_8_.swapped.refs_6_, ...), custom_call_target="tpu_custom_call" | custom-call | tf_op jit(solution)/shard_map/fetch_block/pallas_call | solution.py:274
  135.8 0.0 collective-permute-done.16.refs_6_
  135.8 3.3 %collective-permute-start.18 = (f32[256,128]{1,0:T(8,128)S(1)}, f32[256,128]{1,0:T(8,128)S(1)}, u32[]{:S(2)}, u32[]{:S(2)}) collective-permute-start(f32[256,128]{1,0:T(8,128)S(1)} %collective-permute-done.16.refs_6_), channel_id=1, source_target_pairs={{0,14},{2,0},{4,2},{6,4},{8,6},{10,8},{12,10},{14,12},{1,15},{3,1}... | collective-permute-start | bytes 393224 | tf_op jit(solution)/shard_map/ppermute | solution.py:467
  139.1 2.8 %adam_blocks.5 = (f32[2048,256]{1,0:T(8,128)}, f32[2048,256]{1,0:T(8,128)}, f32[16,128]{1,0:T(8,128)S(1)}) custom-call(s32[2]{0:T(128)S(1)} %and_select_fusion.3.refs_0_, s32[2]{0:T(128)S(1)} %get-tuple-element.83.refs_1_, s32[1]{0:T(128)} %bitcast.7.where_ref.refs_2_, s32[2,16]{1,0:T(2,128)S(1)} %bitcast.29, ...), custom_call_target="tpu_custom_call", output_to_operand_aliasing={{0}: (14, {}), {1}: (15, {})} | custom-call | flops 1048576 | bytes 2621440 | tf_op jit(solution)/shard_map/adam_blocks/pallas_call | solution.py:360
  141.9 0.0 collective-permute-done.14.refs_5_
  141.9 0.0 collective-permute-done.15.refs_7_
  141.9 0.1 collective-permute-start.17
  142.0 0.0 collective-permute-done.7.refs_4_
  142.0 2.0 %collective-permute-start.8 = (f32[256,128]{1,0:T(8,128)S(1)}, f32[256,128]{1,0:T(8,128)S(1)}, u32[]{:S(2)}, u32[]{:S(2)}) collective-permute-start(f32[256,128]{1,0:T(8,128)S(1)} %collective-permute-done.7.refs_4_), channel_id=1, source_target_pairs={{0,2},{2,4},{4,6},{6,8},{8,10},{10,12},{12,14},{14,0},{1,3},{3,5},... | collective-permute-start | bytes 393224 | tf_op jit(solution)/shard_map/ppermute | solution.py:467
  144.0 0.1 and_select_fusion.1.refs_0_
  144.1 0.0 collective-permute-done.18.refs_6_
  144.1 2.8 %adam_blocks.6 = (f32[2048,256]{1,0:T(8,128)}, f32[2048,256]{1,0:T(8,128)}, f32[16,128]{1,0:T(8,128)S(1)}) custom-call(s32[2]{0:T(128)S(1)} %and_select_fusion.1.refs_0_, s32[2]{0:T(128)S(1)} %get-tuple-element.81.refs_1_, s32[1]{0:T(128)} %bitcast.7.where_ref.refs_2_, s32[2,16]{1,0:T(2,128)S(1)} %bitcast.30, ...), custom_call_target="tpu_custom_call", output_to_operand_aliasing={{0}: (14, {}), {1}: (15, {})} | custom-call | flops 1048576 | bytes 2621440 | tf_op jit(solution)/shard_map/adam_blocks/pallas_call | solution.py:360
  146.9 0.0 collective-permute-done.17.refs_5_
  147.0 1.3 collective-permute-done.8.refs_4_
  148.3 2.2 %adam_blocks.7 = (f32[2048,256]{1,0:T(8,128)}, f32[2048,256]{1,0:T(8,128)}, f32[16,128]{1,0:T(8,128)}) custom-call(s32[1]{0:T(128)S(6)} %select_n.97.row_ref.refs_0_, s32[1]{0:T(128)S(6)} %select_n.98.column_ref.refs_1_, s32[1]{0:T(128)} %bitcast.7.where_ref.refs_2_, s32[2,16]{1,0:T(2,128)S(1)} %bitcast.31, ...), custom_call_target="tpu_custom_call", output_to_operand_aliasing={{0}: (13, {}), {1}: (14, {})} | custom-call | flops 524288 | bytes 1310720 | tf_op jit(solution)/shard_map/adam_blocks/pallas_call | solution.py:360
  (18 shorter events, 0.2 us)
Async XLA Ops:
  0.6 2.6 %copy-start.1 = (s32[16,2]{0,1:T(2,128)S(1)}, s32[16,2]{0,1:T(2,128)}, u32[]{:S(2)}) copy-start(s32[16,2]{0,1:T(2,128)} %param.11) | copy-start | bytes 388
  0.6 2.6 %copy-start.2 = (s32[1,16,256]{2,1,0:T(8,128)S(1)}, s32[1,16,256]{2,1,0:T(8,128)}, u32[]{:S(2)}) copy-start(s32[1,16,256]{2,1,0:T(8,128)} %refs_4_.1) | copy-start | bytes 49156
  0.7 2.6 %copy-start.3 = (s32[1,16]{1,0:T(1,128)S(1)}, s32[1,16]{1,0:T(1,128)}, u32[]{:S(2)}) copy-start(s32[1,16]{1,0:T(1,128)} %refs_3_.1) | copy-start | bytes 196
  81.5 10.9 %copy-start.4 = (bf16[256,8192]{1,0:T(8,128)(2,1)}, bf16[256,8192]{1,0:T(8,128)(2,1)S(1)}, u32[]{:S(2)}) copy-start(bf16[256,8192]{1,0:T(8,128)(2,1)S(1)} %get-tuple-element.49.pieces) | copy-start | bytes 12582916
  81.5 10.9 %collective-permute-start = (f32[256,128]{1,0:T(8,128)S(1)}, f32[256,128]{1,0:T(8,128)S(1)}, u32[]{:S(2)}, u32[]{:S(2)}) collective-permute-start(f32[256,128]{1,0:T(8,128)S(1)} %get-tuple-element.92), channel_id=1, source_target_pairs={{0,4},{4,8},{8,12},{12,0},{1,5},{5,9},{9,13},{13,1},{2,6},{6,10},{... | collective-permute-start | bytes 393224 | tf_op jit(solution)/shard_map/ppermute | solution.py:467
  84.9 7.6 %collective-permute-start.1 = (f32[256,128]{1,0:T(8,128)S(1)}, f32[256,128]{1,0:T(8,128)S(1)}, u32[]{:S(2)}, u32[]{:S(2)}) collective-permute-start(f32[256,128]{1,0:T(8,128)S(1)} %get-tuple-element.91), channel_id=1, source_target_pairs={{0,12},{4,0},{8,4},{12,8},{1,13},{5,1},{9,5},{13,9},{2,14},{6,2},{... | collective-permute-start | bytes 393224 | tf_op jit(solution)/shard_map/ppermute | solution.py:467
  92.4 4.4 %copy-start = (f32[2048]{0:T(1024)S(1)}, f32[2048]{0:T(1024)}, u32[]{:S(2)}) copy-start(f32[2048]{0:T(1024)} %param.10) | copy-start | bytes 24580
  92.6 13.3 %collective-permute-start.2 = (f32[512,128]{1,0:T(8,128)S(1)}, f32[512,128]{1,0:T(8,128)S(1)}, u32[]{:S(2)}, u32[]{:S(2)}) collective-permute-start(f32[512,128]{1,0:T(8,128)S(1)} %pad_maximum_fusion), channel_id=1, source_target_pairs={{0,4},{4,8},{8,12},{12,0},{1,5},{5,9},{9,13},{13,1},{2,6},{6,10},{... | collective-permute-start | bytes 786440 | tf_op jit(solution)/shard_map/ppermute | solution.py:467
  96.8 11.4 %collective-permute-start.3 = (f32[512,128]{1,0:T(8,128)S(1)}, f32[512,128]{1,0:T(8,128)S(1)}, u32[]{:S(2)}, u32[]{:S(2)}) collective-permute-start(f32[512,128]{1,0:T(8,128)S(1)} %pad_maximum_fusion.1), channel_id=1, source_target_pairs={{0,12},{4,0},{8,4},{12,8},{1,13},{5,1},{9,5},{13,9},{2,14},{6,2},{... | collective-permute-start | bytes 786440 | tf_op jit(solution)/shard_map/ppermute | solution.py:467
  96.8 3.3 %copy-start.5 = (bf16[256,8192]{1,0:T(8,128)(2,1)S(1)}, bf16[256,8192]{1,0:T(8,128)(2,1)}, u32[]{:S(2)}) copy-start(bf16[256,8192]{1,0:T(8,128)(2,1)} %copy-done.4) | copy-start | bytes 12582916
  98.6 9.6 %collective-permute-start.4 = (f32[264,256]{1,0:T(8,128)S(1)}, f32[264,256]{1,0:T(8,128)S(1)}, u32[]{:S(2)}, u32[]{:S(2)}) collective-permute-start(f32[264,256]{1,0:T(8,128)S(1)} %parcel.1), channel_id=1, source_target_pairs={{0,128},{16,144},{32,160},{48,176},{64,192},{80,208},{96,224},{112... | collective-permute-start | bytes 811016 | tf_op jit(solution)/shard_map/ppermute | solution.py:467
  108.2 13.5 %collective-permute-start.11 = (f32[256,128]{1,0:T(8,128)S(1)}, f32[256,128]{1,0:T(8,128)S(1)}, u32[]{:S(2)}, u32[]{:S(2)}) collective-permute-start(f32[256,128]{1,0:T(8,128)S(1)} %get-tuple-element.87.refs_5_), channel_id=1, source_target_pairs={{0,14},{2,0},{4,2},{6,4},{8,6},{10,8},{12,10},{14,12},{1,15},{3,1}... | collective-permute-start | bytes 393224 | tf_op jit(solution)/shard_map/ppermute | solution.py:467
  108.5 11.2 %collective-permute-start.9 = (f32[256,128]{1,0:T(8,128)S(1)}, f32[256,128]{1,0:T(8,128)S(1)}, u32[]{:S(2)}, u32[]{:S(2)}) collective-permute-start(f32[256,128]{1,0:T(8,128)S(1)} %get-tuple-element.87.refs_5_), channel_id=1, source_target_pairs={{0,2},{2,4},{4,6},{6,8},{8,10},{10,12},{12,14},{14,0},{1,3},{3,5},... | collective-permute-start | bytes 393224 | tf_op jit(solution)/shard_map/ppermute | solution.py:467
  110.3 12.7 %collective-permute-start.5 = (f32[256,128]{1,0:T(8,128)S(1)}, f32[256,128]{1,0:T(8,128)S(1)}, u32[]{:S(2)}, u32[]{:S(2)}) collective-permute-start(f32[256,128]{1,0:T(8,128)S(1)} %get-tuple-element.88.refs_4_), channel_id=1, source_target_pairs={{0,2},{2,4},{4,6},{6,8},{8,10},{10,12},{12,14},{14,0},{1,3},{3,5},... | collective-permute-start | bytes 393224 | tf_op jit(solution)/shard_map/ppermute | solution.py:467
  111.0 12.8 %collective-permute-start.13 = (f32[256,128]{1,0:T(8,128)S(1)}, f32[256,128]{1,0:T(8,128)S(1)}, u32[]{:S(2)}, u32[]{:S(2)}) collective-permute-start(f32[256,128]{1,0:T(8,128)S(1)} %get-tuple-element.88.refs_4_), channel_id=1, source_target_pairs={{0,14},{2,0},{4,2},{6,4},{8,6},{10,8},{12,10},{14,12},{1,15},{3,1}... | collective-permute-start | bytes 393224 | tf_op jit(solution)/shard_map/ppermute | solution.py:467
  114.4 13.2 %all-to-all-start.1 = ((f32[16,8,128]{2,1,0:T(8,128)}), f32[16,8,128]{2,1,0:T(8,128)S(1)}, u32[]{:S(2)}, u32[]{:S(2)}) async-start(f32[16,8,128]{2,1,0:T(8,128)} %broadcast_in_dim.2), calls=%async_computation.1 | async-start | bytes 131072 | tf_op jit(solution)/shard_map/all_to_all | solution.py:489
  119.7 11.0 %collective-permute-start.10 = (f32[256,128]{1,0:T(8,128)S(1)}, f32[256,128]{1,0:T(8,128)S(1)}, u32[]{:S(2)}, u32[]{:S(2)}) collective-permute-start(f32[256,128]{1,0:T(8,128)S(1)} %collective-permute-done.9.refs_7_), channel_id=1, source_target_pairs={{0,2},{2,4},{4,6},{6,8},{8,10},{10,12},{12,14},{14,0},{1,3},{3,5},... | collective-permute-start | bytes 393224 | tf_op jit(solution)/shard_map/ppermute | solution.py:467
  121.7 9.0 %collective-permute-start.12 = (f32[256,128]{1,0:T(8,128)S(1)}, f32[256,128]{1,0:T(8,128)S(1)}, u32[]{:S(2)}, u32[]{:S(2)}) collective-permute-start(f32[256,128]{1,0:T(8,128)S(1)} %collective-permute-done.11.refs_9_), channel_id=1, source_target_pairs={{0,14},{2,0},{4,2},{6,4},{8,6},{10,8},{12,10},{14,12},{1,15},{3,1}... | collective-permute-start | bytes 393224 | tf_op jit(solution)/shard_map/ppermute | solution.py:467
  123.0 11.0 %collective-permute-start.6 = (f32[256,128]{1,0:T(8,128)S(1)}, f32[256,128]{1,0:T(8,128)S(1)}, u32[]{:S(2)}, u32[]{:S(2)}) collective-permute-start(f32[256,128]{1,0:T(8,128)S(1)} %collective-permute-done.5.refs_6_), channel_id=1, source_target_pairs={{0,2},{2,4},{4,6},{6,8},{8,10},{10,12},{12,14},{14,0},{1,3},{3,5},... | collective-permute-start | bytes 393224 | tf_op jit(solution)/shard_map/ppermute | solution.py:467
  123.8 11.9 %collective-permute-start.16 = (f32[256,128]{1,0:T(8,128)S(1)}, f32[256,128]{1,0:T(8,128)S(1)}, u32[]{:S(2)}, u32[]{:S(2)}) collective-permute-start(f32[256,128]{1,0:T(8,128)S(1)} %collective-permute-done.13.refs_8_), channel_id=1, source_target_pairs={{0,14},{2,0},{4,2},{6,4},{8,6},{10,8},{12,10},{14,12},{1,15},{3,1}... | collective-permute-start | bytes 393224 | tf_op jit(solution)/shard_map/ppermute | solution.py:467
  130.7 11.2 %collective-permute-start.14 = (f32[256,128]{1,0:T(8,128)S(1)}, f32[256,128]{1,0:T(8,128)S(1)}, u32[]{:S(2)}, u32[]{:S(2)}) collective-permute-start(f32[256,128]{1,0:T(8,128)S(1)} %collective-permute-done.10.refs_5_), channel_id=1, source_target_pairs={{0,2},{2,4},{4,6},{6,8},{8,10},{10,12},{12,14},{14,0},{1,3},{3,5},... | collective-permute-start | bytes 393224 | tf_op jit(solution)/shard_map/ppermute | solution.py:467
  131.3 10.7 %collective-permute-start.15 = (f32[256,128]{1,0:T(8,128)S(1)}, f32[256,128]{1,0:T(8,128)S(1)}, u32[]{:S(2)}, u32[]{:S(2)}) collective-permute-start(f32[256,128]{1,0:T(8,128)S(1)} %collective-permute-done.12.refs_7_), channel_id=1, source_target_pairs={{0,14},{2,0},{4,2},{6,4},{8,6},{10,8},{12,10},{14,12},{1,15},{3,1}... | collective-permute-start | bytes 393224 | tf_op jit(solution)/shard_map/ppermute | solution.py:467
  134.0 8.0 %collective-permute-start.7 = (f32[256,128]{1,0:T(8,128)S(1)}, f32[256,128]{1,0:T(8,128)S(1)}, u32[]{:S(2)}, u32[]{:S(2)}) collective-permute-start(f32[256,128]{1,0:T(8,128)S(1)} %collective-permute-done.6.refs_4_), channel_id=1, source_target_pairs={{0,2},{2,4},{4,6},{6,8},{8,10},{10,12},{12,14},{14,0},{1,3},{3,5},... | collective-permute-start | bytes 393224 | tf_op jit(solution)/shard_map/ppermute | solution.py:467
  135.8 8.3 %collective-permute-start.18 = (f32[256,128]{1,0:T(8,128)S(1)}, f32[256,128]{1,0:T(8,128)S(1)}, u32[]{:S(2)}, u32[]{:S(2)}) collective-permute-start(f32[256,128]{1,0:T(8,128)S(1)} %collective-permute-done.16.refs_6_), channel_id=1, source_target_pairs={{0,14},{2,0},{4,2},{6,4},{8,6},{10,8},{12,10},{14,12},{1,15},{3,1}... | collective-permute-start | bytes 393224 | tf_op jit(solution)/shard_map/ppermute | solution.py:467
  141.9 5.0 %collective-permute-start.17 = (f32[256,128]{1,0:T(8,128)S(1)}, f32[256,128]{1,0:T(8,128)S(1)}, u32[]{:S(2)}, u32[]{:S(2)}) collective-permute-start(f32[256,128]{1,0:T(8,128)S(1)} %collective-permute-done.15.refs_7_), channel_id=1, source_target_pairs={{0,14},{2,0},{4,2},{6,4},{8,6},{10,8},{12,10},{14,12},{1,15},{3,1}... | collective-permute-start | bytes 393224 | tf_op jit(solution)/shard_map/ppermute | solution.py:467
  142.0 6.3 %collective-permute-start.8 = (f32[256,128]{1,0:T(8,128)S(1)}, f32[256,128]{1,0:T(8,128)S(1)}, u32[]{:S(2)}, u32[]{:S(2)}) collective-permute-start(f32[256,128]{1,0:T(8,128)S(1)} %collective-permute-done.7.refs_4_), channel_id=1, source_target_pairs={{0,2},{2,4},{4,6},{6,8},{8,10},{10,12},{12,14},{14,0},{1,3},{3,5},... | collective-permute-start | bytes 393224 | tf_op jit(solution)/shard_map/ppermute | solution.py:467

commit v9 on v7

--- a/solution.py
+++ b/solution.py
@@ -50,11 +50,7 @@
     return jnp.where(used, target, rows_dev)
 
 
-def slot_kernel(
-    rows_dev, map_ref, grad, hot_ref, count_ref, rows_ref, out_ref, tally, held, natural, grad_ref, sems, sem
-):
-    load = pltpu.make_async_copy(grad, natural, sem)
-    load.start()
+def slot_kernel(rows_dev, map_ref, grad_ref, hot_ref, count_ref, rows_ref, out_ref, tally, held, sems):
     groups, span = map_ref.shape
     owners, _, cap = tally.shape
     per_owner = cap // LOW
@@ -84,8 +80,6 @@
         return carry
 
     lax.fori_loop(0, groups // batch, count, 0)
-    load.wait()
-    grad_ref[...] = natural[...].T
     depth, shares, height, lanes = held.shape
     columns = (height - EXTRA) * lanes // cap
 
@@ -113,27 +107,24 @@
         leave(owner).wait()
 
 
-def slot_sums(slots, grad, hot_slices, row_counts, unique_rows, shares, rows_dev):
+def slot_sums(slots, grad_t, hot_slices, row_counts, unique_rows, shares, rows_dev):
     _, owners, cap = unique_rows.shape
-    samples, columns = grad.shape
+    columns, samples = grad_t.shape
     height = columns // shares * cap // LANES + EXTRA
     depth = 4
     return pl.pallas_call(
         lambda *refs: slot_kernel(rows_dev, *refs),
         out_shape=jax.ShapeDtypeStruct((owners * shares, height, LANES), jnp.float32),
-        in_specs=[VMEM, ANY, SMEM, SMEM, VMEM],
+        in_specs=[VMEM, VMEM, SMEM, SMEM, VMEM],
         out_specs=HBM,
         scratch_shapes=[
             pltpu.VMEM((owners, samples, cap), jnp.bfloat16),
             pltpu.VMEM((depth, shares, height, LANES), jnp.float32),
-            pltpu.VMEM(grad.shape, grad.dtype),
-            pltpu.VMEM((columns, samples), grad.dtype),
             pltpu.SemaphoreType.DMA((depth,)),
-            pltpu.SemaphoreType.DMA,
         ],
         compiler_params=pltpu.CompilerParams(vmem_limit_bytes=50 << 20),
         name="slot_sums",
-    )(slots, grad, hot_slices, row_counts, unique_rows)
+    )(slots, grad_t, hot_slices, row_counts, unique_rows)
 
 
 def add_block(pieces, aims, start, out_ref, select):
@@ -459,7 +450,7 @@
     second_lines = moment_second.reshape(-1, LANES)
     slots = dedup_map.reshape(-1, GROUP * dedup_map.shape[1])
     slot_grad = slot_sums(
-        slots, upstream_grad, hots, row_counts, unique_rows, n_pair, rows_dev
+        slots, upstream_grad.T, hots, row_counts, unique_rows, n_pair, rows_dev
     )
     slot_grad, position, far_at, pair_at = lax.optimization_barrier(
         (slot_grad, position, far_at, pair_at)

time: 151 us -> 148 us (0.980)
  local copies, waits for them, and re-layouts: 5.07 us -> 3.24 us
    unnamed x17 -> x14, local copies, waits for them, and re-layouts: 4.21 us -> 2.38 us
where the time goes in v9:
time: 148 us
  blocking collectives  61 us (41%)
  Pallas kernels  38.8 us (26%)
  starting transfers between devices  28.4 us (19%)
  waiting for transfers between devices  14.4 us (10%)
  local copies, waits for them, and re-layouts  3.24 us (2%)
    all_to_all x1, blocking collectives, on_device(): lax.all_to_all(slot_grad, ('table', 'pair'), split_axis=0, concat_axis=0,...  61 us
    ppermute x13, starting transfers between devices, send(): lax.ppermute(value, axes, [(i, (i + step) % count) for i in range(count)])  23.8 us
    pallas_call x1, Pallas kernels, slot_sums(): pl.pallas_call(lambda *refs: slot_kernel(rows_dev, *refs), out_shape=jax....  12.7 us
    pallas_call x4, Pallas kernels, adam_blocks(): pl.pallas_call(lambda *refs: adam_kernel(groups, full_width, fetched is n...  10.8 us
    ppermute x13, waiting for transfers between devices, send(): lax.ppermute(value, axes, [(i, (i + step) % count) for i in range(count)])  9.86 us
    pallas_call x2, Pallas kernels, place_next(): pl.pallas_call(place_next_kernel, out_shape=tuple((jax.ShapeDtypeStruct((...  7.41 us
    all_to_all x1, starting transfers between devices, on_device(): lax.all_to_all(jnp.broadcast_to(own_squares[None], (n_all,) + own_squares...  4.61 us
    pallas_call x1, Pallas kernels, place_first(): pl.pallas_call(place_first_kernel, out_shape=(jax.ShapeDtypeStruct((2 * c...  4.52 us
  transfers between devices with their start and end apart: 14, of which 6 were waited for; matrix products, arithmetic and copies ran while one was open for 1% of the time, Pallas kernels for 13%

profile of v9, /device:TPU:2, one launch (start us, length us, event | category | flops | bytes accessed | tf_op | source)
XLA Modules:
  0.0 147.8 jit_solution(2187399664401249357)
XLA Ops:
  0.6 0.0 copy-start.3
  0.6 0.0 copy-start.2
  0.7 0.0 copy-start.1
  0.7 1.3 copy.20
  1.9 1.1 copy.19
  3.0 0.2 reshape.26.refs_0_
  3.2 0.0 copy-done.3
  3.2 0.0 copy-done.2
  3.2 0.0 copy-done.1
  3.3 12.7 %slot_sums.1 = f32[32,264,128]{2,1,0:T(8,128)} custom-call(s32[128,256]{1,0:T(8,128)S(1)} %reshape.26.refs_0_, bf16[256,1024]{1,0:T(8,128)(2,1)S(1)} %bitcast.18, s32[2,16]{1,0:T(2,128)S(1)} %bitcast.25, s32[1,16]{1,0:T(1,128)S(1)} %copy-done.3, s32[1,16,256]{2,1,0:T(8,128)S(1)} %copy-done.2), custom_call_target="tpu_custom_call" | custom-call | tf_op jit(solution)/shard_map/slot_sums/pallas_call | solution.py:115
  15.9 61.0 %all_to_all.10.got_ref = f32[32,264,128]{2,1,0:T(8,128)} all-to-all(f32[32,264,128]{2,1,0:T(8,128)} %slot_sums.1), channel_id=1, replica_groups=mesh['table'=16,'far'=4,'pair'=2,'col'=2] {'table','pair'}, dimensions={0} | all-to-all | bytes 8650752 | tf_op jit(solution)/shard_map/all_to_all | solution.py:458
  77.0 4.5 %place_first.1 = (bf16[256,8192]{1,0:T(8,128)(2,1)S(1)}, s32[8,8192]{1,0:T(8,128)S(1)}, f32[512,128]{1,0:T(8,128)S(1)}) custom-call(s32[1]{0:T(128)} %bitcast.6.start_ref, f32[32,264,128]{2,1,0:T(8,128)} %all_to_all.10.got_ref), custom_call_target="tpu_custom_call" | custom-call | flops 2147483648 | bytes 8388608 | tf_op jit(solution)/shard_map/place_first/pallas_call | solution.py:204
  81.5 0.0 copy-start.4
  81.5 5.5 %collective-permute-start.1 = (f32[256,128]{1,0:T(8,128)S(1)}, f32[256,128]{1,0:T(8,128)S(1)}, u32[]{:S(2)}, u32[]{:S(2)}) collective-permute-start(f32[256,128]{1,0:T(8,128)S(1)} %get-tuple-element.89), channel_id=1, source_target_pairs={{0,12},{4,0},{8,4},{12,8},{1,13},{5,1},{9,5},{13,9},{2,14},{6,2},{... | collective-permute-start | bytes 393224 | tf_op jit(solution)/shard_map/ppermute | solution.py:467
  87.0 0.0 collective-permute-start
  87.0 0.1 pad_add_fusion.start_ref
  87.1 5.1 %place_next.2 = (f32[512,128]{1,0:T(8,128)S(1)}, f32[512,128]{1,0:T(8,128)S(1)}) custom-call(s32[2]{0:T(128)S(1)} %pad_add_fusion.start_ref, bf16[256,8192]{1,0:T(8,128)(2,1)S(1)} %get-tuple-element.49.pieces, s32[8,8192]{1,0:T(8,128)S(1)} %get-tuple-element.50.aims), custom_call_target="tpu_custom_call" | custom-call | flops 4294967296 | bytes 8388608 | tf_op jit(solution)/shard_map/place_next/pallas_call | solution.py:227
  92.2 0.0 copy-done.4
  92.2 0.0 copy-start
  92.2 0.0 collective-permute-done.1
  92.2 2.8 %collective-permute-done = f32[256,128]{1,0:T(8,128)S(1)} collective-permute-done((f32[256,128]{1,0:T(8,128)S(1)}, f32[256,128]{1,0:T(8,128)S(1)}, u32[]{:S(2)}, u32[]{:S(2)}) %collective-permute-start) | collective-permute-done | bytes 131104 | tf_op jit(solution)/shard_map/ppermute | solution.py:467
  95.0 0.1 slice_add_fusion.1
  95.1 0.1 collective-permute-start.2
  95.2 4.1 %collective-permute-start.3 = (f32[512,128]{1,0:T(8,128)S(1)}, f32[512,128]{1,0:T(8,128)S(1)}, u32[]{:S(2)}, u32[]{:S(2)}) collective-permute-start(f32[512,128]{1,0:T(8,128)S(1)} %pad_maximum_fusion.1), channel_id=1, source_target_pairs={{0,12},{4,0},{8,4},{12,8},{1,13},{5,1},{9,5},{13,9},{2,14},{6,2},{... | collective-permute-start | bytes 786440 | tf_op jit(solution)/shard_map/ppermute | solution.py:467
  99.3 0.0 copy-done
  99.3 0.0 copy-start.5
  99.3 1.8 %parcel.1 = f32[264,256]{1,0:T(8,128)S(1)} custom-call(s32[1]{0:T(128)} %bitcast.7.where_ref.refs_2_, s32[2,16]{1,0:T(2,128)S(1)} %bitcast.26, f32[2048,256]{1,0:T(8,128)} %refs_8_.5, f32[2048,256]{1,0:T(8,128)} %refs_9_.7, f32[16,128]{1,0:T(8,128)S(1)} %bitcast.19), custom_call_target="tpu_custom_call" | custom-call | tf_op jit(solution)/shard_map/parcel/pallas_call | solution.py:418
  101.1 1.5 collective-permute-start.4
  102.6 0.0 copy-done.5
  102.6 2.4 %place_next.3 = f32[512,128]{1,0:T(8,128)S(1)} custom-call(s32[1]{0:T(128)} %bitcast.8.start_ref, bf16[256,8192]{1,0:T(8,128)(2,1)S(1)} %copy-done.5, s32[8,8192]{1,0:T(8,128)S(1)} %get-tuple-element.50.aims), custom_call_target="tpu_custom_call" | custom-call | flops 2147483648 | bytes 8388608 | tf_op jit(solution)/shard_map/place_next/pallas_call | solution.py:227
  104.9 4.4 %collective-permute-done.2 = f32[512,128]{1,0:T(8,128)S(1)} collective-permute-done((f32[512,128]{1,0:T(8,128)S(1)}, f32[512,128]{1,0:T(8,128)S(1)}, u32[]{:S(2)}, u32[]{:S(2)}) %collective-permute-start.2) | collective-permute-done | bytes 262176 | tf_op jit(solution)/shard_map/ppermute | solution.py:467
  109.4 0.0 collective-permute-done.3
  109.4 0.0 collective-permute-done.4.refs_7_.refs_6_.swapped
  109.4 2.9 %collective-permute-start.7 = (f32[512,128]{1,0:T(8,128)S(1)}, f32[512,128]{1,0:T(8,128)S(1)}, u32[]{:S(2)}, u32[]{:S(2)}) collective-permute-start(f32[512,128]{1,0:T(8,128)S(1)} %add_add_fusion.refs_4_), channel_id=1, source_target_pairs={{0,14},{2,0},{4,2},{6,4},{8,6},{10,8},{12,10},{14,12},{1,15},{3,1}... | collective-permute-start | bytes 786440 | tf_op jit(solution)/shard_map/ppermute | solution.py:467
  112.3 0.0 collective-permute-start.5
  112.3 0.1 and_select_fusion.4
  112.4 0.1 multiply_reduce_fusion
  112.5 0.6 broadcast_in_dim.2
  113.2 4.6 %all-to-all-start.1 = ((f32[16,8,128]{2,1,0:T(8,128)}), f32[16,8,128]{2,1,0:T(8,128)S(1)}, u32[]{:S(2)}, u32[]{:S(2)}) async-start(f32[16,8,128]{2,1,0:T(8,128)} %broadcast_in_dim.2), calls=%async_computation.1 | async-start | bytes 131072 | tf_op jit(solution)/shard_map/all_to_all | solution.py:489
  117.8 0.0 collective-permute-done.7.refs_6_
  117.8 3.2 %collective-permute-start.8 = (f32[512,128]{1,0:T(8,128)S(1)}, f32[512,128]{1,0:T(8,128)S(1)}, u32[]{:S(2)}, u32[]{:S(2)}) collective-permute-start(f32[512,128]{1,0:T(8,128)S(1)} %collective-permute-done.7.refs_6_), channel_id=1, source_target_pairs={{0,14},{2,0},{4,2},{6,4},{8,6},{10,8},{12,10},{14,12},{1,15},{3,1}... | collective-permute-start | bytes 786440 | tf_op jit(solution)/shard_map/ppermute | solution.py:467
  121.0 0.0 collective-permute-done.5.refs_5_
  121.0 0.0 collective-permute-start.6
  121.1 0.1 and_select_fusion.2
  121.1 4.5 %all-to-all-done.1.refs_8_.refs_7_ = f32[16,8,128]{2,1,0:T(8,128)S(1)} async-done(((f32[16,8,128]{2,1,0:T(8,128)}), f32[16,8,128]{2,1,0:T(8,128)S(1)}, u32[]{:S(2)}, u32[]{:S(2)}) %all-to-all-start.1) | async-done | bytes 65568 | tf_op jit(solution)/shard_map/all_to_all | solution.py:489
  125.7 3.0 %adam_blocks.4 = (f32[2048,256]{1,0:T(8,128)}, f32[2048,256]{1,0:T(8,128)}, f32[16,128]{1,0:T(8,128)S(1)}) custom-call(s32[3]{0:T(128)S(1)} %and_select_fusion.5.refs_0_, s32[3]{0:T(128)S(1)} %get-tuple-element.85.refs_1_, s32[1]{0:T(128)} %bitcast.7.where_ref.refs_2_, s32[2,16]{1,0:T(2,128)S(1)} %bitcast.27, f32[512,128]{1,0:T(8,128)S(1)} %add_add_fusion.refs_4_, ...), custom_call_target="tpu_custom_call" | custom-call | flops 1572864 | bytes 3932160 | tf_op jit(solution)/shard_map/adam_blocks/pallas_call | solution.py:360
  128.7 0.0 collective-permute-done.8.refs_5_
  128.7 1.8 %collective-permute-done.6.refs_4_ = f32[512,128]{1,0:T(8,128)S(1)} collective-permute-done((f32[512,128]{1,0:T(8,128)S(1)}, f32[512,128]{1,0:T(8,128)S(1)}, u32[]{:S(2)}, u32[]{:S(2)}) %collective-permute-start.6) | collective-permute-done | bytes 262176 | tf_op jit(solution)/shard_map/ppermute | solution.py:467
  130.5 0.0 collective-permute-start.9
  130.5 3.2 %collective-permute-start.10 = (f32[512,128]{1,0:T(8,128)S(1)}, f32[512,128]{1,0:T(8,128)S(1)}, u32[]{:S(2)}, u32[]{:S(2)}) collective-permute-start(f32[512,128]{1,0:T(8,128)S(1)} %collective-permute-done.8.refs_5_), channel_id=1, source_target_pairs={{0,14},{2,0},{4,2},{6,4},{8,6},{10,8},{12,10},{14,12},{1,15},{3,1}... | collective-permute-start | bytes 786440 | tf_op jit(solution)/shard_map/ppermute | solution.py:467
  133.8 0.1 and_select_fusion
  133.8 0.1 and_select_fusion.3.refs_0_
  133.9 1.6 %fetch_block.1.refs_12_ = f32[2,1,512,128]{3,2,1,0:T(8,128)S(1)} custom-call(s32[1]{0:T(128)S(6)} %select_n.97.row_ref.refs_0_, s32[1]{0:T(128)S(6)} %select_n.98.column_ref.refs_1_, s32[1]{0:T(128)} %bitcast.7.where_ref.refs_2_, s32[2,16]{1,0:T(2,128)S(1)} %bitcast.28, f32[264,256]{1,0:T(8,128)S(1)} %collective-permute-done.4.refs_7_.refs_6_.swapped, ...), custom_call_target="tpu_custom_call" | custom-call | tf_op jit(solution)/shard_map/fetch_block/pallas_call | solution.py:274
  135.5 2.8 %adam_blocks.5 = (f32[2048,256]{1,0:T(8,128)}, f32[2048,256]{1,0:T(8,128)}, f32[16,128]{1,0:T(8,128)S(1)}) custom-call(s32[2]{0:T(128)S(1)} %and_select_fusion.3.refs_0_, s32[2]{0:T(128)S(1)} %get-tuple-element.83.refs_1_, s32[1]{0:T(128)} %bitcast.7.where_ref.refs_2_, s32[2,16]{1,0:T(2,128)S(1)} %bitcast.29, ...), custom_call_target="tpu_custom_call", output_to_operand_aliasing={{0}: (12, {}), {1}: (13, {})} | custom-call | flops 1048576 | bytes 2621440 | tf_op jit(solution)/shard_map/adam_blocks/pallas_call | solution.py:360
  138.3 0.8 collective-permute-done.9.refs_4_
  139.1 0.0 collective-permute-done.10.refs_5_
  139.1 0.6 collective-permute-start.11
  139.7 2.7 %collective-permute-start.12 = (f32[256,128]{1,0:T(8,128)S(1)}, f32[256,128]{1,0:T(8,128)S(1)}, u32[]{:S(2)}, u32[]{:S(2)}) collective-permute-start(f32[256,128]{1,0:T(8,128)S(1)} %slice.31), channel_id=1, source_target_pairs={{0,14},{2,0},{4,2},{6,4},{8,6},{10,8},{12,10},{14,12},{1,15},{3,1}... | collective-permute-start | bytes 393224 | tf_op jit(solution)/shard_map/ppermute | solution.py:467
  142.5 0.1 and_select_fusion.1.refs_0_
  142.5 2.8 %adam_blocks.6 = (f32[2048,256]{1,0:T(8,128)}, f32[2048,256]{1,0:T(8,128)}, f32[16,128]{1,0:T(8,128)S(1)}) custom-call(s32[2]{0:T(128)S(1)} %and_select_fusion.1.refs_0_, s32[2]{0:T(128)S(1)} %get-tuple-element.81.refs_1_, s32[1]{0:T(128)} %bitcast.7.where_ref.refs_2_, s32[2,16]{1,0:T(2,128)S(1)} %bitcast.30, ...), custom_call_target="tpu_custom_call", output_to_operand_aliasing={{0}: (12, {}), {1}: (13, {})} | custom-call | flops 1048576 | bytes 2621440 | tf_op jit(solution)/shard_map/adam_blocks/pallas_call | solution.py:360
  145.3 0.1 collective-permute-done.11.refs_4_
  145.4 0.0 collective-permute-done.12.refs_5_
  145.4 2.2 %adam_blocks.7 = (f32[2048,256]{1,0:T(8,128)}, f32[2048,256]{1,0:T(8,128)}, f32[16,128]{1,0:T(8,128)}) custom-call(s32[1]{0:T(128)S(6)} %select_n.97.row_ref.refs_0_, s32[1]{0:T(128)S(6)} %select_n.98.column_ref.refs_1_, s32[1]{0:T(128)} %bitcast.7.where_ref.refs_2_, s32[2,16]{1,0:T(2,128)S(1)} %bitcast.31, ...), custom_call_target="tpu_custom_call", output_to_operand_aliasing={{0}: (13, {}), {1}: (14, {})} | custom-call | flops 524288 | bytes 1310720 | tf_op jit(solution)/shard_map/adam_blocks/pallas_call | solution.py:360
  (8 shorter events, 0.1 us)
Async XLA Ops:
  0.6 2.6 %copy-start.3 = (s32[1,16]{1,0:T(1,128)S(1)}, s32[1,16]{1,0:T(1,128)}, u32[]{:S(2)}) copy-start(s32[1,16]{1,0:T(1,128)} %refs_3_.1) | copy-start | bytes 196
  0.6 2.6 %copy-start.2 = (s32[1,16,256]{2,1,0:T(8,128)S(1)}, s32[1,16,256]{2,1,0:T(8,128)}, u32[]{:S(2)}) copy-start(s32[1,16,256]{2,1,0:T(8,128)} %refs_4_.1) | copy-start | bytes 49156
  0.7 2.6 %copy-start.1 = (s32[16,2]{0,1:T(2,128)S(1)}, s32[16,2]{0,1:T(2,128)}, u32[]{:S(2)}) copy-start(s32[16,2]{0,1:T(2,128)} %param.11) | copy-start | bytes 388
  81.5 10.7 %copy-start.4 = (bf16[256,8192]{1,0:T(8,128)(2,1)}, bf16[256,8192]{1,0:T(8,128)(2,1)S(1)}, u32[]{:S(2)}) copy-start(bf16[256,8192]{1,0:T(8,128)(2,1)S(1)} %get-tuple-element.49.pieces) | copy-start | bytes 12582916
  81.5 10.6 %collective-permute-start.1 = (f32[256,128]{1,0:T(8,128)S(1)}, f32[256,128]{1,0:T(8,128)S(1)}, u32[]{:S(2)}, u32[]{:S(2)}) collective-permute-start(f32[256,128]{1,0:T(8,128)S(1)} %get-tuple-element.89), channel_id=1, source_target_pairs={{0,12},{4,0},{8,4},{12,8},{1,13},{5,1},{9,5},{13,9},{2,14},{6,2},{... | collective-permute-start | bytes 393224 | tf_op jit(solution)/shard_map/ppermute | solution.py:467
  87.0 7.9 %collective-permute-start = (f32[256,128]{1,0:T(8,128)S(1)}, f32[256,128]{1,0:T(8,128)S(1)}, u32[]{:S(2)}, u32[]{:S(2)}) collective-permute-start(f32[256,128]{1,0:T(8,128)S(1)} %get-tuple-element.90), channel_id=1, source_target_pairs={{0,4},{4,8},{8,12},{12,0},{1,5},{5,9},{9,13},{13,1},{2,6},{6,10},{... | collective-permute-start | bytes 393224 | tf_op jit(solution)/shard_map/ppermute | solution.py:467
  92.2 7.1 %copy-start = (f32[2048]{0:T(1024)S(1)}, f32[2048]{0:T(1024)}, u32[]{:S(2)}) copy-start(f32[2048]{0:T(1024)} %param.10) | copy-start | bytes 24580
  95.1 14.3 %collective-permute-start.2 = (f32[512,128]{1,0:T(8,128)S(1)}, f32[512,128]{1,0:T(8,128)S(1)}, u32[]{:S(2)}, u32[]{:S(2)}) collective-permute-start(f32[512,128]{1,0:T(8,128)S(1)} %pad_maximum_fusion), channel_id=1, source_target_pairs={{0,4},{4,8},{8,12},{12,0},{1,5},{5,9},{9,13},{13,1},{2,6},{6,10},{... | collective-permute-start | bytes 786440 | tf_op jit(solution)/shard_map/ppermute | solution.py:467
  95.2 14.2 %collective-permute-start.3 = (f32[512,128]{1,0:T(8,128)S(1)}, f32[512,128]{1,0:T(8,128)S(1)}, u32[]{:S(2)}, u32[]{:S(2)}) collective-permute-start(f32[512,128]{1,0:T(8,128)S(1)} %pad_maximum_fusion.1), channel_id=1, source_target_pairs={{0,12},{4,0},{8,4},{12,8},{1,13},{5,1},{9,5},{13,9},{2,14},{6,2},{... | collective-permute-start | bytes 786440 | tf_op jit(solution)/shard_map/ppermute | solution.py:467
  99.3 3.3 %copy-start.5 = (bf16[256,8192]{1,0:T(8,128)(2,1)S(1)}, bf16[256,8192]{1,0:T(8,128)(2,1)}, u32[]{:S(2)}) copy-start(bf16[256,8192]{1,0:T(8,128)(2,1)} %copy-done.4) | copy-start | bytes 12582916
  101.1 8.3 %collective-permute-start.4 = (f32[264,256]{1,0:T(8,128)S(1)}, f32[264,256]{1,0:T(8,128)S(1)}, u32[]{:S(2)}, u32[]{:S(2)}) collective-permute-start(f32[264,256]{1,0:T(8,128)S(1)} %parcel.1), channel_id=1, source_target_pairs={{0,128},{16,144},{32,160},{48,176},{64,192},{80,208},{96,224},{112... | collective-permute-start | bytes 811016 | tf_op jit(solution)/shard_map/ppermute | solution.py:467
  109.4 8.4 %collective-permute-start.7 = (f32[512,128]{1,0:T(8,128)S(1)}, f32[512,128]{1,0:T(8,128)S(1)}, u32[]{:S(2)}, u32[]{:S(2)}) collective-permute-start(f32[512,128]{1,0:T(8,128)S(1)} %add_add_fusion.refs_4_), channel_id=1, source_target_pairs={{0,14},{2,0},{4,2},{6,4},{8,6},{10,8},{12,10},{14,12},{1,15},{3,1}... | collective-permute-start | bytes 786440 | tf_op jit(solution)/shard_map/ppermute | solution.py:467
  112.3 8.7 %collective-permute-start.5 = (f32[512,128]{1,0:T(8,128)S(1)}, f32[512,128]{1,0:T(8,128)S(1)}, u32[]{:S(2)}, u32[]{:S(2)}) collective-permute-start(f32[512,128]{1,0:T(8,128)S(1)} %add_add_fusion.refs_4_), channel_id=1, source_target_pairs={{0,2},{2,4},{4,6},{6,8},{8,10},{10,12},{12,14},{14,0},{1,3},{3,5},... | collective-permute-start | bytes 786440 | tf_op jit(solution)/shard_map/ppermute | solution.py:467
  113.2 12.5 %all-to-all-start.1 = ((f32[16,8,128]{2,1,0:T(8,128)}), f32[16,8,128]{2,1,0:T(8,128)S(1)}, u32[]{:S(2)}, u32[]{:S(2)}) async-start(f32[16,8,128]{2,1,0:T(8,128)} %broadcast_in_dim.2), calls=%async_computation.1 | async-start | bytes 131072 | tf_op jit(solution)/shard_map/all_to_all | solution.py:489
  117.8 10.9 %collective-permute-start.8 = (f32[512,128]{1,0:T(8,128)S(1)}, f32[512,128]{1,0:T(8,128)S(1)}, u32[]{:S(2)}, u32[]{:S(2)}) collective-permute-start(f32[512,128]{1,0:T(8,128)S(1)} %collective-permute-done.7.refs_6_), channel_id=1, source_target_pairs={{0,14},{2,0},{4,2},{6,4},{8,6},{10,8},{12,10},{14,12},{1,15},{3,1}... | collective-permute-start | bytes 786440 | tf_op jit(solution)/shard_map/ppermute | solution.py:467
  121.0 9.5 %collective-permute-start.6 = (f32[512,128]{1,0:T(8,128)S(1)}, f32[512,128]{1,0:T(8,128)S(1)}, u32[]{:S(2)}, u32[]{:S(2)}) collective-permute-start(f32[512,128]{1,0:T(8,128)S(1)} %collective-permute-done.5.refs_5_), channel_id=1, source_target_pairs={{0,2},{2,4},{4,6},{6,8},{8,10},{10,12},{12,14},{14,0},{1,3},{3,5},... | collective-permute-start | bytes 786440 | tf_op jit(solution)/shard_map/ppermute | solution.py:467
  130.5 8.6 %collective-permute-start.9 = (f32[512,128]{1,0:T(8,128)S(1)}, f32[512,128]{1,0:T(8,128)S(1)}, u32[]{:S(2)}, u32[]{:S(2)}) collective-permute-start(f32[512,128]{1,0:T(8,128)S(1)} %collective-permute-done.6.refs_4_), channel_id=1, source_target_pairs={{0,2},{2,4},{4,6},{6,8},{8,10},{10,12},{12,14},{14,0},{1,3},{3,5},... | collective-permute-start | bytes 786440 | tf_op jit(solution)/shard_map/ppermute | solution.py:467
  130.5 8.6 %collective-permute-start.10 = (f32[512,128]{1,0:T(8,128)S(1)}, f32[512,128]{1,0:T(8,128)S(1)}, u32[]{:S(2)}, u32[]{:S(2)}) collective-permute-start(f32[512,128]{1,0:T(8,128)S(1)} %collective-permute-done.8.refs_5_), channel_id=1, source_target_pairs={{0,14},{2,0},{4,2},{6,4},{8,6},{10,8},{12,10},{14,12},{1,15},{3,1}... | collective-permute-start | bytes 786440 | tf_op jit(solution)/shard_map/ppermute | solution.py:467
  139.1 6.3 %collective-permute-start.11 = (f32[256,128]{1,0:T(8,128)S(1)}, f32[256,128]{1,0:T(8,128)S(1)}, u32[]{:S(2)}, u32[]{:S(2)}) collective-permute-start(f32[256,128]{1,0:T(8,128)S(1)} %slice.30), channel_id=1, source_target_pairs={{0,2},{2,4},{4,6},{6,8},{8,10},{10,12},{12,14},{14,0},{1,3},{3,5},... | collective-permute-start | bytes 393224 | tf_op jit(solution)/shard_map/ppermute | solution.py:467
  139.7 5.7 %collective-permute-start.12 = (f32[256,128]{1,0:T(8,128)S(1)}, f32[256,128]{1,0:T(8,128)S(1)}, u32[]{:S(2)}, u32[]{:S(2)}) collective-permute-start(f32[256,128]{1,0:T(8,128)S(1)} %slice.31), channel_id=1, source_target_pairs={{0,14},{2,0},{4,2},{6,4},{8,6},{10,8},{12,10},{14,12},{1,15},{3,1}... | collective-permute-start | bytes 393224 | tf_op jit(solution)/shard_map/ppermute | solution.py:467

commit v10 on v9

--- a/solution.py
+++ b/solution.py
@@ -236,13 +236,11 @@
     )(starts, pieces, aims)
 
 
-def block_copies(table, first, held, sems, rows_at, columns_at, i, back):
+def block_copies(table, first, held, sems, rows_at, columns_at, i):
     rows, columns = held.shape[2:]
     at = pl.ds(pl.multiple_of(rows_at * rows, rows), rows)
     cut = pl.ds(pl.multiple_of(columns_at * columns, columns), columns)
     pairs = [(source.at[at, cut], held.at[which, i]) for which, source in enumerate((table, first))]
-    if back:
-        pairs = [(here, there) for there, here in pairs]
     return [pltpu.make_async_copy(a, b, sems.at[which, i]) for which, (a, b) in enumerate(pairs)]
 
 
@@ -262,9 +260,9 @@
 
 
 def fetch_kernel(row_ref, column_ref, where_ref, hots, swapped, table, first, held, sems):
-    for copy in block_copies(table, first, held, sems, row_ref[0], column_ref[0], 0, False):
+    for copy in block_copies(table, first, held, sems, row_ref[0], column_ref[0], 0):
         copy.start()
-    for copy in block_copies(table, first, held, sems, row_ref[0], column_ref[0], 0, False):
+    for copy in block_copies(table, first, held, sems, row_ref[0], column_ref[0], 0):
         copy.wait()
     put_swapped(where_ref, hots, swapped, held, row_ref[0], column_ref[0], 0)
 
@@ -293,10 +291,18 @@
     source = refs[10 + sum(groups)] if fetched else held
 
     def arrivals(i):
-        return block_copies(table, first, held, in_sem, row_ref[i], column_ref[i], i, False)
-
-    def returns(i):
-        return block_copies(out_table, out_first, held, out_sem, row_ref[i], column_ref[i], i, True)
+        return block_copies(table, first, held, in_sem, row_ref[i], column_ref[i], i)
+
+    def returns(i, line):
+        at = pl.ds(pl.multiple_of(row_ref[i] * rows + line * LANES, LANES), LANES)
+        cut = pl.ds(pl.multiple_of(column_ref[i] * columns, columns), columns)
+        here = pl.ds(line * LANES, LANES)
+        return [
+            pltpu.make_async_copy(
+                held.at[which, i, here], there.at[at, cut], out_sem.at[which, i * lines + line]
+            )
+            for which, there in enumerate((out_table, out_first))
+        ]
 
     if not fetched:
         for i in range(count):
@@ -340,12 +346,13 @@
                 weight = source[0, i, span, :] - moment * rate
                 held[1, i, span, :] = moment
                 held[0, i, span, :] = weight
+                for copy in returns(i, line):
+                    copy.start()
                 at += LANES
-        for copy in returns(i):
-            copy.start()
     for i in range(count):
-        for copy in returns(i):
-            copy.wait()
+        for line in range(lines):
+            for copy in returns(i, line):
+                copy.wait()
 
 
 def adam_blocks(rows_at, columns_at, parts, shape, full_width, common, before, held=None, fetched=None):
@@ -373,7 +380,7 @@
         scratch_shapes=[
             pltpu.VMEM((2, count) + shape, jnp.float32),
             pltpu.SemaphoreType.DMA((2, count)),
-            pltpu.SemaphoreType.DMA((2, count)),
+            pltpu.SemaphoreType.DMA((2, count * shape[0] // LANES)),
             pltpu.VMEM(second.shape, jnp.float32),
         ],
         input_output_aliases={n_in: 0, n_in + 1: 1} if kept else {},

time: 148 us -> 148 us (level)
  transfers between devices with their start and end apart: 14 -> 14, of which waited for: 6 -> 5; matrix products, arithmetic and copies ran while one was open for 1% -> 1% of each run, Pallas kernels for 13% -> 13%
where the time goes in v10:
time: 148 us
  blocking collectives  61 us (41%)
  Pallas kernels  39.1 us (26%)
  starting transfers between devices  28.4 us (19%)
  waiting for transfers between devices  14.1 us (10%)
  local copies, waits for them, and re-layouts  3.24 us (2%)
    all_to_all x1, blocking collectives, on_device(): lax.all_to_all(slot_grad, ('table', 'pair'), split_axis=0, concat_axis=0,...  61 us
    ppermute x13, starting transfers between devices, send(): lax.ppermute(value, axes, [(i, (i + step) % count) for i in range(count)])  23.8 us
    pallas_call x1, Pallas kernels, slot_sums(): pl.pallas_call(lambda *refs: slot_kernel(rows_dev, *refs), out_shape=jax....  12.7 us
    pallas_call x4, Pallas kernels, adam_blocks(): pl.pallas_call(lambda *refs: adam_kernel(groups, full_width, fetched is n...  11.1 us
    ppermute x13, waiting for transfers between devices, send(): lax.ppermute(value, axes, [(i, (i + step) % count) for i in range(count)])  9.6 us
    pallas_call x2, Pallas kernels, place_next(): pl.pallas_call(place_next_kernel, out_shape=tuple((jax.ShapeDtypeStruct((...  7.41 us
    all_to_all x1, starting transfers between devices, on_device(): lax.all_to_all(jnp.broadcast_to(own_squares[None], (n_all,) + own_squares...  4.61 us
    pallas_call x1, Pallas kernels, place_first(): pl.pallas_call(place_first_kernel, out_shape=(jax.ShapeDtypeStruct((2 * c...  4.52 us
  transfers between devices with their start and end apart: 14, of which 5 were waited for; matrix products, arithmetic and copies ran while one was open for 1% of the time, Pallas kernels for 13%

profile of v10, /device:TPU:2, one launch (start us, length us, event | category | flops | bytes accessed | tf_op | source)
XLA Modules:
  0.0 147.8 jit_solution(9710820985592994701)
XLA Ops:
  0.6 0.0 copy-start.3
  0.6 0.0 copy-start.2
  0.7 0.0 copy-start.1
  0.7 1.3 copy.20
  1.9 1.1 copy.19
  3.0 0.2 reshape.26.refs_0_
  3.2 0.0 copy-done.3
  3.2 0.0 copy-done.2
  3.2 0.0 copy-done.1
  3.3 12.7 %slot_sums.1 = f32[32,264,128]{2,1,0:T(8,128)} custom-call(s32[128,256]{1,0:T(8,128)S(1)} %reshape.26.refs_0_, bf16[256,1024]{1,0:T(8,128)(2,1)S(1)} %bitcast.18, s32[2,16]{1,0:T(2,128)S(1)} %bitcast.25, s32[1,16]{1,0:T(1,128)S(1)} %copy-done.3, s32[1,16,256]{2,1,0:T(8,128)S(1)} %copy-done.2), custom_call_target="tpu_custom_call" | custom-call | tf_op jit(solution)/shard_map/slot_sums/pallas_call | solution.py:115
  15.9 61.0 %all_to_all.10.got_ref = f32[32,264,128]{2,1,0:T(8,128)} all-to-all(f32[32,264,128]{2,1,0:T(8,128)} %slot_sums.1), channel_id=1, replica_groups=mesh['table'=16,'far'=4,'pair'=2,'col'=2] {'table','pair'}, dimensions={0} | all-to-all | bytes 8650752 | tf_op jit(solution)/shard_map/all_to_all | solution.py:465
  77.0 4.5 %place_first.1 = (bf16[256,8192]{1,0:T(8,128)(2,1)S(1)}, s32[8,8192]{1,0:T(8,128)S(1)}, f32[512,128]{1,0:T(8,128)S(1)}) custom-call(s32[1]{0:T(128)} %bitcast.6.start_ref, f32[32,264,128]{2,1,0:T(8,128)} %all_to_all.10.got_ref), custom_call_target="tpu_custom_call" | custom-call | flops 2147483648 | bytes 8388608 | tf_op jit(solution)/shard_map/place_first/pallas_call | solution.py:204
  81.5 0.0 copy-start.4
  81.5 5.5 %collective-permute-start.1 = (f32[256,128]{1,0:T(8,128)S(1)}, f32[256,128]{1,0:T(8,128)S(1)}, u32[]{:S(2)}, u32[]{:S(2)}) collective-permute-start(f32[256,128]{1,0:T(8,128)S(1)} %get-tuple-element.89), channel_id=1, source_target_pairs={{0,12},{4,0},{8,4},{12,8},{1,13},{5,1},{9,5},{13,9},{2,14},{6,2},{... | collective-permute-start | bytes 393224 | tf_op jit(solution)/shard_map/ppermute | solution.py:474
  87.0 0.0 collective-permute-start
  87.0 0.1 pad_add_fusion.start_ref
  87.1 5.1 %place_next.2 = (f32[512,128]{1,0:T(8,128)S(1)}, f32[512,128]{1,0:T(8,128)S(1)}) custom-call(s32[2]{0:T(128)S(1)} %pad_add_fusion.start_ref, bf16[256,8192]{1,0:T(8,128)(2,1)S(1)} %get-tuple-element.49.pieces, s32[8,8192]{1,0:T(8,128)S(1)} %get-tuple-element.50.aims), custom_call_target="tpu_custom_call" | custom-call | flops 4294967296 | bytes 8388608 | tf_op jit(solution)/shard_map/place_next/pallas_call | solution.py:227
  92.2 0.0 copy-done.4
  92.2 0.0 copy-start
  92.2 0.0 collective-permute-done.1
  92.2 2.8 %collective-permute-done = f32[256,128]{1,0:T(8,128)S(1)} collective-permute-done((f32[256,128]{1,0:T(8,128)S(1)}, f32[256,128]{1,0:T(8,128)S(1)}, u32[]{:S(2)}, u32[]{:S(2)}) %collective-permute-start) | collective-permute-done | bytes 131104 | tf_op jit(solution)/shard_map/ppermute | solution.py:474
  95.0 0.1 slice_add_fusion.1
  95.1 0.1 collective-permute-start.2
  95.2 4.1 %collective-permute-start.3 = (f32[512,128]{1,0:T(8,128)S(1)}, f32[512,128]{1,0:T(8,128)S(1)}, u32[]{:S(2)}, u32[]{:S(2)}) collective-permute-start(f32[512,128]{1,0:T(8,128)S(1)} %pad_maximum_fusion.1), channel_id=1, source_target_pairs={{0,12},{4,0},{8,4},{12,8},{1,13},{5,1},{9,5},{13,9},{2,14},{6,2},{... | collective-permute-start | bytes 786440 | tf_op jit(solution)/shard_map/ppermute | solution.py:474
  99.3 0.0 copy-done
  99.3 0.0 copy-start.5
  99.3 1.8 %parcel.1 = f32[264,256]{1,0:T(8,128)S(1)} custom-call(s32[1]{0:T(128)} %bitcast.7.where_ref.refs_2_, s32[2,16]{1,0:T(2,128)S(1)} %bitcast.26, f32[2048,256]{1,0:T(8,128)} %refs_8_.5, f32[2048,256]{1,0:T(8,128)} %refs_9_.7, f32[16,128]{1,0:T(8,128)S(1)} %bitcast.19), custom_call_target="tpu_custom_call" | custom-call | tf_op jit(solution)/shard_map/parcel/pallas_call | solution.py:425
  101.1 1.5 collective-permute-start.4
  102.6 0.0 copy-done.5
  102.6 2.4 %place_next.3 = f32[512,128]{1,0:T(8,128)S(1)} custom-call(s32[1]{0:T(128)} %bitcast.8.start_ref, bf16[256,8192]{1,0:T(8,128)(2,1)S(1)} %copy-done.5, s32[8,8192]{1,0:T(8,128)S(1)} %get-tuple-element.50.aims), custom_call_target="tpu_custom_call" | custom-call | flops 2147483648 | bytes 8388608 | tf_op jit(solution)/shard_map/place_next/pallas_call | solution.py:227
  104.9 4.4 %collective-permute-done.2 = f32[512,128]{1,0:T(8,128)S(1)} collective-permute-done((f32[512,128]{1,0:T(8,128)S(1)}, f32[512,128]{1,0:T(8,128)S(1)}, u32[]{:S(2)}, u32[]{:S(2)}) %collective-permute-start.2) | collective-permute-done | bytes 262176 | tf_op jit(solution)/shard_map/ppermute | solution.py:474
  109.4 0.0 collective-permute-done.3
  109.4 0.0 collective-permute-done.4.refs_7_.refs_6_.swapped
  109.4 2.9 %collective-permute-start.7 = (f32[512,128]{1,0:T(8,128)S(1)}, f32[512,128]{1,0:T(8,128)S(1)}, u32[]{:S(2)}, u32[]{:S(2)}) collective-permute-start(f32[512,128]{1,0:T(8,128)S(1)} %add_add_fusion.refs_4_), channel_id=1, source_target_pairs={{0,14},{2,0},{4,2},{6,4},{8,6},{10,8},{12,10},{14,12},{1,15},{3,1}... | collective-permute-start | bytes 786440 | tf_op jit(solution)/shard_map/ppermute | solution.py:474
  112.3 0.0 collective-permute-start.5
  112.3 0.1 and_select_fusion.4
  112.4 0.1 multiply_reduce_fusion
  112.5 0.6 broadcast_in_dim.2
  113.2 4.6 %all-to-all-start.1 = ((f32[16,8,128]{2,1,0:T(8,128)}), f32[16,8,128]{2,1,0:T(8,128)S(1)}, u32[]{:S(2)}, u32[]{:S(2)}) async-start(f32[16,8,128]{2,1,0:T(8,128)} %broadcast_in_dim.2), calls=%async_computation.1 | async-start | bytes 131072 | tf_op jit(solution)/shard_map/all_to_all | solution.py:496
  117.8 0.0 collective-permute-done.7.refs_6_
  117.8 3.2 %collective-permute-start.8 = (f32[512,128]{1,0:T(8,128)S(1)}, f32[512,128]{1,0:T(8,128)S(1)}, u32[]{:S(2)}, u32[]{:S(2)}) collective-permute-start(f32[512,128]{1,0:T(8,128)S(1)} %collective-permute-done.7.refs_6_), channel_id=1, source_target_pairs={{0,14},{2,0},{4,2},{6,4},{8,6},{10,8},{12,10},{14,12},{1,15},{3,1}... | collective-permute-start | bytes 786440 | tf_op jit(solution)/shard_map/ppermute | solution.py:474
  121.0 0.0 collective-permute-done.5.refs_5_
  121.0 0.0 collective-permute-start.6
  121.1 0.1 and_select_fusion.2
  121.1 4.5 %all-to-all-done.1.refs_8_.refs_7_ = f32[16,8,128]{2,1,0:T(8,128)S(1)} async-done(((f32[16,8,128]{2,1,0:T(8,128)}), f32[16,8,128]{2,1,0:T(8,128)S(1)}, u32[]{:S(2)}, u32[]{:S(2)}) %all-to-all-start.1) | async-done | bytes 65568 | tf_op jit(solution)/shard_map/all_to_all | solution.py:496
  125.7 3.2 %adam_blocks.4 = (f32[2048,256]{1,0:T(8,128)}, f32[2048,256]{1,0:T(8,128)}, f32[16,128]{1,0:T(8,128)S(1)}) custom-call(s32[3]{0:T(128)S(1)} %and_select_fusion.5.refs_0_, s32[3]{0:T(128)S(1)} %get-tuple-element.85.refs_1_, s32[1]{0:T(128)} %bitcast.7.where_ref.refs_2_, s32[2,16]{1,0:T(2,128)S(1)} %bitcast.27, f32[512,128]{1,0:T(8,128)S(1)} %add_add_fusion.refs_4_, ...), custom_call_target="tpu_custom_call" | custom-call | flops 1572864 | bytes 3932160 | tf_op jit(solution)/shard_map/adam_blocks/pallas_call | solution.py:367
  128.8 0.0 collective-permute-done.8.refs_5_
  128.8 1.7 %collective-permute-done.6.refs_4_ = f32[512,128]{1,0:T(8,128)S(1)} collective-permute-done((f32[512,128]{1,0:T(8,128)S(1)}, f32[512,128]{1,0:T(8,128)S(1)}, u32[]{:S(2)}, u32[]{:S(2)}) %collective-permute-start.6) | collective-permute-done | bytes 262176 | tf_op jit(solution)/shard_map/ppermute | solution.py:474
  130.5 0.0 collective-permute-start.9
  130.5 3.2 %collective-permute-start.10 = (f32[512,128]{1,0:T(8,128)S(1)}, f32[512,128]{1,0:T(8,128)S(1)}, u32[]{:S(2)}, u32[]{:S(2)}) collective-permute-start(f32[512,128]{1,0:T(8,128)S(1)} %collective-permute-done.8.refs_5_), channel_id=1, source_target_pairs={{0,14},{2,0},{4,2},{6,4},{8,6},{10,8},{12,10},{14,12},{1,15},{3,1}... | collective-permute-start | bytes 786440 | tf_op jit(solution)/shard_map/ppermute | solution.py:474
  133.8 0.1 and_select_fusion
  133.8 0.1 and_select_fusion.3.refs_0_
  133.9 1.6 %fetch_block.1.refs_12_ = f32[2,1,512,128]{3,2,1,0:T(8,128)S(1)} custom-call(s32[1]{0:T(128)S(6)} %select_n.97.row_ref.refs_0_, s32[1]{0:T(128)S(6)} %select_n.98.column_ref.refs_1_, s32[1]{0:T(128)} %bitcast.7.where_ref.refs_2_, s32[2,16]{1,0:T(2,128)S(1)} %bitcast.28, f32[264,256]{1,0:T(8,128)S(1)} %collective-permute-done.4.refs_7_.refs_6_.swapped, ...), custom_call_target="tpu_custom_call" | custom-call | tf_op jit(solution)/shard_map/fetch_block/pallas_call | solution.py:272
  135.5 2.9 %adam_blocks.5 = (f32[2048,256]{1,0:T(8,128)}, f32[2048,256]{1,0:T(8,128)}, f32[16,128]{1,0:T(8,128)S(1)}) custom-call(s32[2]{0:T(128)S(1)} %and_select_fusion.3.refs_0_, s32[2]{0:T(128)S(1)} %get-tuple-element.83.refs_1_, s32[1]{0:T(128)} %bitcast.7.where_ref.refs_2_, s32[2,16]{1,0:T(2,128)S(1)} %bitcast.29, ...), custom_call_target="tpu_custom_call", output_to_operand_aliasing={{0}: (12, {}), {1}: (13, {})} | custom-call | flops 1048576 | bytes 2621440 | tf_op jit(solution)/shard_map/adam_blocks/pallas_call | solution.py:367
  138.4 0.7 collective-permute-done.9.refs_4_
  139.1 0.0 collective-permute-done.10.refs_5_
  139.1 0.6 collective-permute-start.11
  139.7 2.7 %collective-permute-start.12 = (f32[256,128]{1,0:T(8,128)S(1)}, f32[256,128]{1,0:T(8,128)S(1)}, u32[]{:S(2)}, u32[]{:S(2)}) collective-permute-start(f32[256,128]{1,0:T(8,128)S(1)} %slice.31), channel_id=1, source_target_pairs={{0,14},{2,0},{4,2},{6,4},{8,6},{10,8},{12,10},{14,12},{1,15},{3,1}... | collective-permute-start | bytes 393224 | tf_op jit(solution)/shard_map/ppermute | solution.py:474
  142.5 0.1 and_select_fusion.1.refs_0_
  142.5 2.9 %adam_blocks.6 = (f32[2048,256]{1,0:T(8,128)}, f32[2048,256]{1,0:T(8,128)}, f32[16,128]{1,0:T(8,128)S(1)}) custom-call(s32[2]{0:T(128)S(1)} %and_select_fusion.1.refs_0_, s32[2]{0:T(128)S(1)} %get-tuple-element.81.refs_1_, s32[1]{0:T(128)} %bitcast.7.where_ref.refs_2_, s32[2,16]{1,0:T(2,128)S(1)} %bitcast.30, ...), custom_call_target="tpu_custom_call", output_to_operand_aliasing={{0}: (12, {}), {1}: (13, {})} | custom-call | flops 1048576 | bytes 2621440 | tf_op jit(solution)/shard_map/adam_blocks/pallas_call | solution.py:367
  145.4 0.0 collective-permute-done.11.refs_4_
  145.4 0.0 collective-permute-done.12.refs_5_
  145.4 2.2 %adam_blocks.7 = (f32[2048,256]{1,0:T(8,128)}, f32[2048,256]{1,0:T(8,128)}, f32[16,128]{1,0:T(8,128)}) custom-call(s32[1]{0:T(128)S(6)} %select_n.97.row_ref.refs_0_, s32[1]{0:T(128)S(6)} %select_n.98.column_ref.refs_1_, s32[1]{0:T(128)} %bitcast.7.where_ref.refs_2_, s32[2,16]{1,0:T(2,128)S(1)} %bitcast.31, ...), custom_call_target="tpu_custom_call", output_to_operand_aliasing={{0}: (13, {}), {1}: (14, {})} | custom-call | flops 524288 | bytes 1310720 | tf_op jit(solution)/shard_map/adam_blocks/pallas_call | solution.py:367
  (8 shorter events, 0.1 us)
Async XLA Ops:
  0.6 2.6 %copy-start.3 = (s32[1,16]{1,0:T(1,128)S(1)}, s32[1,16]{1,0:T(1,128)}, u32[]{:S(2)}) copy-start(s32[1,16]{1,0:T(1,128)} %refs_3_.1) | copy-start | bytes 196
  0.6 2.6 %copy-start.2 = (s32[1,16,256]{2,1,0:T(8,128)S(1)}, s32[1,16,256]{2,1,0:T(8,128)}, u32[]{:S(2)}) copy-start(s32[1,16,256]{2,1,0:T(8,128)} %refs_4_.1) | copy-start | bytes 49156
  0.7 2.6 %copy-start.1 = (s32[16,2]{0,1:T(2,128)S(1)}, s32[16,2]{0,1:T(2,128)}, u32[]{:S(2)}) copy-start(s32[16,2]{0,1:T(2,128)} %param.11) | copy-start | bytes 388
  81.5 10.7 %copy-start.4 = (bf16[256,8192]{1,0:T(8,128)(2,1)}, bf16[256,8192]{1,0:T(8,128)(2,1)S(1)}, u32[]{:S(2)}) copy-start(bf16[256,8192]{1,0:T(8,128)(2,1)S(1)} %get-tuple-element.49.pieces) | copy-start | bytes 12582916
  81.5 10.6 %collective-permute-start.1 = (f32[256,128]{1,0:T(8,128)S(1)}, f32[256,128]{1,0:T(8,128)S(1)}, u32[]{:S(2)}, u32[]{:S(2)}) collective-permute-start(f32[256,128]{1,0:T(8,128)S(1)} %get-tuple-element.89), channel_id=1, source_target_pairs={{0,12},{4,0},{8,4},{12,8},{1,13},{5,1},{9,5},{13,9},{2,14},{6,2},{... | collective-permute-start | bytes 393224 | tf_op jit(solution)/shard_map/ppermute | solution.py:474
  87.0 7.9 %collective-permute-start = (f32[256,128]{1,0:T(8,128)S(1)}, f32[256,128]{1,0:T(8,128)S(1)}, u32[]{:S(2)}, u32[]{:S(2)}) collective-permute-start(f32[256,128]{1,0:T(8,128)S(1)} %get-tuple-element.90), channel_id=1, source_target_pairs={{0,4},{4,8},{8,12},{12,0},{1,5},{5,9},{9,13},{13,1},{2,6},{6,10},{... | collective-permute-start | bytes 393224 | tf_op jit(solution)/shard_map/ppermute | solution.py:474
  92.2 7.1 %copy-start = (f32[2048]{0:T(1024)S(1)}, f32[2048]{0:T(1024)}, u32[]{:S(2)}) copy-start(f32[2048]{0:T(1024)} %param.10) | copy-start | bytes 24580
  95.1 14.3 %collective-permute-start.2 = (f32[512,128]{1,0:T(8,128)S(1)}, f32[512,128]{1,0:T(8,128)S(1)}, u32[]{:S(2)}, u32[]{:S(2)}) collective-permute-start(f32[512,128]{1,0:T(8,128)S(1)} %pad_maximum_fusion), channel_id=1, source_target_pairs={{0,4},{4,8},{8,12},{12,0},{1,5},{5,9},{9,13},{13,1},{2,6},{6,10},{... | collective-permute-start | bytes 786440 | tf_op jit(solution)/shard_map/ppermute | solution.py:474
  95.2 14.2 %collective-permute-start.3 = (f32[512,128]{1,0:T(8,128)S(1)}, f32[512,128]{1,0:T(8,128)S(1)}, u32[]{:S(2)}, u32[]{:S(2)}) collective-permute-start(f32[512,128]{1,0:T(8,128)S(1)} %pad_maximum_fusion.1), channel_id=1, source_target_pairs={{0,12},{4,0},{8,4},{12,8},{1,13},{5,1},{9,5},{13,9},{2,14},{6,2},{... | collective-permute-start | bytes 786440 | tf_op jit(solution)/shard_map/ppermute | solution.py:474
  99.3 3.3 %copy-start.5 = (bf16[256,8192]{1,0:T(8,128)(2,1)S(1)}, bf16[256,8192]{1,0:T(8,128)(2,1)}, u32[]{:S(2)}) copy-start(bf16[256,8192]{1,0:T(8,128)(2,1)} %copy-done.4) | copy-start | bytes 12582916
  101.1 8.3 %collective-permute-start.4 = (f32[264,256]{1,0:T(8,128)S(1)}, f32[264,256]{1,0:T(8,128)S(1)}, u32[]{:S(2)}, u32[]{:S(2)}) collective-permute-start(f32[264,256]{1,0:T(8,128)S(1)} %parcel.1), channel_id=1, source_target_pairs={{0,128},{16,144},{32,160},{48,176},{64,192},{80,208},{96,224},{112... | collective-permute-start | bytes 811016 | tf_op jit(solution)/shard_map/ppermute | solution.py:474
  109.4 8.4 %collective-permute-start.7 = (f32[512,128]{1,0:T(8,128)S(1)}, f32[512,128]{1,0:T(8,128)S(1)}, u32[]{:S(2)}, u32[]{:S(2)}) collective-permute-start(f32[512,128]{1,0:T(8,128)S(1)} %add_add_fusion.refs_4_), channel_id=1, source_target_pairs={{0,14},{2,0},{4,2},{6,4},{8,6},{10,8},{12,10},{14,12},{1,15},{3,1}... | collective-permute-start | bytes 786440 | tf_op jit(solution)/shard_map/ppermute | solution.py:474
  112.3 8.7 %collective-permute-start.5 = (f32[512,128]{1,0:T(8,128)S(1)}, f32[512,128]{1,0:T(8,128)S(1)}, u32[]{:S(2)}, u32[]{:S(2)}) collective-permute-start(f32[512,128]{1,0:T(8,128)S(1)} %add_add_fusion.refs_4_), channel_id=1, source_target_pairs={{0,2},{2,4},{4,6},{6,8},{8,10},{10,12},{12,14},{14,0},{1,3},{3,5},... | collective-permute-start | bytes 786440 | tf_op jit(solution)/shard_map/ppermute | solution.py:474
  113.2 12.5 %all-to-all-start.1 = ((f32[16,8,128]{2,1,0:T(8,128)}), f32[16,8,128]{2,1,0:T(8,128)S(1)}, u32[]{:S(2)}, u32[]{:S(2)}) async-start(f32[16,8,128]{2,1,0:T(8,128)} %broadcast_in_dim.2), calls=%async_computation.1 | async-start | bytes 131072 | tf_op jit(solution)/shard_map/all_to_all | solution.py:496
  117.8 11.0 %collective-permute-start.8 = (f32[512,128]{1,0:T(8,128)S(1)}, f32[512,128]{1,0:T(8,128)S(1)}, u32[]{:S(2)}, u32[]{:S(2)}) collective-permute-start(f32[512,128]{1,0:T(8,128)S(1)} %collective-permute-done.7.refs_6_), channel_id=1, source_target_pairs={{0,14},{2,0},{4,2},{6,4},{8,6},{10,8},{12,10},{14,12},{1,15},{3,1}... | collective-permute-start | bytes 786440 | tf_op jit(solution)/shard_map/ppermute | solution.py:474
  121.0 9.5 %collective-permute-start.6 = (f32[512,128]{1,0:T(8,128)S(1)}, f32[512,128]{1,0:T(8,128)S(1)}, u32[]{:S(2)}, u32[]{:S(2)}) collective-permute-start(f32[512,128]{1,0:T(8,128)S(1)} %collective-permute-done.5.refs_5_), channel_id=1, source_target_pairs={{0,2},{2,4},{4,6},{6,8},{8,10},{10,12},{12,14},{14,0},{1,3},{3,5},... | collective-permute-start | bytes 786440 | tf_op jit(solution)/shard_map/ppermute | solution.py:474
  130.5 8.6 %collective-permute-start.9 = (f32[512,128]{1,0:T(8,128)S(1)}, f32[512,128]{1,0:T(8,128)S(1)}, u32[]{:S(2)}, u32[]{:S(2)}) collective-permute-start(f32[512,128]{1,0:T(8,128)S(1)} %collective-permute-done.6.refs_4_), channel_id=1, source_target_pairs={{0,2},{2,4},{4,6},{6,8},{8,10},{10,12},{12,14},{14,0},{1,3},{3,5},... | collective-permute-start | bytes 786440 | tf_op jit(solution)/shard_map/ppermute | solution.py:474
  130.5 8.6 %collective-permute-start.10 = (f32[512,128]{1,0:T(8,128)S(1)}, f32[512,128]{1,0:T(8,128)S(1)}, u32[]{:S(2)}, u32[]{:S(2)}) collective-permute-start(f32[512,128]{1,0:T(8,128)S(1)} %collective-permute-done.8.refs_5_), channel_id=1, source_target_pairs={{0,14},{2,0},{4,2},{6,4},{8,6},{10,8},{12,10},{14,12},{1,15},{3,1}... | collective-permute-start | bytes 786440 | tf_op jit(solution)/shard_map/ppermute | solution.py:474
  139.1 6.3 %collective-permute-start.11 = (f32[256,128]{1,0:T(8,128)S(1)}, f32[256,128]{1,0:T(8,128)S(1)}, u32[]{:S(2)}, u32[]{:S(2)}) collective-permute-start(f32[256,128]{1,0:T(8,128)S(1)} %slice.30), channel_id=1, source_target_pairs={{0,2},{2,4},{4,6},{6,8},{8,10},{10,12},{12,14},{14,0},{1,3},{3,5},... | collective-permute-start | bytes 393224 | tf_op jit(solution)/shard_map/ppermute | solution.py:474
  139.7 5.7 %collective-permute-start.12 = (f32[256,128]{1,0:T(8,128)S(1)}, f32[256,128]{1,0:T(8,128)S(1)}, u32[]{:S(2)}, u32[]{:S(2)}) collective-permute-start(f32[256,128]{1,0:T(8,128)S(1)} %slice.31), channel_id=1, source_target_pairs={{0,14},{2,0},{4,2},{6,4},{8,6},{10,8},{12,10},{14,12},{1,15},{3,1}... | collective-permute-start | bytes 393224 | tf_op jit(solution)/shard_map/ppermute | solution.py:474
